TPU v7x, 256 devices: a whole 4x4x8 slice. The times are simulated.
256 devices in a mesh: row: 32 (over z, y), col: 8 (over x, core).
Axes of the slice: x: 4, y: 4, z: 8, core: 2. Of those that a mesh axis runs over, the one named last changes fastest.
Arguments:
- positions: float32 [16, 3, 131072], P(None, None, 'row'), may hold values from -4 to 4
- vectors: float32 [8, 131072], P(None, 'row'), may hold values from -6 to 6
- pairs: int32 [32, 8, 10, 2], P('row', 'col'), may hold values from 0 to 31, as said below
- valid: int32 [32, 8, 10], P('row', 'col'), may hold values from 0 to 1, as said below
Outputs:
- leading: float32 [8, 131072], P(None, 'row')
Inputs may be any that keep to these rules, and one draw needn't show every extreme that they name: Live slots of a cell come first and name distinct tile pairs with I <= J; no unordered pair of tiles is listed twice in the whole list; padding slots hold 0 0. a < 8, b < 32. `valid`: at most 10 live slots a cell, and some cell has all 10 live.
All inputs are finite; a program needn't handle non-finite values.
Results may differ from a plain program's by a relative error of at most 0.0003.
Values sent between devices are 32-bit elements; how exact they have to be, the bound alone decides.
No kernel may reach another device: no remote copies, remote signals or barrier semaphores. Data moves between devices by JAX's collectives and lax.ppermute only.
A program may use at most 128 MiB of HBM per device.

v0:
```python
import jax
import jax.numpy as jnp
from jax import lax
from jax.sharding import PartitionSpec as P

TILE = 512


def form_tile(row_part, col_part):
    total = jnp.zeros((row_part.shape[2], col_part.shape[2]), jnp.float32)
    for snapshot in range(row_part.shape[0]):
        distance = jnp.zeros_like(total)
        for component in range(3):
            spacing = (
                row_part[snapshot, component][:, None] - col_part[snapshot, component][None, :]
            )
            distance = distance + spacing * spacing
        total = total + jnp.exp(-0.5 * distance)
    return total


def gather_sets(pos_part, vec_part):
    return (
        lax.all_gather(pos_part, "row", axis=2, tiled=True),
        lax.all_gather(vec_part, "row", axis=1, tiled=True),
    )


def spread_pieces(piece):
    return lax.all_gather(piece, "col", axis=1, tiled=True)


def combine(row_acc, col_acc):
    col_share = lax.psum_scatter(col_acc, "row", scatter_dimension=1, tiled=True)
    return lax.psum(row_acc, "col") + spread_pieces(col_share)


def per_device(positions, vectors, pairs, valid):
    grid_row = lax.axis_index("row")
    grid_col = lax.axis_index("col")
    block = positions.shape[2]
    share = block // lax.axis_size("col")
    row_tiles = block // TILE
    share_tiles = share // TILE
    slot_count = pairs.shape[2]
    local_rows = pairs[0, 0, :, 0]
    local_cols = pairs[0, 0, :, 1]
    weights = valid[0, 0].astype(jnp.float32)
    row_global = grid_row * row_tiles + local_rows
    col_global = (
        local_cols // share_tiles * row_tiles + grid_col * share_tiles + local_cols % share_tiles
    )
    crossing = jnp.where(row_global != col_global, 1.0, 0.0).astype(jnp.float32)
    own_pos = lax.dynamic_slice_in_dim(positions, grid_col * share, share, 2)

    def make_tiles(col_pos):
        formed = []
        for slot in range(slot_count):
            row_part = lax.dynamic_slice_in_dim(positions, local_rows[slot] * TILE, TILE, 2)
            col_part = lax.dynamic_slice_in_dim(col_pos, local_cols[slot] * TILE, TILE, 2)
            formed.append(form_tile(row_part, col_part) * weights[slot])
        return formed

    def apply_tiles(formed, row_vec, col_vec):
        row_acc = jnp.zeros(row_vec.shape, jnp.float32)
        col_acc = jnp.zeros(col_vec.shape, jnp.float32)
        for slot in range(slot_count):
            row_start = local_rows[slot] * TILE
            col_start = local_cols[slot] * TILE
            near_row = lax.dynamic_slice_in_dim(row_vec, row_start, TILE, 1)
            near_col = lax.dynamic_slice_in_dim(col_vec, col_start, TILE, 1)
            to_rows = jnp.einsum(
                "kj,ij->ki", near_col, formed[slot], precision=lax.Precision.HIGHEST
            )
            to_cols = (
                jnp.einsum("ki,ij->kj", near_row, formed[slot], precision=lax.Precision.HIGHEST)
                * crossing[slot]
            )
            row_acc = lax.dynamic_update_slice_in_dim(
                row_acc,
                lax.dynamic_slice_in_dim(row_acc, row_start, TILE, 1) + to_rows,
                row_start,
                1,
            )
            col_acc = lax.dynamic_update_slice_in_dim(
                col_acc,
                lax.dynamic_slice_in_dim(col_acc, col_start, TILE, 1) + to_cols,
                col_start,
                1,
            )
        return (row_acc, col_acc)

    own_vec = lax.dynamic_slice_in_dim(vectors, grid_col * share, share, 1)
    col_pos, col_vec = gather_sets(own_pos, own_vec)
    formed = make_tiles(col_pos)
    first = combine(*apply_tiles(formed, vectors, col_vec))
    own_first = lax.dynamic_slice_in_dim(first, grid_col * share, share, 1)
    col_pos_again, col_first = gather_sets(own_pos, own_first)
    formed_again = make_tiles(col_pos_again)
    second = combine(*apply_tiles(formed_again, first, col_first))
    squares = lax.psum(jnp.sum(second * second, axis=1), "row")
    trajectories = block * lax.axis_size("row")
    total = squares / trajectories
    return second / jnp.sqrt(total + 1e-06)[:, None]


def solution(mesh):
    placed = (
        P(None, None, "row"),
        P(None, "row"),
        P("row", "col", None, None),
        P("row", "col", None),
    )
    return jax.shard_map(
        per_device, mesh=mesh, in_specs=placed, out_specs=P(None, "row"), check_vma=False
    )
```

profile of v0, /device:TPU:0, one launch (start us, length us, event | category | flops | bytes accessed | tf_op | source)
XLA Modules:
  0.0 894.8 jit_solution(10941147549791486297)
XLA Ops:
  31.1 3.7 constant_dynamic-slice_fusion.162
  34.8 4.8 constant_dynamic-slice_fusion.77
  39.6 5.5 constant_dynamic-slice_fusion.102
  45.1 59.7 %all_gather.16 = f32[8,16384]{1,0:T(8,128)} all-gather(f32[8,512]{1,0:T(8,128)S(1)} %constant_dynamic-slice_fusion.438), channel_id=1, replica_groups=mesh['row'=32,'col'=8] {'row'}, dimensions={1}, use_global_device_ids=true | all-gather | bytes 540672 | tf_op jit(solution)/shard_map/all_gather | solution.py:25
  108.0 7.8 add_multiply_fusion.9
  118.5 3.2 constant_dynamic-slice_fusion.79
  121.7 7.9 add_multiply_fusion.8
  132.3 8.2 add_multiply_fusion.7
  145.9 8.5 add_multiply_fusion.6
  157.0 4.3 constant_dynamic-slice_fusion.103
  161.7 8.4 add_multiply_fusion.5
  173.0 8.7 add_multiply_fusion.4
  184.7 8.8 add_multiply_fusion.3
  196.1 8.5 add_multiply_fusion.2
  207.7 8.0 add_multiply_fusion.1
  218.6 8.0 add_multiply_fusion
  248.9 191.1 %reduce-scatter.3.cloned.1.call-done = f32[8,512]{1,0:T(8,128)} async-done(((f32[8,16384]{1,0:T(8,128)}), f32[8,512]{1,0:T(8,128)}) %reduce-scatter.3.cloned.1.call-update) | async-done | bytes 16400 | tf_op jit(solution)/shard_map/reduce_scatter | solution.py:34
  440.0 13.7 %all_gather.18 = f32[8,4096]{1,0:T(8,128)S(1)} all-gather(f32[8,512]{1,0:T(8,128)} %reduce-scatter.3.cloned.1.call-done), channel_id=1, replica_groups=mesh['row'=32,'col'=8] {'col'}, dimensions={1}, use_global_device_ids=true | all-gather | bytes 147456 | tf_op jit(solution)/shard_map/all_gather | solution.py:30
  453.7 51.4 %all-reduce.3.cloned.1.call-done = f32[8,4096]{1,0:T(8,128)} async-done(((f32[8,4096]{1,0:T(8,128)}), f32[8,4096]{1,0:T(8,128)}) %all-reduce.3.cloned.1.call-update) | async-done | bytes 131088 | tf_op jit(solution)/shard_map/psum | solution.py:35
  533.5 50.7 %all_gather.19 = f32[8,16384]{1,0:T(8,128)S(1)} all-gather(f32[8,512]{1,0:T(8,128)S(1)} %constant_dynamic-slice_fusion.378), channel_id=1, replica_groups=mesh['row'=32,'col'=8] {'row'}, dimensions={1}, use_global_device_ids=true | all-gather | bytes 540672 | tf_op jit(solution)/shard_map/all_gather | solution.py:25
  596.0 150.2 %reduce-scatter.5.cloned.1.call-done = f32[8,512]{1,0:T(8,128)} async-done(((f32[8,16384]{1,0:T(8,128)}), f32[8,512]{1,0:T(8,128)}) %reduce-scatter.5.cloned.1.call-update) | async-done | bytes 16400 | tf_op jit(solution)/shard_map/reduce_scatter | solution.py:34
  746.2 13.2 %all_gather.20 = f32[8,4096]{1,0:T(8,128)S(1)} all-gather(f32[8,512]{1,0:T(8,128)} %reduce-scatter.5.cloned.1.call-done), channel_id=1, replica_groups=mesh['row'=32,'col'=8] {'col'}, dimensions={1}, use_global_device_ids=true | all-gather | bytes 147456 | tf_op jit(solution)/shard_map/all_gather | solution.py:30
  759.5 51.7 %all-reduce.5.cloned.1.call-done = f32[8,4096]{1,0:T(8,128)} async-done(((f32[8,4096]{1,0:T(8,128)}), f32[8,4096]{1,0:T(8,128)}) %all-reduce.5.cloned.1.call-update) | async-done | bytes 131088 | tf_op jit(solution)/shard_map/psum | solution.py:35
  812.2 75.1 %psum.23 = f32[8]{0:T(128)S(1)} all-reduce(f32[8]{0:T(128)S(1)} %get-tuple-element.5), channel_id=1, replica_groups=mesh['row'=32,'col'=8] {'row'}, use_global_device_ids=true, to_apply=%region_5.6 | all-reduce | flops 8 | bytes 64 | tf_op jit(solution)/shard_map/psum | solution.py:101
  (363 shorter events, 105.6 us)
Async XLA Ops:
  6.5 18.2 %copy-start = (f32[8,4096]{1,0:T(8,128)S(1)}, f32[8,4096]{1,0:T(8,128)}, u32[]{:S(2)}) copy-start(f32[8,4096]{1,0:T(8,128)} %param.5) | copy-start | bytes 393220
  6.5 98.3 %all-gather.2.cloned.1.call-start = ((), (), s32[]{:S(2)}) async-start(), calls=%async_computation.2 | async-start | bytes 3244032 | tf_op jit(solution)/shard_map/all_gather | solution.py:24
  8.1 431.8 %reduce-scatter.3.cloned.1.call-start = ((), (), s32[]{:S(2)}) async-start(), calls=%async_computation.4 | async-start | bytes 540672 | tf_op jit(solution)/shard_map/reduce_scatter | solution.py:34
  145.5 15.8 %copy-start.105 = (f32[1,1,512]{2,0,1:T(1,128)S(1)}, f32[1,1,512]{2,0,1:T(1,128)}, u32[]{:S(2)}) copy-start(f32[1,1,512]{2,0,1:T(1,128)} %get-tuple-element.767) | copy-start | bytes 6148
  145.5 15.8 %copy-start.106 = (f32[1,1,512]{2,0,1:T(1,128)S(1)}, f32[1,1,512]{2,0,1:T(1,128)}, u32[]{:S(2)}) copy-start(f32[1,1,512]{2,0,1:T(1,128)} %get-tuple-element.768) | copy-start | bytes 6148
  145.5 15.8 %copy-start.107 = (f32[1,1,512]{2,0,1:T(1,128)S(1)}, f32[1,1,512]{2,0,1:T(1,128)}, u32[]{:S(2)}) copy-start(f32[1,1,512]{2,0,1:T(1,128)} %get-tuple-element.882) | copy-start | bytes 6148
  145.5 15.8 %copy-start.108 = (f32[1,1,512]{2,0,1:T(1,128)S(1)}, f32[1,1,512]{2,0,1:T(1,128)}, u32[]{:S(2)}) copy-start(f32[1,1,512]{2,0,1:T(1,128)} %get-tuple-element.498) | copy-start | bytes 6148
  145.5 15.8 %copy-start.109 = (f32[1,1,512]{2,0,1:T(1,128)S(1)}, f32[1,1,512]{2,0,1:T(1,128)}, u32[]{:S(2)}) copy-start(f32[1,1,512]{2,0,1:T(1,128)} %get-tuple-element.499) | copy-start | bytes 6148
  145.6 15.8 %copy-start.110 = (f32[1,1,512]{2,0,1:T(1,128)S(1)}, f32[1,1,512]{2,0,1:T(1,128)}, u32[]{:S(2)}) copy-start(f32[1,1,512]{2,0,1:T(1,128)} %get-tuple-element.500) | copy-start | bytes 6148
  145.6 15.8 %copy-start.111 = (f32[1,1,512]{2,0,1:T(1,128)S(1)}, f32[1,1,512]{2,0,1:T(1,128)}, u32[]{:S(2)}) copy-start(f32[1,1,512]{2,0,1:T(1,128)} %get-tuple-element.501) | copy-start | bytes 6148
  145.6 15.8 %copy-start.112 = (f32[1,1,512]{2,0,1:T(1,128)S(1)}, f32[1,1,512]{2,0,1:T(1,128)}, u32[]{:S(2)}) copy-start(f32[1,1,512]{2,0,1:T(1,128)} %get-tuple-element.502) | copy-start | bytes 6148
  145.6 15.8 %copy-start.113 = (f32[1,1,512]{2,0,1:T(1,128)S(1)}, f32[1,1,512]{2,0,1:T(1,128)}, u32[]{:S(2)}) copy-start(f32[1,1,512]{2,0,1:T(1,128)} %get-tuple-element.503) | copy-start | bytes 6148
  145.6 15.8 %copy-start.114 = (f32[1,1,512]{2,0,1:T(1,128)S(1)}, f32[1,1,512]{2,0,1:T(1,128)}, u32[]{:S(2)}) copy-start(f32[1,1,512]{2,0,1:T(1,128)} %get-tuple-element.504) | copy-start | bytes 6148
  145.6 15.8 %copy-start.115 = (f32[1,1,512]{2,0,1:T(1,128)S(1)}, f32[1,1,512]{2,0,1:T(1,128)}, u32[]{:S(2)}) copy-start(f32[1,1,512]{2,0,1:T(1,128)} %get-tuple-element.505) | copy-start | bytes 6148
  145.6 15.8 %copy-start.116 = (f32[1,1,512]{2,0,1:T(1,128)S(1)}, f32[1,1,512]{2,0,1:T(1,128)}, u32[]{:S(2)}) copy-start(f32[1,1,512]{2,0,1:T(1,128)} %get-tuple-element.506) | copy-start | bytes 6148
  145.6 15.8 %copy-start.117 = (f32[1,1,512]{2,0,1:T(1,128)S(1)}, f32[1,1,512]{2,0,1:T(1,128)}, u32[]{:S(2)}) copy-start(f32[1,1,512]{2,0,1:T(1,128)} %get-tuple-element.507) | copy-start | bytes 6148
  145.6 15.8 %copy-start.118 = (f32[1,1,512]{2,0,1:T(1,128)S(1)}, f32[1,1,512]{2,0,1:T(1,128)}, u32[]{:S(2)}) copy-start(f32[1,1,512]{2,0,1:T(1,128)} %get-tuple-element.508) | copy-start | bytes 6148
  145.6 15.8 %copy-start.119 = (f32[1,1,512]{2,0,1:T(1,128)S(1)}, f32[1,1,512]{2,0,1:T(1,128)}, u32[]{:S(2)}) copy-start(f32[1,1,512]{2,0,1:T(1,128)} %get-tuple-element.509) | copy-start | bytes 6148
  230.2 274.9 %all-reduce.3.cloned.1.call-start = ((), (), s32[]{:S(2)}) async-start(), calls=%async_computation.3 | async-start | bytes 262144 | tf_op jit(solution)/shard_map/psum | solution.py:35
  248.8 497.4 %reduce-scatter.5.cloned.1.call-start = ((), (), s32[]{:S(2)}) async-start(), calls=%async_computation.6 | async-start | bytes 540672 | tf_op jit(solution)/shard_map/reduce_scatter | solution.py:34
  507.0 16.1 %copy-start.11 = (f32[512,512]{1,0:T(8,128)S(1)}, f32[512,512]{1,0:T(8,128)}, u32[]{:S(2)}) copy-start(f32[512,512]{1,0:T(8,128)} %copy-done.9) | copy-start | bytes 3145732
  533.4 277.7 %all-reduce.5.cloned.1.call-start = ((), (), s32[]{:S(2)}) async-start(), calls=%async_computation.5 | async-start | bytes 262144 | tf_op jit(solution)/shard_map/psum | solution.py:35
  533.5 56.0 %copy-start.4 = (f32[512,512]{1,0:T(8,128)S(1)}, f32[512,512]{1,0:T(8,128)}, u32[]{:S(2)}) copy-start(f32[512,512]{1,0:T(8,128)} %copy-done.1) | copy-start | bytes 3145732
  533.5 56.9 %copy-start.8 = (f32[512,512]{1,0:T(8,128)S(1)}, f32[512,512]{1,0:T(8,128)}, u32[]{:S(2)}) copy-start(f32[512,512]{1,0:T(8,128)} %copy-done.5) | copy-start | bytes 3145732
  (126 other events, 1497.3 us)
Sparse Core Ops, SparseCore 0:
  9.9 81.9 all-gather.1
  230.3 209.6 reduce-scatter.2
  442.4 62.5 all-reduce.2
  533.5 212.6 reduce-scatter.4
  748.5 62.5 all-reduce.4
where the time goes:
time: 904 us; the launch traced here: 895 us
  waiting for transfers between devices  444 us (49%)
  blocking collectives  212 us (23%)
  other arithmetic  87.3 us (10%)
  matrix products  80.1 us (9%)
  local copies, waits for them, and re-layouts  42.4 us (5%)
  between operations  27.9 us (3%)
    reduce_scatter x2, waiting for transfers between devices, combine(): lax.psum_scatter(col_acc, 'row', scatter_dimension=1, tiled=True)  341 us
    all_gather x2, blocking collectives, gather_sets(): lax.all_gather(vec_part, 'row', axis=1, tiled=True)  110 us
    psum x2, waiting for transfers between devices, combine(): return lax.psum(row_acc, 'col') + spread_pieces(col_share)  103 us
    mul x10, other arithmetic, make_tiles(): formed.append(form_tile(row_part, col_part) * weights[slot])  83 us
    psum x1, blocking collectives, per_device(): squares = lax.psum(jnp.sum(second * second, axis=1), 'row')  75.1 us
    dot_general x20, matrix products, apply_tiles(): jnp.einsum('ki,ij->kj', near_row, formed[slot], precision=lax.Precision.H...  51.2 us
    dot_general x20, matrix products, apply_tiles(): jnp.einsum('kj,ij->ki', near_col, formed[slot], precision=lax.Precision.H...  28.9 us
    all_gather x2, blocking collectives, spread_pieces(): return lax.all_gather(piece, 'col', axis=1, tiled=True)  26.9 us
  transfers between devices with their start and end apart: 5, of which 4 were waited for; matrix products, arithmetic and copies ran while one was open for 6% of the time, Pallas kernels for 0%

commit v1 on v0

v1 whole, which is shorter than its diff:
```python
import functools
import math

import jax
import jax.numpy as jnp
from jax import lax
from jax.experimental import pallas as pl
from jax.experimental.pallas import tpu as pltpu
from jax.sharding import Mesh
from jax.sharding import PartitionSpec as P

TILE = 512
ROW = ("z", "y")
COL = ("x", "core")
LOG2E = math.log2(math.e)
GROUPS = 6
DEPTH = 8 * GROUPS
CHUNK = 128
HALF = 256


def split3(value):
    high = value.astype(jnp.bfloat16).astype(jnp.float32)
    rest = value - high
    mid = rest.astype(jnp.bfloat16).astype(jnp.float32)
    return high, mid, rest - mid


def rows_of(ref, snapshot, scale, norm_at, one_at):
    width = ref.shape[-1]
    place = lax.broadcasted_iota(jnp.int32, (8, width), 0)
    parts = [
        jnp.broadcast_to(ref[3 * snapshot + q : 3 * snapshot + q + 1, :], (8, width))
        for q in range(3)
    ]
    norm = (-0.5 * LOG2E) * (parts[0] * parts[0] + parts[1] * parts[1] + parts[2] * parts[2])
    out = jnp.where(place == norm_at, norm, jnp.where(place == one_at, 1.0, 0.0))
    for q in range(3):
        out = jnp.where(place == q, parts[q] * scale if scale != 1.0 else parts[q], out)
    return out


def prepare_kernel(pos_ref, out_ref):
    for snapshot in range(16):
        high, mid, low = split3(rows_of(pos_ref, snapshot, LOG2E, 4, 3))
        stacked = jnp.concatenate([high, high, mid, mid, high, low], axis=0)
        out_ref[0, snapshot] = stacked.T.astype(jnp.bfloat16)


def prepare_rows(pos):
    tiles = pos.shape[1] // TILE
    return pl.pallas_call(
        prepare_kernel,
        grid=(tiles,),
        in_specs=[pl.BlockSpec((48, TILE), lambda i: (0, i))],
        out_specs=pl.BlockSpec((1, 16, TILE, DEPTH), lambda i: (i, 0, 0, 0)),
        out_shape=jax.ShapeDtypeStruct((tiles, 16, TILE, DEPTH), jnp.bfloat16),
        compiler_params=pltpu.CompilerParams(vmem_limit_bytes=32 << 20),
        cost_estimate=pl.CostEstimate(flops=10**8, bytes_accessed=20 << 20, transcendentals=0),
        name="prepare_rows",
    )(pos)


def multiply(field, high, low, dims):
    terms = jnp.concatenate(split3(field), axis=0).astype(jnp.bfloat16)
    dot = functools.partial(
        lax.dot_general, dimension_numbers=dims, preferred_element_type=jnp.float32
    )
    by_high = dot(terms, high)
    by_low = dot(terms[:16], low)
    return (by_high[0:8] + by_low[0:8]) + (by_high[8:16] + by_low[8:16]) + by_high[16:24]


def add_products(high, low, row_field, col_field, row_at, col_at, crossing, row_acc, col_acc):
    row_acc[row_at] += multiply(col_field, high, low, (((1,), (1,)), ((), ())))

    @pl.when(crossing)
    def _():
        col_acc[col_at] += multiply(row_field, high, low, (((1,), (0,)), ((), ())))


def clear(row_acc, col_acc):
    @pl.when(pl.program_id(0) == 0)
    def _():
        row_acc[...] = jnp.zeros_like(row_acc)
        col_acc[...] = jnp.zeros_like(col_acc)


def form_kernel(
    table, prepared_ref, col_ref, row_vec, high_ref, low_ref, row_acc, col_acc, cols
):
    clear(row_acc, col_acc)
    slot = pl.program_id(0)

    @pl.when(table[2, slot] != 0)
    def _():
        pos = col_ref.at[0]
        for snapshot in range(16):
            high, mid, low = split3(rows_of(pos, snapshot, 1.0, 3, 4))
            stacked = jnp.concatenate([high, mid, high, mid, low, high], axis=0)
            cols[snapshot] = stacked.astype(jnp.bfloat16)

        def step(at, carry):
            start = pl.multiple_of(at * CHUNK, CHUNK)
            for half in range(TILE // HALF):
                total = None
                for snapshot in range(16):
                    exponent = jnp.dot(
                        prepared_ref[0, snapshot, pl.ds(start, CHUNK), :],
                        cols[snapshot, :, half * HALF : (half + 1) * HALF],
                        preferred_element_type=jnp.float32,
                    )
                    term = jnp.exp2(exponent)
                    total = term if total is None else total + term
                high = total.astype(jnp.bfloat16)
                low = (total - high.astype(jnp.float32)).astype(jnp.bfloat16)
                place = (0, pl.ds(start, CHUNK), pl.ds(half * HALF, HALF))
                high_ref[place] = high
                low_ref[place] = low
            return carry

        lax.fori_loop(0, TILE // CHUNK, step, 0)
        row_at = table[0, slot]
        add_products(
            high_ref[0],
            low_ref[0],
            row_vec[row_at],
            col_ref[0, 48:56, :],
            row_at,
            table[1, slot],
            table[3, slot] != 0,
            row_acc,
            col_acc,
        )


def form_and_apply(table, prepared, gathered, row_vec):
    slots = table.shape[1]
    blocks = gathered.shape[0]
    tiles = row_vec.shape[0]
    whole = pl.BlockSpec((tiles, 8, TILE), lambda s, t: (0, 0, 0))
    grid_spec = pltpu.PrefetchScalarGridSpec(
        num_scalar_prefetch=1,
        grid=(slots,),
        in_specs=[
            pl.BlockSpec((1, 16, TILE, DEPTH), lambda s, t: (t[0, s], 0, 0, 0)),
            pl.BlockSpec((1, 56, TILE), lambda s, t: (t[1, s], 0, 0)),
            whole,
        ],
        out_specs=[
            pl.BlockSpec((1, TILE, TILE), lambda s, t: (s, 0, 0)),
            pl.BlockSpec((1, TILE, TILE), lambda s, t: (s, 0, 0)),
            whole,
            pl.BlockSpec((blocks, 8, TILE), lambda s, t: (0, 0, 0)),
        ],
        scratch_shapes=[pltpu.VMEM((16, DEPTH, TILE), jnp.bfloat16)],
    )
    return pl.pallas_call(
        form_kernel,
        grid_spec=grid_spec,
        out_shape=[
            jax.ShapeDtypeStruct((slots, TILE, TILE), jnp.bfloat16),
            jax.ShapeDtypeStruct((slots, TILE, TILE), jnp.bfloat16),
            jax.ShapeDtypeStruct((tiles, 8, TILE), jnp.float32),
            jax.ShapeDtypeStruct((blocks, 8, TILE), jnp.float32),
        ],
        compiler_params=pltpu.CompilerParams(vmem_limit_bytes=40 << 20),
        name="form_and_apply",
    )(table, prepared, gathered, row_vec)


def apply_kernel(table, high_ref, low_ref, row_vec, col_vec, row_acc, col_acc):
    clear(row_acc, col_acc)
    slot = pl.program_id(0)

    @pl.when(table[2, slot] != 0)
    def _():
        row_at = table[0, slot]
        col_at = table[1, slot]
        add_products(
            high_ref[0],
            low_ref[0],
            row_vec[row_at],
            col_vec[col_at],
            row_at,
            col_at,
            table[3, slot] != 0,
            row_acc,
            col_acc,
        )


def apply_again(table, high, low, row_vec, col_vec):
    slots = table.shape[1]
    blocks = col_vec.shape[0]
    tiles = row_vec.shape[0]
    rows = pl.BlockSpec((tiles, 8, TILE), lambda s, t: (0, 0, 0))
    cols = pl.BlockSpec((blocks, 8, TILE), lambda s, t: (0, 0, 0))
    matrix = pl.BlockSpec((1, TILE, TILE), lambda s, t: (s, 0, 0))
    grid_spec = pltpu.PrefetchScalarGridSpec(
        num_scalar_prefetch=1,
        grid=(slots,),
        in_specs=[matrix, matrix, rows, cols],
        out_specs=[rows, cols],
    )
    return pl.pallas_call(
        apply_kernel,
        grid_spec=grid_spec,
        out_shape=[
            jax.ShapeDtypeStruct((tiles, 8, TILE), jnp.float32),
            jax.ShapeDtypeStruct((blocks, 8, TILE), jnp.float32),
        ],
        compiler_params=pltpu.CompilerParams(vmem_limit_bytes=40 << 20),
        name="apply_again",
    )(table, high, low, row_vec, col_vec)


def spread(piece, axes):
    copies = jnp.broadcast_to(piece, (lax.axis_size(axes),) + piece.shape)
    return lax.all_to_all(copies, axes, 0, 0, tiled=True)


def gather_sets(piece):
    return lax.all_gather(lax.all_gather(piece, "y"), "z")


def combine(row_acc, col_acc):
    by_row = lax.all_to_all(row_acc, COL, 0, 0, tiled=True)
    by_col = lax.all_to_all(col_acc, ROW, 0, 0, tiled=True)
    return jnp.sum(by_row, axis=0) + jnp.sum(by_col, axis=0)


def per_device(positions, vectors, pairs, valid):
    grid_row = lax.axis_index(ROW)
    grid_col = lax.axis_index(COL)
    block = positions.shape[2]
    tiles = block // TILE
    blocks = lax.axis_size(ROW)
    local_rows = pairs[0, 0, :, 0]
    local_cols = pairs[0, 0, :, 1]
    crossing = (grid_row * tiles + local_rows) != (local_cols * tiles + grid_col)
    table = jnp.stack(
        [local_rows, local_cols, valid[0, 0], crossing.astype(jnp.int32)], axis=0
    ).astype(jnp.int32)

    flat = positions.reshape(48, block)
    own = lax.dynamic_slice_in_dim(
        jnp.concatenate([flat, vectors], axis=0), grid_col * TILE, TILE, 1
    )
    gathered = gather_sets(own).reshape(blocks, 56, TILE)
    prepared = prepare_rows(flat)
    row_vec = vectors.reshape(8, tiles, TILE).transpose(1, 0, 2)

    high, low, row_acc, col_acc = form_and_apply(table, prepared, gathered, row_vec)
    first = combine(row_acc, col_acc)
    second = combine(*apply_again(table, high, low, spread(first, COL), spread(first, ROW)))

    rows = spread(second, COL)
    squares = jnp.sum(rows * rows, axis=(0, 2))
    squares = spread(jnp.broadcast_to(squares[:, None], (8, 128)), ROW)
    total = jnp.sum(squares[:, :, 0], axis=0) / (block * blocks)
    scaled = rows / jnp.sqrt(total + 1e-06)[None, :, None]
    return scaled.transpose(1, 0, 2).reshape(8, block)


def solution(mesh):
    physical = Mesh(mesh.devices.reshape(8, 4, 4, 2), ("z", "y", "x", "core"))
    placed = (
        P(None, None, ROW),
        P(None, ROW),
        P(ROW, COL, None, None),
        P(ROW, COL, None),
    )
    return jax.shard_map(
        per_device, mesh=physical, in_specs=placed, out_specs=P(None, ROW), check_vma=False
    )
```

time: 904 us -> 261 us (0.29)
  waiting for transfers between devices: 444 us -> 75.5 us
  blocking collectives: 212 us -> 84.6 us
  other arithmetic: 87.3 us -> 1.94 us
  matrix products: 80.1 us -> 0 us
  Pallas kernels: 0 us -> 53.1 us
  local copies, waits for them, and re-layouts: 42.4 us -> 17.3 us
  between operations: 27.9 us -> 13.6 us
  starting transfers between devices: 0.17 us -> 13.2 us
    reduce_scatter x2 -> x0, waiting for transfers between devices: 341 us -> none  [combine(): lax.psum_scatter(col_acc, 'row', scatter_dimension=1, tiled=True)]
    all_gather x4 -> x1, blocking collectives: 137 us -> 13.6 us  [gather_sets(): return lax.all_gather(lax.all_gather(piece, 'y'), 'z')]
    psum x2 -> x0, waiting for transfers between devices: 103 us -> none  [combine(): return lax.psum(row_acc, 'col') + spread_pieces(col_share)]
    mul x10 -> x0, other arithmetic: 83 us -> none  [make_tiles(): formed.append(form_tile(row_part, col_part) * weights[slot])]
    dot_general x40 -> x0, matrix products: 80.1 us -> none  [the longest x20 51.2 us: apply_tiles(): jnp.einsum('ki,ij->kj', near_row, formed[slot], precision=lax.Precision.H...]
    psum x1 -> x0, blocking collectives: 75.1 us -> none  [per_device(): squares = lax.psum(jnp.sum(second * second, axis=1), 'row')]
    all_to_all x0 -> x6, blocking collectives: none -> 71 us  [the longest x4 54 us: spread(): return lax.all_to_all(copies, axes, 0, 0, tiled=True)]
    pallas_call x0 -> x3, Pallas kernels: none -> 53.1 us  [the longest x1 39.8 us: form_and_apply(): pl.pallas_call(form_kernel, grid_spec=grid_spec, out_shape=[jax.ShapeDtyp...]
  transfers between devices with their start and end apart: 5 -> 3, of which waited for: 4 -> 3; matrix products, arithmetic and copies ran while one was open for 6% -> 0% of each run, Pallas kernels for 0% -> 2%
where the time goes in v1:
time: 261 us; the launch traced here: 259 us
  blocking collectives  84.6 us (32%)
  waiting for transfers between devices  75.5 us (29%)
  Pallas kernels  53.1 us (20%)
  local copies, waits for them, and re-layouts  17.3 us (7%)
  between operations  13.6 us (5%)
  starting transfers between devices  13.2 us (5%)
    all_to_all x4, blocking collectives, spread(): return lax.all_to_all(copies, axes, 0, 0, tiled=True)  54 us
    all_gather x1, waiting for transfers between devices, gather_sets(): return lax.all_gather(lax.all_gather(piece, 'y'), 'z')  40.3 us
    pallas_call x1, Pallas kernels, form_and_apply(): pl.pallas_call(form_kernel, grid_spec=grid_spec, out_shape=[jax.ShapeDtyp...  39.8 us
    all_to_all x2, waiting for transfers between devices, combine(): by_col = lax.all_to_all(col_acc, ROW, 0, 0, tiled=True)  35.2 us
    all_to_all x2, blocking collectives, combine(): by_row = lax.all_to_all(row_acc, COL, 0, 0, tiled=True)  17 us
    unnamed x17, local copies, waits for them, and re-layouts  16.7 us
    all_gather x1, blocking collectives, gather_sets(): return lax.all_gather(lax.all_gather(piece, 'y'), 'z')  13.6 us
    all_to_all x2, starting transfers between devices, combine(): by_col = lax.all_to_all(col_acc, ROW, 0, 0, tiled=True)  13.2 us
  transfers between devices with their start and end apart: 3, of which 3 were waited for; matrix products, arithmetic and copies ran while one was open for 0% of the time, Pallas kernels for 2%

profile of v1, /device:TPU:0, one launch (start us, length us, event | category | flops | bytes accessed | tf_op | source)
XLA Modules:
  0.0 259.1 jit_solution(17064545324903750157)
XLA Ops:
  6.5 1.7 copy.9
  8.2 0.4 reshape.46.pos_ref
  8.6 0.7 fusion
  9.4 13.6 %all-gather = f32[224,512]{1,0:T(8,128)} all-gather(f32[56,512]{1,0:T(8,128)S(1)} %fusion), channel_id=2, replica_groups=mesh['z'=8,'y'=4,'x'=4,'core'=2] {'y'}, dimensions={0}, use_global_device_ids=true | all-gather | bytes 573440 | tf_op jit(solution)/shard_map/all_gather | solution.py:224
  23.0 5.3 %prepare_rows.1.prepared_ref = bf16[8,16,512,48]{3,2,1,0:T(8,128)(2,1)S(1)} custom-call(f32[48,4096]{1,0:T(8,128)S(1)} %reshape.46.pos_ref), custom_call_target="tpu_custom_call" | custom-call | flops 100000000 | bytes 20971520 | tf_op jit(solution)/shard_map/prepare_rows/pallas_call | solution.py:52
  28.3 5.7 %copy-done = bf16[8,16,512,48]{3,2,1,0:T(8,128)(2,1)} copy-done((bf16[8,16,512,48]{3,2,1,0:T(8,128)(2,1)}, bf16[8,16,512,48]{3,2,1,0:T(8,128)(2,1)S(1)}, u32[]{:S(2)}) %copy-start) | copy-done | bytes 6291480
  34.1 40.3 %all-gather.4.cloned.1.call-done.col_ref = f32[32,56,512]{2,1,0:T(8,128)} async-done(((f32[4,56,512]{2,1,0:T(8,128)}), f32[32,56,512]{2,1,0:T(8,128)}) %all-gather.4.cloned.1.call-update) | async-done | bytes 3670032 | tf_op jit(solution)/shard_map/all_gather | solution.py:224
  74.4 2.0 copy-done.4
  76.4 39.8 %form_and_apply.1 = (bf16[10,512,512]{2,1,0:T(8,128)(2,1)S(1)}, bf16[10,512,512]{2,1,0:T(8,128)(2,1)}, f32[8,8,512]{2,1,0:T(8,128)S(1)}, f32[32,8,512]{2,1,0:T(8,128)}) custom-call(s32[4,10]{1,0:T(4,128)S(1)} %pad_add_fusion.table, bf16[8,16,512,48]{3,2,1,0:T(8,128)(2,1)} %copy-done, f32[32,56,512]{2,1,0:T(8,128)S(1)} %copy-done.4, f32[8,8,512]{2,1,0:T(8,128)S(1)} %bitcast.16), custom_call_target="tpu_custom_call" | custom-call | tf_op jit(solution)/shard_map/form_and_apply/pallas_call | solution.py:158
  116.3 2.3 copy-done.1
  118.6 8.5 %all_to_all.40 = f32[8,8,512]{2,1,0:T(8,128)S(1)} all-to-all(f32[8,8,512]{2,1,0:T(8,128)S(1)} %get-tuple-element.13), channel_id=1, replica_groups=mesh['z'=8,'y'=4,'x'=4,'core'=2] {'x','core'}, dimensions={0} | all-to-all | bytes 262144 | tf_op jit(solution)/shard_map/all_to_all | solution.py:228
  127.1 8.8 %all-to-all-start.1 = ((f32[32,8,512]{2,1,0:T(8,128)}), f32[32,8,512]{2,1,0:T(8,128)S(1)}, u32[]{:S(2)}, u32[]{:S(2)}) async-start(f32[32,8,512]{2,1,0:T(8,128)} %get-tuple-element.14), calls=%async_computation.1 | async-start | bytes 1048576 | tf_op jit(solution)/shard_map/all_to_all | solution.py:229
  135.9 17.6 %all-to-all-done.1 = f32[32,8,512]{2,1,0:T(8,128)S(1)} async-done(((f32[32,8,512]{2,1,0:T(8,128)}), f32[32,8,512]{2,1,0:T(8,128)S(1)}, u32[]{:S(2)}, u32[]{:S(2)}) %all-to-all-start.1) | async-done | bytes 524320 | tf_op jit(solution)/shard_map/all_to_all | solution.py:229
  153.6 8.5 %all_to_all.41.row_vec = f32[8,8,512]{2,1,0:T(8,128)S(1)} all-to-all(f32[8,8,512]{2,1,0:T(8,128)S(1)} %broadcast_in_dim.11), channel_id=1, replica_groups=mesh['z'=8,'y'=4,'x'=4,'core'=2] {'x','core'}, dimensions={0} | all-to-all | bytes 262144 | tf_op jit(solution)/shard_map/all_to_all | solution.py:220
  162.2 22.0 %all_to_all.42.col_vec = f32[32,8,512]{2,1,0:T(8,128)S(1)} all-to-all(f32[32,8,512]{2,1,0:T(8,128)S(1)} %broadcast_in_dim.12), channel_id=1, replica_groups=mesh['z'=8,'y'=4,'x'=4,'core'=2] {'z','y'}, dimensions={0} | all-to-all | bytes 1048576 | tf_op jit(solution)/shard_map/all_to_all | solution.py:220
  184.2 2.5 copy-done.2
  186.7 2.5 copy-done.3
  189.2 8.0 %apply_again.1 = (f32[8,8,512]{2,1,0:T(8,128)S(1)}, f32[32,8,512]{2,1,0:T(8,128)}) custom-call(s32[4,10]{1,0:T(4,128)S(1)} %pad_add_fusion.table, bf16[10,512,512]{2,1,0:T(8,128)(2,1)S(1)} %copy-done.2, bf16[10,512,512]{2,1,0:T(8,128)(2,1)S(1)} %copy-done.3, f32[8,8,512]{2,1,0:T(8,128)S(1)} %all_to_all.41.row_vec, f32[32,8,512]{2,1,0:T(8,128)S(1)} %all_to_all.42.col_vec), custom_call_target="tpu_custom_call" | custom-call | tf_op jit(solution)/shard_map/apply_again/pallas_call | solution.py:206
  197.1 8.5 %all_to_all.43 = f32[8,8,512]{2,1,0:T(8,128)S(1)} all-to-all(f32[8,8,512]{2,1,0:T(8,128)S(1)} %get-tuple-element.15), channel_id=1, replica_groups=mesh['z'=8,'y'=4,'x'=4,'core'=2] {'x','core'}, dimensions={0} | all-to-all | bytes 262144 | tf_op jit(solution)/shard_map/all_to_all | solution.py:228
  205.6 4.3 %all-to-all-start.5 = ((f32[32,8,512]{2,1,0:T(8,128)}), f32[32,8,512]{2,1,0:T(8,128)S(1)}, u32[]{:S(2)}, u32[]{:S(2)}) async-start(f32[32,8,512]{2,1,0:T(8,128)} %get-tuple-element.16), calls=%async_computation.5 | async-start | bytes 1048576 | tf_op jit(solution)/shard_map/all_to_all | solution.py:229
  210.0 17.6 %all-to-all-done.5 = f32[32,8,512]{2,1,0:T(8,128)S(1)} async-done(((f32[32,8,512]{2,1,0:T(8,128)}), f32[32,8,512]{2,1,0:T(8,128)S(1)}, u32[]{:S(2)}, u32[]{:S(2)}) %all-to-all-start.5) | async-done | bytes 524320 | tf_op jit(solution)/shard_map/all_to_all | solution.py:229
  227.7 8.5 %all_to_all.44 = f32[8,8,512]{2,1,0:T(8,128)S(1)} all-to-all(f32[8,8,512]{2,1,0:T(8,128)S(1)} %broadcast_in_dim.13), channel_id=1, replica_groups=mesh['z'=8,'y'=4,'x'=4,'core'=2] {'x','core'}, dimensions={0} | all-to-all | bytes 262144 | tf_op jit(solution)/shard_map/all_to_all | solution.py:220
  236.4 14.9 %all_to_all.45 = f32[32,8,128]{2,1,0:T(8,128)S(1)} all-to-all(f32[32,8,128]{2,1,0:T(8,128)S(1)} %broadcast_in_dim_broadcast_in_dim.2), channel_id=1, replica_groups=mesh['z'=8,'y'=4,'x'=4,'core'=2] {'z','y'}, dimensions={0} | all-to-all | bytes 262144 | tf_op jit(solution)/shard_map/all_to_all | solution.py:220
  251.5 0.7 broadcast_divide_fusion
  (29 shorter events, 0.7 us)
Async XLA Ops:
  6.5 67.8 %all-gather.4.cloned.1.call-start = ((), (), s32[]{:S(2)}) async-start(), calls=%async_computation.8 | async-start | bytes 4128768 | tf_op jit(solution)/shard_map/all_gather | solution.py:224
  23.0 11.0 %copy-start.6 = (s32[1,1,10,2]{2,3,1,0:T(2,128)S(1)}, s32[1,1,10,2]{2,3,1,0:T(2,128)}, u32[]{:S(2)}) copy-start(s32[1,1,10,2]{2,3,1,0:T(2,128)} %param.6) | copy-start | bytes 244
  23.0 11.1 %copy-start.7 = (s32[1,1,10]{2,1,0:T(1,128)S(1)}, s32[1,1,10]{2,1,0:T(1,128)}, u32[]{:S(2)}) copy-start(s32[1,1,10]{2,1,0:T(1,128)} %param.7) | copy-start | bytes 124
  23.0 51.4 %copy-start.5 = (f32[8,4096]{1,0:T(8,128)S(1)}, f32[8,4096]{1,0:T(8,128)}, u32[]{:S(2)}) copy-start(f32[8,4096]{1,0:T(8,128)} %param.5) | copy-start | bytes 393220
  28.3 5.7 %copy-start = (bf16[8,16,512,48]{3,2,1,0:T(8,128)(2,1)}, bf16[8,16,512,48]{3,2,1,0:T(8,128)(2,1)S(1)}, u32[]{:S(2)}) copy-start(bf16[8,16,512,48]{3,2,1,0:T(8,128)(2,1)S(1)} %prepare_rows.1.prepared_ref) | copy-start | bytes 18874372
  74.4 2.0 copy-start.4
  116.3 2.3 copy-start.1
  127.1 26.5 %all-to-all-start.1 = ((f32[32,8,512]{2,1,0:T(8,128)}), f32[32,8,512]{2,1,0:T(8,128)S(1)}, u32[]{:S(2)}, u32[]{:S(2)}) async-start(f32[32,8,512]{2,1,0:T(8,128)} %get-tuple-element.14), calls=%async_computation.1 | async-start | bytes 1048576 | tf_op jit(solution)/shard_map/all_to_all | solution.py:229
  184.2 2.5 copy-start.2
  186.7 2.5 copy-start.3
  205.6 21.9 %all-to-all-start.5 = ((f32[32,8,512]{2,1,0:T(8,128)}), f32[32,8,512]{2,1,0:T(8,128)S(1)}, u32[]{:S(2)}, u32[]{:S(2)}) async-start(f32[32,8,512]{2,1,0:T(8,128)} %get-tuple-element.16), calls=%async_computation.5 | async-start | bytes 1048576 | tf_op jit(solution)/shard_map/all_to_all | solution.py:229
Sparse Core Ops, SparseCore 0:
  23.1 51.2 all-gather.3

commit v2 on v1

v2 whole, which is shorter than its diff:
```python
import functools
import math

import jax
import jax.numpy as jnp
from jax import lax
from jax.experimental import pallas as pl
from jax.experimental.pallas import tpu as pltpu
from jax.sharding import Mesh
from jax.sharding import PartitionSpec as P

TILE = 512
ROW = ("z", "y")
COL = ("x", "core")
ALL = ROW + COL
ROW_AT, ROW_NEAR, COL_AT, COL_NEAR, LIVE, CROSSING = range(6)
BY_ROWS = (((1,), (0,)), ((), ()))
BY_COLS = (((1,), (1,)), ((), ()))
LOG2E = math.log2(math.e)
GROUPS = 6
DEPTH = 8 * GROUPS
CHUNK = 128
HALF = 256


def in_hbm(value):
    return pltpu.with_memory_space_constraint(value, pltpu.HBM)


def split3(value):
    high = value.astype(jnp.bfloat16).astype(jnp.float32)
    rest = value - high
    mid = rest.astype(jnp.bfloat16).astype(jnp.float32)
    return high, mid, rest - mid


def rows_of(ref, snapshot, scale, norm_at, one_at):
    width = ref.shape[-1]
    place = lax.broadcasted_iota(jnp.int32, (8, width), 0)
    parts = [
        jnp.broadcast_to(ref[16 * q + snapshot : 16 * q + snapshot + 1, :], (8, width))
        for q in range(3)
    ]
    norm = (-0.5 * LOG2E) * (parts[0] * parts[0] + parts[1] * parts[1] + parts[2] * parts[2])
    out = jnp.where(place == norm_at, norm, jnp.where(place == one_at, 1.0, 0.0))
    for q in range(3):
        out = jnp.where(place == q, parts[q] * scale if scale != 1.0 else parts[q], out)
    return out


def prepare_kernel(pos_ref, out_ref):
    for snapshot in range(16):
        high, mid, low = split3(rows_of(pos_ref, snapshot, LOG2E, 4, 3))
        stacked = jnp.concatenate([high, high, mid, mid, high, low], axis=0)
        out_ref[0, snapshot] = stacked.T.astype(jnp.bfloat16)


def prepare_rows(pos):
    tiles = pos.shape[1] // TILE
    return pl.pallas_call(
        prepare_kernel,
        grid=(tiles,),
        in_specs=[pl.BlockSpec((48, TILE), lambda i: (0, i))],
        out_specs=pl.BlockSpec((1, 16, TILE, DEPTH), lambda i: (i, 0, 0, 0)),
        out_shape=pltpu.HBM((tiles, 16, TILE, DEPTH), jnp.bfloat16),
        compiler_params=pltpu.CompilerParams(vmem_limit_bytes=32 << 20),
        cost_estimate=pl.CostEstimate(flops=10**8, bytes_accessed=20 << 20, transcendentals=0),
        name="prepare_rows",
    )(pos)


def multiply(field, high, low, dims):
    terms = jnp.concatenate(split3(field), axis=0).astype(jnp.bfloat16)
    dot = functools.partial(
        lax.dot_general, dimension_numbers=dims, preferred_element_type=jnp.float32
    )
    by_high = dot(terms, high)
    by_low = dot(terms[:16], low)
    return (by_high[0:8] + by_low[0:8]) + (by_high[8:16] + by_low[8:16]) + by_high[16:24]


def clear(acc):
    @pl.when(pl.program_id(0) == 0)
    def _():
        acc[...] = jnp.zeros_like(acc)


def form_kernel(table, prepared_ref, col_ref, row_vec, high_ref, low_ref, col_acc, cols):
    clear(col_acc)
    slot = pl.program_id(0)

    @pl.when(table[LIVE, slot] != 0)
    def _():
        pos = col_ref.at[0]
        for snapshot in range(16):
            high, mid, low = split3(rows_of(pos, snapshot, 1.0, 3, 4))
            stacked = jnp.concatenate([high, mid, high, mid, low, high], axis=0)
            cols[snapshot] = stacked.astype(jnp.bfloat16)

        def step(at, carry):
            start = pl.multiple_of(at * CHUNK, CHUNK)
            for half in range(TILE // HALF):
                total = None
                for snapshot in range(16):
                    exponent = jnp.dot(
                        prepared_ref[0, snapshot, pl.ds(start, CHUNK), :],
                        cols[snapshot, :, half * HALF : (half + 1) * HALF],
                        preferred_element_type=jnp.float32,
                    )
                    term = jnp.exp2(exponent)
                    total = term if total is None else total + term
                high = total.astype(jnp.bfloat16)
                low = (total - high.astype(jnp.float32)).astype(jnp.bfloat16)
                place = (0, pl.ds(start, CHUNK), pl.ds(half * HALF, HALF))
                high_ref[place] = high
                low_ref[place] = low
            return carry

        lax.fori_loop(0, TILE // CHUNK, step, 0)

        @pl.when(table[CROSSING, slot] != 0)
        def _():
            col_acc[table[COL_AT, slot]] += multiply(
                row_vec[table[ROW_AT, slot]], high_ref[0], low_ref[0], BY_ROWS
            )


def form_and_apply(table, prepared, gathered, row_vec):
    slots = table.shape[1]
    blocks = gathered.shape[0]
    tiles = row_vec.shape[0]
    grid_spec = pltpu.PrefetchScalarGridSpec(
        num_scalar_prefetch=1,
        grid=(slots,),
        in_specs=[
            pl.BlockSpec((1, 16, TILE, DEPTH), lambda s, t: (t[ROW_AT, s], 0, 0, 0)),
            pl.BlockSpec((1, 48, TILE), lambda s, t: (t[COL_NEAR, s], 0, 0)),
            pl.BlockSpec((tiles, 8, TILE), lambda s, t: (0, 0, 0)),
        ],
        out_specs=[
            pl.BlockSpec((1, TILE, TILE), lambda s, t: (s, 0, 0)),
            pl.BlockSpec((1, TILE, TILE), lambda s, t: (s, 0, 0)),
            pl.BlockSpec((blocks, 8, TILE), lambda s, t: (0, 0, 0)),
        ],
        scratch_shapes=[pltpu.VMEM((16, DEPTH, TILE), jnp.bfloat16)],
    )
    return pl.pallas_call(
        form_kernel,
        grid_spec=grid_spec,
        out_shape=[
            pltpu.HBM((slots, TILE, TILE), jnp.bfloat16),
            pltpu.HBM((slots, TILE, TILE), jnp.bfloat16),
            jax.ShapeDtypeStruct((blocks, 8, TILE), jnp.float32),
        ],
        compiler_params=pltpu.CompilerParams(vmem_limit_bytes=16 << 20),
        cost_estimate=pl.CostEstimate(
            flops=3 * 10**10, bytes_accessed=30 << 20, transcendentals=4 * 10**7
        ),
        name="form_and_apply",
    )(table, in_hbm(prepared), in_hbm(gathered), row_vec)


def rows_kernel(table, high_ref, low_ref, col_vec, row_acc):
    clear(row_acc)
    slot = pl.program_id(0)

    @pl.when(table[LIVE, slot] != 0)
    def _():
        row_acc[table[ROW_NEAR, slot]] += multiply(
            col_vec[table[COL_AT, slot]], high_ref[0], low_ref[0], BY_COLS
        )


def cols_kernel(table, high_ref, low_ref, row_vec, col_acc):
    clear(col_acc)
    slot = pl.program_id(0)

    @pl.when(table[CROSSING, slot] != 0)
    def _():
        col_acc[table[COL_AT, slot]] += multiply(
            row_vec[table[ROW_NEAR, slot]], high_ref[0], low_ref[0], BY_ROWS
        )


def apply_tiles(kernel, name, table, high, low, field, count):
    slots = table.shape[1]
    matrix = pl.BlockSpec((1, TILE, TILE), lambda s, t: (s, 0, 0))
    grid_spec = pltpu.PrefetchScalarGridSpec(
        num_scalar_prefetch=1,
        grid=(slots,),
        in_specs=[matrix, matrix, pl.BlockSpec(field.shape, lambda s, t: (0, 0, 0))],
        out_specs=pl.BlockSpec((count, 8, TILE), lambda s, t: (0, 0, 0)),
    )
    return pl.pallas_call(
        kernel,
        grid_spec=grid_spec,
        out_shape=jax.ShapeDtypeStruct((count, 8, TILE), jnp.float32),
        compiler_params=pltpu.CompilerParams(vmem_limit_bytes=8 << 20),
        cost_estimate=pl.CostEstimate(
            flops=3 * 10**9, bytes_accessed=12 << 20, transcendentals=0
        ),
        name=name,
    )(table, in_hbm(high), in_hbm(low), field)


def finish_kernel(near, rows_ref, total_ref, out_ref):
    scale = total_ref[...]
    for tile in range(near.shape[0]):
        out_ref[:, tile * TILE : (tile + 1) * TILE] = rows_ref[near[tile]] / scale


def finish(near, rows, root):
    tiles = rows.shape[0]
    return pl.pallas_call(
        finish_kernel,
        in_specs=[
            pl.BlockSpec(memory_space=pltpu.SMEM),
            pl.BlockSpec(memory_space=pltpu.VMEM),
            pl.BlockSpec(memory_space=pltpu.VMEM),
        ],
        out_specs=pl.BlockSpec(memory_space=pltpu.VMEM),
        out_shape=jax.ShapeDtypeStruct((8, tiles * TILE), jnp.float32),
        name="finish",
    )(near, rows, root)


def shift(value, axis, distance):
    size = lax.axis_size(axis)
    return lax.ppermute(value, axis, [(i, (i + distance) % size) for i in range(size)])


def spread(piece, axes):
    copies = jnp.broadcast_to(piece, (lax.axis_size(axes),) + piece.shape)
    return lax.all_to_all(copies, axes, 0, 0, tiled=True)


def spread_near(piece):
    mine = jnp.stack([piece] + [shift(piece, "x", d) for d in range(1, lax.axis_size("x"))])
    return jnp.concatenate([mine, shift(mine, "core", 1)], axis=0)


def reduce_near(row_acc):
    size = lax.axis_size("x")
    mine = row_acc[:size] + shift(row_acc[size:], "core", 1)
    total = mine[0]
    for d in range(1, size):
        total = total + shift(mine[d], "x", size - d)
    return total


def gather_sets(piece):
    near = jnp.stack([piece] + [shift(piece, "y", d) for d in range(1, lax.axis_size("y"))])
    return lax.all_gather(near, "z")


def combine(row_acc, col_acc):
    by_col = lax.all_to_all(col_acc, ROW, 0, 0, tiled=True)
    return reduce_near(row_acc) + jnp.sum(by_col, axis=0)


def near_tile(tile, x, core, size):
    return jnp.where(tile % 2 == core, 0, size) + (x - tile // 2) % size


def per_device(positions, vectors, pairs, valid):
    grid_row = lax.axis_index(ROW)
    grid_col = lax.axis_index(COL)
    x, core, y = lax.axis_index("x"), lax.axis_index("core"), lax.axis_index("y")
    size_x, size_y = lax.axis_size("x"), lax.axis_size("y")
    block = positions.shape[2]
    tiles = block // TILE
    blocks = lax.axis_size(ROW)
    local_rows = pairs[0, 0, :, 0]
    local_cols = pairs[0, 0, :, 1]
    live = valid[0, 0] != 0
    crossing = (grid_row * tiles + local_rows) != (local_cols * tiles + grid_col)
    near_cols = local_cols // size_y * size_y + (y - local_cols % size_y) % size_y
    table = jnp.stack(
        [
            local_rows,
            near_tile(local_rows, x, core, size_x),
            local_cols,
            near_cols,
            live.astype(jnp.int32),
            (live & crossing).astype(jnp.int32),
        ],
        axis=0,
    ).astype(jnp.int32)

    flat = positions.transpose(1, 0, 2).reshape(48, block)
    gathered = gather_sets(lax.dynamic_slice_in_dim(flat, grid_col * TILE, TILE, 1))
    gathered = gathered.reshape(blocks, 48, TILE)
    prepared = prepare_rows(flat)
    row_vec = vectors.reshape(8, tiles, TILE).transpose(1, 0, 2)
    own_vec = lax.dynamic_index_in_dim(row_vec, grid_col, 0, keepdims=False)
    gathered, own_vec = lax.optimization_barrier((gathered, own_vec))
    col_vec = spread(own_vec, ROW)

    high, low, col_acc = form_and_apply(table, prepared, gathered, row_vec)
    row_acc = apply_tiles(rows_kernel, "apply_rows", table, high, low, col_vec, tiles)
    first = combine(row_acc, col_acc)

    col_vec = spread(first, ROW)
    col_acc = apply_tiles(cols_kernel, "apply_cols", table, high, low, spread_near(first), blocks)
    row_acc = apply_tiles(rows_kernel, "apply_rows", table, high, low, col_vec, tiles)
    second = combine(row_acc, col_acc)

    squares = jnp.sum(second * second, axis=1)
    width = 128
    squares = spread(jnp.pad(squares[None, :], ((0, 0), (0, width - 8))), ALL)
    rows = spread_near(second)
    total = jnp.sum(squares[:, 0, :8], axis=0) / (block * blocks)
    root = jnp.sqrt(total + 1e-06)[:, None]
    near = near_tile(jnp.arange(tiles, dtype=jnp.int32), x, core, size_x)
    return finish(near.astype(jnp.int32), rows, jnp.broadcast_to(root, (8, TILE)))


def solution(mesh):
    physical = Mesh(mesh.devices.reshape(8, 4, 4, 2), ("z", "y", "x", "core"))
    placed = (
        P(None, None, ROW),
        P(None, ROW),
        P(ROW, COL, None, None),
        P(ROW, COL, None),
    )
    return jax.shard_map(
        per_device, mesh=physical, in_specs=placed, out_specs=P(None, ROW), check_vma=False
    )
```

time: 261 us -> 232 us (0.89)
  blocking collectives: 84.6 us -> 0 us
  starting transfers between devices: 13.2 us -> 74.1 us
  Pallas kernels: 53.1 us -> 68 us
  waiting for transfers between devices: 75.5 us -> 61.6 us
  local copies, waits for them, and re-layouts: 17.3 us -> 6.91 us
    all_to_all x6 -> x0, blocking collectives: 71 us -> none  [the longest x4 54 us: spread(): return lax.all_to_all(copies, axes, 0, 0, tiled=True)]
    all_to_all x2, waiting for transfers between devices: 35.2 us -> 1.8 us  [combine(): by_col = lax.all_to_all(col_acc, ROW, 0, 0, tiled=True)]
    all_to_all x0 -> x3, starting transfers between devices: none -> 29.7 us  [spread(): return lax.all_to_all(copies, axes, 0, 0, tiled=True)]
    ppermute x0 -> x19, starting transfers between devices: none -> 27.4 us  [shift(): lax.ppermute(value, axis, [(i, (i + distance) % size) for i in range(size)])]
    unnamed x17 -> x13, local copies, waits for them, and re-layouts: 16.7 us -> 1.16 us
    all_to_all x0 -> x3, waiting for transfers between devices: none -> 15.4 us  [spread(): return lax.all_to_all(copies, axes, 0, 0, tiled=True)]
    all_gather x1 -> x0, blocking collectives: 13.6 us -> none  [gather_sets(): return lax.all_gather(lax.all_gather(piece, 'y'), 'z')]
    ppermute x0 -> x19, waiting for transfers between devices: none -> 11.6 us  [shift(): lax.ppermute(value, axis, [(i, (i + distance) % size) for i in range(size)])]
  transfers between devices with their start and end apart: 3 -> 25, of which waited for: 3 -> 12; matrix products, arithmetic and copies ran while one was open for 0% -> 3% of each run, Pallas kernels for 2% -> 29%
where the time goes in v2:
time: 232 us; the launch traced here: 228 us
  starting transfers between devices  74.1 us (32%)
  Pallas kernels  68 us (29%)
  waiting for transfers between devices  61.6 us (27%)
  between operations  13.7 us (6%)
  local copies, waits for them, and re-layouts  6.91 us (3%)
  other arithmetic  4.15 us (2%)
    all_gather x1, waiting for transfers between devices, gather_sets(): return lax.all_gather(near, 'z')  32.8 us
    pallas_call x1, Pallas kernels, form_and_apply(): pl.pallas_call(form_kernel, grid_spec=grid_spec, out_shape=[pltpu.HBM((sl...  30.7 us
    all_to_all x3, starting transfers between devices, spread(): return lax.all_to_all(copies, axes, 0, 0, tiled=True)  29.7 us
    ppermute x19, starting transfers between devices, shift(): lax.ppermute(value, axis, [(i, (i + distance) % size) for i in range(size)])  27.4 us
    pallas_call x3, Pallas kernels, apply_tiles(): pl.pallas_call(kernel, grid_spec=grid_spec, out_shape=jax.ShapeDtypeStruc...  27.1 us
    all_to_all x2, starting transfers between devices, combine(): by_col = lax.all_to_all(col_acc, ROW, 0, 0, tiled=True)  16.9 us
    all_to_all x3, waiting for transfers between devices, spread(): return lax.all_to_all(copies, axes, 0, 0, tiled=True)  15.4 us
    ppermute x19, waiting for transfers between devices, shift(): lax.ppermute(value, axis, [(i, (i + distance) % size) for i in range(size)])  11.6 us
  transfers between devices with their start and end apart: 25, of which 12 were waited for; matrix products, arithmetic and copies ran while one was open for 3% of the time, Pallas kernels for 29%

profile of v2, /device:TPU:0, one launch (start us, length us, event | category | flops | bytes accessed | tf_op | source)
XLA Modules:
  0.0 228.5 jit_solution(9386882903029587183)
XLA Ops:
  12.9 2.7 %collective-permute-done.1 = f32[48,512]{1,0:T(8,128)S(1)} collective-permute-done((f32[48,512]{1,0:T(8,128)S(1)}, f32[48,512]{1,0:T(8,128)S(1)}, u32[]{:S(2)}, u32[]{:S(2)}) %collective-permute-start.1) | collective-permute-done | bytes 98336 | tf_op jit(solution)/shard_map/ppermute | solution.py:229
  21.5 8.7 %prepare_rows.1.prepared_ref = bf16[8,16,512,48]{3,2,1,0:T(8,128)(2,1)} custom-call(f32[48,4096]{1,0:T(8,128)S(1)} %bitcast.85), custom_call_target="tpu_custom_call" | custom-call | flops 100000000 | bytes 20971520 | tf_op jit(solution)/shard_map/prepare_rows/pallas_call | solution.py:60
  30.2 32.8 %all-gather.3.cloned.1.call-done.col_ref = f32[32,48,512]{2,1,0:T(8,128)} async-done(((f32[4,48,512]{2,1,0:T(8,128)}), f32[32,48,512]{2,1,0:T(8,128)}) %all-gather.3.cloned.1.call-update) | async-done | bytes 3145744 | tf_op jit(solution)/shard_map/all_gather | solution.py:253
  63.9 7.2 %all-to-all-start = ((f32[32,8,512]{2,1,0:T(8,128)}), f32[32,8,512]{2,1,0:T(8,128)S(1)}, u32[]{:S(2)}, u32[]{:S(2)}) async-start(f32[32,8,512]{2,1,0:T(8,128)} %broadcast_in_dim.32), calls=%async_computation | async-start | bytes 1048576 | tf_op jit(solution)/shard_map/all_to_all | solution.py:234
  71.1 30.7 %form_and_apply.1 = (bf16[10,512,512]{2,1,0:T(8,128)(2,1)}, bf16[10,512,512]{2,1,0:T(8,128)(2,1)}, f32[32,8,512]{2,1,0:T(8,128)}) custom-call(s32[6,10]{1,0:T(8,128)S(1)} %stack.52.table, bf16[8,16,512,48]{3,2,1,0:T(8,128)(2,1)} %prepare_rows.1.prepared_ref, f32[32,48,512]{2,1,0:T(8,128)} %all-gather.3.cloned.1.call-done.col_ref, f32[8,8,512]{2,1,0:T(8,128)S(1)} %bitcast.87), custom_call_target="tpu_custom_call" | custom-call | flops 30000001024 | bytes 31457280 | tf_op jit(solution)/shard_map/form_and_apply/pallas_call | solution.py:147
  101.8 12.4 %all-to-all-start.1 = ((f32[32,8,512]{2,1,0:T(8,128)}), f32[32,8,512]{2,1,0:T(8,128)S(1)}, u32[]{:S(2)}, u32[]{:S(2)}) async-start(f32[32,8,512]{2,1,0:T(8,128)} %get-tuple-element.14), calls=%async_computation.1 | async-start | bytes 1048576 | tf_op jit(solution)/shard_map/all_to_all | solution.py:257
  114.2 9.0 %apply_rows.2 = f32[8,8,512]{2,1,0:T(8,128)S(1)} custom-call(s32[6,10]{1,0:T(8,128)S(1)} %stack.52.table, bf16[10,512,512]{2,1,0:T(8,128)(2,1)} %get-tuple-element.11.high_ref, bf16[10,512,512]{2,1,0:T(8,128)(2,1)} %get-tuple-element.12.low_ref, f32[32,8,512]{2,1,0:T(8,128)S(1)} %all-to-all-done.col_vec), custom_call_target="tpu_custom_call" | custom-call | flops 3000000000 | bytes 12582912 | tf_op jit(solution)/shard_map/apply_rows/pallas_call | solution.py:194
  123.1 1.9 collective-permute-start.3
  126.9 4.8 %collective-permute-start.5 = (f32[8,512]{1,0:T(8,128)S(1)}, f32[8,512]{1,0:T(8,128)S(1)}, u32[]{:S(2)}, u32[]{:S(2)}) collective-permute-start(f32[8,512]{1,0:T(8,128)S(1)} %get-tuple-element.24), channel_id=1, source_target_pairs={{0,4},{2,6},{4,0},{6,2},{1,5},{3,7},{5,1},{7,3},{8,12},{10,14},{12... | collective-permute-start | bytes 49160 | tf_op jit(solution)/shard_map/ppermute | solution.py:229
  131.6 1.9 collective-permute-start.4
  133.6 1.7 collective-permute-done.4
  136.2 3.8 %collective-permute-start.12 = (f32[8,512]{1,0:T(8,128)S(1)}, f32[8,512]{1,0:T(8,128)S(1)}, u32[]{:S(2)}, u32[]{:S(2)}) collective-permute-start(f32[8,512]{1,0:T(8,128)S(1)} %get-tuple-element.18), channel_id=1, source_target_pairs={{0,4},{2,6},{4,0},{6,2},{1,5},{3,7},{5,1},{7,3},{8,12},{10,14},{12... | collective-permute-start | bytes 49160 | tf_op jit(solution)/shard_map/ppermute | solution.py:229
  140.9 9.8 %all-to-all-start.2 = ((f32[32,8,512]{2,1,0:T(8,128)}), f32[32,8,512]{2,1,0:T(8,128)S(1)}, u32[]{:S(2)}, u32[]{:S(2)}) async-start(f32[32,8,512]{2,1,0:T(8,128)} %broadcast_in_dim.33), calls=%async_computation.2 | async-start | bytes 1048576 | tf_op jit(solution)/shard_map/all_to_all | solution.py:234
  152.1 9.2 %apply_cols.1 = f32[32,8,512]{2,1,0:T(8,128)} custom-call(s32[6,10]{1,0:T(8,128)S(1)} %stack.52.table, bf16[10,512,512]{2,1,0:T(8,128)(2,1)} %get-tuple-element.11.high_ref, bf16[10,512,512]{2,1,0:T(8,128)(2,1)} %get-tuple-element.12.low_ref, f32[8,8,512]{2,1,0:T(8,128)S(1)} %constant_dynamic-update-slice_fusion.row_vec), custom_call_target="tpu_custom_call" | custom-call | flops 3000000000 | bytes 12582912 | tf_op jit(solution)/shard_map/apply_cols/pallas_call | solution.py:194
  161.3 5.5 %all-to-all-done.2.col_vec = f32[32,8,512]{2,1,0:T(8,128)S(1)} async-done(((f32[32,8,512]{2,1,0:T(8,128)}), f32[32,8,512]{2,1,0:T(8,128)S(1)}, u32[]{:S(2)}, u32[]{:S(2)}) %all-to-all-start.2) | async-done | bytes 524320 | tf_op jit(solution)/shard_map/all_to_all | solution.py:234
  166.8 4.5 %all-to-all-start.3 = ((f32[32,8,512]{2,1,0:T(8,128)}), f32[32,8,512]{2,1,0:T(8,128)S(1)}, u32[]{:S(2)}, u32[]{:S(2)}) async-start(f32[32,8,512]{2,1,0:T(8,128)} %apply_cols.1), calls=%async_computation.3 | async-start | bytes 1048576 | tf_op jit(solution)/shard_map/all_to_all | solution.py:257
  171.4 9.0 %apply_rows.3 = f32[8,8,512]{2,1,0:T(8,128)S(1)} custom-call(s32[6,10]{1,0:T(8,128)S(1)} %stack.52.table, bf16[10,512,512]{2,1,0:T(8,128)(2,1)} %get-tuple-element.11.high_ref, bf16[10,512,512]{2,1,0:T(8,128)(2,1)} %get-tuple-element.12.low_ref, f32[32,8,512]{2,1,0:T(8,128)S(1)} %all-to-all-done.2.col_vec), custom_call_target="tpu_custom_call" | custom-call | flops 3000000000 | bytes 12582912 | tf_op jit(solution)/shard_map/apply_rows/pallas_call | solution.py:194
  181.7 2.0 collective-permute-start.10
  184.5 2.5 %collective-permute-start.8 = (f32[8,512]{1,0:T(8,128)S(1)}, f32[8,512]{1,0:T(8,128)S(1)}, u32[]{:S(2)}, u32[]{:S(2)}) collective-permute-start(f32[8,512]{1,0:T(8,128)S(1)} %get-tuple-element.19), channel_id=1, source_target_pairs={{0,6},{2,0},{4,2},{6,4},{1,7},{3,1},{5,3},{7,5},{8,14},{10,8},{12,... | collective-permute-start | bytes 49160 | tf_op jit(solution)/shard_map/ppermute | solution.py:229
  187.6 1.8 all-to-all-done.3
  189.6 1.9 collective-permute-start.15
  191.5 2.1 collective-permute-start.16
  195.0 12.7 %all-to-all-start.4 = ((f32[256,1,128]{2,1,0:T(1,128)}), f32[256,1,128]{2,1,0:T(1,128)S(1)}, u32[]{:S(2)}, u32[]{:S(2)}) async-start(f32[256,1,128]{2,1,0:T(1,128)} %broadcast_in_dim.35), calls=%async_computation.4 | async-start | bytes 262144 | tf_op jit(solution)/shard_map/all_to_all | solution.py:234
  209.2 9.9 %all-to-all-done.4 = f32[256,1,128]{2,1,0:T(1,128)S(1)} async-done(((f32[256,1,128]{2,1,0:T(1,128)}), f32[256,1,128]{2,1,0:T(1,128)S(1)}, u32[]{:S(2)}, u32[]{:S(2)}) %all-to-all-start.4) | async-done | bytes 131104 | tf_op jit(solution)/shard_map/all_to_all | solution.py:234
  (77 shorter events, 26.3 us)
Async XLA Ops:
  6.5 56.5 %all-gather.3.cloned.1.call-start = ((), (), s32[]{:S(2)}) async-start(), calls=%async_computation.5 | async-start | bytes 3538944 | tf_op jit(solution)/shard_map/all_gather | solution.py:253
  7.4 5.5 %collective-permute-start.2 = (f32[48,512]{1,0:T(8,128)S(1)}, f32[48,512]{1,0:T(8,128)S(1)}, u32[]{:S(2)}, u32[]{:S(2)}) collective-permute-start(f32[48,512]{1,0:T(8,128)S(1)} %constant_dynamic-slice_fusion), channel_id=1, source_target_pairs={{0,24},{8,0},{16,8},{24,16},{1,25},{9,1},{17,9},{25,17},{2,26},{10... | collective-permute-start | bytes 294920 | tf_op jit(solution)/shard_map/ppermute | solution.py:229
  8.7 6.9 %collective-permute-start.1 = (f32[48,512]{1,0:T(8,128)S(1)}, f32[48,512]{1,0:T(8,128)S(1)}, u32[]{:S(2)}, u32[]{:S(2)}) collective-permute-start(f32[48,512]{1,0:T(8,128)S(1)} %constant_dynamic-slice_fusion), channel_id=1, source_target_pairs={{0,16},{8,24},{16,0},{24,8},{1,17},{9,25},{17,1},{25,9},{2,18},{10... | collective-permute-start | bytes 294920 | tf_op jit(solution)/shard_map/ppermute | solution.py:229
  9.3 7.2 %collective-permute-start = (f32[48,512]{1,0:T(8,128)S(1)}, f32[48,512]{1,0:T(8,128)S(1)}, u32[]{:S(2)}, u32[]{:S(2)}) collective-permute-start(f32[48,512]{1,0:T(8,128)S(1)} %constant_dynamic-slice_fusion), channel_id=1, source_target_pairs={{0,8},{8,16},{16,24},{24,0},{1,9},{9,17},{17,25},{25,1},{2,10},{10... | collective-permute-start | bytes 294920 | tf_op jit(solution)/shard_map/ppermute | solution.py:229
  63.9 37.9 %all-to-all-start = ((f32[32,8,512]{2,1,0:T(8,128)}), f32[32,8,512]{2,1,0:T(8,128)S(1)}, u32[]{:S(2)}, u32[]{:S(2)}) async-start(f32[32,8,512]{2,1,0:T(8,128)} %broadcast_in_dim.32), calls=%async_computation | async-start | bytes 1048576 | tf_op jit(solution)/shard_map/all_to_all | solution.py:234
  101.8 31.8 %all-to-all-start.1 = ((f32[32,8,512]{2,1,0:T(8,128)}), f32[32,8,512]{2,1,0:T(8,128)S(1)}, u32[]{:S(2)}, u32[]{:S(2)}) async-start(f32[32,8,512]{2,1,0:T(8,128)} %get-tuple-element.14), calls=%async_computation.1 | async-start | bytes 1048576 | tf_op jit(solution)/shard_map/all_to_all | solution.py:257
  123.1 2.8 %collective-permute-start.3 = (f32[4,8,512]{2,1,0:T(8,128)S(1)}, f32[4,8,512]{2,1,0:T(8,128)S(1)}, u32[]{:S(2)}, u32[]{:S(2)}) collective-permute-start(f32[4,8,512]{2,1,0:T(8,128)S(1)} %slice.61), channel_id=1, source_target_pairs={{0,1},{1,0},{2,3},{3,2},{4,5},{5,4},{6,7},{7,6},{8,9},{9,8},{10,11... | collective-permute-start | bytes 196616 | tf_op jit(solution)/shard_map/ppermute | solution.py:229
  126.0 7.6 %collective-permute-start.6 = (f32[8,512]{1,0:T(8,128)S(1)}, f32[8,512]{1,0:T(8,128)S(1)}, u32[]{:S(2)}, u32[]{:S(2)}) collective-permute-start(f32[8,512]{1,0:T(8,128)S(1)} %get-tuple-element.23), channel_id=1, source_target_pairs={{0,2},{2,4},{4,6},{6,0},{1,3},{3,5},{5,7},{7,1},{8,10},{10,12},{12... | collective-permute-start | bytes 49160 | tf_op jit(solution)/shard_map/ppermute | solution.py:229
  126.9 6.8 %collective-permute-start.5 = (f32[8,512]{1,0:T(8,128)S(1)}, f32[8,512]{1,0:T(8,128)S(1)}, u32[]{:S(2)}, u32[]{:S(2)}) collective-permute-start(f32[8,512]{1,0:T(8,128)S(1)} %get-tuple-element.24), channel_id=1, source_target_pairs={{0,4},{2,6},{4,0},{6,2},{1,5},{3,7},{5,1},{7,3},{8,12},{10,14},{12... | collective-permute-start | bytes 49160 | tf_op jit(solution)/shard_map/ppermute | solution.py:229
  131.6 3.7 %collective-permute-start.4 = (f32[8,512]{1,0:T(8,128)S(1)}, f32[8,512]{1,0:T(8,128)S(1)}, u32[]{:S(2)}, u32[]{:S(2)}) collective-permute-start(f32[8,512]{1,0:T(8,128)S(1)} %get-tuple-element.22), channel_id=1, source_target_pairs={{0,6},{2,0},{4,2},{6,4},{1,7},{3,1},{5,3},{7,5},{8,14},{10,8},{12,... | collective-permute-start | bytes 49160 | tf_op jit(solution)/shard_map/ppermute | solution.py:229
  135.4 15.3 %collective-permute-start.11 = (f32[8,512]{1,0:T(8,128)S(1)}, f32[8,512]{1,0:T(8,128)S(1)}, u32[]{:S(2)}, u32[]{:S(2)}) collective-permute-start(f32[8,512]{1,0:T(8,128)S(1)} %get-tuple-element.18), channel_id=1, source_target_pairs={{0,2},{2,4},{4,6},{6,0},{1,3},{3,5},{5,7},{7,1},{8,10},{10,12},{12... | collective-permute-start | bytes 49160 | tf_op jit(solution)/shard_map/ppermute | solution.py:229
  136.2 14.5 %collective-permute-start.12 = (f32[8,512]{1,0:T(8,128)S(1)}, f32[8,512]{1,0:T(8,128)S(1)}, u32[]{:S(2)}, u32[]{:S(2)}) collective-permute-start(f32[8,512]{1,0:T(8,128)S(1)} %get-tuple-element.18), channel_id=1, source_target_pairs={{0,4},{2,6},{4,0},{6,2},{1,5},{3,7},{5,1},{7,3},{8,12},{10,14},{12... | collective-permute-start | bytes 49160 | tf_op jit(solution)/shard_map/ppermute | solution.py:229
  140.1 10.7 %collective-permute-start.13 = (f32[8,512]{1,0:T(8,128)S(1)}, f32[8,512]{1,0:T(8,128)S(1)}, u32[]{:S(2)}, u32[]{:S(2)}) collective-permute-start(f32[8,512]{1,0:T(8,128)S(1)} %get-tuple-element.18), channel_id=1, source_target_pairs={{0,6},{2,0},{4,2},{6,4},{1,7},{3,1},{5,3},{7,5},{8,14},{10,8},{12,... | collective-permute-start | bytes 49160 | tf_op jit(solution)/shard_map/ppermute | solution.py:229
  140.9 25.9 %all-to-all-start.2 = ((f32[32,8,512]{2,1,0:T(8,128)}), f32[32,8,512]{2,1,0:T(8,128)S(1)}, u32[]{:S(2)}, u32[]{:S(2)}) async-start(f32[32,8,512]{2,1,0:T(8,128)} %broadcast_in_dim.33), calls=%async_computation.2 | async-start | bytes 1048576 | tf_op jit(solution)/shard_map/all_to_all | solution.py:234
  150.8 1.3 collective-permute-start.14
  166.8 22.6 %all-to-all-start.3 = ((f32[32,8,512]{2,1,0:T(8,128)}), f32[32,8,512]{2,1,0:T(8,128)S(1)}, u32[]{:S(2)}, u32[]{:S(2)}) async-start(f32[32,8,512]{2,1,0:T(8,128)} %apply_cols.1), calls=%async_computation.3 | async-start | bytes 1048576 | tf_op jit(solution)/shard_map/all_to_all | solution.py:257
  181.7 7.8 %collective-permute-start.10 = (f32[8,512]{1,0:T(8,128)S(1)}, f32[8,512]{1,0:T(8,128)S(1)}, u32[]{:S(2)}, u32[]{:S(2)}) collective-permute-start(f32[8,512]{1,0:T(8,128)S(1)} %get-tuple-element.20), channel_id=1, source_target_pairs={{0,2},{2,4},{4,6},{6,0},{1,3},{3,5},{5,7},{7,1},{8,10},{10,12},{12... | collective-permute-start | bytes 49160 | tf_op jit(solution)/shard_map/ppermute | solution.py:229
  183.7 5.8 %collective-permute-start.9 = (f32[8,512]{1,0:T(8,128)S(1)}, f32[8,512]{1,0:T(8,128)S(1)}, u32[]{:S(2)}, u32[]{:S(2)}) collective-permute-start(f32[8,512]{1,0:T(8,128)S(1)} %get-tuple-element.21), channel_id=1, source_target_pairs={{0,4},{2,6},{4,0},{6,2},{1,5},{3,7},{5,1},{7,3},{8,12},{10,14},{12... | collective-permute-start | bytes 49160 | tf_op jit(solution)/shard_map/ppermute | solution.py:229
  184.5 5.0 %collective-permute-start.8 = (f32[8,512]{1,0:T(8,128)S(1)}, f32[8,512]{1,0:T(8,128)S(1)}, u32[]{:S(2)}, u32[]{:S(2)}) collective-permute-start(f32[8,512]{1,0:T(8,128)S(1)} %get-tuple-element.19), channel_id=1, source_target_pairs={{0,6},{2,0},{4,2},{6,4},{1,7},{3,1},{5,3},{7,5},{8,14},{10,8},{12,... | collective-permute-start | bytes 49160 | tf_op jit(solution)/shard_map/ppermute | solution.py:229
  189.6 18.2 %collective-permute-start.15 = (f32[8,512]{1,0:T(8,128)S(1)}, f32[8,512]{1,0:T(8,128)S(1)}, u32[]{:S(2)}, u32[]{:S(2)}) collective-permute-start(f32[8,512]{1,0:T(8,128)S(1)} %get-tuple-element.16), channel_id=1, source_target_pairs={{0,2},{2,4},{4,6},{6,0},{1,3},{3,5},{5,7},{7,1},{8,10},{10,12},{12... | collective-permute-start | bytes 49160 | tf_op jit(solution)/shard_map/ppermute | solution.py:229
  191.5 16.3 %collective-permute-start.16 = (f32[8,512]{1,0:T(8,128)S(1)}, f32[8,512]{1,0:T(8,128)S(1)}, u32[]{:S(2)}, u32[]{:S(2)}) collective-permute-start(f32[8,512]{1,0:T(8,128)S(1)} %get-tuple-element.16), channel_id=1, source_target_pairs={{0,4},{2,6},{4,0},{6,2},{1,5},{3,7},{5,1},{7,3},{8,12},{10,14},{12... | collective-permute-start | bytes 49160 | tf_op jit(solution)/shard_map/ppermute | solution.py:229
  193.6 14.2 %collective-permute-start.17 = (f32[8,512]{1,0:T(8,128)S(1)}, f32[8,512]{1,0:T(8,128)S(1)}, u32[]{:S(2)}, u32[]{:S(2)}) collective-permute-start(f32[8,512]{1,0:T(8,128)S(1)} %get-tuple-element.16), channel_id=1, source_target_pairs={{0,6},{2,0},{4,2},{6,4},{1,7},{3,1},{5,3},{7,5},{8,14},{10,8},{12,... | collective-permute-start | bytes 49160 | tf_op jit(solution)/shard_map/ppermute | solution.py:229
  195.0 24.0 %all-to-all-start.4 = ((f32[256,1,128]{2,1,0:T(1,128)}), f32[256,1,128]{2,1,0:T(1,128)S(1)}, u32[]{:S(2)}, u32[]{:S(2)}) async-start(f32[256,1,128]{2,1,0:T(1,128)} %broadcast_in_dim.35), calls=%async_computation.4 | async-start | bytes 262144 | tf_op jit(solution)/shard_map/all_to_all | solution.py:234
  207.8 1.3 collective-permute-start.18
  (4 other events, 22.0 us)
Sparse Core Ops, SparseCore 0:
  17.5 45.4 all-gather.2

commit v3 on v2

v3 whole, which is shorter than its diff:
```python
import functools
import math

import jax
import jax.numpy as jnp
from jax import lax
from jax.experimental import pallas as pl
from jax.experimental.pallas import tpu as pltpu
from jax.sharding import Mesh
from jax.sharding import PartitionSpec as P

TILE = 512
ROW = ("z", "y")
COL = ("x", "core")
ROW_AT, ROW_NEAR, COL_AT, SOURCE, PLACE, STAGE, LIVE, CROSSING = range(8)
PER_STAGE = 3
LAST_STAGE = 4
BY_ROWS = (((1,), (0,)), ((), ()))
BY_COLS = (((1,), (1,)), ((), ()))
LOG2E = math.log2(math.e)
GROUPS = 6
DEPTH = 8 * GROUPS
CHUNK = 256
HALF = 256


def in_hbm(value):
    return pltpu.with_memory_space_constraint(value, pltpu.HBM)


def split3(value):
    high = value.astype(jnp.bfloat16).astype(jnp.float32)
    rest = value - high
    mid = rest.astype(jnp.bfloat16).astype(jnp.float32)
    return high, mid, rest - mid


def rows_of(ref, snapshot, scale, norm_at, one_at):
    width = ref.shape[-1]
    place = lax.broadcasted_iota(jnp.int32, (8, width), 0)
    parts = [
        jnp.broadcast_to(ref[16 * q + snapshot : 16 * q + snapshot + 1, :], (8, width))
        for q in range(3)
    ]
    norm = (-0.5 * LOG2E) * (parts[0] * parts[0] + parts[1] * parts[1] + parts[2] * parts[2])
    out = jnp.where(place == norm_at, norm, jnp.where(place == one_at, 1.0, 0.0))
    for q in range(3):
        out = jnp.where(place == q, parts[q] * scale if scale != 1.0 else parts[q], out)
    return out


def prepare_kernel(pos_ref, out_ref):
    for snapshot in range(16):
        high, mid, low = split3(rows_of(pos_ref, snapshot, LOG2E, 4, 3))
        stacked = jnp.concatenate([high, high, mid, mid, high, low], axis=0)
        out_ref[0, snapshot] = stacked.T.astype(jnp.bfloat16)


def prepare_rows(pos):
    tiles = pos.shape[1] // TILE
    return pl.pallas_call(
        prepare_kernel,
        grid=(tiles,),
        in_specs=[pl.BlockSpec((48, TILE), lambda i: (0, i))],
        out_specs=pl.BlockSpec((1, 16, TILE, DEPTH), lambda i: (i, 0, 0, 0)),
        out_shape=jax.ShapeDtypeStruct((tiles, 16, TILE, DEPTH), jnp.bfloat16),
        compiler_params=pltpu.CompilerParams(vmem_limit_bytes=32 << 20),
        cost_estimate=pl.CostEstimate(flops=10**8, bytes_accessed=20 << 20, transcendentals=0),
        name="prepare_rows",
    )(pos)


def multiply(field, high, low, dims):
    terms = jnp.concatenate(split3(field), axis=0).astype(jnp.bfloat16)
    dot = functools.partial(
        lax.dot_general, dimension_numbers=dims, preferred_element_type=jnp.float32
    )
    by_high = dot(terms, high)
    by_low = dot(terms[:16], low)
    return (by_high[0:8] + by_low[0:8]) + (by_high[8:16] + by_low[8:16]) + by_high[16:24]


def stage_kernel(stage, sources, table, prepared_ref, row_vec, *refs):
    places = refs[:sources]
    high_ref, low_ref, row_acc, col_acc, tile, cols, high_tile, low_tile, sems = refs[-9:]
    if stage == 0:
        row_acc[...] = jnp.zeros_like(row_acc)
        col_acc[...] = jnp.zeros_like(col_acc)
    else:
        row_acc[...] = refs[sources + 2][...]
        col_acc[...] = refs[sources + 3][...]

    def form(slot):
        for source in range(sources):

            @pl.when(table[SOURCE, slot] == source)
            def _():
                tile[...] = places[source][table[PLACE, slot]]

        for snapshot in range(16):
            high, mid, low = split3(rows_of(tile, snapshot, 1.0, 3, 4))
            stacked = jnp.concatenate([high, mid, high, mid, low, high], axis=0)
            cols[snapshot] = stacked.astype(jnp.bfloat16)
        row_at = table[ROW_AT, slot]

        def step(at, carry):
            start = pl.multiple_of(at * CHUNK, CHUNK)
            for half in range(TILE // HALF):
                total = None
                for snapshot in range(16):
                    exponent = jnp.dot(
                        prepared_ref[row_at, snapshot, pl.ds(start, CHUNK), :],
                        cols[snapshot, :, half * HALF : (half + 1) * HALF],
                        preferred_element_type=jnp.float32,
                    )
                    term = jnp.exp2(exponent)
                    total = term if total is None else total + term
                high = total.astype(jnp.bfloat16)
                low = (total - high.astype(jnp.float32)).astype(jnp.bfloat16)
                place = (pl.ds(start, CHUNK), pl.ds(half * HALF, HALF))
                high_tile[place] = high
                low_tile[place] = low
            return carry

        lax.fori_loop(0, TILE // CHUNK, step, 0)
        copies = [
            pltpu.make_async_copy(high_tile, high_ref.at[slot], sems.at[0]),
            pltpu.make_async_copy(low_tile, low_ref.at[slot], sems.at[1]),
        ]
        for copy in copies:
            copy.start()
        row_acc[table[ROW_NEAR, slot]] += multiply(
            tile[48:56, :], high_tile[...], low_tile[...], BY_COLS
        )

        @pl.when(table[CROSSING, slot] != 0)
        def _():
            col_acc[table[COL_AT, slot]] += multiply(
                row_vec[row_at], high_tile[...], low_tile[...], BY_ROWS
            )

        for copy in copies:
            copy.wait()

    def visit(slot, carry):
        @pl.when(table[STAGE, slot] == stage)
        def _():
            form(slot)

        return carry

    lax.fori_loop(0, high_ref.shape[0], visit, 0)


def form_stage(stage, table, prepared, row_vec, places, state, blocks):
    slots = table.shape[1]
    tiles = row_vec.shape[0]
    vmem = pl.BlockSpec(memory_space=pltpu.VMEM)
    hbm = pl.BlockSpec(memory_space=pltpu.HBM)
    shapes = [
        pltpu.HBM((slots, TILE, TILE), jnp.bfloat16),
        pltpu.HBM((slots, TILE, TILE), jnp.bfloat16),
        jax.ShapeDtypeStruct((tiles, 8, TILE), jnp.float32),
        jax.ShapeDtypeStruct((blocks, 8, TILE), jnp.float32),
    ]
    first = 3 + len(places)
    return pl.pallas_call(
        functools.partial(stage_kernel, stage, len(places)),
        in_specs=[pl.BlockSpec(memory_space=pltpu.SMEM)]
        + [vmem] * (2 + len(places))
        + ([hbm, hbm, vmem, vmem] if state else []),
        out_specs=[hbm, hbm, vmem, vmem],
        out_shape=shapes,
        input_output_aliases={first + i: i for i in range(len(state))},
        scratch_shapes=[
            pltpu.VMEM((56, TILE), jnp.float32),
            pltpu.VMEM((16, DEPTH, TILE), jnp.bfloat16),
            pltpu.VMEM((TILE, TILE), jnp.bfloat16),
            pltpu.VMEM((TILE, TILE), jnp.bfloat16),
            pltpu.SemaphoreType.DMA((2,)),
        ],
        compiler_params=pltpu.CompilerParams(vmem_limit_bytes=8 << 20),
        cost_estimate=pl.CostEstimate(
            flops=8 * 10**9, bytes_accessed=8 << 20, transcendentals=10**7
        ),
        name=f"form_{stage}",
    )(table, prepared, row_vec, *places, *state)


def apply_kernel(wanted, table, high_ref, low_ref, field, acc, high, low, sems):
    slots = high_ref.shape[0]

    def copies(slot):
        return [
            pltpu.make_async_copy(high_ref.at[slot], high.at[slot], sems.at[0, slot]),
            pltpu.make_async_copy(low_ref.at[slot], low.at[slot], sems.at[1, slot]),
        ]

    for slot in range(slots):

        @pl.when(table[wanted, slot] != 0)
        def _():
            for copy in copies(slot):
                copy.start()

    acc[...] = jnp.zeros_like(acc)

    def visit(slot, carry):
        @pl.when(table[wanted, slot] != 0)
        def _():
            for copy in copies(slot):
                copy.wait()
            row_at, col_at = table[ROW_NEAR, slot], table[COL_AT, slot]
            if wanted == LIVE:
                acc[row_at] += multiply(field[col_at], high[slot], low[slot], BY_COLS)
            else:
                acc[col_at] += multiply(field[row_at], high[slot], low[slot], BY_ROWS)

        return carry

    lax.fori_loop(0, slots, visit, 0)


def apply_tiles(wanted, name, table, high, low, field, count):
    vmem = pl.BlockSpec(memory_space=pltpu.VMEM)
    hbm = pl.BlockSpec(memory_space=pltpu.HBM)
    return pl.pallas_call(
        functools.partial(apply_kernel, wanted),
        in_specs=[pl.BlockSpec(memory_space=pltpu.SMEM), hbm, hbm, vmem],
        out_specs=vmem,
        out_shape=jax.ShapeDtypeStruct((count, 8, TILE), jnp.float32),
        scratch_shapes=[
            pltpu.VMEM(high.shape, high.dtype),
            pltpu.VMEM(low.shape, low.dtype),
            pltpu.SemaphoreType.DMA((2, high.shape[0])),
        ],
        compiler_params=pltpu.CompilerParams(vmem_limit_bytes=16 << 20),
        cost_estimate=pl.CostEstimate(
            flops=3 * 10**9, bytes_accessed=12 << 20, transcendentals=0
        ),
        name=name,
    )(table, in_hbm(high), in_hbm(low), field)


def shift(value, axis, distance):
    size = lax.axis_size(axis)
    return lax.ppermute(value, axis, [(i, (i + distance) % size) for i in range(size)])


def spread(piece, axes):
    copies = jnp.broadcast_to(piece, (lax.axis_size(axes),) + piece.shape)
    return lax.all_to_all(copies, axes, 0, 0, tiled=True)


def spread_near(piece):
    mine = jnp.stack([piece] + [shift(piece, "x", d) for d in range(1, lax.axis_size("x"))])
    return jnp.concatenate([mine, shift(mine, "core", 1)], axis=0)


def reduce_near(row_acc):
    size = lax.axis_size("x")
    mine = row_acc[:size] + shift(row_acc[size:], "core", 1)
    total = mine[0]
    for d in range(1, size):
        total = total + shift(mine[d], "x", size - d)
    return total


def gather_near(piece):
    near = jnp.stack([piece] + [shift(piece, "y", d) for d in range(1, lax.axis_size("y"))])
    size, half = lax.axis_size("z"), near.shape[0] // 2
    arrived = [[near]]
    behind = ahead = near
    for distance in range(1, size // 2 + 1):
        if distance == size // 2:
            behind, ahead = behind[:half], ahead[half:]
        behind, ahead = shift(behind, "z", 1), shift(ahead, "z", size - 1)
        arrived.append([behind, ahead])
    return arrived


def plan(source, live):
    stage = jnp.where(live, (source + 1) // 2, LAST_STAGE)
    slots = jnp.arange(source.shape[0])
    key = stage * source.shape[0] + slots
    before = key[None, :] <= key[:, None]
    rank = jnp.sum(before.astype(jnp.int32), axis=1)
    turn = jnp.max(
        jnp.where(before, PER_STAGE * stage[None, :] + rank[:, None] - rank[None, :], 0), axis=1
    )
    return jnp.where(live, jnp.minimum(turn // PER_STAGE, LAST_STAGE), -1)


def combine(row_acc, col_acc):
    by_col = lax.all_to_all(col_acc, ROW, 0, 0, tiled=True)
    return reduce_near(row_acc) + jnp.sum(by_col, axis=0)


def near_tile(tile, x, core, size):
    return jnp.where(tile % 2 == core, 0, size) + (x - tile // 2) % size


def per_device(positions, vectors, pairs, valid):
    grid_row = lax.axis_index(ROW)
    grid_col = lax.axis_index(COL)
    x, core = lax.axis_index("x"), lax.axis_index("core")
    y, z = lax.axis_index("y"), lax.axis_index("z")
    size_x, size_y = lax.axis_size("x"), lax.axis_size("y")
    block = positions.shape[2]
    tiles = block // TILE
    blocks = lax.axis_size(ROW)
    local_rows = pairs[0, 0, :, 0]
    local_cols = pairs[0, 0, :, 1]
    live = valid[0, 0] != 0
    crossing = (grid_row * tiles + local_rows) != (local_cols * tiles + grid_col)
    size_z = lax.axis_size("z")
    behind = (z - local_cols // size_y) % size_z
    place = (y - local_cols % size_y) % size_y
    far = behind == size_z // 2
    upper = place >= size_y // 2
    source = jnp.where(behind < size_z // 2, 2 * behind - 1, 2 * (size_z - behind))
    source = jnp.where(behind == 0, 0, jnp.where(far & ~upper, size_z - 1, source))
    place = jnp.where(far & upper, place - size_y // 2, place)
    table = jnp.stack(
        [
            local_rows,
            near_tile(local_rows, x, core, size_x),
            local_cols,
            source,
            place,
            plan(source, live),
            live.astype(jnp.int32),
            (live & crossing).astype(jnp.int32),
        ],
        axis=0,
    ).astype(jnp.int32)

    flat = positions.transpose(1, 0, 2).reshape(48, block)
    own = jnp.concatenate(
        [
            lax.dynamic_slice_in_dim(flat, grid_col * TILE, TILE, 1),
            lax.dynamic_slice_in_dim(vectors, grid_col * TILE, TILE, 1),
        ],
        axis=0,
    )
    row_vec = vectors.reshape(8, tiles, TILE).transpose(1, 0, 2)
    prepared = prepare_rows(flat)
    places, state = [], []
    for stage, arrived in enumerate(gather_near(own)):
        places = places + arrived
        state = form_stage(stage, table, prepared, row_vec, places, state, blocks)
    high, low, row_acc, col_acc = state
    first = combine(row_acc, col_acc)

    col_vec = spread(first, ROW)
    col_acc = apply_tiles(CROSSING, "apply_cols", table, high, low, spread_near(first), blocks)
    row_acc = apply_tiles(LIVE, "apply_rows", table, high, low, col_vec, tiles)
    second = combine(row_acc, col_acc)

    rows = spread(second, COL)
    squares = jnp.sum(rows * rows, axis=(0, 2))
    squares = spread(jnp.broadcast_to(squares[:, None], (8, 128)), ROW)
    total = jnp.sum(squares[:, :, 0], axis=0) / (block * blocks)
    scaled = rows / jnp.sqrt(total + 1e-06)[None, :, None]
    return scaled.transpose(1, 0, 2).reshape(8, block)


def solution(mesh):
    physical = Mesh(mesh.devices.reshape(8, 4, 4, 2), ("z", "y", "x", "core"))
    placed = (
        P(None, None, ROW),
        P(None, ROW),
        P(ROW, COL, None, None),
        P(ROW, COL, None),
    )
    return jax.shard_map(
        per_device, mesh=physical, in_specs=placed, out_specs=P(None, ROW), check_vma=False
    )
```

time: 232 us -> 197 us (0.85)
  waiting for transfers between devices: 61.6 us -> 31.6 us
  blocking collectives: 0 us -> 28.6 us
  Pallas kernels: 68 us -> 50.8 us
  between operations: 13.7 us -> 0.4 us
  local copies, waits for them, and re-layouts: 6.91 us -> 4.55 us
    all_gather x1 -> x0, waiting for transfers between devices: 32.8 us -> none  [gather_sets(): return lax.all_gather(near, 'z')]
    all_to_all x0 -> x2, blocking collectives: none -> 28.6 us  [spread(): return lax.all_to_all(copies, axes, 0, 0, tiled=True)]
    all_to_all x3 -> x1, starting transfers between devices: 29.7 us -> 4.52 us  [spread(): return lax.all_to_all(copies, axes, 0, 0, tiled=True)]
    ppermute x19 -> x23, starting transfers between devices: 27.4 us -> 46.4 us  [shift(): lax.ppermute(value, axis, [(i, (i + distance) % size) for i in range(size)])]
    pallas_call x5 -> x7, Pallas kernels: 59.3 us -> 45.6 us  [the longest x5 35.8 us: form_stage(): pl.pallas_call(functools.partial(stage_kernel, stage, len(places)), in_sp...]
    all_to_all x2, waiting for transfers between devices: 1.8 us -> 11.1 us  [combine(): by_col = lax.all_to_all(col_acc, ROW, 0, 0, tiled=True)]
    all_to_all x2, starting transfers between devices: 16.9 us -> 22.5 us  [combine(): by_col = lax.all_to_all(col_acc, ROW, 0, 0, tiled=True)]
    all_to_all x3 -> x1, waiting for transfers between devices: 15.4 us -> 9.88 us  [spread(): return lax.all_to_all(copies, axes, 0, 0, tiled=True)]
  transfers between devices with their start and end apart: 25 -> 26, of which waited for: 12 -> 7; matrix products, arithmetic and copies ran while one was open for 3% -> 3% of each run, Pallas kernels for 29% -> 25%
where the time goes in v3:
time: 197 us; the launch traced here: 195 us
  starting transfers between devices  73.4 us (37%)
  Pallas kernels  50.8 us (26%)
  waiting for transfers between devices  31.6 us (16%)
  blocking collectives  28.6 us (15%)
  other arithmetic  5.21 us (3%)
  local copies, waits for them, and re-layouts  4.55 us (2%)
    ppermute x23, starting transfers between devices, shift(): lax.ppermute(value, axis, [(i, (i + distance) % size) for i in range(size)])  46.4 us
    pallas_call x5, Pallas kernels, form_stage(): pl.pallas_call(functools.partial(stage_kernel, stage, len(places)), in_sp...  35.8 us
    all_to_all x2, blocking collectives, spread(): return lax.all_to_all(copies, axes, 0, 0, tiled=True)  28.6 us
    all_to_all x2, starting transfers between devices, combine(): by_col = lax.all_to_all(col_acc, ROW, 0, 0, tiled=True)  22.5 us
    all_to_all x2, waiting for transfers between devices, combine(): by_col = lax.all_to_all(col_acc, ROW, 0, 0, tiled=True)  11.1 us
    ppermute x23, waiting for transfers between devices, shift(): lax.ppermute(value, axis, [(i, (i + distance) % size) for i in range(size)])  10.7 us
    all_to_all x1, waiting for transfers between devices, spread(): return lax.all_to_all(copies, axes, 0, 0, tiled=True)  9.88 us
    pallas_call x2, Pallas kernels, apply_tiles(): pl.pallas_call(functools.partial(apply_kernel, wanted), in_specs=[pl.Bloc...  9.79 us
  transfers between devices with their start and end apart: 26, of which 7 were waited for; matrix products, arithmetic and copies ran while one was open for 3% of the time, Pallas kernels for 25%

profile of v3, /device:TPU:0, one launch (start us, length us, event | category | flops | bytes accessed | tf_op | source)
XLA Modules:
  0.0 194.6 jit_solution(10973528687825441445)
XLA Ops:
  3.9 2.6 %collective-permute-start.2 = (f32[56,512]{1,0:T(8,128)S(1)}, f32[56,512]{1,0:T(8,128)S(1)}, u32[]{:S(2)}, u32[]{:S(2)}) collective-permute-start(f32[56,512]{1,0:T(8,128)S(1)} %get-tuple-element.53), channel_id=1, source_target_pairs={{0,24},{8,0},{16,8},{24,16},{1,25},{9,1},{17,9},{25,17},{2,26},{10... | collective-permute-start | bytes 344072 | tf_op jit(solution)/shard_map/ppermute | solution.py:247
  12.3 5.3 %prepare_rows.1.prepared_ref = bf16[8,16,512,48]{3,2,1,0:T(8,128)(2,1)S(1)} custom-call(f32[48,4096]{1,0:T(8,128)S(1)} %bitcast.112), custom_call_target="tpu_custom_call" | custom-call | flops 100000000 | bytes 20971520 | tf_op jit(solution)/shard_map/prepare_rows/pallas_call | solution.py:61
  17.7 5.9 %collective-permute-start.4 = (f32[4,56,512]{2,1,0:T(8,128)S(1)}, f32[4,56,512]{2,1,0:T(8,128)S(1)}, u32[]{:S(2)}, u32[]{:S(2)}) collective-permute-start(f32[4,56,512]{2,1,0:T(8,128)S(1)} %pad_maximum_fusion.refs_0_), channel_id=1, source_target_pairs={{0,224},{32,0},{64,32},{96,64},{128,96},{160,128},{192,160},{224,1... | collective-permute-start | bytes 1376264 | tf_op jit(solution)/shard_map/ppermute | solution.py:247
  25.3 7.3 %collective-permute-done.4.refs_2_ = f32[4,56,512]{2,1,0:T(8,128)S(1)} collective-permute-done((f32[4,56,512]{2,1,0:T(8,128)S(1)}, f32[4,56,512]{2,1,0:T(8,128)S(1)}, u32[]{:S(2)}, u32[]{:S(2)}) %collective-permute-start.4) | collective-permute-done | bytes 458784 | tf_op jit(solution)/shard_map/ppermute | solution.py:247
  32.5 7.0 %collective-permute-start.6 = (f32[4,56,512]{2,1,0:T(8,128)S(1)}, f32[4,56,512]{2,1,0:T(8,128)S(1)}, u32[]{:S(2)}, u32[]{:S(2)}) collective-permute-start(f32[4,56,512]{2,1,0:T(8,128)S(1)} %collective-permute-done.4.refs_2_), channel_id=1, source_target_pairs={{0,224},{32,0},{64,32},{96,64},{128,96},{160,128},{192,160},{224,1... | collective-permute-start | bytes 1376264 | tf_op jit(solution)/shard_map/ppermute | solution.py:247
  39.5 13.1 %form_1.1 = (bf16[10,512,512]{2,1,0:T(8,128)(2,1)}, bf16[10,512,512]{2,1,0:T(8,128)(2,1)}, f32[8,8,512]{2,1,0:T(8,128)S(1)}, f32[32,8,512]{2,1,0:T(8,128)}) custom-call(s32[8,10]{1,0:T(8,128)S(1)} %stack.39.table, bf16[8,16,512,48]{3,2,1,0:T(8,128)(2,1)S(1)} %prepare_rows.1.prepared_ref, ...), custom_call_target="tpu_custom_call", output_to_operand_aliasing={{0}: (6, {}), {1}: (7, {}), {2}: (8, {}), {3}: (9, {})} | custom-call | flops 8000000000 | bytes 8388608 | tf_op jit(solution)/shard_map/form_1/pallas_call | solution.py:167
  52.7 3.3 %collective-permute-start.8 = (f32[4,56,512]{2,1,0:T(8,128)S(1)}, f32[4,56,512]{2,1,0:T(8,128)S(1)}, u32[]{:S(2)}, u32[]{:S(2)}) collective-permute-start(f32[4,56,512]{2,1,0:T(8,128)S(1)} %collective-permute-done.6.refs_4_), channel_id=1, source_target_pairs={{0,224},{32,0},{64,32},{96,64},{128,96},{160,128},{192,160},{224,1... | collective-permute-start | bytes 1376264 | tf_op jit(solution)/shard_map/ppermute | solution.py:247
  56.0 9.4 %form_2.1 = (bf16[10,512,512]{2,1,0:T(8,128)(2,1)}, bf16[10,512,512]{2,1,0:T(8,128)(2,1)}, f32[8,8,512]{2,1,0:T(8,128)S(1)}, f32[32,8,512]{2,1,0:T(8,128)}) custom-call(s32[8,10]{1,0:T(8,128)S(1)} %stack.39.table, bf16[8,16,512,48]{3,2,1,0:T(8,128)(2,1)S(1)} %prepare_rows.1.prepared_ref, ...), custom_call_target="tpu_custom_call", output_to_operand_aliasing={{0}: (8, {}), {1}: (9, {}), {2}: (10, {}), {3}: (11, {})} | custom-call | flops 8000000000 | bytes 8388608 | tf_op jit(solution)/shard_map/form_2/pallas_call | solution.py:167
  65.5 3.4 %collective-permute-start.10 = (f32[2,56,512]{2,1,0:T(8,128)S(1)}, f32[2,56,512]{2,1,0:T(8,128)S(1)}, u32[]{:S(2)}, u32[]{:S(2)}) collective-permute-start(f32[2,56,512]{2,1,0:T(8,128)S(1)} %slice.69), channel_id=1, source_target_pairs={{0,224},{32,0},{64,32},{96,64},{128,96},{160,128},{192,160},{224,1... | collective-permute-start | bytes 688136 | tf_op jit(solution)/shard_map/ppermute | solution.py:247
  69.0 9.4 %form_3.1 = (bf16[10,512,512]{2,1,0:T(8,128)(2,1)}, bf16[10,512,512]{2,1,0:T(8,128)(2,1)}, f32[8,8,512]{2,1,0:T(8,128)S(1)}, f32[32,8,512]{2,1,0:T(8,128)}) custom-call(s32[8,10]{1,0:T(8,128)S(1)} %stack.39.table, bf16[8,16,512,48]{3,2,1,0:T(8,128)(2,1)S(1)} %prepare_rows.1.prepared_ref, ...), custom_call_target="tpu_custom_call", output_to_operand_aliasing={{0}: (10, {}), {1}: (11, {}), {2}: (12, {}), {3}: (13, {})} | custom-call | flops 8000000000 | bytes 8388608 | tf_op jit(solution)/shard_map/form_3/pallas_call | solution.py:167
  80.6 18.1 %all-to-all-start = ((f32[32,8,512]{2,1,0:T(8,128)}), f32[32,8,512]{2,1,0:T(8,128)S(1)}, u32[]{:S(2)}, u32[]{:S(2)}) async-start(f32[32,8,512]{2,1,0:T(8,128)} %get-tuple-element.44), calls=%async_computation | async-start | bytes 1048576 | tf_op jit(solution)/shard_map/all_to_all | solution.py:295
  101.5 6.6 %collective-permute-start.12 = (f32[8,512]{1,0:T(8,128)S(1)}, f32[8,512]{1,0:T(8,128)S(1)}, u32[]{:S(2)}, u32[]{:S(2)}) collective-permute-start(f32[8,512]{1,0:T(8,128)S(1)} %get-tuple-element.57), channel_id=1, source_target_pairs={{0,6},{2,0},{4,2},{6,4},{1,7},{3,1},{5,3},{7,5},{8,14},{10,8},{12,... | collective-permute-start | bytes 49160 | tf_op jit(solution)/shard_map/ppermute | solution.py:247
  109.7 6.9 %all-to-all-done = f32[32,8,512]{2,1,0:T(8,128)S(1)} async-done(((f32[32,8,512]{2,1,0:T(8,128)}), f32[32,8,512]{2,1,0:T(8,128)S(1)}, u32[]{:S(2)}, u32[]{:S(2)}) %all-to-all-start) | async-done | bytes 524320 | tf_op jit(solution)/shard_map/all_to_all | solution.py:295
  116.7 5.2 %collective-permute-start.21 = (f32[8,512]{1,0:T(8,128)S(1)}, f32[8,512]{1,0:T(8,128)S(1)}, u32[]{:S(2)}, u32[]{:S(2)}) collective-permute-start(f32[8,512]{1,0:T(8,128)S(1)} %get-tuple-element.46), channel_id=1, source_target_pairs={{0,6},{2,0},{4,2},{6,4},{1,7},{3,1},{5,3},{7,5},{8,14},{10,8},{12,... | collective-permute-start | bytes 49160 | tf_op jit(solution)/shard_map/ppermute | solution.py:247
  123.8 4.5 %all-to-all-start.1 = ((f32[32,8,512]{2,1,0:T(8,128)}), f32[32,8,512]{2,1,0:T(8,128)S(1)}, u32[]{:S(2)}, u32[]{:S(2)}) async-start(f32[32,8,512]{2,1,0:T(8,128)} %broadcast_in_dim.34), calls=%async_computation.1 | async-start | bytes 1048576 | tf_op jit(solution)/shard_map/all_to_all | solution.py:252
  129.7 5.0 %apply_cols.1 = f32[32,8,512]{2,1,0:T(8,128)} custom-call(s32[8,10]{1,0:T(8,128)S(1)} %stack.39.table, bf16[10,512,512]{2,1,0:T(8,128)(2,1)} %get-tuple-element.41.high_ref, bf16[10,512,512]{2,1,0:T(8,128)(2,1)} %get-tuple-element.42.low_ref, f32[8,8,512]{2,1,0:T(8,128)S(1)} %constant_dynamic-update-slice_fusion.field), custom_call_target="tpu_custom_call" | custom-call | flops 3000000000 | bytes 12582912 | tf_op jit(solution)/shard_map/apply_cols/pallas_call | solution.py:227
  134.7 9.9 %all-to-all-done.1.field = f32[32,8,512]{2,1,0:T(8,128)S(1)} async-done(((f32[32,8,512]{2,1,0:T(8,128)}), f32[32,8,512]{2,1,0:T(8,128)S(1)}, u32[]{:S(2)}, u32[]{:S(2)}) %all-to-all-start.1) | async-done | bytes 524320 | tf_op jit(solution)/shard_map/all_to_all | solution.py:252
  144.5 4.4 %all-to-all-start.2 = ((f32[32,8,512]{2,1,0:T(8,128)}), f32[32,8,512]{2,1,0:T(8,128)S(1)}, u32[]{:S(2)}, u32[]{:S(2)}) async-start(f32[32,8,512]{2,1,0:T(8,128)} %apply_cols.1), calls=%async_computation.2 | async-start | bytes 1048576 | tf_op jit(solution)/shard_map/all_to_all | solution.py:295
  148.9 4.8 %apply_rows.1 = f32[8,8,512]{2,1,0:T(8,128)S(1)} custom-call(s32[8,10]{1,0:T(8,128)S(1)} %stack.39.table, bf16[10,512,512]{2,1,0:T(8,128)(2,1)} %get-tuple-element.41.high_ref, bf16[10,512,512]{2,1,0:T(8,128)(2,1)} %get-tuple-element.42.low_ref, f32[32,8,512]{2,1,0:T(8,128)S(1)} %all-to-all-done.1.field), custom_call_target="tpu_custom_call" | custom-call | flops 3000000000 | bytes 12582912 | tf_op jit(solution)/shard_map/apply_rows/pallas_call | solution.py:227
  155.2 2.8 %collective-permute-start.16 = (f32[8,512]{1,0:T(8,128)S(1)}, f32[8,512]{1,0:T(8,128)S(1)}, u32[]{:S(2)}, u32[]{:S(2)}) collective-permute-start(f32[8,512]{1,0:T(8,128)S(1)} %get-tuple-element.54), channel_id=1, source_target_pairs={{0,6},{2,0},{4,2},{6,4},{1,7},{3,1},{5,3},{7,5},{8,14},{10,8},{12,... | collective-permute-start | bytes 49160 | tf_op jit(solution)/shard_map/ppermute | solution.py:247
  157.9 2.7 %collective-permute-start.17 = (f32[8,512]{1,0:T(8,128)S(1)}, f32[8,512]{1,0:T(8,128)S(1)}, u32[]{:S(2)}, u32[]{:S(2)}) collective-permute-start(f32[8,512]{1,0:T(8,128)S(1)} %get-tuple-element.56), channel_id=1, source_target_pairs={{0,4},{2,6},{4,0},{6,2},{1,5},{3,7},{5,1},{7,3},{8,12},{10,14},{12... | collective-permute-start | bytes 49160 | tf_op jit(solution)/shard_map/ppermute | solution.py:247
  160.7 4.1 %all-to-all-done.2 = f32[32,8,512]{2,1,0:T(8,128)S(1)} async-done(((f32[32,8,512]{2,1,0:T(8,128)}), f32[32,8,512]{2,1,0:T(8,128)S(1)}, u32[]{:S(2)}, u32[]{:S(2)}) %all-to-all-start.2) | async-done | bytes 524320 | tf_op jit(solution)/shard_map/all_to_all | solution.py:295
  164.9 9.8 %all_to_all.25 = f32[8,8,512]{2,1,0:T(8,128)S(1)} all-to-all(f32[8,8,512]{2,1,0:T(8,128)S(1)} %broadcast_in_dim.35), channel_id=1, replica_groups=mesh['z'=8,'y'=4,'x'=4,'core'=2] {'x','core'}, dimensions={0} | all-to-all | bytes 262144 | tf_op jit(solution)/shard_map/all_to_all | solution.py:252
  174.9 18.8 %all_to_all.26 = f32[32,8,128]{2,1,0:T(8,128)S(1)} all-to-all(f32[32,8,128]{2,1,0:T(8,128)S(1)} %broadcast_in_dim_broadcast_in_dim.2), channel_id=1, replica_groups=mesh['z'=8,'y'=4,'x'=4,'core'=2] {'z','y'}, dimensions={0} | all-to-all | bytes 262144 | tf_op jit(solution)/shard_map/all_to_all | solution.py:252
  (80 shorter events, 23.8 us)
Async XLA Ops:
  1.6 16.0 %collective-permute-start.1 = (f32[56,512]{1,0:T(8,128)S(1)}, f32[56,512]{1,0:T(8,128)S(1)}, u32[]{:S(2)}, u32[]{:S(2)}) collective-permute-start(f32[56,512]{1,0:T(8,128)S(1)} %get-tuple-element.53), channel_id=1, source_target_pairs={{0,16},{8,24},{16,0},{24,8},{1,17},{9,25},{17,1},{25,9},{2,18},{10... | collective-permute-start | bytes 344072 | tf_op jit(solution)/shard_map/ppermute | solution.py:247
  3.2 14.4 %collective-permute-start = (f32[56,512]{1,0:T(8,128)S(1)}, f32[56,512]{1,0:T(8,128)S(1)}, u32[]{:S(2)}, u32[]{:S(2)}) collective-permute-start(f32[56,512]{1,0:T(8,128)S(1)} %get-tuple-element.53), channel_id=1, source_target_pairs={{0,8},{8,16},{16,24},{24,0},{1,9},{9,17},{17,25},{25,1},{2,10},{10... | collective-permute-start | bytes 344072 | tf_op jit(solution)/shard_map/ppermute | solution.py:247
  3.9 13.8 %collective-permute-start.2 = (f32[56,512]{1,0:T(8,128)S(1)}, f32[56,512]{1,0:T(8,128)S(1)}, u32[]{:S(2)}, u32[]{:S(2)}) collective-permute-start(f32[56,512]{1,0:T(8,128)S(1)} %get-tuple-element.53), channel_id=1, source_target_pairs={{0,24},{8,0},{16,8},{24,16},{1,25},{9,1},{17,9},{25,17},{2,26},{10... | collective-permute-start | bytes 344072 | tf_op jit(solution)/shard_map/ppermute | solution.py:247
  17.7 14.9 %collective-permute-start.4 = (f32[4,56,512]{2,1,0:T(8,128)S(1)}, f32[4,56,512]{2,1,0:T(8,128)S(1)}, u32[]{:S(2)}, u32[]{:S(2)}) collective-permute-start(f32[4,56,512]{2,1,0:T(8,128)S(1)} %pad_maximum_fusion.refs_0_), channel_id=1, source_target_pairs={{0,224},{32,0},{64,32},{96,64},{128,96},{160,128},{192,160},{224,1... | collective-permute-start | bytes 1376264 | tf_op jit(solution)/shard_map/ppermute | solution.py:247
  23.6 15.9 %collective-permute-start.3 = (f32[4,56,512]{2,1,0:T(8,128)S(1)}, f32[4,56,512]{2,1,0:T(8,128)S(1)}, u32[]{:S(2)}, u32[]{:S(2)}) collective-permute-start(f32[4,56,512]{2,1,0:T(8,128)S(1)} %pad_maximum_fusion.refs_0_), channel_id=1, source_target_pairs={{0,32},{32,64},{64,96},{96,128},{128,160},{160,192},{192,224},{224... | collective-permute-start | bytes 1376264 | tf_op jit(solution)/shard_map/ppermute | solution.py:247
  32.5 20.1 %collective-permute-start.6 = (f32[4,56,512]{2,1,0:T(8,128)S(1)}, f32[4,56,512]{2,1,0:T(8,128)S(1)}, u32[]{:S(2)}, u32[]{:S(2)}) collective-permute-start(f32[4,56,512]{2,1,0:T(8,128)S(1)} %collective-permute-done.4.refs_2_), channel_id=1, source_target_pairs={{0,224},{32,0},{64,32},{96,64},{128,96},{160,128},{192,160},{224,1... | collective-permute-start | bytes 1376264 | tf_op jit(solution)/shard_map/ppermute | solution.py:247
  39.5 16.5 %collective-permute-start.5 = (f32[4,56,512]{2,1,0:T(8,128)S(1)}, f32[4,56,512]{2,1,0:T(8,128)S(1)}, u32[]{:S(2)}, u32[]{:S(2)}) collective-permute-start(f32[4,56,512]{2,1,0:T(8,128)S(1)} %collective-permute-done.3.refs_1_), channel_id=1, source_target_pairs={{0,32},{32,64},{64,96},{96,128},{128,160},{160,192},{192,224},{224... | collective-permute-start | bytes 1376264 | tf_op jit(solution)/shard_map/ppermute | solution.py:247
  52.7 12.8 %collective-permute-start.8 = (f32[4,56,512]{2,1,0:T(8,128)S(1)}, f32[4,56,512]{2,1,0:T(8,128)S(1)}, u32[]{:S(2)}, u32[]{:S(2)}) collective-permute-start(f32[4,56,512]{2,1,0:T(8,128)S(1)} %collective-permute-done.6.refs_4_), channel_id=1, source_target_pairs={{0,224},{32,0},{64,32},{96,64},{128,96},{160,128},{192,160},{224,1... | collective-permute-start | bytes 1376264 | tf_op jit(solution)/shard_map/ppermute | solution.py:247
  56.0 12.9 %collective-permute-start.7 = (f32[4,56,512]{2,1,0:T(8,128)S(1)}, f32[4,56,512]{2,1,0:T(8,128)S(1)}, u32[]{:S(2)}, u32[]{:S(2)}) collective-permute-start(f32[4,56,512]{2,1,0:T(8,128)S(1)} %collective-permute-done.5.refs_3_), channel_id=1, source_target_pairs={{0,32},{32,64},{64,96},{96,128},{128,160},{160,192},{192,224},{224... | collective-permute-start | bytes 1376264 | tf_op jit(solution)/shard_map/ppermute | solution.py:247
  65.5 13.0 %collective-permute-start.10 = (f32[2,56,512]{2,1,0:T(8,128)S(1)}, f32[2,56,512]{2,1,0:T(8,128)S(1)}, u32[]{:S(2)}, u32[]{:S(2)}) collective-permute-start(f32[2,56,512]{2,1,0:T(8,128)S(1)} %slice.69), channel_id=1, source_target_pairs={{0,224},{32,0},{64,32},{96,64},{128,96},{160,128},{192,160},{224,1... | collective-permute-start | bytes 688136 | tf_op jit(solution)/shard_map/ppermute | solution.py:247
  68.9 9.5 %collective-permute-start.9 = (f32[2,56,512]{2,1,0:T(8,128)S(1)}, f32[2,56,512]{2,1,0:T(8,128)S(1)}, u32[]{:S(2)}, u32[]{:S(2)}) collective-permute-start(f32[2,56,512]{2,1,0:T(8,128)S(1)} %slice.68), channel_id=1, source_target_pairs={{0,32},{32,64},{64,96},{96,128},{128,160},{160,192},{192,224},{224... | collective-permute-start | bytes 688136 | tf_op jit(solution)/shard_map/ppermute | solution.py:247
  80.6 36.0 %all-to-all-start = ((f32[32,8,512]{2,1,0:T(8,128)}), f32[32,8,512]{2,1,0:T(8,128)S(1)}, u32[]{:S(2)}, u32[]{:S(2)}) async-start(f32[32,8,512]{2,1,0:T(8,128)} %get-tuple-element.44), calls=%async_computation | async-start | bytes 1048576 | tf_op jit(solution)/shard_map/all_to_all | solution.py:295
  98.7 2.8 %collective-permute-start.11 = (f32[4,8,512]{2,1,0:T(8,128)S(1)}, f32[4,8,512]{2,1,0:T(8,128)S(1)}, u32[]{:S(2)}, u32[]{:S(2)}) collective-permute-start(f32[4,8,512]{2,1,0:T(8,128)S(1)} %slice.56), channel_id=1, source_target_pairs={{0,1},{1,0},{2,3},{3,2},{4,5},{5,4},{6,7},{7,6},{8,9},{9,8},{10,11... | collective-permute-start | bytes 196616 | tf_op jit(solution)/shard_map/ppermute | solution.py:247
  101.5 15.2 %collective-permute-start.12 = (f32[8,512]{1,0:T(8,128)S(1)}, f32[8,512]{1,0:T(8,128)S(1)}, u32[]{:S(2)}, u32[]{:S(2)}) collective-permute-start(f32[8,512]{1,0:T(8,128)S(1)} %get-tuple-element.57), channel_id=1, source_target_pairs={{0,6},{2,0},{4,2},{6,4},{1,7},{3,1},{5,3},{7,5},{8,14},{10,8},{12,... | collective-permute-start | bytes 49160 | tf_op jit(solution)/shard_map/ppermute | solution.py:247
  108.1 8.6 %collective-permute-start.14 = (f32[8,512]{1,0:T(8,128)S(1)}, f32[8,512]{1,0:T(8,128)S(1)}, u32[]{:S(2)}, u32[]{:S(2)}) collective-permute-start(f32[8,512]{1,0:T(8,128)S(1)} %get-tuple-element.58), channel_id=1, source_target_pairs={{0,2},{2,4},{4,6},{6,0},{1,3},{3,5},{5,7},{7,1},{8,10},{10,12},{12... | collective-permute-start | bytes 49160 | tf_op jit(solution)/shard_map/ppermute | solution.py:247
  108.1 8.6 %collective-permute-start.13 = (f32[8,512]{1,0:T(8,128)S(1)}, f32[8,512]{1,0:T(8,128)S(1)}, u32[]{:S(2)}, u32[]{:S(2)}) collective-permute-start(f32[8,512]{1,0:T(8,128)S(1)} %get-tuple-element.59), channel_id=1, source_target_pairs={{0,4},{2,6},{4,0},{6,2},{1,5},{3,7},{5,1},{7,3},{8,12},{10,14},{12... | collective-permute-start | bytes 49160 | tf_op jit(solution)/shard_map/ppermute | solution.py:247
  116.7 11.6 %collective-permute-start.21 = (f32[8,512]{1,0:T(8,128)S(1)}, f32[8,512]{1,0:T(8,128)S(1)}, u32[]{:S(2)}, u32[]{:S(2)}) collective-permute-start(f32[8,512]{1,0:T(8,128)S(1)} %get-tuple-element.46), channel_id=1, source_target_pairs={{0,6},{2,0},{4,2},{6,4},{1,7},{3,1},{5,3},{7,5},{8,14},{10,8},{12,... | collective-permute-start | bytes 49160 | tf_op jit(solution)/shard_map/ppermute | solution.py:247
  122.0 6.4 %collective-permute-start.20 = (f32[8,512]{1,0:T(8,128)S(1)}, f32[8,512]{1,0:T(8,128)S(1)}, u32[]{:S(2)}, u32[]{:S(2)}) collective-permute-start(f32[8,512]{1,0:T(8,128)S(1)} %get-tuple-element.46), channel_id=1, source_target_pairs={{0,4},{2,6},{4,0},{6,2},{1,5},{3,7},{5,1},{7,3},{8,12},{10,14},{12... | collective-permute-start | bytes 49160 | tf_op jit(solution)/shard_map/ppermute | solution.py:247
  122.0 6.4 %collective-permute-start.19 = (f32[8,512]{1,0:T(8,128)S(1)}, f32[8,512]{1,0:T(8,128)S(1)}, u32[]{:S(2)}, u32[]{:S(2)}) collective-permute-start(f32[8,512]{1,0:T(8,128)S(1)} %get-tuple-element.46), channel_id=1, source_target_pairs={{0,2},{2,4},{4,6},{6,0},{1,3},{3,5},{5,7},{7,1},{8,10},{10,12},{12... | collective-permute-start | bytes 49160 | tf_op jit(solution)/shard_map/ppermute | solution.py:247
  123.8 20.8 %all-to-all-start.1 = ((f32[32,8,512]{2,1,0:T(8,128)}), f32[32,8,512]{2,1,0:T(8,128)S(1)}, u32[]{:S(2)}, u32[]{:S(2)}) async-start(f32[32,8,512]{2,1,0:T(8,128)} %broadcast_in_dim.34), calls=%async_computation.1 | async-start | bytes 1048576 | tf_op jit(solution)/shard_map/all_to_all | solution.py:252
  144.5 20.2 %all-to-all-start.2 = ((f32[32,8,512]{2,1,0:T(8,128)}), f32[32,8,512]{2,1,0:T(8,128)S(1)}, u32[]{:S(2)}, u32[]{:S(2)}) async-start(f32[32,8,512]{2,1,0:T(8,128)} %apply_cols.1), calls=%async_computation.2 | async-start | bytes 1048576 | tf_op jit(solution)/shard_map/all_to_all | solution.py:295
  155.2 9.7 %collective-permute-start.16 = (f32[8,512]{1,0:T(8,128)S(1)}, f32[8,512]{1,0:T(8,128)S(1)}, u32[]{:S(2)}, u32[]{:S(2)}) collective-permute-start(f32[8,512]{1,0:T(8,128)S(1)} %get-tuple-element.54), channel_id=1, source_target_pairs={{0,6},{2,0},{4,2},{6,4},{1,7},{3,1},{5,3},{7,5},{8,14},{10,8},{12,... | collective-permute-start | bytes 49160 | tf_op jit(solution)/shard_map/ppermute | solution.py:247
  157.9 6.9 %collective-permute-start.18 = (f32[8,512]{1,0:T(8,128)S(1)}, f32[8,512]{1,0:T(8,128)S(1)}, u32[]{:S(2)}, u32[]{:S(2)}) collective-permute-start(f32[8,512]{1,0:T(8,128)S(1)} %get-tuple-element.55), channel_id=1, source_target_pairs={{0,2},{2,4},{4,6},{6,0},{1,3},{3,5},{5,7},{7,1},{8,10},{10,12},{12... | collective-permute-start | bytes 49160 | tf_op jit(solution)/shard_map/ppermute | solution.py:247
  157.9 6.9 %collective-permute-start.17 = (f32[8,512]{1,0:T(8,128)S(1)}, f32[8,512]{1,0:T(8,128)S(1)}, u32[]{:S(2)}, u32[]{:S(2)}) collective-permute-start(f32[8,512]{1,0:T(8,128)S(1)} %get-tuple-element.56), channel_id=1, source_target_pairs={{0,4},{2,6},{4,0},{6,2},{1,5},{3,7},{5,1},{7,3},{8,12},{10,14},{12... | collective-permute-start | bytes 49160 | tf_op jit(solution)/shard_map/ppermute | solution.py:247
  (4 other events, 15.1 us)

commit v4 on v3

--- a/solution.py
+++ b/solution.py
@@ -13,7 +13,6 @@
 ROW = ("z", "y")
 COL = ("x", "core")
 ROW_AT, ROW_NEAR, COL_AT, SOURCE, PLACE, STAGE, LIVE, CROSSING = range(8)
-PER_STAGE = 3
 LAST_STAGE = 4
 BY_ROWS = (((1,), (0,)), ((), ()))
 BY_COLS = (((1,), (1,)), ((), ()))
@@ -90,7 +89,13 @@
         row_acc[...] = refs[sources + 2][...]
         col_acc[...] = refs[sources + 3][...]
 
-    def form(slot):
+    def copies(slot):
+        return [
+            pltpu.make_async_copy(high_tile, high_ref.at[slot], sems.at[0]),
+            pltpu.make_async_copy(low_tile, low_ref.at[slot], sems.at[1]),
+        ]
+
+    def form(slot, pending):
         for source in range(sources):
 
             @pl.when(table[SOURCE, slot] == source)
@@ -102,6 +107,11 @@
             stacked = jnp.concatenate([high, mid, high, mid, low, high], axis=0)
             cols[snapshot] = stacked.astype(jnp.bfloat16)
         row_at = table[ROW_AT, slot]
+
+        @pl.when(pending != 0)
+        def _():
+            for copy in copies(slot):
+                copy.wait()
 
         def step(at, carry):
             start = pl.multiple_of(at * CHUNK, CHUNK)
@@ -123,11 +133,7 @@
             return carry
 
         lax.fori_loop(0, TILE // CHUNK, step, 0)
-        copies = [
-            pltpu.make_async_copy(high_tile, high_ref.at[slot], sems.at[0]),
-            pltpu.make_async_copy(low_tile, low_ref.at[slot], sems.at[1]),
-        ]
-        for copy in copies:
+        for copy in copies(slot):
             copy.start()
         row_acc[table[ROW_NEAR, slot]] += multiply(
             tile[48:56, :], high_tile[...], low_tile[...], BY_COLS
@@ -139,17 +145,21 @@
                 row_vec[row_at], high_tile[...], low_tile[...], BY_ROWS
             )
 
-        for copy in copies:
+    def visit(slot, pending):
+        mine = table[STAGE, slot] == stage
+
+        @pl.when(mine)
+        def _():
+            form(slot, pending)
+
+        return jnp.where(mine, 1, pending)
+
+    pending = lax.fori_loop(0, high_ref.shape[0], visit, 0)
+
+    @pl.when(pending != 0)
+    def _():
+        for copy in copies(0):
             copy.wait()
-
-    def visit(slot, carry):
-        @pl.when(table[STAGE, slot] == stage)
-        def _():
-            form(slot)
-
-        return carry
-
-    lax.fori_loop(0, high_ref.shape[0], visit, 0)
 
 
 def form_stage(stage, table, prepared, row_vec, places, state, blocks):
@@ -171,7 +181,9 @@
         + ([hbm, hbm, vmem, vmem] if state else []),
         out_specs=[hbm, hbm, vmem, vmem],
         out_shape=shapes,
-        input_output_aliases={first + i: i for i in range(len(state))},
+        input_output_aliases={
+            first + i: i for i in range(2 if stage == LAST_STAGE else len(state))
+        },
         scratch_shapes=[
             pltpu.VMEM((56, TILE), jnp.float32),
             pltpu.VMEM((16, DEPTH, TILE), jnp.bfloat16),
@@ -266,8 +278,11 @@
     return total
 
 
-def gather_near(piece):
-    near = jnp.stack([piece] + [shift(piece, "y", d) for d in range(1, lax.axis_size("y"))])
+def gather_y(piece):
+    return jnp.stack([piece] + [shift(piece, "y", d) for d in range(1, lax.axis_size("y"))])
+
+
+def gather_z(near):
     size, half = lax.axis_size("z"), near.shape[0] // 2
     arrived = [[near]]
     behind = ahead = near
@@ -285,10 +300,9 @@
     key = stage * source.shape[0] + slots
     before = key[None, :] <= key[:, None]
     rank = jnp.sum(before.astype(jnp.int32), axis=1)
-    turn = jnp.max(
-        jnp.where(before, PER_STAGE * stage[None, :] + rank[:, None] - rank[None, :], 0), axis=1
-    )
-    return jnp.where(live, jnp.minimum(turn // PER_STAGE, LAST_STAGE), -1)
+    start = jnp.maximum(3 * stage - 1, 0)
+    turn = jnp.max(jnp.where(before, start[None, :] + rank[:, None] - rank[None, :], 0), axis=1)
+    return jnp.where(live, jnp.minimum((turn + 1) // 3, LAST_STAGE), -1)
 
 
 def combine(row_acc, col_acc):
@@ -344,9 +358,11 @@
         axis=0,
     )
     row_vec = vectors.reshape(8, tiles, TILE).transpose(1, 0, 2)
+    near = gather_y(own)
+    flat, near = lax.optimization_barrier((flat, near))
     prepared = prepare_rows(flat)
     places, state = [], []
-    for stage, arrived in enumerate(gather_near(own)):
+    for stage, arrived in enumerate(gather_z(near)):
         places = places + arrived
         state = form_stage(stage, table, prepared, row_vec, places, state, blocks)
     high, low, row_acc, col_acc = state
@@ -359,8 +375,8 @@
 
     rows = spread(second, COL)
     squares = jnp.sum(rows * rows, axis=(0, 2))
-    squares = spread(jnp.broadcast_to(squares[:, None], (8, 128)), ROW)
-    total = jnp.sum(squares[:, :, 0], axis=0) / (block * blocks)
+    squares = spread(jnp.pad(squares[None, :], ((0, 0), (0, 120))), ROW)
+    total = jnp.sum(squares[:, 0, :8], axis=0) / (block * blocks)
     scaled = rows / jnp.sqrt(total + 1e-06)[None, :, None]
     return scaled.transpose(1, 0, 2).reshape(8, block)
 

time: 197 us -> 185 us (0.939)
  starting transfers between devices: 73.4 us -> 56.7 us
  Pallas kernels: 50.8 us -> 58.2 us
    ppermute x23, starting transfers between devices: 46.4 us -> 33.5 us  [shift(): lax.ppermute(value, axis, [(i, (i + distance) % size) for i in range(size)])]
    pallas_call x5, Pallas kernels: 35.8 us -> 41 us  [form_stage(): pl.pallas_call(functools.partial(stage_kernel, stage, len(places)), in_sp...]
    all_to_all x2, waiting for transfers between devices: 11.1 us -> 15.3 us  [combine(): by_col = lax.all_to_all(col_acc, ROW, 0, 0, tiled=True)]
    ppermute x23, waiting for transfers between devices: 10.7 us -> 6.58 us  [shift(): lax.ppermute(value, axis, [(i, (i + distance) % size) for i in range(size)])]
    all_to_all x2, starting transfers between devices: 22.5 us -> 18.8 us  [combine(): by_col = lax.all_to_all(col_acc, ROW, 0, 0, tiled=True)]
    pallas_call x2, Pallas kernels: 9.79 us -> 11.9 us  [apply_tiles(): pl.pallas_call(functools.partial(apply_kernel, wanted), in_specs=[pl.Bloc...]
  transfers between devices with their start and end apart: 26 -> 26, of which waited for: 7 -> 8; matrix products, arithmetic and copies ran while one was open for 3% -> 3% of each run, Pallas kernels for 25% -> 27%
where the time goes in v4:
time: 185 us; the launch traced here: 184 us
  Pallas kernels  58.2 us (31%)
  starting transfers between devices  56.7 us (31%)
  waiting for transfers between devices  31.6 us (17%)
  blocking collectives  27.6 us (15%)
  other arithmetic  5.11 us (3%)
  local copies, waits for them, and re-layouts  4.5 us (2%)
    pallas_call x5, Pallas kernels, form_stage(): pl.pallas_call(functools.partial(stage_kernel, stage, len(places)), in_sp...  41 us
    ppermute x23, starting transfers between devices, shift(): lax.ppermute(value, axis, [(i, (i + distance) % size) for i in range(size)])  33.5 us
    all_to_all x2, blocking collectives, spread(): return lax.all_to_all(copies, axes, 0, 0, tiled=True)  27.6 us
    all_to_all x2, starting transfers between devices, combine(): by_col = lax.all_to_all(col_acc, ROW, 0, 0, tiled=True)  18.8 us
    all_to_all x2, waiting for transfers between devices, combine(): by_col = lax.all_to_all(col_acc, ROW, 0, 0, tiled=True)  15.3 us
    pallas_call x2, Pallas kernels, apply_tiles(): pl.pallas_call(functools.partial(apply_kernel, wanted), in_specs=[pl.Bloc...  11.9 us
    all_to_all x1, waiting for transfers between devices, spread(): return lax.all_to_all(copies, axes, 0, 0, tiled=True)  9.69 us
    ppermute x23, waiting for transfers between devices, shift(): lax.ppermute(value, axis, [(i, (i + distance) % size) for i in range(size)])  6.58 us
  transfers between devices with their start and end apart: 26, of which 8 were waited for; matrix products, arithmetic and copies ran while one was open for 3% of the time, Pallas kernels for 27%

profile of v4, /device:TPU:0, one launch (start us, length us, event | category | flops | bytes accessed | tf_op | source)
XLA Modules:
  0.0 184.1 jit_solution(15761995181595470252)
XLA Ops:
  3.9 2.6 %collective-permute-start.2 = (f32[56,512]{1,0:T(8,128)S(1)}, f32[56,512]{1,0:T(8,128)S(1)}, u32[]{:S(2)}, u32[]{:S(2)}) collective-permute-start(f32[56,512]{1,0:T(8,128)S(1)} %get-tuple-element.57), channel_id=1, source_target_pairs={{0,24},{8,0},{16,8},{24,16},{1,25},{9,1},{17,9},{25,17},{2,26},{10... | collective-permute-start | bytes 344072 | tf_op jit(solution)/shard_map/ppermute | solution.py:259
  11.3 5.9 %collective-permute-start.4 = (f32[4,56,512]{2,1,0:T(8,128)S(1)}, f32[4,56,512]{2,1,0:T(8,128)S(1)}, u32[]{:S(2)}, u32[]{:S(2)}) collective-permute-start(f32[4,56,512]{2,1,0:T(8,128)S(1)} %pad_maximum_fusion.refs_0_), channel_id=1, source_target_pairs={{0,224},{32,0},{64,32},{96,64},{128,96},{160,128},{192,160},{224,1... | collective-permute-start | bytes 1376264 | tf_op jit(solution)/shard_map/ppermute | solution.py:259
  18.3 5.3 %prepare_rows.1.prepared_ref = bf16[8,16,512,48]{3,2,1,0:T(8,128)(2,1)S(1)} custom-call(f32[48,4096]{1,0:T(8,128)S(1)} %bitcast.115), custom_call_target="tpu_custom_call" | custom-call | flops 100000000 | bytes 20971520 | tf_op jit(solution)/shard_map/prepare_rows/pallas_call | solution.py:60
  23.6 7.9 %form_0.1 = (bf16[10,512,512]{2,1,0:T(8,128)(2,1)}, bf16[10,512,512]{2,1,0:T(8,128)(2,1)}, f32[8,8,512]{2,1,0:T(8,128)S(1)}, f32[32,8,512]{2,1,0:T(8,128)S(1)}) custom-call(s32[8,10]{1,0:T(8,128)S(1)} %stack.39.table, bf16[8,16,512,48]{3,2,1,0:T(8,128)(2,1)S(1)} %prepare_rows.1.prepared_ref, f32[8,8,512]{2,1,0:T(8,128)S(1)} %bitcast.109, ...), custom_call_target="tpu_custom_call" | custom-call | flops 8000000000 | bytes 8388608 | tf_op jit(solution)/shard_map/form_0/pallas_call | solution.py:177
  31.6 3.3 %collective-permute-start.6 = (f32[4,56,512]{2,1,0:T(8,128)S(1)}, f32[4,56,512]{2,1,0:T(8,128)S(1)}, u32[]{:S(2)}, u32[]{:S(2)}) collective-permute-start(f32[4,56,512]{2,1,0:T(8,128)S(1)} %collective-permute-done.4.refs_2_), channel_id=1, source_target_pairs={{0,224},{32,0},{64,32},{96,64},{128,96},{160,128},{192,160},{224,1... | collective-permute-start | bytes 1376264 | tf_op jit(solution)/shard_map/ppermute | solution.py:259
  34.9 8.1 %form_1.1 = (bf16[10,512,512]{2,1,0:T(8,128)(2,1)}, bf16[10,512,512]{2,1,0:T(8,128)(2,1)}, f32[8,8,512]{2,1,0:T(8,128)S(1)}, f32[32,8,512]{2,1,0:T(8,128)S(1)}) custom-call(s32[8,10]{1,0:T(8,128)S(1)} %stack.39.table, bf16[8,16,512,48]{3,2,1,0:T(8,128)(2,1)S(1)} %prepare_rows.1.prepared_ref, ...), custom_call_target="tpu_custom_call", output_to_operand_aliasing={{0}: (6, {}), {1}: (7, {}), {2}: (8, {}), {3}: (9, {})} | custom-call | flops 8000000000 | bytes 8388608 | tf_op jit(solution)/shard_map/form_1/pallas_call | solution.py:177
  43.2 6.5 %collective-permute-start.8 = (f32[4,56,512]{2,1,0:T(8,128)S(1)}, f32[4,56,512]{2,1,0:T(8,128)S(1)}, u32[]{:S(2)}, u32[]{:S(2)}) collective-permute-start(f32[4,56,512]{2,1,0:T(8,128)S(1)} %collective-permute-done.6.refs_4_), channel_id=1, source_target_pairs={{0,224},{32,0},{64,32},{96,64},{128,96},{160,128},{192,160},{224,1... | collective-permute-start | bytes 1376264 | tf_op jit(solution)/shard_map/ppermute | solution.py:259
  49.7 11.6 %form_2.1 = (bf16[10,512,512]{2,1,0:T(8,128)(2,1)}, bf16[10,512,512]{2,1,0:T(8,128)(2,1)}, f32[8,8,512]{2,1,0:T(8,128)S(1)}, f32[32,8,512]{2,1,0:T(8,128)S(1)}) custom-call(s32[8,10]{1,0:T(8,128)S(1)} %stack.39.table, ...), custom_call_target="tpu_custom_call", output_to_operand_aliasing={{0}: (8, {}), {1}: (9, {}), {2}: (10, {}), {3}: (11, {})} | custom-call | flops 8000000000 | bytes 8388608 | tf_op jit(solution)/shard_map/form_2/pallas_call | solution.py:177
  61.3 3.4 %collective-permute-start.10 = (f32[2,56,512]{2,1,0:T(8,128)S(1)}, f32[2,56,512]{2,1,0:T(8,128)S(1)}, u32[]{:S(2)}, u32[]{:S(2)}) collective-permute-start(f32[2,56,512]{2,1,0:T(8,128)S(1)} %slice.69), channel_id=1, source_target_pairs={{0,224},{32,0},{64,32},{96,64},{128,96},{160,128},{192,160},{224,1... | collective-permute-start | bytes 688136 | tf_op jit(solution)/shard_map/ppermute | solution.py:259
  64.9 4.7 %form_3.1 = (bf16[10,512,512]{2,1,0:T(8,128)(2,1)}, bf16[10,512,512]{2,1,0:T(8,128)(2,1)}, f32[8,8,512]{2,1,0:T(8,128)S(1)}, f32[32,8,512]{2,1,0:T(8,128)S(1)}) custom-call(s32[8,10]{1,0:T(8,128)S(1)} %stack.39.table, ...), custom_call_target="tpu_custom_call", output_to_operand_aliasing={{0}: (10, {}), {1}: (11, {}), {2}: (12, {}), {3}: (13, {})} | custom-call | flops 8000000000 | bytes 8388608 | tf_op jit(solution)/shard_map/form_3/pallas_call | solution.py:177
  69.5 2.5 %collective-permute-done.9.refs_7_ = f32[2,56,512]{2,1,0:T(8,128)S(1)} collective-permute-done((f32[2,56,512]{2,1,0:T(8,128)S(1)}, f32[2,56,512]{2,1,0:T(8,128)S(1)}, u32[]{:S(2)}, u32[]{:S(2)}) %collective-permute-start.9) | collective-permute-done | bytes 229408 | tf_op jit(solution)/shard_map/ppermute | solution.py:259
  72.1 8.8 %form_4.1 = (bf16[10,512,512]{2,1,0:T(8,128)(2,1)}, bf16[10,512,512]{2,1,0:T(8,128)(2,1)}, f32[8,8,512]{2,1,0:T(8,128)S(1)}, f32[32,8,512]{2,1,0:T(8,128)}) custom-call(s32[8,10]{1,0:T(8,128)S(1)} %stack.39.table, bf16[8,16,512,48]{3,2,1,0:T(8,128)(2,1)S(1)} %prepare_rows.1.prepared_ref, ...), custom_call_target="tpu_custom_call", output_to_operand_aliasing={{0}: (12, {}), {1}: (13, {})} | custom-call | flops 8000000000 | bytes 8388608 | tf_op jit(solution)/shard_map/form_4/pallas_call | solution.py:177
  80.9 14.3 %all-to-all-start = ((f32[32,8,512]{2,1,0:T(8,128)}), f32[32,8,512]{2,1,0:T(8,128)S(1)}, u32[]{:S(2)}, u32[]{:S(2)}) async-start(f32[32,8,512]{2,1,0:T(8,128)} %get-tuple-element.48), calls=%async_computation | async-start | bytes 1048576 | tf_op jit(solution)/shard_map/all_to_all | solution.py:309
  98.7 10.3 %all-to-all-done = f32[32,8,512]{2,1,0:T(8,128)S(1)} async-done(((f32[32,8,512]{2,1,0:T(8,128)}), f32[32,8,512]{2,1,0:T(8,128)S(1)}, u32[]{:S(2)}, u32[]{:S(2)}) %all-to-all-start) | async-done | bytes 524320 | tf_op jit(solution)/shard_map/all_to_all | solution.py:309
  109.2 2.6 %collective-permute-start.20 = (f32[8,512]{1,0:T(8,128)S(1)}, f32[8,512]{1,0:T(8,128)S(1)}, u32[]{:S(2)}, u32[]{:S(2)}) collective-permute-start(f32[8,512]{1,0:T(8,128)S(1)} %get-tuple-element.50), channel_id=1, source_target_pairs={{0,4},{2,6},{4,0},{6,2},{1,5},{3,7},{5,1},{7,3},{8,12},{10,14},{12... | collective-permute-start | bytes 49160 | tf_op jit(solution)/shard_map/ppermute | solution.py:259
  112.7 4.4 %all-to-all-start.1 = ((f32[32,8,512]{2,1,0:T(8,128)}), f32[32,8,512]{2,1,0:T(8,128)S(1)}, u32[]{:S(2)}, u32[]{:S(2)}) async-start(f32[32,8,512]{2,1,0:T(8,128)} %broadcast_in_dim.39), calls=%async_computation.1 | async-start | bytes 1048576 | tf_op jit(solution)/shard_map/all_to_all | solution.py:264
  118.5 5.8 %apply_cols.1 = f32[32,8,512]{2,1,0:T(8,128)} custom-call(s32[8,10]{1,0:T(8,128)S(1)} %stack.39.table, bf16[10,512,512]{2,1,0:T(8,128)(2,1)} %get-tuple-element.45.high_ref, bf16[10,512,512]{2,1,0:T(8,128)(2,1)} %get-tuple-element.46.low_ref, f32[8,8,512]{2,1,0:T(8,128)S(1)} %constant_dynamic-update-slice_fusion.field), custom_call_target="tpu_custom_call" | custom-call | flops 3000000000 | bytes 12582912 | tf_op jit(solution)/shard_map/apply_cols/pallas_call | solution.py:239
  124.3 9.7 %all-to-all-done.1.field = f32[32,8,512]{2,1,0:T(8,128)S(1)} async-done(((f32[32,8,512]{2,1,0:T(8,128)}), f32[32,8,512]{2,1,0:T(8,128)S(1)}, u32[]{:S(2)}, u32[]{:S(2)}) %all-to-all-start.1) | async-done | bytes 524320 | tf_op jit(solution)/shard_map/all_to_all | solution.py:264
  134.0 4.5 %all-to-all-start.2 = ((f32[32,8,512]{2,1,0:T(8,128)}), f32[32,8,512]{2,1,0:T(8,128)S(1)}, u32[]{:S(2)}, u32[]{:S(2)}) async-start(f32[32,8,512]{2,1,0:T(8,128)} %apply_cols.1), calls=%async_computation.2 | async-start | bytes 1048576 | tf_op jit(solution)/shard_map/all_to_all | solution.py:309
  138.5 6.1 %apply_rows.1 = f32[8,8,512]{2,1,0:T(8,128)S(1)} custom-call(s32[8,10]{1,0:T(8,128)S(1)} %stack.39.table, bf16[10,512,512]{2,1,0:T(8,128)(2,1)} %get-tuple-element.45.high_ref, bf16[10,512,512]{2,1,0:T(8,128)(2,1)} %get-tuple-element.46.low_ref, f32[32,8,512]{2,1,0:T(8,128)S(1)} %all-to-all-done.1.field), custom_call_target="tpu_custom_call" | custom-call | flops 3000000000 | bytes 12582912 | tf_op jit(solution)/shard_map/apply_rows/pallas_call | solution.py:239
  146.0 2.4 %collective-permute-start.16 = (f32[8,512]{1,0:T(8,128)S(1)}, f32[8,512]{1,0:T(8,128)S(1)}, u32[]{:S(2)}, u32[]{:S(2)}) collective-permute-start(f32[8,512]{1,0:T(8,128)S(1)} %get-tuple-element.58), channel_id=1, source_target_pairs={{0,6},{2,0},{4,2},{6,4},{1,7},{3,1},{5,3},{7,5},{8,14},{10,8},{12,... | collective-permute-start | bytes 49160 | tf_op jit(solution)/shard_map/ppermute | solution.py:259
  150.4 5.0 %all-to-all-done.2 = f32[32,8,512]{2,1,0:T(8,128)S(1)} async-done(((f32[32,8,512]{2,1,0:T(8,128)}), f32[32,8,512]{2,1,0:T(8,128)S(1)}, u32[]{:S(2)}, u32[]{:S(2)}) %all-to-all-start.2) | async-done | bytes 524320 | tf_op jit(solution)/shard_map/all_to_all | solution.py:309
  155.5 9.3 %all_to_all.25 = f32[8,8,512]{2,1,0:T(8,128)S(1)} all-to-all(f32[8,8,512]{2,1,0:T(8,128)S(1)} %broadcast_in_dim.40), channel_id=1, replica_groups=mesh['z'=8,'y'=4,'x'=4,'core'=2] {'x','core'}, dimensions={0} | all-to-all | bytes 262144 | tf_op jit(solution)/shard_map/all_to_all | solution.py:264
  165.1 18.2 %all_to_all.26 = f32[32,1,128]{2,1,0:T(1,128)S(1)} all-to-all(f32[32,1,128]{2,1,0:T(1,128)S(1)} %broadcast_in_dim.42), channel_id=1, replica_groups=mesh['z'=8,'y'=4,'x'=4,'core'=2] {'z','y'}, dimensions={0} | all-to-all | bytes 32768 | tf_op jit(solution)/shard_map/all_to_all | solution.py:264
  (81 shorter events, 20.5 us)
Async XLA Ops:
  1.6 9.6 %collective-permute-start.1 = (f32[56,512]{1,0:T(8,128)S(1)}, f32[56,512]{1,0:T(8,128)S(1)}, u32[]{:S(2)}, u32[]{:S(2)}) collective-permute-start(f32[56,512]{1,0:T(8,128)S(1)} %get-tuple-element.57), channel_id=1, source_target_pairs={{0,16},{8,24},{16,0},{24,8},{1,17},{9,25},{17,1},{25,9},{2,18},{10... | collective-permute-start | bytes 344072 | tf_op jit(solution)/shard_map/ppermute | solution.py:259
  3.2 8.0 %collective-permute-start = (f32[56,512]{1,0:T(8,128)S(1)}, f32[56,512]{1,0:T(8,128)S(1)}, u32[]{:S(2)}, u32[]{:S(2)}) collective-permute-start(f32[56,512]{1,0:T(8,128)S(1)} %get-tuple-element.57), channel_id=1, source_target_pairs={{0,8},{8,16},{16,24},{24,0},{1,9},{9,17},{17,25},{25,1},{2,10},{10... | collective-permute-start | bytes 344072 | tf_op jit(solution)/shard_map/ppermute | solution.py:259
  3.9 7.3 %collective-permute-start.2 = (f32[56,512]{1,0:T(8,128)S(1)}, f32[56,512]{1,0:T(8,128)S(1)}, u32[]{:S(2)}, u32[]{:S(2)}) collective-permute-start(f32[56,512]{1,0:T(8,128)S(1)} %get-tuple-element.57), channel_id=1, source_target_pairs={{0,24},{8,0},{16,8},{24,16},{1,25},{9,1},{17,9},{25,17},{2,26},{10... | collective-permute-start | bytes 344072 | tf_op jit(solution)/shard_map/ppermute | solution.py:259
  11.3 20.3 %collective-permute-start.4 = (f32[4,56,512]{2,1,0:T(8,128)S(1)}, f32[4,56,512]{2,1,0:T(8,128)S(1)}, u32[]{:S(2)}, u32[]{:S(2)}) collective-permute-start(f32[4,56,512]{2,1,0:T(8,128)S(1)} %pad_maximum_fusion.refs_0_), channel_id=1, source_target_pairs={{0,224},{32,0},{64,32},{96,64},{128,96},{160,128},{192,160},{224,1... | collective-permute-start | bytes 1376264 | tf_op jit(solution)/shard_map/ppermute | solution.py:259
  17.2 17.6 %collective-permute-start.3 = (f32[4,56,512]{2,1,0:T(8,128)S(1)}, f32[4,56,512]{2,1,0:T(8,128)S(1)}, u32[]{:S(2)}, u32[]{:S(2)}) collective-permute-start(f32[4,56,512]{2,1,0:T(8,128)S(1)} %pad_maximum_fusion.refs_0_), channel_id=1, source_target_pairs={{0,32},{32,64},{64,96},{96,128},{128,160},{160,192},{192,224},{224... | collective-permute-start | bytes 1376264 | tf_op jit(solution)/shard_map/ppermute | solution.py:259
  31.6 11.7 %collective-permute-start.6 = (f32[4,56,512]{2,1,0:T(8,128)S(1)}, f32[4,56,512]{2,1,0:T(8,128)S(1)}, u32[]{:S(2)}, u32[]{:S(2)}) collective-permute-start(f32[4,56,512]{2,1,0:T(8,128)S(1)} %collective-permute-done.4.refs_2_), channel_id=1, source_target_pairs={{0,224},{32,0},{64,32},{96,64},{128,96},{160,128},{192,160},{224,1... | collective-permute-start | bytes 1376264 | tf_op jit(solution)/shard_map/ppermute | solution.py:259
  34.8 14.8 %collective-permute-start.5 = (f32[4,56,512]{2,1,0:T(8,128)S(1)}, f32[4,56,512]{2,1,0:T(8,128)S(1)}, u32[]{:S(2)}, u32[]{:S(2)}) collective-permute-start(f32[4,56,512]{2,1,0:T(8,128)S(1)} %collective-permute-done.3.refs_1_), channel_id=1, source_target_pairs={{0,32},{32,64},{64,96},{96,128},{128,160},{160,192},{192,224},{224... | collective-permute-start | bytes 1376264 | tf_op jit(solution)/shard_map/ppermute | solution.py:259
  43.2 18.1 %collective-permute-start.8 = (f32[4,56,512]{2,1,0:T(8,128)S(1)}, f32[4,56,512]{2,1,0:T(8,128)S(1)}, u32[]{:S(2)}, u32[]{:S(2)}) collective-permute-start(f32[4,56,512]{2,1,0:T(8,128)S(1)} %collective-permute-done.6.refs_4_), channel_id=1, source_target_pairs={{0,224},{32,0},{64,32},{96,64},{128,96},{160,128},{192,160},{224,1... | collective-permute-start | bytes 1376264 | tf_op jit(solution)/shard_map/ppermute | solution.py:259
  49.7 15.1 %collective-permute-start.7 = (f32[4,56,512]{2,1,0:T(8,128)S(1)}, f32[4,56,512]{2,1,0:T(8,128)S(1)}, u32[]{:S(2)}, u32[]{:S(2)}) collective-permute-start(f32[4,56,512]{2,1,0:T(8,128)S(1)} %collective-permute-done.5.refs_3_), channel_id=1, source_target_pairs={{0,32},{32,64},{64,96},{96,128},{128,160},{160,192},{192,224},{224... | collective-permute-start | bytes 1376264 | tf_op jit(solution)/shard_map/ppermute | solution.py:259
  61.3 8.2 %collective-permute-start.10 = (f32[2,56,512]{2,1,0:T(8,128)S(1)}, f32[2,56,512]{2,1,0:T(8,128)S(1)}, u32[]{:S(2)}, u32[]{:S(2)}) collective-permute-start(f32[2,56,512]{2,1,0:T(8,128)S(1)} %slice.69), channel_id=1, source_target_pairs={{0,224},{32,0},{64,32},{96,64},{128,96},{160,128},{192,160},{224,1... | collective-permute-start | bytes 688136 | tf_op jit(solution)/shard_map/ppermute | solution.py:259
  64.8 7.3 %collective-permute-start.9 = (f32[2,56,512]{2,1,0:T(8,128)S(1)}, f32[2,56,512]{2,1,0:T(8,128)S(1)}, u32[]{:S(2)}, u32[]{:S(2)}) collective-permute-start(f32[2,56,512]{2,1,0:T(8,128)S(1)} %slice.68), channel_id=1, source_target_pairs={{0,32},{32,64},{64,96},{96,128},{128,160},{160,192},{192,224},{224... | collective-permute-start | bytes 688136 | tf_op jit(solution)/shard_map/ppermute | solution.py:259
  80.9 28.1 %all-to-all-start = ((f32[32,8,512]{2,1,0:T(8,128)}), f32[32,8,512]{2,1,0:T(8,128)S(1)}, u32[]{:S(2)}, u32[]{:S(2)}) async-start(f32[32,8,512]{2,1,0:T(8,128)} %get-tuple-element.48), calls=%async_computation | async-start | bytes 1048576 | tf_op jit(solution)/shard_map/all_to_all | solution.py:309
  96.6 12.5 %collective-permute-start.12 = (f32[8,512]{1,0:T(8,128)S(1)}, f32[8,512]{1,0:T(8,128)S(1)}, u32[]{:S(2)}, u32[]{:S(2)}) collective-permute-start(f32[8,512]{1,0:T(8,128)S(1)} %get-tuple-element.61), channel_id=1, source_target_pairs={{0,6},{2,0},{4,2},{6,4},{1,7},{3,1},{5,3},{7,5},{8,14},{10,8},{12,... | collective-permute-start | bytes 49160 | tf_op jit(solution)/shard_map/ppermute | solution.py:259
  96.7 12.4 %collective-permute-start.14 = (f32[8,512]{1,0:T(8,128)S(1)}, f32[8,512]{1,0:T(8,128)S(1)}, u32[]{:S(2)}, u32[]{:S(2)}) collective-permute-start(f32[8,512]{1,0:T(8,128)S(1)} %get-tuple-element.62), channel_id=1, source_target_pairs={{0,2},{2,4},{4,6},{6,0},{1,3},{3,5},{5,7},{7,1},{8,10},{10,12},{12... | collective-permute-start | bytes 49160 | tf_op jit(solution)/shard_map/ppermute | solution.py:259
  98.7 10.4 %collective-permute-start.13 = (f32[8,512]{1,0:T(8,128)S(1)}, f32[8,512]{1,0:T(8,128)S(1)}, u32[]{:S(2)}, u32[]{:S(2)}) collective-permute-start(f32[8,512]{1,0:T(8,128)S(1)} %get-tuple-element.63), channel_id=1, source_target_pairs={{0,4},{2,6},{4,0},{6,2},{1,5},{3,7},{5,1},{7,3},{8,12},{10,14},{12... | collective-permute-start | bytes 49160 | tf_op jit(solution)/shard_map/ppermute | solution.py:259
  109.1 8.0 %collective-permute-start.21 = (f32[8,512]{1,0:T(8,128)S(1)}, f32[8,512]{1,0:T(8,128)S(1)}, u32[]{:S(2)}, u32[]{:S(2)}) collective-permute-start(f32[8,512]{1,0:T(8,128)S(1)} %get-tuple-element.50), channel_id=1, source_target_pairs={{0,6},{2,0},{4,2},{6,4},{1,7},{3,1},{5,3},{7,5},{8,14},{10,8},{12,... | collective-permute-start | bytes 49160 | tf_op jit(solution)/shard_map/ppermute | solution.py:259
  109.2 7.9 %collective-permute-start.20 = (f32[8,512]{1,0:T(8,128)S(1)}, f32[8,512]{1,0:T(8,128)S(1)}, u32[]{:S(2)}, u32[]{:S(2)}) collective-permute-start(f32[8,512]{1,0:T(8,128)S(1)} %get-tuple-element.50), channel_id=1, source_target_pairs={{0,4},{2,6},{4,0},{6,2},{1,5},{3,7},{5,1},{7,3},{8,12},{10,14},{12... | collective-permute-start | bytes 49160 | tf_op jit(solution)/shard_map/ppermute | solution.py:259
  111.8 5.3 %collective-permute-start.19 = (f32[8,512]{1,0:T(8,128)S(1)}, f32[8,512]{1,0:T(8,128)S(1)}, u32[]{:S(2)}, u32[]{:S(2)}) collective-permute-start(f32[8,512]{1,0:T(8,128)S(1)} %get-tuple-element.50), channel_id=1, source_target_pairs={{0,2},{2,4},{4,6},{6,0},{1,3},{3,5},{5,7},{7,1},{8,10},{10,12},{12... | collective-permute-start | bytes 49160 | tf_op jit(solution)/shard_map/ppermute | solution.py:259
  112.7 21.3 %all-to-all-start.1 = ((f32[32,8,512]{2,1,0:T(8,128)}), f32[32,8,512]{2,1,0:T(8,128)S(1)}, u32[]{:S(2)}, u32[]{:S(2)}) async-start(f32[32,8,512]{2,1,0:T(8,128)} %broadcast_in_dim.39), calls=%async_computation.1 | async-start | bytes 1048576 | tf_op jit(solution)/shard_map/all_to_all | solution.py:264
  117.1 1.3 collective-permute-start.22
  134.0 21.4 %all-to-all-start.2 = ((f32[32,8,512]{2,1,0:T(8,128)}), f32[32,8,512]{2,1,0:T(8,128)S(1)}, u32[]{:S(2)}, u32[]{:S(2)}) async-start(f32[32,8,512]{2,1,0:T(8,128)} %apply_cols.1), calls=%async_computation.2 | async-start | bytes 1048576 | tf_op jit(solution)/shard_map/all_to_all | solution.py:309
  146.0 9.5 %collective-permute-start.16 = (f32[8,512]{1,0:T(8,128)S(1)}, f32[8,512]{1,0:T(8,128)S(1)}, u32[]{:S(2)}, u32[]{:S(2)}) collective-permute-start(f32[8,512]{1,0:T(8,128)S(1)} %get-tuple-element.58), channel_id=1, source_target_pairs={{0,6},{2,0},{4,2},{6,4},{1,7},{3,1},{5,3},{7,5},{8,14},{10,8},{12,... | collective-permute-start | bytes 49160 | tf_op jit(solution)/shard_map/ppermute | solution.py:259
  148.4 7.1 %collective-permute-start.18 = (f32[8,512]{1,0:T(8,128)S(1)}, f32[8,512]{1,0:T(8,128)S(1)}, u32[]{:S(2)}, u32[]{:S(2)}) collective-permute-start(f32[8,512]{1,0:T(8,128)S(1)} %get-tuple-element.59), channel_id=1, source_target_pairs={{0,2},{2,4},{4,6},{6,0},{1,3},{3,5},{5,7},{7,1},{8,10},{10,12},{12... | collective-permute-start | bytes 49160 | tf_op jit(solution)/shard_map/ppermute | solution.py:259
  148.4 7.1 %collective-permute-start.17 = (f32[8,512]{1,0:T(8,128)S(1)}, f32[8,512]{1,0:T(8,128)S(1)}, u32[]{:S(2)}, u32[]{:S(2)}) collective-permute-start(f32[8,512]{1,0:T(8,128)S(1)} %get-tuple-element.60), channel_id=1, source_target_pairs={{0,4},{2,6},{4,0},{6,2},{1,5},{3,7},{5,1},{7,3},{8,12},{10,14},{12... | collective-permute-start | bytes 49160 | tf_op jit(solution)/shard_map/ppermute | solution.py:259
  (4 other events, 16.2 us)

commit v5 on v4

--- a/solution.py
+++ b/solution.py
@@ -19,7 +19,6 @@
 LOG2E = math.log2(math.e)
 GROUPS = 6
 DEPTH = 8 * GROUPS
-CHUNK = 256
 HALF = 256
 
 
@@ -49,22 +48,27 @@
 
 
 def prepare_kernel(pos_ref, out_ref):
-    for snapshot in range(16):
-        high, mid, low = split3(rows_of(pos_ref, snapshot, LOG2E, 4, 3))
-        stacked = jnp.concatenate([high, high, mid, mid, high, low], axis=0)
-        out_ref[0, snapshot] = stacked.T.astype(jnp.bfloat16)
+    def visit(tile, carry):
+        part = pos_ref.at[:, pl.ds(pl.multiple_of(tile * TILE, TILE), TILE)]
+        for snapshot in range(16):
+            high, mid, low = split3(rows_of(part, snapshot, LOG2E, 4, 3))
+            stacked = jnp.concatenate([high, high, mid, mid, high, low], axis=0)
+            out_ref[tile, snapshot] = stacked.T.astype(jnp.bfloat16)
+        return carry
+
+    lax.fori_loop(0, out_ref.shape[0], visit, 0)
 
 
 def prepare_rows(pos):
     tiles = pos.shape[1] // TILE
+    vmem = pl.BlockSpec(memory_space=pltpu.VMEM)
     return pl.pallas_call(
         prepare_kernel,
-        grid=(tiles,),
-        in_specs=[pl.BlockSpec((48, TILE), lambda i: (0, i))],
-        out_specs=pl.BlockSpec((1, 16, TILE, DEPTH), lambda i: (i, 0, 0, 0)),
+        in_specs=[vmem],
+        out_specs=vmem,
         out_shape=jax.ShapeDtypeStruct((tiles, 16, TILE, DEPTH), jnp.bfloat16),
-        compiler_params=pltpu.CompilerParams(vmem_limit_bytes=32 << 20),
-        cost_estimate=pl.CostEstimate(flops=10**8, bytes_accessed=20 << 20, transcendentals=0),
+        compiler_params=pltpu.CompilerParams(vmem_limit_bytes=4 << 20),
+        cost_estimate=pl.CostEstimate(flops=10**8, bytes_accessed=8 << 20, transcendentals=0),
         name="prepare_rows",
     )(pos)
 
@@ -81,12 +85,11 @@
 
 def stage_kernel(stage, sources, table, prepared_ref, row_vec, *refs):
     places = refs[:sources]
-    high_ref, low_ref, row_acc, col_acc, tile, cols, high_tile, low_tile, sems = refs[-9:]
+    high_ref, low_ref, slot_vec, col_acc, tile, cols, high_tile, low_tile, sems = refs[-9:]
     if stage == 0:
-        row_acc[...] = jnp.zeros_like(row_acc)
         col_acc[...] = jnp.zeros_like(col_acc)
     else:
-        row_acc[...] = refs[sources + 2][...]
+        slot_vec[...] = refs[sources + 2][...]
         col_acc[...] = refs[sources + 3][...]
 
     def copies(slot):
@@ -114,30 +117,25 @@
                 copy.wait()
 
         def step(at, carry):
-            start = pl.multiple_of(at * CHUNK, CHUNK)
-            for half in range(TILE // HALF):
-                total = None
-                for snapshot in range(16):
-                    exponent = jnp.dot(
-                        prepared_ref[row_at, snapshot, pl.ds(start, CHUNK), :],
-                        cols[snapshot, :, half * HALF : (half + 1) * HALF],
-                        preferred_element_type=jnp.float32,
-                    )
-                    term = jnp.exp2(exponent)
-                    total = term if total is None else total + term
-                high = total.astype(jnp.bfloat16)
-                low = (total - high.astype(jnp.float32)).astype(jnp.bfloat16)
-                place = (pl.ds(start, CHUNK), pl.ds(half * HALF, HALF))
-                high_tile[place] = high
-                low_tile[place] = low
+            part = pl.ds(pl.multiple_of(at * HALF, HALF), HALF)
+            total = None
+            for snapshot in range(16):
+                exponent = jnp.dot(
+                    prepared_ref[row_at, snapshot],
+                    cols[snapshot, :, part],
+                    preferred_element_type=jnp.float32,
+                )
+                term = jnp.exp2(exponent)
+                total = term if total is None else total + term
+            high = total.astype(jnp.bfloat16)
+            high_tile[:, part] = high
+            low_tile[:, part] = (total - high.astype(jnp.float32)).astype(jnp.bfloat16)
             return carry
 
-        lax.fori_loop(0, TILE // CHUNK, step, 0)
+        lax.fori_loop(0, TILE // HALF, step, 0)
         for copy in copies(slot):
             copy.start()
-        row_acc[table[ROW_NEAR, slot]] += multiply(
-            tile[48:56, :], high_tile[...], low_tile[...], BY_COLS
-        )
+        slot_vec[slot] = tile[48:56, :]
 
         @pl.when(table[CROSSING, slot] != 0)
         def _():
@@ -164,13 +162,12 @@
 
 def form_stage(stage, table, prepared, row_vec, places, state, blocks):
     slots = table.shape[1]
-    tiles = row_vec.shape[0]
     vmem = pl.BlockSpec(memory_space=pltpu.VMEM)
     hbm = pl.BlockSpec(memory_space=pltpu.HBM)
     shapes = [
         pltpu.HBM((slots, TILE, TILE), jnp.bfloat16),
         pltpu.HBM((slots, TILE, TILE), jnp.bfloat16),
-        jax.ShapeDtypeStruct((tiles, 8, TILE), jnp.float32),
+        jax.ShapeDtypeStruct((slots, 8, TILE), jnp.float32),
         jax.ShapeDtypeStruct((blocks, 8, TILE), jnp.float32),
     ]
     first = 3 + len(places)
@@ -199,7 +196,7 @@
     )(table, prepared, row_vec, *places, *state)
 
 
-def apply_kernel(wanted, table, high_ref, low_ref, field, acc, high, low, sems):
+def apply_kernel(wanted, col_at, table, high_ref, low_ref, field, acc, high, low, sems):
     slots = high_ref.shape[0]
 
     def copies(slot):
@@ -222,22 +219,23 @@
         def _():
             for copy in copies(slot):
                 copy.wait()
-            row_at, col_at = table[ROW_NEAR, slot], table[COL_AT, slot]
+            row = table[ROW_NEAR, slot]
+            col = slot if col_at is None else table[col_at, slot]
             if wanted == LIVE:
-                acc[row_at] += multiply(field[col_at], high[slot], low[slot], BY_COLS)
+                acc[row] += multiply(field[col], high[slot], low[slot], BY_COLS)
             else:
-                acc[col_at] += multiply(field[row_at], high[slot], low[slot], BY_ROWS)
+                acc[col] += multiply(field[row], high[slot], low[slot], BY_ROWS)
 
         return carry
 
     lax.fori_loop(0, slots, visit, 0)
 
 
-def apply_tiles(wanted, name, table, high, low, field, count):
+def apply_tiles(wanted, col_at, name, table, high, low, field, count):
     vmem = pl.BlockSpec(memory_space=pltpu.VMEM)
     hbm = pl.BlockSpec(memory_space=pltpu.HBM)
     return pl.pallas_call(
-        functools.partial(apply_kernel, wanted),
+        functools.partial(apply_kernel, wanted, col_at),
         in_specs=[pl.BlockSpec(memory_space=pltpu.SMEM), hbm, hbm, vmem],
         out_specs=vmem,
         out_shape=jax.ShapeDtypeStruct((count, 8, TILE), jnp.float32),
@@ -294,15 +292,61 @@
     return arrived
 
 
-def plan(source, live):
-    stage = jnp.where(live, (source + 1) // 2, LAST_STAGE)
-    slots = jnp.arange(source.shape[0])
-    key = stage * source.shape[0] + slots
-    before = key[None, :] <= key[:, None]
-    rank = jnp.sum(before.astype(jnp.int32), axis=1)
-    start = jnp.maximum(3 * stage - 1, 0)
-    turn = jnp.max(jnp.where(before, start[None, :] + rank[:, None] - rank[None, :], 0), axis=1)
-    return jnp.where(live, jnp.minimum((turn + 1) // 3, LAST_STAGE), -1)
+def table_kernel(pairs, valid, sizes, out):
+    size_z, size_y, size_x, tiles = sizes
+    z, y = lax.axis_index("z"), lax.axis_index("y")
+    x, core = lax.axis_index("x"), lax.axis_index("core")
+    slots = out.shape[1]
+    arrival, keys = [], []
+    for slot in range(slots):
+        row, col, live = pairs[0, slot], pairs[1, slot], valid[0, slot] != 0
+        behind = lax.rem(z - col // size_y + size_z, size_z)
+        place = lax.rem(y - lax.rem(col, size_y) + size_y, size_y)
+        upper = place >= size_y // 2
+        far = jnp.where(upper, size_z, size_z - 1)
+        source = jnp.where(behind < size_z // 2, 2 * behind - 1, 2 * (size_z - behind))
+        source = jnp.where(behind == size_z // 2, far, source)
+        source = jnp.where(behind == 0, 0, source)
+        place = jnp.where((behind == size_z // 2) & upper, place - size_y // 2, place)
+        crossing = ((z * size_y + y) * tiles + row) != (col * tiles + 2 * x + core)
+        near = jnp.where(lax.rem(row, 2) == core, 0, size_x)
+        near = near + lax.rem(x - row // 2 + size_x, size_x)
+        out[ROW_AT, slot] = row
+        out[ROW_NEAR, slot] = near
+        out[COL_AT, slot] = col
+        out[SOURCE, slot] = source
+        out[PLACE, slot] = place
+        out[LIVE, slot] = jnp.where(live, 1, 0)
+        out[CROSSING, slot] = jnp.where(live & crossing, 1, 0)
+        stage = jnp.where(live, (source + 1) // 2, LAST_STAGE)
+        arrival.append(jnp.maximum(3 * stage - 1, 0))
+        keys.append(stage * slots + slot)
+    ranks = [
+        sum(jnp.where(other <= key, 1, 0) for other in keys) for key in keys
+    ]
+    for slot in range(slots):
+        turn = arrival[slot]
+        for other in range(slots):
+            if other != slot:
+                wait = arrival[other] + ranks[slot] - ranks[other]
+                turn = jnp.maximum(turn, jnp.where(keys[other] <= keys[slot], wait, 0))
+        stage = jnp.minimum((turn + 1) // 3, LAST_STAGE)
+        out[STAGE, slot] = jnp.where(valid[0, slot] != 0, stage, -1)
+
+
+def slot_table(pairs, valid, sizes):
+    smem = pl.BlockSpec(memory_space=pltpu.SMEM)
+
+    def kernel(pairs_ref, valid_ref, out_ref):
+        table_kernel(pairs_ref, valid_ref, sizes, out_ref)
+
+    return pl.pallas_call(
+        kernel,
+        in_specs=[smem, smem],
+        out_specs=smem,
+        out_shape=jax.ShapeDtypeStruct((8, pairs.shape[1]), jnp.int32),
+        name="slot_table",
+    )(pairs, valid)
 
 
 def combine(row_acc, col_acc):
@@ -310,44 +354,13 @@
     return reduce_near(row_acc) + jnp.sum(by_col, axis=0)
 
 
-def near_tile(tile, x, core, size):
-    return jnp.where(tile % 2 == core, 0, size) + (x - tile // 2) % size
-
-
 def per_device(positions, vectors, pairs, valid):
-    grid_row = lax.axis_index(ROW)
     grid_col = lax.axis_index(COL)
-    x, core = lax.axis_index("x"), lax.axis_index("core")
-    y, z = lax.axis_index("y"), lax.axis_index("z")
-    size_x, size_y = lax.axis_size("x"), lax.axis_size("y")
     block = positions.shape[2]
     tiles = block // TILE
     blocks = lax.axis_size(ROW)
-    local_rows = pairs[0, 0, :, 0]
-    local_cols = pairs[0, 0, :, 1]
-    live = valid[0, 0] != 0
-    crossing = (grid_row * tiles + local_rows) != (local_cols * tiles + grid_col)
-    size_z = lax.axis_size("z")
-    behind = (z - local_cols // size_y) % size_z
-    place = (y - local_cols % size_y) % size_y
-    far = behind == size_z // 2
-    upper = place >= size_y // 2
-    source = jnp.where(behind < size_z // 2, 2 * behind - 1, 2 * (size_z - behind))
-    source = jnp.where(behind == 0, 0, jnp.where(far & ~upper, size_z - 1, source))
-    place = jnp.where(far & upper, place - size_y // 2, place)
-    table = jnp.stack(
-        [
-            local_rows,
-            near_tile(local_rows, x, core, size_x),
-            local_cols,
-            source,
-            place,
-            plan(source, live),
-            live.astype(jnp.int32),
-            (live & crossing).astype(jnp.int32),
-        ],
-        axis=0,
-    ).astype(jnp.int32)
+    sizes = (lax.axis_size("z"), lax.axis_size("y"), lax.axis_size("x"), tiles)
+    table = slot_table(pairs[0, 0].transpose(1, 0), valid[0], sizes)
 
     flat = positions.transpose(1, 0, 2).reshape(48, block)
     own = jnp.concatenate(
@@ -359,18 +372,18 @@
     )
     row_vec = vectors.reshape(8, tiles, TILE).transpose(1, 0, 2)
     near = gather_y(own)
-    flat, near = lax.optimization_barrier((flat, near))
     prepared = prepare_rows(flat)
     places, state = [], []
     for stage, arrived in enumerate(gather_z(near)):
         places = places + arrived
         state = form_stage(stage, table, prepared, row_vec, places, state, blocks)
-    high, low, row_acc, col_acc = state
+    high, low, slot_vec, col_acc = state
+    row_acc = apply_tiles(LIVE, None, "apply_first", table, high, low, slot_vec, tiles)
     first = combine(row_acc, col_acc)
 
     col_vec = spread(first, ROW)
-    col_acc = apply_tiles(CROSSING, "apply_cols", table, high, low, spread_near(first), blocks)
-    row_acc = apply_tiles(LIVE, "apply_rows", table, high, low, col_vec, tiles)
+    col_acc = apply_tiles(CROSSING, COL_AT, "apply_cols", table, high, low, spread_near(first), blocks)
+    row_acc = apply_tiles(LIVE, COL_AT, "apply_rows", table, high, low, col_vec, tiles)
     second = combine(row_acc, col_acc)
 
     rows = spread(second, COL)

time: 185 us -> 190 us (1.027)
  Pallas kernels: 58.2 us -> 66.1 us
  other arithmetic: 5.11 us -> 1.14 us
  starting transfers between devices: 56.7 us -> 54.1 us
  waiting for transfers between devices: 31.6 us -> 33.9 us
    ppermute x23, waiting for transfers between devices: 6.58 us -> 16.3 us  [shift(): lax.ppermute(value, axis, [(i, (i + distance) % size) for i in range(size)])]
    pallas_call x3 -> x5, Pallas kernels: 17.2 us -> 25.1 us  [the longest x3 18 us: apply_tiles(): pl.pallas_call(functools.partial(apply_kernel, wanted, col_at), in_specs=...]
    all_to_all x2, starting transfers between devices: 18.8 us -> 11.5 us  [combine(): by_col = lax.all_to_all(col_acc, ROW, 0, 0, tiled=True)]
    all_to_all x2, waiting for transfers between devices: 15.3 us -> 8.45 us  [combine(): by_col = lax.all_to_all(col_acc, ROW, 0, 0, tiled=True)]
    all_to_all x1, starting transfers between devices: 4.36 us -> 9.07 us  [spread(): return lax.all_to_all(copies, axes, 0, 0, tiled=True)]
  transfers between devices with their start and end apart: 26 -> 26, of which waited for: 8 -> 9; matrix products, arithmetic and copies ran while one was open for 3% -> 1% of each run, Pallas kernels for 27% -> 29%
where the time goes in v5:
time: 190 us; the launch traced here: 188 us
  Pallas kernels  66.1 us (35%)
  starting transfers between devices  54.1 us (28%)
  waiting for transfers between devices  33.9 us (18%)
  blocking collectives  29.1 us (15%)
  local copies, waits for them, and re-layouts  3.7 us (2%)
    pallas_call x5, Pallas kernels, form_stage(): pl.pallas_call(functools.partial(stage_kernel, stage, len(places)), in_sp...  41 us
    ppermute x23, starting transfers between devices, shift(): lax.ppermute(value, axis, [(i, (i + distance) % size) for i in range(size)])  33.6 us
    all_to_all x2, blocking collectives, spread(): return lax.all_to_all(copies, axes, 0, 0, tiled=True)  29.1 us
    pallas_call x3, Pallas kernels, apply_tiles(): pl.pallas_call(functools.partial(apply_kernel, wanted, col_at), in_specs=...  18 us
    ppermute x23, waiting for transfers between devices, shift(): lax.ppermute(value, axis, [(i, (i + distance) % size) for i in range(size)])  16.3 us
    all_to_all x2, starting transfers between devices, combine(): by_col = lax.all_to_all(col_acc, ROW, 0, 0, tiled=True)  11.5 us
    all_to_all x1, waiting for transfers between devices, spread(): return lax.all_to_all(copies, axes, 0, 0, tiled=True)  9.13 us
    all_to_all x1, starting transfers between devices, spread(): return lax.all_to_all(copies, axes, 0, 0, tiled=True)  9.07 us
  transfers between devices with their start and end apart: 26, of which 9 were waited for; matrix products, arithmetic and copies ran while one was open for 1% of the time, Pallas kernels for 29%

profile of v5, /device:TPU:0, one launch (start us, length us, event | category | flops | bytes accessed | tf_op | source)
XLA Modules:
  0.0 188.4 jit_solution(8140466385115403566)
XLA Ops:
  3.9 2.6 %collective-permute-start.2 = (f32[56,512]{1,0:T(8,128)S(1)}, f32[56,512]{1,0:T(8,128)S(1)}, u32[]{:S(2)}, u32[]{:S(2)}) collective-permute-start(f32[56,512]{1,0:T(8,128)S(1)} %get-tuple-element.48), channel_id=1, source_target_pairs={{0,24},{8,0},{16,8},{24,16},{1,25},{9,1},{17,9},{25,17},{2,26},{10... | collective-permute-start | bytes 344072 | tf_op jit(solution)/shard_map/ppermute | solution.py:257
  9.6 5.1 %prepare_rows.1.prepared_ref = bf16[8,16,512,48]{3,2,1,0:T(8,128)(2,1)S(1)} custom-call(f32[48,4096]{1,0:T(8,128)S(1)} %bitcast.68), custom_call_target="tpu_custom_call" | custom-call | flops 100000000 | bytes 8388608 | tf_op jit(solution)/shard_map/prepare_rows/pallas_call | solution.py:65
  14.8 5.9 %collective-permute-start.4 = (f32[4,56,512]{2,1,0:T(8,128)S(1)}, f32[4,56,512]{2,1,0:T(8,128)S(1)}, u32[]{:S(2)}, u32[]{:S(2)}) collective-permute-start(f32[4,56,512]{2,1,0:T(8,128)S(1)} %pad_maximum_fusion.refs_0_), channel_id=1, source_target_pairs={{0,224},{32,0},{64,32},{96,64},{128,96},{160,128},{192,160},{224,1... | collective-permute-start | bytes 1376264 | tf_op jit(solution)/shard_map/ppermute | solution.py:257
  21.5 8.1 %collective-permute-done.4.refs_2_ = f32[4,56,512]{2,1,0:T(8,128)S(1)} collective-permute-done((f32[4,56,512]{2,1,0:T(8,128)S(1)}, f32[4,56,512]{2,1,0:T(8,128)S(1)}, u32[]{:S(2)}, u32[]{:S(2)}) %collective-permute-start.4) | collective-permute-done | bytes 458784 | tf_op jit(solution)/shard_map/ppermute | solution.py:257
  29.6 3.7 %collective-permute-start.6 = (f32[4,56,512]{2,1,0:T(8,128)S(1)}, f32[4,56,512]{2,1,0:T(8,128)S(1)}, u32[]{:S(2)}, u32[]{:S(2)}) collective-permute-start(f32[4,56,512]{2,1,0:T(8,128)S(1)} %collective-permute-done.4.refs_2_), channel_id=1, source_target_pairs={{0,224},{32,0},{64,32},{96,64},{128,96},{160,128},{192,160},{224,1... | collective-permute-start | bytes 1376264 | tf_op jit(solution)/shard_map/ppermute | solution.py:257
  33.3 4.5 %form_1.1 = (bf16[10,512,512]{2,1,0:T(8,128)(2,1)}, bf16[10,512,512]{2,1,0:T(8,128)(2,1)}, f32[10,8,512]{2,1,0:T(8,128)S(1)}, f32[32,8,512]{2,1,0:T(8,128)S(1)}) custom-call(s32[8,10]{1,0:T(8,128)S(1)} %copy-done.2, bf16[8,16,512,48]{3,2,1,0:T(8,128)(2,1)S(1)} %prepare_rows.1.prepared_ref, ...), custom_call_target="tpu_custom_call", output_to_operand_aliasing={{0}: (6, {}), {1}: (7, {}), {2}: (8, {}), {3}: (9, {})} | custom-call | flops 8000000000 | bytes 8388608 | tf_op jit(solution)/shard_map/form_1/pallas_call | solution.py:174
  37.8 3.5 %collective-permute-done.6.refs_4_ = f32[4,56,512]{2,1,0:T(8,128)S(1)} collective-permute-done((f32[4,56,512]{2,1,0:T(8,128)S(1)}, f32[4,56,512]{2,1,0:T(8,128)S(1)}, u32[]{:S(2)}, u32[]{:S(2)}) %collective-permute-start.6) | collective-permute-done | bytes 458784 | tf_op jit(solution)/shard_map/ppermute | solution.py:257
  41.3 6.9 %collective-permute-start.8 = (f32[4,56,512]{2,1,0:T(8,128)S(1)}, f32[4,56,512]{2,1,0:T(8,128)S(1)}, u32[]{:S(2)}, u32[]{:S(2)}) collective-permute-start(f32[4,56,512]{2,1,0:T(8,128)S(1)} %collective-permute-done.6.refs_4_), channel_id=1, source_target_pairs={{0,224},{32,0},{64,32},{96,64},{128,96},{160,128},{192,160},{224,1... | collective-permute-start | bytes 1376264 | tf_op jit(solution)/shard_map/ppermute | solution.py:257
  48.3 11.8 %form_2.1 = (bf16[10,512,512]{2,1,0:T(8,128)(2,1)}, bf16[10,512,512]{2,1,0:T(8,128)(2,1)}, f32[10,8,512]{2,1,0:T(8,128)S(1)}, f32[32,8,512]{2,1,0:T(8,128)S(1)}) custom-call(s32[8,10]{1,0:T(8,128)S(1)} %copy-done.2, bf16[8,16,512,48]{3,2,1,0:T(8,128)(2,1)S(1)} %prepare_rows.1.prepared_ref, ...), custom_call_target="tpu_custom_call", output_to_operand_aliasing={{0}: (8, {}), {1}: (9, {}), {2}: (10, {}), {3}: (11, {})} | custom-call | flops 8000000000 | bytes 8388608 | tf_op jit(solution)/shard_map/form_2/pallas_call | solution.py:174
  60.1 3.2 %collective-permute-start.10 = (f32[2,56,512]{2,1,0:T(8,128)S(1)}, f32[2,56,512]{2,1,0:T(8,128)S(1)}, u32[]{:S(2)}, u32[]{:S(2)}) collective-permute-start(f32[2,56,512]{2,1,0:T(8,128)S(1)} %slice.61), channel_id=1, source_target_pairs={{0,224},{32,0},{64,32},{96,64},{128,96},{160,128},{192,160},{224,1... | collective-permute-start | bytes 688136 | tf_op jit(solution)/shard_map/ppermute | solution.py:257
  63.5 11.5 %form_3.1 = (bf16[10,512,512]{2,1,0:T(8,128)(2,1)}, bf16[10,512,512]{2,1,0:T(8,128)(2,1)}, f32[10,8,512]{2,1,0:T(8,128)S(1)}, f32[32,8,512]{2,1,0:T(8,128)S(1)}) custom-call(s32[8,10]{1,0:T(8,128)S(1)} %copy-done.2, ...), custom_call_target="tpu_custom_call", output_to_operand_aliasing={{0}: (10, {}), {1}: (11, {}), {2}: (12, {}), {3}: (13, {})} | custom-call | flops 8000000000 | bytes 8388608 | tf_op jit(solution)/shard_map/form_3/pallas_call | solution.py:174
  75.0 12.4 %form_4.1 = (bf16[10,512,512]{2,1,0:T(8,128)(2,1)}, bf16[10,512,512]{2,1,0:T(8,128)(2,1)}, f32[10,8,512]{2,1,0:T(8,128)S(1)}, f32[32,8,512]{2,1,0:T(8,128)}) custom-call(s32[8,10]{1,0:T(8,128)S(1)} %copy-done.2, bf16[8,16,512,48]{3,2,1,0:T(8,128)(2,1)S(1)} %prepare_rows.1.prepared_ref, ...), custom_call_target="tpu_custom_call", output_to_operand_aliasing={{0}: (12, {}), {1}: (13, {})} | custom-call | flops 8000000000 | bytes 8388608 | tf_op jit(solution)/shard_map/form_4/pallas_call | solution.py:174
  87.4 7.1 %all-to-all-start = ((f32[32,8,512]{2,1,0:T(8,128)}), f32[32,8,512]{2,1,0:T(8,128)S(1)}, u32[]{:S(2)}, u32[]{:S(2)}) async-start(f32[32,8,512]{2,1,0:T(8,128)} %get-tuple-element.44), calls=%async_computation | async-start | bytes 1048576 | tf_op jit(solution)/shard_map/all_to_all | solution.py:353
  94.5 6.1 %apply_first.1 = f32[8,8,512]{2,1,0:T(8,128)S(1)} custom-call(s32[8,10]{1,0:T(8,128)S(1)} %copy-done.2, bf16[10,512,512]{2,1,0:T(8,128)(2,1)} %get-tuple-element.41.high_ref, bf16[10,512,512]{2,1,0:T(8,128)(2,1)} %get-tuple-element.42.low_ref, f32[10,8,512]{2,1,0:T(8,128)S(1)} %get-tuple-element.43.field), custom_call_target="tpu_custom_call" | custom-call | flops 3000000000 | bytes 12582912 | tf_op jit(solution)/shard_map/apply_first/pallas_call | solution.py:237
  104.1 4.3 %all-to-all-done = f32[32,8,512]{2,1,0:T(8,128)S(1)} async-done(((f32[32,8,512]{2,1,0:T(8,128)}), f32[32,8,512]{2,1,0:T(8,128)S(1)}, u32[]{:S(2)}, u32[]{:S(2)}) %all-to-all-start) | async-done | bytes 524320 | tf_op jit(solution)/shard_map/all_to_all | solution.py:353
  112.5 9.1 %all-to-all-start.1 = ((f32[32,8,512]{2,1,0:T(8,128)}), f32[32,8,512]{2,1,0:T(8,128)S(1)}, u32[]{:S(2)}, u32[]{:S(2)}) async-start(f32[32,8,512]{2,1,0:T(8,128)} %broadcast_in_dim.13), calls=%async_computation.1 | async-start | bytes 1048576 | tf_op jit(solution)/shard_map/all_to_all | solution.py:262
  123.0 5.8 %apply_cols.1 = f32[32,8,512]{2,1,0:T(8,128)} custom-call(s32[8,10]{1,0:T(8,128)S(1)} %copy-done.2, bf16[10,512,512]{2,1,0:T(8,128)(2,1)} %get-tuple-element.41.high_ref, bf16[10,512,512]{2,1,0:T(8,128)(2,1)} %get-tuple-element.42.low_ref, f32[8,8,512]{2,1,0:T(8,128)S(1)} %constant_dynamic-update-slice_fusion.field), custom_call_target="tpu_custom_call" | custom-call | flops 3000000000 | bytes 12582912 | tf_op jit(solution)/shard_map/apply_cols/pallas_call | solution.py:237
  128.9 9.1 %all-to-all-done.1.field = f32[32,8,512]{2,1,0:T(8,128)S(1)} async-done(((f32[32,8,512]{2,1,0:T(8,128)}), f32[32,8,512]{2,1,0:T(8,128)S(1)}, u32[]{:S(2)}, u32[]{:S(2)}) %all-to-all-start.1) | async-done | bytes 524320 | tf_op jit(solution)/shard_map/all_to_all | solution.py:262
  138.0 4.4 %all-to-all-start.2 = ((f32[32,8,512]{2,1,0:T(8,128)}), f32[32,8,512]{2,1,0:T(8,128)S(1)}, u32[]{:S(2)}, u32[]{:S(2)}) async-start(f32[32,8,512]{2,1,0:T(8,128)} %apply_cols.1), calls=%async_computation.2 | async-start | bytes 1048576 | tf_op jit(solution)/shard_map/all_to_all | solution.py:353
  142.4 6.1 %apply_rows.1 = f32[8,8,512]{2,1,0:T(8,128)S(1)} custom-call(s32[8,10]{1,0:T(8,128)S(1)} %copy-done.2, bf16[10,512,512]{2,1,0:T(8,128)(2,1)} %get-tuple-element.41.high_ref, bf16[10,512,512]{2,1,0:T(8,128)(2,1)} %get-tuple-element.42.low_ref, f32[32,8,512]{2,1,0:T(8,128)S(1)} %all-to-all-done.1.field), custom_call_target="tpu_custom_call" | custom-call | flops 3000000000 | bytes 12582912 | tf_op jit(solution)/shard_map/apply_rows/pallas_call | solution.py:237
  151.9 2.1 %collective-permute-start.17 = (f32[8,512]{1,0:T(8,128)S(1)}, f32[8,512]{1,0:T(8,128)S(1)}, u32[]{:S(2)}, u32[]{:S(2)}) collective-permute-start(f32[8,512]{1,0:T(8,128)S(1)} %get-tuple-element.51), channel_id=1, source_target_pairs={{0,4},{2,6},{4,0},{6,2},{1,5},{3,7},{5,1},{7,3},{8,12},{10,14},{12... | collective-permute-start | bytes 49160 | tf_op jit(solution)/shard_map/ppermute | solution.py:257
  154.0 4.2 %all-to-all-done.2 = f32[32,8,512]{2,1,0:T(8,128)S(1)} async-done(((f32[32,8,512]{2,1,0:T(8,128)}), f32[32,8,512]{2,1,0:T(8,128)S(1)}, u32[]{:S(2)}, u32[]{:S(2)}) %all-to-all-start.2) | async-done | bytes 524320 | tf_op jit(solution)/shard_map/all_to_all | solution.py:353
  158.3 9.8 %all_to_all.25 = f32[8,8,512]{2,1,0:T(8,128)S(1)} all-to-all(f32[8,8,512]{2,1,0:T(8,128)S(1)} %broadcast_in_dim.14), channel_id=1, replica_groups=mesh['z'=8,'y'=4,'x'=4,'core'=2] {'x','core'}, dimensions={0} | all-to-all | bytes 262144 | tf_op jit(solution)/shard_map/all_to_all | solution.py:262
  168.3 19.3 %all_to_all.26 = f32[32,1,128]{2,1,0:T(1,128)S(1)} all-to-all(f32[32,1,128]{2,1,0:T(1,128)S(1)} %broadcast_in_dim.16), channel_id=1, replica_groups=mesh['z'=8,'y'=4,'x'=4,'core'=2] {'z','y'}, dimensions={0} | all-to-all | bytes 32768 | tf_op jit(solution)/shard_map/all_to_all | solution.py:262
  (75 shorter events, 21.4 us)
Async XLA Ops:
  1.6 13.1 %collective-permute-start.1 = (f32[56,512]{1,0:T(8,128)S(1)}, f32[56,512]{1,0:T(8,128)S(1)}, u32[]{:S(2)}, u32[]{:S(2)}) collective-permute-start(f32[56,512]{1,0:T(8,128)S(1)} %get-tuple-element.48), channel_id=1, source_target_pairs={{0,16},{8,24},{16,0},{24,8},{1,17},{9,25},{17,1},{25,9},{2,18},{10... | collective-permute-start | bytes 344072 | tf_op jit(solution)/shard_map/ppermute | solution.py:257
  3.2 11.5 %collective-permute-start = (f32[56,512]{1,0:T(8,128)S(1)}, f32[56,512]{1,0:T(8,128)S(1)}, u32[]{:S(2)}, u32[]{:S(2)}) collective-permute-start(f32[56,512]{1,0:T(8,128)S(1)} %get-tuple-element.48), channel_id=1, source_target_pairs={{0,8},{8,16},{16,24},{24,0},{1,9},{9,17},{17,25},{25,1},{2,10},{10... | collective-permute-start | bytes 344072 | tf_op jit(solution)/shard_map/ppermute | solution.py:257
  3.9 10.9 %collective-permute-start.2 = (f32[56,512]{1,0:T(8,128)S(1)}, f32[56,512]{1,0:T(8,128)S(1)}, u32[]{:S(2)}, u32[]{:S(2)}) collective-permute-start(f32[56,512]{1,0:T(8,128)S(1)} %get-tuple-element.48), channel_id=1, source_target_pairs={{0,24},{8,0},{16,8},{24,16},{1,25},{9,1},{17,9},{25,17},{2,26},{10... | collective-permute-start | bytes 344072 | tf_op jit(solution)/shard_map/ppermute | solution.py:257
  14.8 14.9 %collective-permute-start.4 = (f32[4,56,512]{2,1,0:T(8,128)S(1)}, f32[4,56,512]{2,1,0:T(8,128)S(1)}, u32[]{:S(2)}, u32[]{:S(2)}) collective-permute-start(f32[4,56,512]{2,1,0:T(8,128)S(1)} %pad_maximum_fusion.refs_0_), channel_id=1, source_target_pairs={{0,224},{32,0},{64,32},{96,64},{128,96},{160,128},{192,160},{224,1... | collective-permute-start | bytes 1376264 | tf_op jit(solution)/shard_map/ppermute | solution.py:257
  20.7 12.6 %collective-permute-start.3 = (f32[4,56,512]{2,1,0:T(8,128)S(1)}, f32[4,56,512]{2,1,0:T(8,128)S(1)}, u32[]{:S(2)}, u32[]{:S(2)}) collective-permute-start(f32[4,56,512]{2,1,0:T(8,128)S(1)} %pad_maximum_fusion.refs_0_), channel_id=1, source_target_pairs={{0,32},{32,64},{64,96},{96,128},{128,160},{160,192},{192,224},{224... | collective-permute-start | bytes 1376264 | tf_op jit(solution)/shard_map/ppermute | solution.py:257
  29.6 11.7 %collective-permute-start.6 = (f32[4,56,512]{2,1,0:T(8,128)S(1)}, f32[4,56,512]{2,1,0:T(8,128)S(1)}, u32[]{:S(2)}, u32[]{:S(2)}) collective-permute-start(f32[4,56,512]{2,1,0:T(8,128)S(1)} %collective-permute-done.4.refs_2_), channel_id=1, source_target_pairs={{0,224},{32,0},{64,32},{96,64},{128,96},{160,128},{192,160},{224,1... | collective-permute-start | bytes 1376264 | tf_op jit(solution)/shard_map/ppermute | solution.py:257
  33.3 14.9 %collective-permute-start.5 = (f32[4,56,512]{2,1,0:T(8,128)S(1)}, f32[4,56,512]{2,1,0:T(8,128)S(1)}, u32[]{:S(2)}, u32[]{:S(2)}) collective-permute-start(f32[4,56,512]{2,1,0:T(8,128)S(1)} %collective-permute-done.3.refs_1_), channel_id=1, source_target_pairs={{0,32},{32,64},{64,96},{96,128},{128,160},{160,192},{192,224},{224... | collective-permute-start | bytes 1376264 | tf_op jit(solution)/shard_map/ppermute | solution.py:257
  41.3 18.7 %collective-permute-start.8 = (f32[4,56,512]{2,1,0:T(8,128)S(1)}, f32[4,56,512]{2,1,0:T(8,128)S(1)}, u32[]{:S(2)}, u32[]{:S(2)}) collective-permute-start(f32[4,56,512]{2,1,0:T(8,128)S(1)} %collective-permute-done.6.refs_4_), channel_id=1, source_target_pairs={{0,224},{32,0},{64,32},{96,64},{128,96},{160,128},{192,160},{224,1... | collective-permute-start | bytes 1376264 | tf_op jit(solution)/shard_map/ppermute | solution.py:257
  48.3 15.1 %collective-permute-start.7 = (f32[4,56,512]{2,1,0:T(8,128)S(1)}, f32[4,56,512]{2,1,0:T(8,128)S(1)}, u32[]{:S(2)}, u32[]{:S(2)}) collective-permute-start(f32[4,56,512]{2,1,0:T(8,128)S(1)} %collective-permute-done.5.refs_3_), channel_id=1, source_target_pairs={{0,32},{32,64},{64,96},{96,128},{128,160},{160,192},{192,224},{224... | collective-permute-start | bytes 1376264 | tf_op jit(solution)/shard_map/ppermute | solution.py:257
  60.1 14.9 %collective-permute-start.10 = (f32[2,56,512]{2,1,0:T(8,128)S(1)}, f32[2,56,512]{2,1,0:T(8,128)S(1)}, u32[]{:S(2)}, u32[]{:S(2)}) collective-permute-start(f32[2,56,512]{2,1,0:T(8,128)S(1)} %slice.61), channel_id=1, source_target_pairs={{0,224},{32,0},{64,32},{96,64},{128,96},{160,128},{192,160},{224,1... | collective-permute-start | bytes 688136 | tf_op jit(solution)/shard_map/ppermute | solution.py:257
  63.4 11.6 %collective-permute-start.9 = (f32[2,56,512]{2,1,0:T(8,128)S(1)}, f32[2,56,512]{2,1,0:T(8,128)S(1)}, u32[]{:S(2)}, u32[]{:S(2)}) collective-permute-start(f32[2,56,512]{2,1,0:T(8,128)S(1)} %slice.60), channel_id=1, source_target_pairs={{0,32},{32,64},{64,96},{96,128},{128,160},{160,192},{192,224},{224... | collective-permute-start | bytes 688136 | tf_op jit(solution)/shard_map/ppermute | solution.py:257
  87.4 20.9 %all-to-all-start = ((f32[32,8,512]{2,1,0:T(8,128)}), f32[32,8,512]{2,1,0:T(8,128)S(1)}, u32[]{:S(2)}, u32[]{:S(2)}) async-start(f32[32,8,512]{2,1,0:T(8,128)} %get-tuple-element.44), calls=%async_computation | async-start | bytes 1048576 | tf_op jit(solution)/shard_map/all_to_all | solution.py:353
  100.6 1.3 collective-permute-start.11
  102.0 6.4 %collective-permute-start.12 = (f32[8,512]{1,0:T(8,128)S(1)}, f32[8,512]{1,0:T(8,128)S(1)}, u32[]{:S(2)}, u32[]{:S(2)}) collective-permute-start(f32[8,512]{1,0:T(8,128)S(1)} %get-tuple-element.52), channel_id=1, source_target_pairs={{0,6},{2,0},{4,2},{6,4},{1,7},{3,1},{5,3},{7,5},{8,14},{10,8},{12,... | collective-permute-start | bytes 49160 | tf_op jit(solution)/shard_map/ppermute | solution.py:257
  102.1 6.3 %collective-permute-start.14 = (f32[8,512]{1,0:T(8,128)S(1)}, f32[8,512]{1,0:T(8,128)S(1)}, u32[]{:S(2)}, u32[]{:S(2)}) collective-permute-start(f32[8,512]{1,0:T(8,128)S(1)} %get-tuple-element.53), channel_id=1, source_target_pairs={{0,2},{2,4},{4,6},{6,0},{1,3},{3,5},{5,7},{7,1},{8,10},{10,12},{12... | collective-permute-start | bytes 49160 | tf_op jit(solution)/shard_map/ppermute | solution.py:257
  104.1 5.2 %collective-permute-start.13 = (f32[8,512]{1,0:T(8,128)S(1)}, f32[8,512]{1,0:T(8,128)S(1)}, u32[]{:S(2)}, u32[]{:S(2)}) collective-permute-start(f32[8,512]{1,0:T(8,128)S(1)} %get-tuple-element.54), channel_id=1, source_target_pairs={{0,4},{2,6},{4,0},{6,2},{1,5},{3,7},{5,1},{7,3},{8,12},{10,14},{12... | collective-permute-start | bytes 49160 | tf_op jit(solution)/shard_map/ppermute | solution.py:257
  109.4 12.3 %collective-permute-start.21 = (f32[8,512]{1,0:T(8,128)S(1)}, f32[8,512]{1,0:T(8,128)S(1)}, u32[]{:S(2)}, u32[]{:S(2)}) collective-permute-start(f32[8,512]{1,0:T(8,128)S(1)} %get-tuple-element.46), channel_id=1, source_target_pairs={{0,6},{2,0},{4,2},{6,4},{1,7},{3,1},{5,3},{7,5},{8,14},{10,8},{12,... | collective-permute-start | bytes 49160 | tf_op jit(solution)/shard_map/ppermute | solution.py:257
  110.7 10.9 %collective-permute-start.20 = (f32[8,512]{1,0:T(8,128)S(1)}, f32[8,512]{1,0:T(8,128)S(1)}, u32[]{:S(2)}, u32[]{:S(2)}) collective-permute-start(f32[8,512]{1,0:T(8,128)S(1)} %get-tuple-element.46), channel_id=1, source_target_pairs={{0,4},{2,6},{4,0},{6,2},{1,5},{3,7},{5,1},{7,3},{8,12},{10,14},{12... | collective-permute-start | bytes 49160 | tf_op jit(solution)/shard_map/ppermute | solution.py:257
  111.5 10.1 %collective-permute-start.19 = (f32[8,512]{1,0:T(8,128)S(1)}, f32[8,512]{1,0:T(8,128)S(1)}, u32[]{:S(2)}, u32[]{:S(2)}) collective-permute-start(f32[8,512]{1,0:T(8,128)S(1)} %get-tuple-element.46), channel_id=1, source_target_pairs={{0,2},{2,4},{4,6},{6,0},{1,3},{3,5},{5,7},{7,1},{8,10},{10,12},{12... | collective-permute-start | bytes 49160 | tf_op jit(solution)/shard_map/ppermute | solution.py:257
  112.5 25.4 %all-to-all-start.1 = ((f32[32,8,512]{2,1,0:T(8,128)}), f32[32,8,512]{2,1,0:T(8,128)S(1)}, u32[]{:S(2)}, u32[]{:S(2)}) async-start(f32[32,8,512]{2,1,0:T(8,128)} %broadcast_in_dim.13), calls=%async_computation.1 | async-start | bytes 1048576 | tf_op jit(solution)/shard_map/all_to_all | solution.py:262
  138.0 20.2 %all-to-all-start.2 = ((f32[32,8,512]{2,1,0:T(8,128)}), f32[32,8,512]{2,1,0:T(8,128)S(1)}, u32[]{:S(2)}, u32[]{:S(2)}) async-start(f32[32,8,512]{2,1,0:T(8,128)} %apply_cols.1), calls=%async_computation.2 | async-start | bytes 1048576 | tf_op jit(solution)/shard_map/all_to_all | solution.py:353
  149.8 8.5 %collective-permute-start.16 = (f32[8,512]{1,0:T(8,128)S(1)}, f32[8,512]{1,0:T(8,128)S(1)}, u32[]{:S(2)}, u32[]{:S(2)}) collective-permute-start(f32[8,512]{1,0:T(8,128)S(1)} %get-tuple-element.49), channel_id=1, source_target_pairs={{0,6},{2,0},{4,2},{6,4},{1,7},{3,1},{5,3},{7,5},{8,14},{10,8},{12,... | collective-permute-start | bytes 49160 | tf_op jit(solution)/shard_map/ppermute | solution.py:257
  151.4 6.9 %collective-permute-start.18 = (f32[8,512]{1,0:T(8,128)S(1)}, f32[8,512]{1,0:T(8,128)S(1)}, u32[]{:S(2)}, u32[]{:S(2)}) collective-permute-start(f32[8,512]{1,0:T(8,128)S(1)} %get-tuple-element.50), channel_id=1, source_target_pairs={{0,2},{2,4},{4,6},{6,0},{1,3},{3,5},{5,7},{7,1},{8,10},{10,12},{12... | collective-permute-start | bytes 49160 | tf_op jit(solution)/shard_map/ppermute | solution.py:257
  151.9 6.4 %collective-permute-start.17 = (f32[8,512]{1,0:T(8,128)S(1)}, f32[8,512]{1,0:T(8,128)S(1)}, u32[]{:S(2)}, u32[]{:S(2)}) collective-permute-start(f32[8,512]{1,0:T(8,128)S(1)} %get-tuple-element.51), channel_id=1, source_target_pairs={{0,4},{2,6},{4,0},{6,2},{1,5},{3,7},{5,1},{7,3},{8,12},{10,14},{12... | collective-permute-start | bytes 49160 | tf_op jit(solution)/shard_map/ppermute | solution.py:257
  (5 other events, 26.1 us)

commit v6 on v5

--- a/solution.py
+++ b/solution.py
@@ -12,7 +12,7 @@
 TILE = 512
 ROW = ("z", "y")
 COL = ("x", "core")
-ROW_AT, ROW_NEAR, COL_AT, SOURCE, PLACE, STAGE, LIVE, CROSSING = range(8)
+ROW_AT, ROW_NEAR, COL_AT, SOURCE, PLACE, STAGE, LIVE, CROSSING, LATE = range(9)
 LAST_STAGE = 4
 BY_ROWS = (((1,), (0,)), ((), ()))
 BY_COLS = (((1,), (1,)), ((), ()))
@@ -85,20 +85,24 @@
 
 def stage_kernel(stage, sources, table, prepared_ref, row_vec, *refs):
     places = refs[:sources]
-    high_ref, low_ref, slot_vec, col_acc, tile, cols, high_tile, low_tile, sems = refs[-9:]
+    last = stage == LAST_STAGE
+    high_ref, low_ref, rows_out, col_acc, tile, cols, high_tile, low_tile, sems = refs[-9:]
     if stage == 0:
+        rows_out[...] = jnp.zeros_like(rows_out)
         col_acc[...] = jnp.zeros_like(col_acc)
     else:
-        slot_vec[...] = refs[sources + 2][...]
+        if not last:
+            rows_out[...] = refs[sources + 2][...]
         col_acc[...] = refs[sources + 3][...]
 
-    def copies(slot):
+    def copies(slot, buffer):
         return [
-            pltpu.make_async_copy(high_tile, high_ref.at[slot], sems.at[0]),
-            pltpu.make_async_copy(low_tile, low_ref.at[slot], sems.at[1]),
+            pltpu.make_async_copy(high_tile.at[buffer], high_ref.at[slot], sems.at[0, buffer]),
+            pltpu.make_async_copy(low_tile.at[buffer], low_ref.at[slot], sems.at[1, buffer]),
         ]
 
-    def form(slot, pending):
+    def form(slot, formed):
+        buffer = lax.rem(formed, 2)
         for source in range(sources):
 
             @pl.when(table[SOURCE, slot] == source)
@@ -111,9 +115,9 @@
             cols[snapshot] = stacked.astype(jnp.bfloat16)
         row_at = table[ROW_AT, slot]
 
-        @pl.when(pending != 0)
-        def _():
-            for copy in copies(slot):
+        @pl.when(formed >= 2)
+        def _():
+            for copy in copies(slot, buffer):
                 copy.wait()
 
         def step(at, carry):
@@ -128,36 +132,42 @@
                 term = jnp.exp2(exponent)
                 total = term if total is None else total + term
             high = total.astype(jnp.bfloat16)
-            high_tile[:, part] = high
-            low_tile[:, part] = (total - high.astype(jnp.float32)).astype(jnp.bfloat16)
+            high_tile[buffer, :, part] = high
+            low_tile[buffer, :, part] = (total - high.astype(jnp.float32)).astype(jnp.bfloat16)
             return carry
 
         lax.fori_loop(0, TILE // HALF, step, 0)
-        for copy in copies(slot):
+        for copy in copies(slot, buffer):
             copy.start()
-        slot_vec[slot] = tile[48:56, :]
+        if last:
+            rows_out[slot] = tile[48:56, :]
+        else:
+            rows_out[table[ROW_NEAR, slot]] += multiply(
+                tile[48:56, :], high_tile[buffer], low_tile[buffer], BY_COLS
+            )
 
         @pl.when(table[CROSSING, slot] != 0)
         def _():
             col_acc[table[COL_AT, slot]] += multiply(
-                row_vec[row_at], high_tile[...], low_tile[...], BY_ROWS
+                row_vec[row_at], high_tile[buffer], low_tile[buffer], BY_ROWS
             )
 
-    def visit(slot, pending):
+    def visit(slot, formed):
         mine = table[STAGE, slot] == stage
 
         @pl.when(mine)
         def _():
-            form(slot, pending)
-
-        return jnp.where(mine, 1, pending)
-
-    pending = lax.fori_loop(0, high_ref.shape[0], visit, 0)
-
-    @pl.when(pending != 0)
-    def _():
-        for copy in copies(0):
-            copy.wait()
+            form(slot, formed)
+
+        return formed + jnp.where(mine, 1, 0)
+
+    formed = lax.fori_loop(0, high_ref.shape[0], visit, 0)
+    for back in (1, 2):
+
+        @pl.when(formed >= back)
+        def _():
+            for copy in copies(0, lax.rem(formed + back, 2)):
+                copy.wait()
 
 
 def form_stage(stage, table, prepared, row_vec, places, state, blocks):
@@ -167,7 +177,9 @@
     shapes = [
         pltpu.HBM((slots, TILE, TILE), jnp.bfloat16),
         pltpu.HBM((slots, TILE, TILE), jnp.bfloat16),
-        jax.ShapeDtypeStruct((slots, 8, TILE), jnp.float32),
+        jax.ShapeDtypeStruct(
+            (slots if stage == LAST_STAGE else row_vec.shape[0], 8, TILE), jnp.float32
+        ),
         jax.ShapeDtypeStruct((blocks, 8, TILE), jnp.float32),
     ]
     first = 3 + len(places)
@@ -184,9 +196,9 @@
         scratch_shapes=[
             pltpu.VMEM((56, TILE), jnp.float32),
             pltpu.VMEM((16, DEPTH, TILE), jnp.bfloat16),
-            pltpu.VMEM((TILE, TILE), jnp.bfloat16),
-            pltpu.VMEM((TILE, TILE), jnp.bfloat16),
-            pltpu.SemaphoreType.DMA((2,)),
+            pltpu.VMEM((2, TILE, TILE), jnp.bfloat16),
+            pltpu.VMEM((2, TILE, TILE), jnp.bfloat16),
+            pltpu.SemaphoreType.DMA((2, 2)),
         ],
         compiler_params=pltpu.CompilerParams(vmem_limit_bytes=8 << 20),
         cost_estimate=pl.CostEstimate(
@@ -196,7 +208,8 @@
     )(table, prepared, row_vec, *places, *state)
 
 
-def apply_kernel(wanted, col_at, table, high_ref, low_ref, field, acc, high, low, sems):
+def apply_kernel(wanted, col_at, table, high_ref, low_ref, field, *refs):
+    acc, high, low, sems = refs[-4:]
     slots = high_ref.shape[0]
 
     def copies(slot):
@@ -212,7 +225,7 @@
             for copy in copies(slot):
                 copy.start()
 
-    acc[...] = jnp.zeros_like(acc)
+    acc[...] = jnp.zeros_like(acc) if len(refs) == 4 else refs[0][...]
 
     def visit(slot, carry):
         @pl.when(table[wanted, slot] != 0)
@@ -221,7 +234,7 @@
                 copy.wait()
             row = table[ROW_NEAR, slot]
             col = slot if col_at is None else table[col_at, slot]
-            if wanted == LIVE:
+            if wanted != CROSSING:
                 acc[row] += multiply(field[col], high[slot], low[slot], BY_COLS)
             else:
                 acc[col] += multiply(field[row], high[slot], low[slot], BY_ROWS)
@@ -231,12 +244,12 @@
     lax.fori_loop(0, slots, visit, 0)
 
 
-def apply_tiles(wanted, col_at, name, table, high, low, field, count):
+def apply_tiles(wanted, col_at, name, table, high, low, field, count, start=()):
     vmem = pl.BlockSpec(memory_space=pltpu.VMEM)
     hbm = pl.BlockSpec(memory_space=pltpu.HBM)
     return pl.pallas_call(
         functools.partial(apply_kernel, wanted, col_at),
-        in_specs=[pl.BlockSpec(memory_space=pltpu.SMEM), hbm, hbm, vmem],
+        in_specs=[pl.BlockSpec(memory_space=pltpu.SMEM), hbm, hbm, vmem] + [vmem] * len(start),
         out_specs=vmem,
         out_shape=jax.ShapeDtypeStruct((count, 8, TILE), jnp.float32),
         scratch_shapes=[
@@ -249,7 +262,7 @@
             flops=3 * 10**9, bytes_accessed=12 << 20, transcendentals=0
         ),
         name=name,
-    )(table, in_hbm(high), in_hbm(low), field)
+    )(table, in_hbm(high), in_hbm(low), field, *start)
 
 
 def shift(value, axis, distance):
@@ -331,7 +344,9 @@
                 wait = arrival[other] + ranks[slot] - ranks[other]
                 turn = jnp.maximum(turn, jnp.where(keys[other] <= keys[slot], wait, 0))
         stage = jnp.minimum((turn + 1) // 3, LAST_STAGE)
-        out[STAGE, slot] = jnp.where(valid[0, slot] != 0, stage, -1)
+        live = valid[0, slot] != 0
+        out[STAGE, slot] = jnp.where(live, stage, -1)
+        out[LATE, slot] = jnp.where(live & (stage == LAST_STAGE), 1, 0)
 
 
 def slot_table(pairs, valid, sizes):
@@ -344,7 +359,7 @@
         kernel,
         in_specs=[smem, smem],
         out_specs=smem,
-        out_shape=jax.ShapeDtypeStruct((8, pairs.shape[1]), jnp.int32),
+        out_shape=jax.ShapeDtypeStruct((9, pairs.shape[1]), jnp.int32),
         name="slot_table",
     )(pairs, valid)
 
@@ -376,9 +391,12 @@
     places, state = [], []
     for stage, arrived in enumerate(gather_z(near)):
         places = places + arrived
+        early = state
         state = form_stage(stage, table, prepared, row_vec, places, state, blocks)
     high, low, slot_vec, col_acc = state
-    row_acc = apply_tiles(LIVE, None, "apply_first", table, high, low, slot_vec, tiles)
+    row_acc = apply_tiles(
+        LATE, None, "apply_late", table, high, low, slot_vec, tiles, (early[2],)
+    )
     first = combine(row_acc, col_acc)
 
     col_vec = spread(first, ROW)

time: 190 us -> 187 us (0.984)
  starting transfers between devices: 54.1 us -> 61.4 us
  waiting for transfers between devices: 33.9 us -> 27.6 us
  Pallas kernels: 66.1 us -> 62.3 us
    ppermute x23, starting transfers between devices: 33.6 us -> 44.4 us  [shift(): lax.ppermute(value, axis, [(i, (i + distance) % size) for i in range(size)])]
    all_to_all x2, waiting for transfers between devices: 8.45 us -> 4.39 us  [combine(): by_col = lax.all_to_all(col_acc, ROW, 0, 0, tiled=True)]
    all_to_all x2, starting transfers between devices: 11.5 us -> 8.26 us  [combine(): by_col = lax.all_to_all(col_acc, ROW, 0, 0, tiled=True)]
    pallas_call x3, Pallas kernels: 18 us -> 14.9 us  [apply_tiles(): pl.pallas_call(functools.partial(apply_kernel, wanted, col_at), in_specs=...]
where the time goes in v6:
time: 187 us; the launch traced here: 185 us
  Pallas kernels  62.3 us (33%)
  starting transfers between devices  61.4 us (33%)
  blocking collectives  28.5 us (15%)
  waiting for transfers between devices  27.6 us (15%)
  local copies, waits for them, and re-layouts  3.7 us (2%)
    ppermute x23, starting transfers between devices, shift(): lax.ppermute(value, axis, [(i, (i + distance) % size) for i in range(size)])  44.4 us
    pallas_call x5, Pallas kernels, form_stage(): pl.pallas_call(functools.partial(stage_kernel, stage, len(places)), in_sp...  40.2 us
    all_to_all x2, blocking collectives, spread(): return lax.all_to_all(copies, axes, 0, 0, tiled=True)  28.5 us
    pallas_call x3, Pallas kernels, apply_tiles(): pl.pallas_call(functools.partial(apply_kernel, wanted, col_at), in_specs=...  14.9 us
    ppermute x23, waiting for transfers between devices, shift(): lax.ppermute(value, axis, [(i, (i + distance) % size) for i in range(size)])  14.4 us
    all_to_all x1, starting transfers between devices, spread(): return lax.all_to_all(copies, axes, 0, 0, tiled=True)  8.8 us
    all_to_all x1, waiting for transfers between devices, spread(): return lax.all_to_all(copies, axes, 0, 0, tiled=True)  8.78 us
    all_to_all x2, starting transfers between devices, combine(): by_col = lax.all_to_all(col_acc, ROW, 0, 0, tiled=True)  8.26 us
  transfers between devices with their start and end apart: 26, of which 9 were waited for; matrix products, arithmetic and copies ran while one was open for 1% of the time, Pallas kernels for 29%

profile of v6, /device:TPU:0, one launch (start us, length us, event | category | flops | bytes accessed | tf_op | source)
XLA Modules:
  0.0 185.1 jit_solution(6574021417676051376)
XLA Ops:
  3.9 2.6 %collective-permute-start.2 = (f32[56,512]{1,0:T(8,128)S(1)}, f32[56,512]{1,0:T(8,128)S(1)}, u32[]{:S(2)}, u32[]{:S(2)}) collective-permute-start(f32[56,512]{1,0:T(8,128)S(1)} %get-tuple-element.48), channel_id=1, source_target_pairs={{0,24},{8,0},{16,8},{24,16},{1,25},{9,1},{17,9},{25,17},{2,26},{10... | collective-permute-start | bytes 344072 | tf_op jit(solution)/shard_map/ppermute | solution.py:270
  9.6 5.1 %prepare_rows.1.prepared_ref = bf16[8,16,512,48]{3,2,1,0:T(8,128)(2,1)S(1)} custom-call(f32[48,4096]{1,0:T(8,128)S(1)} %bitcast.68), custom_call_target="tpu_custom_call" | custom-call | flops 100000000 | bytes 8388608 | tf_op jit(solution)/shard_map/prepare_rows/pallas_call | solution.py:65
  14.8 5.9 %collective-permute-start.4 = (f32[4,56,512]{2,1,0:T(8,128)S(1)}, f32[4,56,512]{2,1,0:T(8,128)S(1)}, u32[]{:S(2)}, u32[]{:S(2)}) collective-permute-start(f32[4,56,512]{2,1,0:T(8,128)S(1)} %pad_maximum_fusion.refs_0_), channel_id=1, source_target_pairs={{0,224},{32,0},{64,32},{96,64},{128,96},{160,128},{192,160},{224,1... | collective-permute-start | bytes 1376264 | tf_op jit(solution)/shard_map/ppermute | solution.py:270
  21.7 8.0 %collective-permute-done.4.refs_2_ = f32[4,56,512]{2,1,0:T(8,128)S(1)} collective-permute-done((f32[4,56,512]{2,1,0:T(8,128)S(1)}, f32[4,56,512]{2,1,0:T(8,128)S(1)}, u32[]{:S(2)}, u32[]{:S(2)}) %collective-permute-start.4) | collective-permute-done | bytes 458784 | tf_op jit(solution)/shard_map/ppermute | solution.py:270
  29.7 3.7 %collective-permute-start.6 = (f32[4,56,512]{2,1,0:T(8,128)S(1)}, f32[4,56,512]{2,1,0:T(8,128)S(1)}, u32[]{:S(2)}, u32[]{:S(2)}) collective-permute-start(f32[4,56,512]{2,1,0:T(8,128)S(1)} %collective-permute-done.4.refs_2_), channel_id=1, source_target_pairs={{0,224},{32,0},{64,32},{96,64},{128,96},{160,128},{192,160},{224,1... | collective-permute-start | bytes 1376264 | tf_op jit(solution)/shard_map/ppermute | solution.py:270
  33.4 11.3 %form_1.1 = (bf16[10,512,512]{2,1,0:T(8,128)(2,1)}, bf16[10,512,512]{2,1,0:T(8,128)(2,1)}, f32[8,8,512]{2,1,0:T(8,128)S(1)}, f32[32,8,512]{2,1,0:T(8,128)S(1)}) custom-call(s32[9,10]{1,0:T(8,128)S(1)} %copy-done.2, bf16[8,16,512,48]{3,2,1,0:T(8,128)(2,1)S(1)} %prepare_rows.1.prepared_ref, ...), custom_call_target="tpu_custom_call", output_to_operand_aliasing={{0}: (6, {}), {1}: (7, {}), {2}: (8, {}), {3}: (9, {})} | custom-call | flops 8000000000 | bytes 8388608 | tf_op jit(solution)/shard_map/form_1/pallas_call | solution.py:186
  44.8 3.4 %collective-permute-start.8 = (f32[4,56,512]{2,1,0:T(8,128)S(1)}, f32[4,56,512]{2,1,0:T(8,128)S(1)}, u32[]{:S(2)}, u32[]{:S(2)}) collective-permute-start(f32[4,56,512]{2,1,0:T(8,128)S(1)} %collective-permute-done.6.refs_4_), channel_id=1, source_target_pairs={{0,224},{32,0},{64,32},{96,64},{128,96},{160,128},{192,160},{224,1... | collective-permute-start | bytes 1376264 | tf_op jit(solution)/shard_map/ppermute | solution.py:270
  48.2 8.0 %form_2.1 = (bf16[10,512,512]{2,1,0:T(8,128)(2,1)}, bf16[10,512,512]{2,1,0:T(8,128)(2,1)}, f32[8,8,512]{2,1,0:T(8,128)S(1)}, f32[32,8,512]{2,1,0:T(8,128)S(1)}) custom-call(s32[9,10]{1,0:T(8,128)S(1)} %copy-done.2, bf16[8,16,512,48]{3,2,1,0:T(8,128)(2,1)S(1)} %prepare_rows.1.prepared_ref, ...), custom_call_target="tpu_custom_call", output_to_operand_aliasing={{0}: (8, {}), {1}: (9, {}), {2}: (10, {}), {3}: (11, {})} | custom-call | flops 8000000000 | bytes 8388608 | tf_op jit(solution)/shard_map/form_2/pallas_call | solution.py:186
  56.2 6.8 %collective-permute-start.10 = (f32[2,56,512]{2,1,0:T(8,128)S(1)}, f32[2,56,512]{2,1,0:T(8,128)S(1)}, u32[]{:S(2)}, u32[]{:S(2)}) collective-permute-start(f32[2,56,512]{2,1,0:T(8,128)S(1)} %slice.61), channel_id=1, source_target_pairs={{0,224},{32,0},{64,32},{96,64},{128,96},{160,128},{192,160},{224,1... | collective-permute-start | bytes 688136 | tf_op jit(solution)/shard_map/ppermute | solution.py:270
  63.1 11.4 %form_3.1 = (bf16[10,512,512]{2,1,0:T(8,128)(2,1)}, bf16[10,512,512]{2,1,0:T(8,128)(2,1)}, f32[8,8,512]{2,1,0:T(8,128)S(1)}, f32[32,8,512]{2,1,0:T(8,128)S(1)}) custom-call(s32[9,10]{1,0:T(8,128)S(1)} %copy-done.2, ...), custom_call_target="tpu_custom_call", output_to_operand_aliasing={{0}: (10, {}), {1}: (11, {}), {2}: (12, {}), {3}: (13, {})} | custom-call | flops 8000000000 | bytes 8388608 | tf_op jit(solution)/shard_map/form_3/pallas_call | solution.py:186
  74.5 8.5 %form_4.1 = (bf16[10,512,512]{2,1,0:T(8,128)(2,1)}, bf16[10,512,512]{2,1,0:T(8,128)(2,1)}, f32[10,8,512]{2,1,0:T(8,128)S(1)}, f32[32,8,512]{2,1,0:T(8,128)}) custom-call(s32[9,10]{1,0:T(8,128)S(1)} %copy-done.2, bf16[8,16,512,48]{3,2,1,0:T(8,128)(2,1)S(1)} %prepare_rows.1.prepared_ref, ...), custom_call_target="tpu_custom_call", output_to_operand_aliasing={{0}: (12, {}), {1}: (13, {})} | custom-call | flops 8000000000 | bytes 8388608 | tf_op jit(solution)/shard_map/form_4/pallas_call | solution.py:186
  83.1 3.9 %all-to-all-start = ((f32[32,8,512]{2,1,0:T(8,128)}), f32[32,8,512]{2,1,0:T(8,128)S(1)}, u32[]{:S(2)}, u32[]{:S(2)}) async-start(f32[32,8,512]{2,1,0:T(8,128)} %get-tuple-element.44), calls=%async_computation | async-start | bytes 1048576 | tf_op jit(solution)/shard_map/all_to_all | solution.py:368
  87.0 2.9 %apply_late.1 = f32[8,8,512]{2,1,0:T(8,128)S(1)} custom-call(s32[9,10]{1,0:T(8,128)S(1)} %copy-done.2, bf16[10,512,512]{2,1,0:T(8,128)(2,1)} %get-tuple-element.41.high_ref, bf16[10,512,512]{2,1,0:T(8,128)(2,1)} %get-tuple-element.42.low_ref, f32[10,8,512]{2,1,0:T(8,128)S(1)} %get-tuple-element.43.field, f32[8,8,512]{2,1,0:T(8,128)S(1)} %get-tuple-element.39.refs_11_.refs_0_), custom_call_target="tpu_custom_call" | custom-call | flops 3000000000 | bytes 12582912 | tf_op jit(solution)/shard_map/apply_late/pallas_call | solution.py:250
  91.2 8.1 %collective-permute-start.12 = (f32[8,512]{1,0:T(8,128)S(1)}, f32[8,512]{1,0:T(8,128)S(1)}, u32[]{:S(2)}, u32[]{:S(2)}) collective-permute-start(f32[8,512]{1,0:T(8,128)S(1)} %get-tuple-element.52), channel_id=1, source_target_pairs={{0,6},{2,0},{4,2},{6,4},{1,7},{3,1},{5,3},{7,5},{8,14},{10,8},{12,... | collective-permute-start | bytes 49160 | tf_op jit(solution)/shard_map/ppermute | solution.py:270
  101.9 2.4 %collective-permute-done.14 = f32[8,512]{1,0:T(8,128)S(1)} collective-permute-done((f32[8,512]{1,0:T(8,128)S(1)}, f32[8,512]{1,0:T(8,128)S(1)}, u32[]{:S(2)}, u32[]{:S(2)}) %collective-permute-start.14) | collective-permute-done | bytes 16416 | tf_op jit(solution)/shard_map/ppermute | solution.py:270
  104.6 4.4 %collective-permute-start.21 = (f32[8,512]{1,0:T(8,128)S(1)}, f32[8,512]{1,0:T(8,128)S(1)}, u32[]{:S(2)}, u32[]{:S(2)}) collective-permute-start(f32[8,512]{1,0:T(8,128)S(1)} %get-tuple-element.46), channel_id=1, source_target_pairs={{0,6},{2,0},{4,2},{6,4},{1,7},{3,1},{5,3},{7,5},{8,14},{10,8},{12,... | collective-permute-start | bytes 49160 | tf_op jit(solution)/shard_map/ppermute | solution.py:270
  110.8 8.8 %all-to-all-start.1 = ((f32[32,8,512]{2,1,0:T(8,128)}), f32[32,8,512]{2,1,0:T(8,128)S(1)}, u32[]{:S(2)}, u32[]{:S(2)}) async-start(f32[32,8,512]{2,1,0:T(8,128)} %broadcast_in_dim.13), calls=%async_computation.1 | async-start | bytes 1048576 | tf_op jit(solution)/shard_map/all_to_all | solution.py:275
  121.0 5.9 %apply_cols.1 = f32[32,8,512]{2,1,0:T(8,128)} custom-call(s32[9,10]{1,0:T(8,128)S(1)} %copy-done.2, bf16[10,512,512]{2,1,0:T(8,128)(2,1)} %get-tuple-element.41.high_ref, bf16[10,512,512]{2,1,0:T(8,128)(2,1)} %get-tuple-element.42.low_ref, f32[8,8,512]{2,1,0:T(8,128)S(1)} %constant_dynamic-update-slice_fusion.field), custom_call_target="tpu_custom_call" | custom-call | flops 3000000000 | bytes 12582912 | tf_op jit(solution)/shard_map/apply_cols/pallas_call | solution.py:250
  127.0 8.8 %all-to-all-done.1.field = f32[32,8,512]{2,1,0:T(8,128)S(1)} async-done(((f32[32,8,512]{2,1,0:T(8,128)}), f32[32,8,512]{2,1,0:T(8,128)S(1)}, u32[]{:S(2)}, u32[]{:S(2)}) %all-to-all-start.1) | async-done | bytes 524320 | tf_op jit(solution)/shard_map/all_to_all | solution.py:275
  135.7 4.4 %all-to-all-start.2 = ((f32[32,8,512]{2,1,0:T(8,128)}), f32[32,8,512]{2,1,0:T(8,128)S(1)}, u32[]{:S(2)}, u32[]{:S(2)}) async-start(f32[32,8,512]{2,1,0:T(8,128)} %apply_cols.1), calls=%async_computation.2 | async-start | bytes 1048576 | tf_op jit(solution)/shard_map/all_to_all | solution.py:368
  140.1 6.1 %apply_rows.1 = f32[8,8,512]{2,1,0:T(8,128)S(1)} custom-call(s32[9,10]{1,0:T(8,128)S(1)} %copy-done.2, bf16[10,512,512]{2,1,0:T(8,128)(2,1)} %get-tuple-element.41.high_ref, bf16[10,512,512]{2,1,0:T(8,128)(2,1)} %get-tuple-element.42.low_ref, f32[32,8,512]{2,1,0:T(8,128)S(1)} %all-to-all-done.1.field), custom_call_target="tpu_custom_call" | custom-call | flops 3000000000 | bytes 12582912 | tf_op jit(solution)/shard_map/apply_rows/pallas_call | solution.py:250
  152.0 3.5 %all-to-all-done.2 = f32[32,8,512]{2,1,0:T(8,128)S(1)} async-done(((f32[32,8,512]{2,1,0:T(8,128)}), f32[32,8,512]{2,1,0:T(8,128)S(1)}, u32[]{:S(2)}, u32[]{:S(2)}) %all-to-all-start.2) | async-done | bytes 524320 | tf_op jit(solution)/shard_map/all_to_all | solution.py:368
  155.6 9.8 %all_to_all.25 = f32[8,8,512]{2,1,0:T(8,128)S(1)} all-to-all(f32[8,8,512]{2,1,0:T(8,128)S(1)} %broadcast_in_dim.14), channel_id=1, replica_groups=mesh['z'=8,'y'=4,'x'=4,'core'=2] {'x','core'}, dimensions={0} | all-to-all | bytes 262144 | tf_op jit(solution)/shard_map/all_to_all | solution.py:275
  165.6 18.7 %all_to_all.26 = f32[32,1,128]{2,1,0:T(1,128)S(1)} all-to-all(f32[32,1,128]{2,1,0:T(1,128)S(1)} %broadcast_in_dim.16), channel_id=1, replica_groups=mesh['z'=8,'y'=4,'x'=4,'core'=2] {'z','y'}, dimensions={0} | all-to-all | bytes 32768 | tf_op jit(solution)/shard_map/all_to_all | solution.py:275
  (75 shorter events, 22.3 us)
Async XLA Ops:
  1.6 13.1 %collective-permute-start.1 = (f32[56,512]{1,0:T(8,128)S(1)}, f32[56,512]{1,0:T(8,128)S(1)}, u32[]{:S(2)}, u32[]{:S(2)}) collective-permute-start(f32[56,512]{1,0:T(8,128)S(1)} %get-tuple-element.48), channel_id=1, source_target_pairs={{0,16},{8,24},{16,0},{24,8},{1,17},{9,25},{17,1},{25,9},{2,18},{10... | collective-permute-start | bytes 344072 | tf_op jit(solution)/shard_map/ppermute | solution.py:270
  3.2 11.6 %collective-permute-start = (f32[56,512]{1,0:T(8,128)S(1)}, f32[56,512]{1,0:T(8,128)S(1)}, u32[]{:S(2)}, u32[]{:S(2)}) collective-permute-start(f32[56,512]{1,0:T(8,128)S(1)} %get-tuple-element.48), channel_id=1, source_target_pairs={{0,8},{8,16},{16,24},{24,0},{1,9},{9,17},{17,25},{25,1},{2,10},{10... | collective-permute-start | bytes 344072 | tf_op jit(solution)/shard_map/ppermute | solution.py:270
  3.9 10.9 %collective-permute-start.2 = (f32[56,512]{1,0:T(8,128)S(1)}, f32[56,512]{1,0:T(8,128)S(1)}, u32[]{:S(2)}, u32[]{:S(2)}) collective-permute-start(f32[56,512]{1,0:T(8,128)S(1)} %get-tuple-element.48), channel_id=1, source_target_pairs={{0,24},{8,0},{16,8},{24,16},{1,25},{9,1},{17,9},{25,17},{2,26},{10... | collective-permute-start | bytes 344072 | tf_op jit(solution)/shard_map/ppermute | solution.py:270
  14.8 14.9 %collective-permute-start.4 = (f32[4,56,512]{2,1,0:T(8,128)S(1)}, f32[4,56,512]{2,1,0:T(8,128)S(1)}, u32[]{:S(2)}, u32[]{:S(2)}) collective-permute-start(f32[4,56,512]{2,1,0:T(8,128)S(1)} %pad_maximum_fusion.refs_0_), channel_id=1, source_target_pairs={{0,224},{32,0},{64,32},{96,64},{128,96},{160,128},{192,160},{224,1... | collective-permute-start | bytes 1376264 | tf_op jit(solution)/shard_map/ppermute | solution.py:270
  20.8 12.6 %collective-permute-start.3 = (f32[4,56,512]{2,1,0:T(8,128)S(1)}, f32[4,56,512]{2,1,0:T(8,128)S(1)}, u32[]{:S(2)}, u32[]{:S(2)}) collective-permute-start(f32[4,56,512]{2,1,0:T(8,128)S(1)} %pad_maximum_fusion.refs_0_), channel_id=1, source_target_pairs={{0,32},{32,64},{64,96},{96,128},{128,160},{160,192},{192,224},{224... | collective-permute-start | bytes 1376264 | tf_op jit(solution)/shard_map/ppermute | solution.py:270
  29.7 15.0 %collective-permute-start.6 = (f32[4,56,512]{2,1,0:T(8,128)S(1)}, f32[4,56,512]{2,1,0:T(8,128)S(1)}, u32[]{:S(2)}, u32[]{:S(2)}) collective-permute-start(f32[4,56,512]{2,1,0:T(8,128)S(1)} %collective-permute-done.4.refs_2_), channel_id=1, source_target_pairs={{0,224},{32,0},{64,32},{96,64},{128,96},{160,128},{192,160},{224,1... | collective-permute-start | bytes 1376264 | tf_op jit(solution)/shard_map/ppermute | solution.py:270
  33.4 14.8 %collective-permute-start.5 = (f32[4,56,512]{2,1,0:T(8,128)S(1)}, f32[4,56,512]{2,1,0:T(8,128)S(1)}, u32[]{:S(2)}, u32[]{:S(2)}) collective-permute-start(f32[4,56,512]{2,1,0:T(8,128)S(1)} %collective-permute-done.3.refs_1_), channel_id=1, source_target_pairs={{0,32},{32,64},{64,96},{96,128},{128,160},{160,192},{192,224},{224... | collective-permute-start | bytes 1376264 | tf_op jit(solution)/shard_map/ppermute | solution.py:270
  44.8 11.4 %collective-permute-start.8 = (f32[4,56,512]{2,1,0:T(8,128)S(1)}, f32[4,56,512]{2,1,0:T(8,128)S(1)}, u32[]{:S(2)}, u32[]{:S(2)}) collective-permute-start(f32[4,56,512]{2,1,0:T(8,128)S(1)} %collective-permute-done.6.refs_4_), channel_id=1, source_target_pairs={{0,224},{32,0},{64,32},{96,64},{128,96},{160,128},{192,160},{224,1... | collective-permute-start | bytes 1376264 | tf_op jit(solution)/shard_map/ppermute | solution.py:270
  48.2 14.8 %collective-permute-start.7 = (f32[4,56,512]{2,1,0:T(8,128)S(1)}, f32[4,56,512]{2,1,0:T(8,128)S(1)}, u32[]{:S(2)}, u32[]{:S(2)}) collective-permute-start(f32[4,56,512]{2,1,0:T(8,128)S(1)} %collective-permute-done.5.refs_3_), channel_id=1, source_target_pairs={{0,32},{32,64},{64,96},{96,128},{128,160},{160,192},{192,224},{224... | collective-permute-start | bytes 1376264 | tf_op jit(solution)/shard_map/ppermute | solution.py:270
  56.2 18.3 %collective-permute-start.10 = (f32[2,56,512]{2,1,0:T(8,128)S(1)}, f32[2,56,512]{2,1,0:T(8,128)S(1)}, u32[]{:S(2)}, u32[]{:S(2)}) collective-permute-start(f32[2,56,512]{2,1,0:T(8,128)S(1)} %slice.61), channel_id=1, source_target_pairs={{0,224},{32,0},{64,32},{96,64},{128,96},{160,128},{192,160},{224,1... | collective-permute-start | bytes 688136 | tf_op jit(solution)/shard_map/ppermute | solution.py:270
  63.0 11.5 %collective-permute-start.9 = (f32[2,56,512]{2,1,0:T(8,128)S(1)}, f32[2,56,512]{2,1,0:T(8,128)S(1)}, u32[]{:S(2)}, u32[]{:S(2)}) collective-permute-start(f32[2,56,512]{2,1,0:T(8,128)S(1)} %slice.60), channel_id=1, source_target_pairs={{0,32},{32,64},{64,96},{96,128},{128,160},{160,192},{192,224},{224... | collective-permute-start | bytes 688136 | tf_op jit(solution)/shard_map/ppermute | solution.py:270
  83.1 18.8 %all-to-all-start = ((f32[32,8,512]{2,1,0:T(8,128)}), f32[32,8,512]{2,1,0:T(8,128)S(1)}, u32[]{:S(2)}, u32[]{:S(2)}) async-start(f32[32,8,512]{2,1,0:T(8,128)} %get-tuple-element.44), calls=%async_computation | async-start | bytes 1048576 | tf_op jit(solution)/shard_map/all_to_all | solution.py:368
  89.9 1.3 collective-permute-start.11
  91.2 10.7 %collective-permute-start.12 = (f32[8,512]{1,0:T(8,128)S(1)}, f32[8,512]{1,0:T(8,128)S(1)}, u32[]{:S(2)}, u32[]{:S(2)}) collective-permute-start(f32[8,512]{1,0:T(8,128)S(1)} %get-tuple-element.52), channel_id=1, source_target_pairs={{0,6},{2,0},{4,2},{6,4},{1,7},{3,1},{5,3},{7,5},{8,14},{10,8},{12,... | collective-permute-start | bytes 49160 | tf_op jit(solution)/shard_map/ppermute | solution.py:270
  99.4 4.9 %collective-permute-start.14 = (f32[8,512]{1,0:T(8,128)S(1)}, f32[8,512]{1,0:T(8,128)S(1)}, u32[]{:S(2)}, u32[]{:S(2)}) collective-permute-start(f32[8,512]{1,0:T(8,128)S(1)} %get-tuple-element.53), channel_id=1, source_target_pairs={{0,2},{2,4},{4,6},{6,0},{1,3},{3,5},{5,7},{7,1},{8,10},{10,12},{12... | collective-permute-start | bytes 49160 | tf_op jit(solution)/shard_map/ppermute | solution.py:270
  99.4 5.2 %collective-permute-start.13 = (f32[8,512]{1,0:T(8,128)S(1)}, f32[8,512]{1,0:T(8,128)S(1)}, u32[]{:S(2)}, u32[]{:S(2)}) collective-permute-start(f32[8,512]{1,0:T(8,128)S(1)} %get-tuple-element.54), channel_id=1, source_target_pairs={{0,4},{2,6},{4,0},{6,2},{1,5},{3,7},{5,1},{7,3},{8,12},{10,14},{12... | collective-permute-start | bytes 49160 | tf_op jit(solution)/shard_map/ppermute | solution.py:270
  104.6 15.0 %collective-permute-start.21 = (f32[8,512]{1,0:T(8,128)S(1)}, f32[8,512]{1,0:T(8,128)S(1)}, u32[]{:S(2)}, u32[]{:S(2)}) collective-permute-start(f32[8,512]{1,0:T(8,128)S(1)} %get-tuple-element.46), channel_id=1, source_target_pairs={{0,6},{2,0},{4,2},{6,4},{1,7},{3,1},{5,3},{7,5},{8,14},{10,8},{12,... | collective-permute-start | bytes 49160 | tf_op jit(solution)/shard_map/ppermute | solution.py:270
  109.0 10.6 %collective-permute-start.20 = (f32[8,512]{1,0:T(8,128)S(1)}, f32[8,512]{1,0:T(8,128)S(1)}, u32[]{:S(2)}, u32[]{:S(2)}) collective-permute-start(f32[8,512]{1,0:T(8,128)S(1)} %get-tuple-element.46), channel_id=1, source_target_pairs={{0,4},{2,6},{4,0},{6,2},{1,5},{3,7},{5,1},{7,3},{8,12},{10,14},{12... | collective-permute-start | bytes 49160 | tf_op jit(solution)/shard_map/ppermute | solution.py:270
  109.0 10.6 %collective-permute-start.19 = (f32[8,512]{1,0:T(8,128)S(1)}, f32[8,512]{1,0:T(8,128)S(1)}, u32[]{:S(2)}, u32[]{:S(2)}) collective-permute-start(f32[8,512]{1,0:T(8,128)S(1)} %get-tuple-element.46), channel_id=1, source_target_pairs={{0,2},{2,4},{4,6},{6,0},{1,3},{3,5},{5,7},{7,1},{8,10},{10,12},{12... | collective-permute-start | bytes 49160 | tf_op jit(solution)/shard_map/ppermute | solution.py:270
  110.8 24.9 %all-to-all-start.1 = ((f32[32,8,512]{2,1,0:T(8,128)}), f32[32,8,512]{2,1,0:T(8,128)S(1)}, u32[]{:S(2)}, u32[]{:S(2)}) async-start(f32[32,8,512]{2,1,0:T(8,128)} %broadcast_in_dim.13), calls=%async_computation.1 | async-start | bytes 1048576 | tf_op jit(solution)/shard_map/all_to_all | solution.py:275
  135.7 19.8 %all-to-all-start.2 = ((f32[32,8,512]{2,1,0:T(8,128)}), f32[32,8,512]{2,1,0:T(8,128)S(1)}, u32[]{:S(2)}, u32[]{:S(2)}) async-start(f32[32,8,512]{2,1,0:T(8,128)} %apply_cols.1), calls=%async_computation.2 | async-start | bytes 1048576 | tf_op jit(solution)/shard_map/all_to_all | solution.py:368
  147.6 7.9 %collective-permute-start.16 = (f32[8,512]{1,0:T(8,128)S(1)}, f32[8,512]{1,0:T(8,128)S(1)}, u32[]{:S(2)}, u32[]{:S(2)}) collective-permute-start(f32[8,512]{1,0:T(8,128)S(1)} %get-tuple-element.49), channel_id=1, source_target_pairs={{0,6},{2,0},{4,2},{6,4},{1,7},{3,1},{5,3},{7,5},{8,14},{10,8},{12,... | collective-permute-start | bytes 49160 | tf_op jit(solution)/shard_map/ppermute | solution.py:270
  149.2 6.4 %collective-permute-start.18 = (f32[8,512]{1,0:T(8,128)S(1)}, f32[8,512]{1,0:T(8,128)S(1)}, u32[]{:S(2)}, u32[]{:S(2)}) collective-permute-start(f32[8,512]{1,0:T(8,128)S(1)} %get-tuple-element.50), channel_id=1, source_target_pairs={{0,2},{2,4},{4,6},{6,0},{1,3},{3,5},{5,7},{7,1},{8,10},{10,12},{12... | collective-permute-start | bytes 49160 | tf_op jit(solution)/shard_map/ppermute | solution.py:270
  150.1 5.5 %collective-permute-start.17 = (f32[8,512]{1,0:T(8,128)S(1)}, f32[8,512]{1,0:T(8,128)S(1)}, u32[]{:S(2)}, u32[]{:S(2)}) collective-permute-start(f32[8,512]{1,0:T(8,128)S(1)} %get-tuple-element.51), channel_id=1, source_target_pairs={{0,4},{2,6},{4,0},{6,2},{1,5},{3,7},{5,1},{7,3},{8,12},{10,14},{12... | collective-permute-start | bytes 49160 | tf_op jit(solution)/shard_map/ppermute | solution.py:270
  (5 other events, 26.1 us)

commit v7 on v6

--- a/solution.py
+++ b/solution.py
@@ -14,6 +14,7 @@
 COL = ("x", "core")
 ROW_AT, ROW_NEAR, COL_AT, SOURCE, PLACE, STAGE, LIVE, CROSSING, LATE = range(9)
 LAST_STAGE = 4
+PER_STAGE = 2
 BY_ROWS = (((1,), (0,)), ((), ()))
 BY_COLS = (((1,), (1,)), ((), ()))
 LOG2E = math.log2(math.e)
@@ -332,7 +333,7 @@
         out[LIVE, slot] = jnp.where(live, 1, 0)
         out[CROSSING, slot] = jnp.where(live & crossing, 1, 0)
         stage = jnp.where(live, (source + 1) // 2, LAST_STAGE)
-        arrival.append(jnp.maximum(3 * stage - 1, 0))
+        arrival.append(PER_STAGE * stage)
         keys.append(stage * slots + slot)
     ranks = [
         sum(jnp.where(other <= key, 1, 0) for other in keys) for key in keys
@@ -343,7 +344,7 @@
             if other != slot:
                 wait = arrival[other] + ranks[slot] - ranks[other]
                 turn = jnp.maximum(turn, jnp.where(keys[other] <= keys[slot], wait, 0))
-        stage = jnp.minimum((turn + 1) // 3, LAST_STAGE)
+        stage = jnp.minimum(turn // PER_STAGE, LAST_STAGE)
         live = valid[0, slot] != 0
         out[STAGE, slot] = jnp.where(live, stage, -1)
         out[LATE, slot] = jnp.where(live & (stage == LAST_STAGE), 1, 0)

time: 187 us -> 182 us (0.973)
  Pallas kernels: 62.3 us -> 49.9 us
  waiting for transfers between devices: 27.6 us -> 33.5 us
    pallas_call x5, Pallas kernels: 40.2 us -> 30 us  [form_stage(): pl.pallas_call(functools.partial(stage_kernel, stage, len(places)), in_sp...]
    all_to_all x2, starting transfers between devices: 8.26 us -> 15 us  [combine(): by_col = lax.all_to_all(col_acc, ROW, 0, 0, tiled=True)]
    all_to_all x2, waiting for transfers between devices: 4.39 us -> 9.82 us  [combine(): by_col = lax.all_to_all(col_acc, ROW, 0, 0, tiled=True)]
    ppermute x23, starting transfers between devices: 44.4 us -> 39.2 us  [shift(): lax.ppermute(value, axis, [(i, (i + distance) % size) for i in range(size)])]
    pallas_call x3, Pallas kernels: 14.9 us -> 12.8 us  [apply_tiles(): pl.pallas_call(functools.partial(apply_kernel, wanted, col_at), in_specs=...]
  transfers between devices with their start and end apart: 26 -> 26, of which waited for: 9 -> 8; matrix products, arithmetic and copies ran while one was open for 1% -> 1% of each run, Pallas kernels for 29% -> 23%
where the time goes in v7:
time: 182 us; the launch traced here: 179 us
  starting transfers between devices  61.5 us (34%)
  Pallas kernels  49.9 us (27%)
  waiting for transfers between devices  33.5 us (18%)
  blocking collectives  28.7 us (16%)
  local copies, waits for them, and re-layouts  3.7 us (2%)
    ppermute x23, starting transfers between devices, shift(): lax.ppermute(value, axis, [(i, (i + distance) % size) for i in range(size)])  39.2 us
    pallas_call x5, Pallas kernels, form_stage(): pl.pallas_call(functools.partial(stage_kernel, stage, len(places)), in_sp...  30 us
    all_to_all x2, blocking collectives, spread(): return lax.all_to_all(copies, axes, 0, 0, tiled=True)  28.7 us
    all_to_all x2, starting transfers between devices, combine(): by_col = lax.all_to_all(col_acc, ROW, 0, 0, tiled=True)  15 us
    ppermute x23, waiting for transfers between devices, shift(): lax.ppermute(value, axis, [(i, (i + distance) % size) for i in range(size)])  14 us
    pallas_call x3, Pallas kernels, apply_tiles(): pl.pallas_call(functools.partial(apply_kernel, wanted, col_at), in_specs=...  12.8 us
    all_to_all x2, waiting for transfers between devices, combine(): by_col = lax.all_to_all(col_acc, ROW, 0, 0, tiled=True)  9.82 us
    all_to_all x1, waiting for transfers between devices, spread(): return lax.all_to_all(copies, axes, 0, 0, tiled=True)  9.67 us
  transfers between devices with their start and end apart: 26, of which 8 were waited for; matrix products, arithmetic and copies ran while one was open for 1% of the time, Pallas kernels for 23%

profile of v7, /device:TPU:0, one launch (start us, length us, event | category | flops | bytes accessed | tf_op | source)
XLA Modules:
  0.0 178.8 jit_solution(7236665922824527716)
XLA Ops:
  9.6 5.1 %prepare_rows.1.prepared_ref = bf16[8,16,512,48]{3,2,1,0:T(8,128)(2,1)S(1)} custom-call(f32[48,4096]{1,0:T(8,128)S(1)} %bitcast.68), custom_call_target="tpu_custom_call" | custom-call | flops 100000000 | bytes 8388608 | tf_op jit(solution)/shard_map/prepare_rows/pallas_call | solution.py:66
  14.8 5.9 %collective-permute-start.4 = (f32[4,56,512]{2,1,0:T(8,128)S(1)}, f32[4,56,512]{2,1,0:T(8,128)S(1)}, u32[]{:S(2)}, u32[]{:S(2)}) collective-permute-start(f32[4,56,512]{2,1,0:T(8,128)S(1)} %pad_maximum_fusion.refs_0_), channel_id=1, source_target_pairs={{0,224},{32,0},{64,32},{96,64},{128,96},{160,128},{192,160},{224,1... | collective-permute-start | bytes 1376264 | tf_op jit(solution)/shard_map/ppermute | solution.py:271
  21.7 8.0 %collective-permute-done.4.refs_2_ = f32[4,56,512]{2,1,0:T(8,128)S(1)} collective-permute-done((f32[4,56,512]{2,1,0:T(8,128)S(1)}, f32[4,56,512]{2,1,0:T(8,128)S(1)}, u32[]{:S(2)}, u32[]{:S(2)}) %collective-permute-start.4) | collective-permute-done | bytes 458784 | tf_op jit(solution)/shard_map/ppermute | solution.py:271
  29.7 3.7 %collective-permute-start.6 = (f32[4,56,512]{2,1,0:T(8,128)S(1)}, f32[4,56,512]{2,1,0:T(8,128)S(1)}, u32[]{:S(2)}, u32[]{:S(2)}) collective-permute-start(f32[4,56,512]{2,1,0:T(8,128)S(1)} %collective-permute-done.4.refs_2_), channel_id=1, source_target_pairs={{0,224},{32,0},{64,32},{96,64},{128,96},{160,128},{192,160},{224,1... | collective-permute-start | bytes 1376264 | tf_op jit(solution)/shard_map/ppermute | solution.py:271
  33.4 8.1 %form_1.1 = (bf16[10,512,512]{2,1,0:T(8,128)(2,1)}, bf16[10,512,512]{2,1,0:T(8,128)(2,1)}, f32[8,8,512]{2,1,0:T(8,128)S(1)}, f32[32,8,512]{2,1,0:T(8,128)S(1)}) custom-call(s32[9,10]{1,0:T(8,128)S(1)} %copy-done.2, bf16[8,16,512,48]{3,2,1,0:T(8,128)(2,1)S(1)} %prepare_rows.1.prepared_ref, ...), custom_call_target="tpu_custom_call", output_to_operand_aliasing={{0}: (6, {}), {1}: (7, {}), {2}: (8, {}), {3}: (9, {})} | custom-call | flops 8000000000 | bytes 8388608 | tf_op jit(solution)/shard_map/form_1/pallas_call | solution.py:187
  41.5 3.6 %collective-permute-start.8 = (f32[4,56,512]{2,1,0:T(8,128)S(1)}, f32[4,56,512]{2,1,0:T(8,128)S(1)}, u32[]{:S(2)}, u32[]{:S(2)}) collective-permute-start(f32[4,56,512]{2,1,0:T(8,128)S(1)} %collective-permute-done.6.refs_4_), channel_id=1, source_target_pairs={{0,224},{32,0},{64,32},{96,64},{128,96},{160,128},{192,160},{224,1... | collective-permute-start | bytes 1376264 | tf_op jit(solution)/shard_map/ppermute | solution.py:271
  45.1 7.9 %form_2.1 = (bf16[10,512,512]{2,1,0:T(8,128)(2,1)}, bf16[10,512,512]{2,1,0:T(8,128)(2,1)}, f32[8,8,512]{2,1,0:T(8,128)S(1)}, f32[32,8,512]{2,1,0:T(8,128)S(1)}) custom-call(s32[9,10]{1,0:T(8,128)S(1)} %copy-done.2, bf16[8,16,512,48]{3,2,1,0:T(8,128)(2,1)S(1)} %prepare_rows.1.prepared_ref, ...), custom_call_target="tpu_custom_call", output_to_operand_aliasing={{0}: (8, {}), {1}: (9, {}), {2}: (10, {}), {3}: (11, {})} | custom-call | flops 8000000000 | bytes 8388608 | tf_op jit(solution)/shard_map/form_2/pallas_call | solution.py:187
  53.1 3.5 %collective-permute-start.10 = (f32[2,56,512]{2,1,0:T(8,128)S(1)}, f32[2,56,512]{2,1,0:T(8,128)S(1)}, u32[]{:S(2)}, u32[]{:S(2)}) collective-permute-start(f32[2,56,512]{2,1,0:T(8,128)S(1)} %slice.61), channel_id=1, source_target_pairs={{0,224},{32,0},{64,32},{96,64},{128,96},{160,128},{192,160},{224,1... | collective-permute-start | bytes 688136 | tf_op jit(solution)/shard_map/ppermute | solution.py:271
  56.6 4.6 %form_3.1 = (bf16[10,512,512]{2,1,0:T(8,128)(2,1)}, bf16[10,512,512]{2,1,0:T(8,128)(2,1)}, f32[8,8,512]{2,1,0:T(8,128)S(1)}, f32[32,8,512]{2,1,0:T(8,128)S(1)}) custom-call(s32[9,10]{1,0:T(8,128)S(1)} %copy-done.2, ...), custom_call_target="tpu_custom_call", output_to_operand_aliasing={{0}: (10, {}), {1}: (11, {}), {2}: (12, {}), {3}: (13, {})} | custom-call | flops 8000000000 | bytes 8388608 | tf_op jit(solution)/shard_map/form_3/pallas_call | solution.py:187
  63.8 8.4 %form_4.1 = (bf16[10,512,512]{2,1,0:T(8,128)(2,1)}, bf16[10,512,512]{2,1,0:T(8,128)(2,1)}, f32[10,8,512]{2,1,0:T(8,128)S(1)}, f32[32,8,512]{2,1,0:T(8,128)}) custom-call(s32[9,10]{1,0:T(8,128)S(1)} %copy-done.2, bf16[8,16,512,48]{3,2,1,0:T(8,128)(2,1)S(1)} %prepare_rows.1.prepared_ref, ...), custom_call_target="tpu_custom_call", output_to_operand_aliasing={{0}: (12, {}), {1}: (13, {})} | custom-call | flops 8000000000 | bytes 8388608 | tf_op jit(solution)/shard_map/form_4/pallas_call | solution.py:187
  72.3 10.7 %all-to-all-start = ((f32[32,8,512]{2,1,0:T(8,128)}), f32[32,8,512]{2,1,0:T(8,128)S(1)}, u32[]{:S(2)}, u32[]{:S(2)}) async-start(f32[32,8,512]{2,1,0:T(8,128)} %get-tuple-element.44), calls=%async_computation | async-start | bytes 1048576 | tf_op jit(solution)/shard_map/all_to_all | solution.py:369
  83.0 2.9 %apply_late.1 = f32[8,8,512]{2,1,0:T(8,128)S(1)} custom-call(s32[9,10]{1,0:T(8,128)S(1)} %copy-done.2, bf16[10,512,512]{2,1,0:T(8,128)(2,1)} %get-tuple-element.41.high_ref, bf16[10,512,512]{2,1,0:T(8,128)(2,1)} %get-tuple-element.42.low_ref, f32[10,8,512]{2,1,0:T(8,128)S(1)} %get-tuple-element.43.field, f32[8,8,512]{2,1,0:T(8,128)S(1)} %get-tuple-element.39.refs_11_.refs_0_), custom_call_target="tpu_custom_call" | custom-call | flops 3000000000 | bytes 12582912 | tf_op jit(solution)/shard_map/apply_late/pallas_call | solution.py:251
  85.9 3.0 %collective-permute-start.11 = (f32[4,8,512]{2,1,0:T(8,128)S(1)}, f32[4,8,512]{2,1,0:T(8,128)S(1)}, u32[]{:S(2)}, u32[]{:S(2)}) collective-permute-start(f32[4,8,512]{2,1,0:T(8,128)S(1)} %slice.63), channel_id=1, source_target_pairs={{0,1},{1,0},{2,3},{3,2},{4,5},{5,4},{6,7},{7,6},{8,9},{9,8},{10,11... | collective-permute-start | bytes 196616 | tf_op jit(solution)/shard_map/ppermute | solution.py:271
  89.8 3.5 %collective-permute-start.12 = (f32[8,512]{1,0:T(8,128)S(1)}, f32[8,512]{1,0:T(8,128)S(1)}, u32[]{:S(2)}, u32[]{:S(2)}) collective-permute-start(f32[8,512]{1,0:T(8,128)S(1)} %get-tuple-element.52), channel_id=1, source_target_pairs={{0,6},{2,0},{4,2},{6,4},{1,7},{3,1},{5,3},{7,5},{8,14},{10,8},{12,... | collective-permute-start | bytes 49160 | tf_op jit(solution)/shard_map/ppermute | solution.py:271
  94.8 5.9 %all-to-all-done = f32[32,8,512]{2,1,0:T(8,128)S(1)} async-done(((f32[32,8,512]{2,1,0:T(8,128)}), f32[32,8,512]{2,1,0:T(8,128)S(1)}, u32[]{:S(2)}, u32[]{:S(2)}) %all-to-all-start) | async-done | bytes 524320 | tf_op jit(solution)/shard_map/all_to_all | solution.py:369
  105.9 7.2 %all-to-all-start.1 = ((f32[32,8,512]{2,1,0:T(8,128)}), f32[32,8,512]{2,1,0:T(8,128)S(1)}, u32[]{:S(2)}, u32[]{:S(2)}) async-start(f32[32,8,512]{2,1,0:T(8,128)} %broadcast_in_dim.13), calls=%async_computation.1 | async-start | bytes 1048576 | tf_op jit(solution)/shard_map/all_to_all | solution.py:276
  114.6 5.0 %apply_cols.1 = f32[32,8,512]{2,1,0:T(8,128)} custom-call(s32[9,10]{1,0:T(8,128)S(1)} %copy-done.2, bf16[10,512,512]{2,1,0:T(8,128)(2,1)} %get-tuple-element.41.high_ref, bf16[10,512,512]{2,1,0:T(8,128)(2,1)} %get-tuple-element.42.low_ref, f32[8,8,512]{2,1,0:T(8,128)S(1)} %constant_dynamic-update-slice_fusion.field), custom_call_target="tpu_custom_call" | custom-call | flops 3000000000 | bytes 12582912 | tf_op jit(solution)/shard_map/apply_cols/pallas_call | solution.py:251
  119.6 9.7 %all-to-all-done.1.field = f32[32,8,512]{2,1,0:T(8,128)S(1)} async-done(((f32[32,8,512]{2,1,0:T(8,128)}), f32[32,8,512]{2,1,0:T(8,128)S(1)}, u32[]{:S(2)}, u32[]{:S(2)}) %all-to-all-start.1) | async-done | bytes 524320 | tf_op jit(solution)/shard_map/all_to_all | solution.py:276
  129.3 4.4 %all-to-all-start.2 = ((f32[32,8,512]{2,1,0:T(8,128)}), f32[32,8,512]{2,1,0:T(8,128)S(1)}, u32[]{:S(2)}, u32[]{:S(2)}) async-start(f32[32,8,512]{2,1,0:T(8,128)} %apply_cols.1), calls=%async_computation.2 | async-start | bytes 1048576 | tf_op jit(solution)/shard_map/all_to_all | solution.py:369
  133.6 4.9 %apply_rows.1 = f32[8,8,512]{2,1,0:T(8,128)S(1)} custom-call(s32[9,10]{1,0:T(8,128)S(1)} %copy-done.2, bf16[10,512,512]{2,1,0:T(8,128)(2,1)} %get-tuple-element.41.high_ref, bf16[10,512,512]{2,1,0:T(8,128)(2,1)} %get-tuple-element.42.low_ref, f32[32,8,512]{2,1,0:T(8,128)S(1)} %all-to-all-done.1.field), custom_call_target="tpu_custom_call" | custom-call | flops 3000000000 | bytes 12582912 | tf_op jit(solution)/shard_map/apply_rows/pallas_call | solution.py:251
  139.9 3.6 %collective-permute-start.16 = (f32[8,512]{1,0:T(8,128)S(1)}, f32[8,512]{1,0:T(8,128)S(1)}, u32[]{:S(2)}, u32[]{:S(2)}) collective-permute-start(f32[8,512]{1,0:T(8,128)S(1)} %get-tuple-element.49), channel_id=1, source_target_pairs={{0,6},{2,0},{4,2},{6,4},{1,7},{3,1},{5,3},{7,5},{8,14},{10,8},{12,... | collective-permute-start | bytes 49160 | tf_op jit(solution)/shard_map/ppermute | solution.py:271
  145.1 3.9 %all-to-all-done.2 = f32[32,8,512]{2,1,0:T(8,128)S(1)} async-done(((f32[32,8,512]{2,1,0:T(8,128)}), f32[32,8,512]{2,1,0:T(8,128)S(1)}, u32[]{:S(2)}, u32[]{:S(2)}) %all-to-all-start.2) | async-done | bytes 524320 | tf_op jit(solution)/shard_map/all_to_all | solution.py:369
  149.1 10.1 %all_to_all.25 = f32[8,8,512]{2,1,0:T(8,128)S(1)} all-to-all(f32[8,8,512]{2,1,0:T(8,128)S(1)} %broadcast_in_dim.14), channel_id=1, replica_groups=mesh['z'=8,'y'=4,'x'=4,'core'=2] {'x','core'}, dimensions={0} | all-to-all | bytes 262144 | tf_op jit(solution)/shard_map/all_to_all | solution.py:276
  159.4 18.6 %all_to_all.26 = f32[32,1,128]{2,1,0:T(1,128)S(1)} all-to-all(f32[32,1,128]{2,1,0:T(1,128)S(1)} %broadcast_in_dim.16), channel_id=1, replica_groups=mesh['z'=8,'y'=4,'x'=4,'core'=2] {'z','y'}, dimensions={0} | all-to-all | bytes 32768 | tf_op jit(solution)/shard_map/all_to_all | solution.py:276
  (75 shorter events, 26.2 us)
Async XLA Ops:
  1.6 13.1 %collective-permute-start.1 = (f32[56,512]{1,0:T(8,128)S(1)}, f32[56,512]{1,0:T(8,128)S(1)}, u32[]{:S(2)}, u32[]{:S(2)}) collective-permute-start(f32[56,512]{1,0:T(8,128)S(1)} %get-tuple-element.48), channel_id=1, source_target_pairs={{0,16},{8,24},{16,0},{24,8},{1,17},{9,25},{17,1},{25,9},{2,18},{10... | collective-permute-start | bytes 344072 | tf_op jit(solution)/shard_map/ppermute | solution.py:271
  3.2 11.6 %collective-permute-start = (f32[56,512]{1,0:T(8,128)S(1)}, f32[56,512]{1,0:T(8,128)S(1)}, u32[]{:S(2)}, u32[]{:S(2)}) collective-permute-start(f32[56,512]{1,0:T(8,128)S(1)} %get-tuple-element.48), channel_id=1, source_target_pairs={{0,8},{8,16},{16,24},{24,0},{1,9},{9,17},{17,25},{25,1},{2,10},{10... | collective-permute-start | bytes 344072 | tf_op jit(solution)/shard_map/ppermute | solution.py:271
  3.9 10.9 %collective-permute-start.2 = (f32[56,512]{1,0:T(8,128)S(1)}, f32[56,512]{1,0:T(8,128)S(1)}, u32[]{:S(2)}, u32[]{:S(2)}) collective-permute-start(f32[56,512]{1,0:T(8,128)S(1)} %get-tuple-element.48), channel_id=1, source_target_pairs={{0,24},{8,0},{16,8},{24,16},{1,25},{9,1},{17,9},{25,17},{2,26},{10... | collective-permute-start | bytes 344072 | tf_op jit(solution)/shard_map/ppermute | solution.py:271
  14.8 14.9 %collective-permute-start.4 = (f32[4,56,512]{2,1,0:T(8,128)S(1)}, f32[4,56,512]{2,1,0:T(8,128)S(1)}, u32[]{:S(2)}, u32[]{:S(2)}) collective-permute-start(f32[4,56,512]{2,1,0:T(8,128)S(1)} %pad_maximum_fusion.refs_0_), channel_id=1, source_target_pairs={{0,224},{32,0},{64,32},{96,64},{128,96},{160,128},{192,160},{224,1... | collective-permute-start | bytes 1376264 | tf_op jit(solution)/shard_map/ppermute | solution.py:271
  20.7 12.6 %collective-permute-start.3 = (f32[4,56,512]{2,1,0:T(8,128)S(1)}, f32[4,56,512]{2,1,0:T(8,128)S(1)}, u32[]{:S(2)}, u32[]{:S(2)}) collective-permute-start(f32[4,56,512]{2,1,0:T(8,128)S(1)} %pad_maximum_fusion.refs_0_), channel_id=1, source_target_pairs={{0,32},{32,64},{64,96},{96,128},{128,160},{160,192},{192,224},{224... | collective-permute-start | bytes 1376264 | tf_op jit(solution)/shard_map/ppermute | solution.py:271
  29.7 11.8 %collective-permute-start.6 = (f32[4,56,512]{2,1,0:T(8,128)S(1)}, f32[4,56,512]{2,1,0:T(8,128)S(1)}, u32[]{:S(2)}, u32[]{:S(2)}) collective-permute-start(f32[4,56,512]{2,1,0:T(8,128)S(1)} %collective-permute-done.4.refs_2_), channel_id=1, source_target_pairs={{0,224},{32,0},{64,32},{96,64},{128,96},{160,128},{192,160},{224,1... | collective-permute-start | bytes 1376264 | tf_op jit(solution)/shard_map/ppermute | solution.py:271
  33.4 11.7 %collective-permute-start.5 = (f32[4,56,512]{2,1,0:T(8,128)S(1)}, f32[4,56,512]{2,1,0:T(8,128)S(1)}, u32[]{:S(2)}, u32[]{:S(2)}) collective-permute-start(f32[4,56,512]{2,1,0:T(8,128)S(1)} %collective-permute-done.3.refs_1_), channel_id=1, source_target_pairs={{0,32},{32,64},{64,96},{96,128},{128,160},{160,192},{192,224},{224... | collective-permute-start | bytes 1376264 | tf_op jit(solution)/shard_map/ppermute | solution.py:271
  41.5 11.5 %collective-permute-start.8 = (f32[4,56,512]{2,1,0:T(8,128)S(1)}, f32[4,56,512]{2,1,0:T(8,128)S(1)}, u32[]{:S(2)}, u32[]{:S(2)}) collective-permute-start(f32[4,56,512]{2,1,0:T(8,128)S(1)} %collective-permute-done.6.refs_4_), channel_id=1, source_target_pairs={{0,224},{32,0},{64,32},{96,64},{128,96},{160,128},{192,160},{224,1... | collective-permute-start | bytes 1376264 | tf_op jit(solution)/shard_map/ppermute | solution.py:271
  45.1 11.4 %collective-permute-start.7 = (f32[4,56,512]{2,1,0:T(8,128)S(1)}, f32[4,56,512]{2,1,0:T(8,128)S(1)}, u32[]{:S(2)}, u32[]{:S(2)}) collective-permute-start(f32[4,56,512]{2,1,0:T(8,128)S(1)} %collective-permute-done.5.refs_3_), channel_id=1, source_target_pairs={{0,32},{32,64},{64,96},{96,128},{128,160},{160,192},{192,224},{224... | collective-permute-start | bytes 1376264 | tf_op jit(solution)/shard_map/ppermute | solution.py:271
  53.1 8.2 %collective-permute-start.10 = (f32[2,56,512]{2,1,0:T(8,128)S(1)}, f32[2,56,512]{2,1,0:T(8,128)S(1)}, u32[]{:S(2)}, u32[]{:S(2)}) collective-permute-start(f32[2,56,512]{2,1,0:T(8,128)S(1)} %slice.61), channel_id=1, source_target_pairs={{0,224},{32,0},{64,32},{96,64},{128,96},{160,128},{192,160},{224,1... | collective-permute-start | bytes 688136 | tf_op jit(solution)/shard_map/ppermute | solution.py:271
  56.5 7.3 %collective-permute-start.9 = (f32[2,56,512]{2,1,0:T(8,128)S(1)}, f32[2,56,512]{2,1,0:T(8,128)S(1)}, u32[]{:S(2)}, u32[]{:S(2)}) collective-permute-start(f32[2,56,512]{2,1,0:T(8,128)S(1)} %slice.60), channel_id=1, source_target_pairs={{0,32},{32,64},{64,96},{96,128},{128,160},{160,192},{192,224},{224... | collective-permute-start | bytes 688136 | tf_op jit(solution)/shard_map/ppermute | solution.py:271
  72.3 28.4 %all-to-all-start = ((f32[32,8,512]{2,1,0:T(8,128)}), f32[32,8,512]{2,1,0:T(8,128)S(1)}, u32[]{:S(2)}, u32[]{:S(2)}) async-start(f32[32,8,512]{2,1,0:T(8,128)} %get-tuple-element.44), calls=%async_computation | async-start | bytes 1048576 | tf_op jit(solution)/shard_map/all_to_all | solution.py:369
  85.9 3.9 %collective-permute-start.11 = (f32[4,8,512]{2,1,0:T(8,128)S(1)}, f32[4,8,512]{2,1,0:T(8,128)S(1)}, u32[]{:S(2)}, u32[]{:S(2)}) collective-permute-start(f32[4,8,512]{2,1,0:T(8,128)S(1)} %slice.63), channel_id=1, source_target_pairs={{0,1},{1,0},{2,3},{3,2},{4,5},{5,4},{6,7},{7,6},{8,9},{9,8},{10,11... | collective-permute-start | bytes 196616 | tf_op jit(solution)/shard_map/ppermute | solution.py:271
  89.8 11.0 %collective-permute-start.12 = (f32[8,512]{1,0:T(8,128)S(1)}, f32[8,512]{1,0:T(8,128)S(1)}, u32[]{:S(2)}, u32[]{:S(2)}) collective-permute-start(f32[8,512]{1,0:T(8,128)S(1)} %get-tuple-element.52), channel_id=1, source_target_pairs={{0,6},{2,0},{4,2},{6,4},{1,7},{3,1},{5,3},{7,5},{8,14},{10,8},{12,... | collective-permute-start | bytes 49160 | tf_op jit(solution)/shard_map/ppermute | solution.py:271
  93.3 7.5 %collective-permute-start.14 = (f32[8,512]{1,0:T(8,128)S(1)}, f32[8,512]{1,0:T(8,128)S(1)}, u32[]{:S(2)}, u32[]{:S(2)}) collective-permute-start(f32[8,512]{1,0:T(8,128)S(1)} %get-tuple-element.53), channel_id=1, source_target_pairs={{0,2},{2,4},{4,6},{6,0},{1,3},{3,5},{5,7},{7,1},{8,10},{10,12},{12... | collective-permute-start | bytes 49160 | tf_op jit(solution)/shard_map/ppermute | solution.py:271
  93.3 7.5 %collective-permute-start.13 = (f32[8,512]{1,0:T(8,128)S(1)}, f32[8,512]{1,0:T(8,128)S(1)}, u32[]{:S(2)}, u32[]{:S(2)}) collective-permute-start(f32[8,512]{1,0:T(8,128)S(1)} %get-tuple-element.54), channel_id=1, source_target_pairs={{0,4},{2,6},{4,0},{6,2},{1,5},{3,7},{5,1},{7,3},{8,12},{10,14},{12... | collective-permute-start | bytes 49160 | tf_op jit(solution)/shard_map/ppermute | solution.py:271
  100.8 12.4 %collective-permute-start.21 = (f32[8,512]{1,0:T(8,128)S(1)}, f32[8,512]{1,0:T(8,128)S(1)}, u32[]{:S(2)}, u32[]{:S(2)}) collective-permute-start(f32[8,512]{1,0:T(8,128)S(1)} %get-tuple-element.46), channel_id=1, source_target_pairs={{0,6},{2,0},{4,2},{6,4},{1,7},{3,1},{5,3},{7,5},{8,14},{10,8},{12,... | collective-permute-start | bytes 49160 | tf_op jit(solution)/shard_map/ppermute | solution.py:271
  102.9 10.3 %collective-permute-start.20 = (f32[8,512]{1,0:T(8,128)S(1)}, f32[8,512]{1,0:T(8,128)S(1)}, u32[]{:S(2)}, u32[]{:S(2)}) collective-permute-start(f32[8,512]{1,0:T(8,128)S(1)} %get-tuple-element.46), channel_id=1, source_target_pairs={{0,4},{2,6},{4,0},{6,2},{1,5},{3,7},{5,1},{7,3},{8,12},{10,14},{12... | collective-permute-start | bytes 49160 | tf_op jit(solution)/shard_map/ppermute | solution.py:271
  105.1 8.1 %collective-permute-start.19 = (f32[8,512]{1,0:T(8,128)S(1)}, f32[8,512]{1,0:T(8,128)S(1)}, u32[]{:S(2)}, u32[]{:S(2)}) collective-permute-start(f32[8,512]{1,0:T(8,128)S(1)} %get-tuple-element.46), channel_id=1, source_target_pairs={{0,2},{2,4},{4,6},{6,0},{1,3},{3,5},{5,7},{7,1},{8,10},{10,12},{12... | collective-permute-start | bytes 49160 | tf_op jit(solution)/shard_map/ppermute | solution.py:271
  105.9 23.3 %all-to-all-start.1 = ((f32[32,8,512]{2,1,0:T(8,128)}), f32[32,8,512]{2,1,0:T(8,128)S(1)}, u32[]{:S(2)}, u32[]{:S(2)}) async-start(f32[32,8,512]{2,1,0:T(8,128)} %broadcast_in_dim.13), calls=%async_computation.1 | async-start | bytes 1048576 | tf_op jit(solution)/shard_map/all_to_all | solution.py:276
  129.3 19.8 %all-to-all-start.2 = ((f32[32,8,512]{2,1,0:T(8,128)}), f32[32,8,512]{2,1,0:T(8,128)S(1)}, u32[]{:S(2)}, u32[]{:S(2)}) async-start(f32[32,8,512]{2,1,0:T(8,128)} %apply_cols.1), calls=%async_computation.2 | async-start | bytes 1048576 | tf_op jit(solution)/shard_map/all_to_all | solution.py:369
  139.9 9.1 %collective-permute-start.16 = (f32[8,512]{1,0:T(8,128)S(1)}, f32[8,512]{1,0:T(8,128)S(1)}, u32[]{:S(2)}, u32[]{:S(2)}) collective-permute-start(f32[8,512]{1,0:T(8,128)S(1)} %get-tuple-element.49), channel_id=1, source_target_pairs={{0,6},{2,0},{4,2},{6,4},{1,7},{3,1},{5,3},{7,5},{8,14},{10,8},{12,... | collective-permute-start | bytes 49160 | tf_op jit(solution)/shard_map/ppermute | solution.py:271
  143.5 5.6 %collective-permute-start.18 = (f32[8,512]{1,0:T(8,128)S(1)}, f32[8,512]{1,0:T(8,128)S(1)}, u32[]{:S(2)}, u32[]{:S(2)}) collective-permute-start(f32[8,512]{1,0:T(8,128)S(1)} %get-tuple-element.50), channel_id=1, source_target_pairs={{0,2},{2,4},{4,6},{6,0},{1,3},{3,5},{5,7},{7,1},{8,10},{10,12},{12... | collective-permute-start | bytes 49160 | tf_op jit(solution)/shard_map/ppermute | solution.py:271
  143.5 5.6 %collective-permute-start.17 = (f32[8,512]{1,0:T(8,128)S(1)}, f32[8,512]{1,0:T(8,128)S(1)}, u32[]{:S(2)}, u32[]{:S(2)}) collective-permute-start(f32[8,512]{1,0:T(8,128)S(1)} %get-tuple-element.51), channel_id=1, source_target_pairs={{0,4},{2,6},{4,0},{6,2},{1,5},{3,7},{5,1},{7,3},{8,12},{10,14},{12... | collective-permute-start | bytes 49160 | tf_op jit(solution)/shard_map/ppermute | solution.py:271
  (5 other events, 26.1 us)

commit v8 on v7

--- a/solution.py
+++ b/solution.py
@@ -277,8 +277,9 @@
 
 
 def spread_near(piece):
-    mine = jnp.stack([piece] + [shift(piece, "x", d) for d in range(1, lax.axis_size("x"))])
-    return jnp.concatenate([mine, shift(mine, "core", 1)], axis=0)
+    both = jnp.stack([piece, shift(piece, "core", 1)])
+    near = [both] + [shift(both, "x", d) for d in range(1, lax.axis_size("x"))]
+    return jnp.stack(near, axis=1).reshape(2 * len(near), *piece.shape)
 
 
 def reduce_near(row_acc):
@@ -333,7 +334,7 @@
         out[LIVE, slot] = jnp.where(live, 1, 0)
         out[CROSSING, slot] = jnp.where(live & crossing, 1, 0)
         stage = jnp.where(live, (source + 1) // 2, LAST_STAGE)
-        arrival.append(PER_STAGE * stage)
+        arrival.append(jnp.maximum(PER_STAGE * stage - 1, 0))
         keys.append(stage * slots + slot)
     ranks = [
         sum(jnp.where(other <= key, 1, 0) for other in keys) for key in keys
@@ -344,7 +345,7 @@
             if other != slot:
                 wait = arrival[other] + ranks[slot] - ranks[other]
                 turn = jnp.maximum(turn, jnp.where(keys[other] <= keys[slot], wait, 0))
-        stage = jnp.minimum(turn // PER_STAGE, LAST_STAGE)
+        stage = jnp.minimum((turn + 1) // PER_STAGE, LAST_STAGE)
         live = valid[0, slot] != 0
         out[STAGE, slot] = jnp.where(live, stage, -1)
         out[LATE, slot] = jnp.where(live & (stage == LAST_STAGE), 1, 0)
@@ -388,6 +389,7 @@
     )
     row_vec = vectors.reshape(8, tiles, TILE).transpose(1, 0, 2)
     near = gather_y(own)
+    flat, near = lax.optimization_barrier((flat, near))
     prepared = prepare_rows(flat)
     places, state = [], []
     for stage, arrived in enumerate(gather_z(near)):

time: 182 us -> 181 us (level)
  waiting for transfers between devices: 33.5 us -> 18.2 us
  Pallas kernels: 49.9 us -> 62.4 us
  starting transfers between devices: 61.5 us -> 65.1 us
    pallas_call x5, Pallas kernels: 30 us -> 39.5 us  [form_stage(): pl.pallas_call(functools.partial(stage_kernel, stage, len(places)), in_sp...]
    all_to_all x1, waiting for transfers between devices: 9.67 us -> 1.04 us  [spread(): return lax.all_to_all(copies, axes, 0, 0, tiled=True)]
    ppermute x23, waiting for transfers between devices: 14 us -> 9.57 us  [shift(): lax.ppermute(value, axis, [(i, (i + distance) % size) for i in range(size)])]
    pallas_call x3, Pallas kernels: 12.8 us -> 15.7 us  [apply_tiles(): pl.pallas_call(functools.partial(apply_kernel, wanted, col_at), in_specs=...]
    all_to_all x2, waiting for transfers between devices: 9.82 us -> 7.57 us  [combine(): by_col = lax.all_to_all(col_acc, ROW, 0, 0, tiled=True)]
  transfers between devices with their start and end apart: 26 -> 26, of which waited for: 8 -> 10; matrix products, arithmetic and copies ran while one was open for 1% -> 0% of each run, Pallas kernels for 23% -> 27%
where the time goes in v8:
time: 181 us; the launch traced here: 178 us
  starting transfers between devices  65.1 us (36%)
  Pallas kernels  62.4 us (34%)
  blocking collectives  27.3 us (15%)
  waiting for transfers between devices  18.2 us (10%)
  local copies, waits for them, and re-layouts  3.7 us (2%)
    ppermute x23, starting transfers between devices, shift(): lax.ppermute(value, axis, [(i, (i + distance) % size) for i in range(size)])  41 us
    pallas_call x5, Pallas kernels, form_stage(): pl.pallas_call(functools.partial(stage_kernel, stage, len(places)), in_sp...  39.5 us
    all_to_all x2, blocking collectives, spread(): return lax.all_to_all(copies, axes, 0, 0, tiled=True)  27.3 us
    pallas_call x3, Pallas kernels, apply_tiles(): pl.pallas_call(functools.partial(apply_kernel, wanted, col_at), in_specs=...  15.7 us
    all_to_all x2, starting transfers between devices, combine(): by_col = lax.all_to_all(col_acc, ROW, 0, 0, tiled=True)  15.3 us
    ppermute x23, waiting for transfers between devices, shift(): lax.ppermute(value, axis, [(i, (i + distance) % size) for i in range(size)])  9.57 us
    all_to_all x1, starting transfers between devices, spread(): return lax.all_to_all(copies, axes, 0, 0, tiled=True)  8.91 us
    all_to_all x2, waiting for transfers between devices, combine(): by_col = lax.all_to_all(col_acc, ROW, 0, 0, tiled=True)  7.57 us
  transfers between devices with their start and end apart: 26, of which 10 were waited for; matrix products, arithmetic and copies ran while one was open for 0% of the time, Pallas kernels for 27%

profile of v8, /device:TPU:0, one launch (start us, length us, event | category | flops | bytes accessed | tf_op | source)
XLA Modules:
  0.0 178.2 jit_solution(13148831602674149935)
XLA Ops:
  3.9 2.6 %collective-permute-start.2 = (f32[56,512]{1,0:T(8,128)S(1)}, f32[56,512]{1,0:T(8,128)S(1)}, u32[]{:S(2)}, u32[]{:S(2)}) collective-permute-start(f32[56,512]{1,0:T(8,128)S(1)} %get-tuple-element.50), channel_id=1, source_target_pairs={{0,24},{8,0},{16,8},{24,16},{1,25},{9,1},{17,9},{25,17},{2,26},{10... | collective-permute-start | bytes 344072 | tf_op jit(solution)/shard_map/ppermute | solution.py:271
  10.3 4.9 %collective-permute-start.4 = (f32[4,56,512]{2,1,0:T(8,128)S(1)}, f32[4,56,512]{2,1,0:T(8,128)S(1)}, u32[]{:S(2)}, u32[]{:S(2)}) collective-permute-start(f32[4,56,512]{2,1,0:T(8,128)S(1)} %pad_maximum_fusion.refs_0_), channel_id=1, source_target_pairs={{0,224},{32,0},{64,32},{96,64},{128,96},{160,128},{192,160},{224,1... | collective-permute-start | bytes 1376264 | tf_op jit(solution)/shard_map/ppermute | solution.py:271
  16.3 5.1 %prepare_rows.1.prepared_ref = bf16[8,16,512,48]{3,2,1,0:T(8,128)(2,1)S(1)} custom-call(f32[48,4096]{1,0:T(8,128)S(1)} %bitcast.67), custom_call_target="tpu_custom_call" | custom-call | flops 100000000 | bytes 8388608 | tf_op jit(solution)/shard_map/prepare_rows/pallas_call | solution.py:66
  24.2 5.1 %collective-permute-start.6 = (f32[4,56,512]{2,1,0:T(8,128)S(1)}, f32[4,56,512]{2,1,0:T(8,128)S(1)}, u32[]{:S(2)}, u32[]{:S(2)}) collective-permute-start(f32[4,56,512]{2,1,0:T(8,128)S(1)} %collective-permute-done.4.refs_2_), channel_id=1, source_target_pairs={{0,224},{32,0},{64,32},{96,64},{128,96},{160,128},{192,160},{224,1... | collective-permute-start | bytes 1376264 | tf_op jit(solution)/shard_map/ppermute | solution.py:271
  29.3 8.0 %form_1.1 = (bf16[10,512,512]{2,1,0:T(8,128)(2,1)}, bf16[10,512,512]{2,1,0:T(8,128)(2,1)}, f32[8,8,512]{2,1,0:T(8,128)S(1)}, f32[32,8,512]{2,1,0:T(8,128)S(1)}) custom-call(s32[9,10]{1,0:T(8,128)S(1)} %copy-done.2, bf16[8,16,512,48]{3,2,1,0:T(8,128)(2,1)S(1)} %prepare_rows.1.prepared_ref, ...), custom_call_target="tpu_custom_call", output_to_operand_aliasing={{0}: (6, {}), {1}: (7, {}), {2}: (8, {}), {3}: (9, {})} | custom-call | flops 8000000000 | bytes 8388608 | tf_op jit(solution)/shard_map/form_1/pallas_call | solution.py:187
  37.8 3.7 %collective-permute-start.8 = (f32[4,56,512]{2,1,0:T(8,128)S(1)}, f32[4,56,512]{2,1,0:T(8,128)S(1)}, u32[]{:S(2)}, u32[]{:S(2)}) collective-permute-start(f32[4,56,512]{2,1,0:T(8,128)S(1)} %collective-permute-done.6.refs_4_), channel_id=1, source_target_pairs={{0,224},{32,0},{64,32},{96,64},{128,96},{160,128},{192,160},{224,1... | collective-permute-start | bytes 1376264 | tf_op jit(solution)/shard_map/ppermute | solution.py:271
  41.5 8.0 %form_2.1 = (bf16[10,512,512]{2,1,0:T(8,128)(2,1)}, bf16[10,512,512]{2,1,0:T(8,128)(2,1)}, f32[8,8,512]{2,1,0:T(8,128)S(1)}, f32[32,8,512]{2,1,0:T(8,128)S(1)}) custom-call(s32[9,10]{1,0:T(8,128)S(1)} %copy-done.2, bf16[8,16,512,48]{3,2,1,0:T(8,128)(2,1)S(1)} %prepare_rows.1.prepared_ref, ...), custom_call_target="tpu_custom_call", output_to_operand_aliasing={{0}: (8, {}), {1}: (9, {}), {2}: (10, {}), {3}: (11, {})} | custom-call | flops 8000000000 | bytes 8388608 | tf_op jit(solution)/shard_map/form_2/pallas_call | solution.py:187
  49.6 3.3 %collective-permute-start.10 = (f32[2,56,512]{2,1,0:T(8,128)S(1)}, f32[2,56,512]{2,1,0:T(8,128)S(1)}, u32[]{:S(2)}, u32[]{:S(2)}) collective-permute-start(f32[2,56,512]{2,1,0:T(8,128)S(1)} %slice.61), channel_id=1, source_target_pairs={{0,224},{32,0},{64,32},{96,64},{128,96},{160,128},{192,160},{224,1... | collective-permute-start | bytes 688136 | tf_op jit(solution)/shard_map/ppermute | solution.py:271
  53.0 8.1 %form_3.1 = (bf16[10,512,512]{2,1,0:T(8,128)(2,1)}, bf16[10,512,512]{2,1,0:T(8,128)(2,1)}, f32[8,8,512]{2,1,0:T(8,128)S(1)}, f32[32,8,512]{2,1,0:T(8,128)S(1)}) custom-call(s32[9,10]{1,0:T(8,128)S(1)} %copy-done.2, ...), custom_call_target="tpu_custom_call", output_to_operand_aliasing={{0}: (10, {}), {1}: (11, {}), {2}: (12, {}), {3}: (13, {})} | custom-call | flops 8000000000 | bytes 8388608 | tf_op jit(solution)/shard_map/form_3/pallas_call | solution.py:187
  61.2 14.4 %form_4.1 = (bf16[10,512,512]{2,1,0:T(8,128)(2,1)}, bf16[10,512,512]{2,1,0:T(8,128)(2,1)}, f32[10,8,512]{2,1,0:T(8,128)S(1)}, f32[32,8,512]{2,1,0:T(8,128)}) custom-call(s32[9,10]{1,0:T(8,128)S(1)} %copy-done.2, bf16[8,16,512,48]{3,2,1,0:T(8,128)(2,1)S(1)} %prepare_rows.1.prepared_ref, ...), custom_call_target="tpu_custom_call", output_to_operand_aliasing={{0}: (12, {}), {1}: (13, {})} | custom-call | flops 8000000000 | bytes 8388608 | tf_op jit(solution)/shard_map/form_4/pallas_call | solution.py:187
  75.5 6.8 %all-to-all-start = ((f32[32,8,512]{2,1,0:T(8,128)}), f32[32,8,512]{2,1,0:T(8,128)S(1)}, u32[]{:S(2)}, u32[]{:S(2)}) async-start(f32[32,8,512]{2,1,0:T(8,128)} %get-tuple-element.48), calls=%async_computation | async-start | bytes 1048576 | tf_op jit(solution)/shard_map/all_to_all | solution.py:370
  82.3 3.7 %apply_late.1 = f32[8,8,512]{2,1,0:T(8,128)S(1)} custom-call(s32[9,10]{1,0:T(8,128)S(1)} %copy-done.2, bf16[10,512,512]{2,1,0:T(8,128)(2,1)} %get-tuple-element.45.high_ref, bf16[10,512,512]{2,1,0:T(8,128)(2,1)} %get-tuple-element.46.low_ref, f32[10,8,512]{2,1,0:T(8,128)S(1)} %get-tuple-element.47.field, f32[8,8,512]{2,1,0:T(8,128)S(1)} %get-tuple-element.43.refs_11_.refs_0_), custom_call_target="tpu_custom_call" | custom-call | flops 3000000000 | bytes 12582912 | tf_op jit(solution)/shard_map/apply_late/pallas_call | solution.py:251
  87.4 2.9 %collective-permute-start.12 = (f32[8,512]{1,0:T(8,128)S(1)}, f32[8,512]{1,0:T(8,128)S(1)}, u32[]{:S(2)}, u32[]{:S(2)}) collective-permute-start(f32[8,512]{1,0:T(8,128)S(1)} %get-tuple-element.54), channel_id=1, source_target_pairs={{0,6},{2,0},{4,2},{6,4},{1,7},{3,1},{5,3},{7,5},{8,14},{10,8},{12,... | collective-permute-start | bytes 49160 | tf_op jit(solution)/shard_map/ppermute | solution.py:271
  90.3 4.7 %collective-permute-start.13 = (f32[8,512]{1,0:T(8,128)S(1)}, f32[8,512]{1,0:T(8,128)S(1)}, u32[]{:S(2)}, u32[]{:S(2)}) collective-permute-start(f32[8,512]{1,0:T(8,128)S(1)} %get-tuple-element.56), channel_id=1, source_target_pairs={{0,4},{2,6},{4,0},{6,2},{1,5},{3,7},{5,1},{7,3},{8,12},{10,14},{12... | collective-permute-start | bytes 49160 | tf_op jit(solution)/shard_map/ppermute | solution.py:271
  98.4 8.9 %all-to-all-start.1 = ((f32[32,8,512]{2,1,0:T(8,128)}), f32[32,8,512]{2,1,0:T(8,128)S(1)}, u32[]{:S(2)}, u32[]{:S(2)}) async-start(f32[32,8,512]{2,1,0:T(8,128)} %broadcast_in_dim.13), calls=%async_computation.1 | async-start | bytes 1048576 | tf_op jit(solution)/shard_map/all_to_all | solution.py:276
  108.6 3.4 %collective-permute-start.21 = (f32[2,8,512]{2,1,0:T(8,128)S(1)}, f32[2,8,512]{2,1,0:T(8,128)S(1)}, u32[]{:S(2)}, u32[]{:S(2)}) collective-permute-start(f32[2,8,512]{2,1,0:T(8,128)S(1)} %get-tuple-element.58), channel_id=1, source_target_pairs={{0,4},{2,6},{4,0},{6,2},{1,5},{3,7},{5,1},{7,3},{8,12},{10,14},{12... | collective-permute-start | bytes 98312 | tf_op jit(solution)/shard_map/ppermute | solution.py:271
  111.9 3.2 %collective-permute-start.22 = (f32[2,8,512]{2,1,0:T(8,128)S(1)}, f32[2,8,512]{2,1,0:T(8,128)S(1)}, u32[]{:S(2)}, u32[]{:S(2)}) collective-permute-start(f32[2,8,512]{2,1,0:T(8,128)S(1)} %get-tuple-element.58), channel_id=1, source_target_pairs={{0,6},{2,0},{4,2},{6,4},{1,7},{3,1},{5,3},{7,5},{8,14},{10,8},{12,... | collective-permute-start | bytes 98312 | tf_op jit(solution)/shard_map/ppermute | solution.py:271
  117.1 5.9 %apply_cols.1 = f32[32,8,512]{2,1,0:T(8,128)} custom-call(s32[9,10]{1,0:T(8,128)S(1)} %copy-done.2, bf16[10,512,512]{2,1,0:T(8,128)(2,1)} %get-tuple-element.45.high_ref, bf16[10,512,512]{2,1,0:T(8,128)(2,1)} %get-tuple-element.46.low_ref, f32[8,8,512]{2,1,0:T(8,128)S(1)} %bitcast.68), custom_call_target="tpu_custom_call" | custom-call | flops 3000000000 | bytes 12582912 | tf_op jit(solution)/shard_map/apply_cols/pallas_call | solution.py:251
  124.0 8.5 %all-to-all-start.2 = ((f32[32,8,512]{2,1,0:T(8,128)}), f32[32,8,512]{2,1,0:T(8,128)S(1)}, u32[]{:S(2)}, u32[]{:S(2)}) async-start(f32[32,8,512]{2,1,0:T(8,128)} %apply_cols.1), calls=%async_computation.2 | async-start | bytes 1048576 | tf_op jit(solution)/shard_map/all_to_all | solution.py:370
  132.5 6.1 %apply_rows.1 = f32[8,8,512]{2,1,0:T(8,128)S(1)} custom-call(s32[9,10]{1,0:T(8,128)S(1)} %copy-done.2, bf16[10,512,512]{2,1,0:T(8,128)(2,1)} %get-tuple-element.45.high_ref, bf16[10,512,512]{2,1,0:T(8,128)(2,1)} %get-tuple-element.46.low_ref, f32[32,8,512]{2,1,0:T(8,128)S(1)} %all-to-all-done.1.field), custom_call_target="tpu_custom_call" | custom-call | flops 3000000000 | bytes 12582912 | tf_op jit(solution)/shard_map/apply_rows/pallas_call | solution.py:251
  140.0 3.0 %collective-permute-start.16 = (f32[8,512]{1,0:T(8,128)S(1)}, f32[8,512]{1,0:T(8,128)S(1)}, u32[]{:S(2)}, u32[]{:S(2)}) collective-permute-start(f32[8,512]{1,0:T(8,128)S(1)} %get-tuple-element.51), channel_id=1, source_target_pairs={{0,6},{2,0},{4,2},{6,4},{1,7},{3,1},{5,3},{7,5},{8,14},{10,8},{12,... | collective-permute-start | bytes 49160 | tf_op jit(solution)/shard_map/ppermute | solution.py:271
  144.6 5.2 %all-to-all-done.2 = f32[32,8,512]{2,1,0:T(8,128)S(1)} async-done(((f32[32,8,512]{2,1,0:T(8,128)}), f32[32,8,512]{2,1,0:T(8,128)S(1)}, u32[]{:S(2)}, u32[]{:S(2)}) %all-to-all-start.2) | async-done | bytes 524320 | tf_op jit(solution)/shard_map/all_to_all | solution.py:370
  149.9 9.9 %all_to_all.25 = f32[8,8,512]{2,1,0:T(8,128)S(1)} all-to-all(f32[8,8,512]{2,1,0:T(8,128)S(1)} %broadcast_in_dim.14), channel_id=1, replica_groups=mesh['z'=8,'y'=4,'x'=4,'core'=2] {'x','core'}, dimensions={0} | all-to-all | bytes 262144 | tf_op jit(solution)/shard_map/all_to_all | solution.py:276
  160.0 17.4 %all_to_all.26 = f32[32,1,128]{2,1,0:T(1,128)S(1)} all-to-all(f32[32,1,128]{2,1,0:T(1,128)S(1)} %broadcast_in_dim.16), channel_id=1, replica_groups=mesh['z'=8,'y'=4,'x'=4,'core'=2] {'z','y'}, dimensions={0} | all-to-all | bytes 32768 | tf_op jit(solution)/shard_map/all_to_all | solution.py:276
  (73 shorter events, 24.9 us)
Async XLA Ops:
  1.6 6.8 %collective-permute-start.1 = (f32[56,512]{1,0:T(8,128)S(1)}, f32[56,512]{1,0:T(8,128)S(1)}, u32[]{:S(2)}, u32[]{:S(2)}) collective-permute-start(f32[56,512]{1,0:T(8,128)S(1)} %get-tuple-element.50), channel_id=1, source_target_pairs={{0,16},{8,24},{16,0},{24,8},{1,17},{9,25},{17,1},{25,9},{2,18},{10... | collective-permute-start | bytes 344072 | tf_op jit(solution)/shard_map/ppermute | solution.py:271
  3.2 7.0 %collective-permute-start = (f32[56,512]{1,0:T(8,128)S(1)}, f32[56,512]{1,0:T(8,128)S(1)}, u32[]{:S(2)}, u32[]{:S(2)}) collective-permute-start(f32[56,512]{1,0:T(8,128)S(1)} %get-tuple-element.50), channel_id=1, source_target_pairs={{0,8},{8,16},{16,24},{24,0},{1,9},{9,17},{17,25},{25,1},{2,10},{10... | collective-permute-start | bytes 344072 | tf_op jit(solution)/shard_map/ppermute | solution.py:271
  3.9 6.4 %collective-permute-start.2 = (f32[56,512]{1,0:T(8,128)S(1)}, f32[56,512]{1,0:T(8,128)S(1)}, u32[]{:S(2)}, u32[]{:S(2)}) collective-permute-start(f32[56,512]{1,0:T(8,128)S(1)} %get-tuple-element.50), channel_id=1, source_target_pairs={{0,24},{8,0},{16,8},{24,16},{1,25},{9,1},{17,9},{25,17},{2,26},{10... | collective-permute-start | bytes 344072 | tf_op jit(solution)/shard_map/ppermute | solution.py:271
  10.3 13.9 %collective-permute-start.4 = (f32[4,56,512]{2,1,0:T(8,128)S(1)}, f32[4,56,512]{2,1,0:T(8,128)S(1)}, u32[]{:S(2)}, u32[]{:S(2)}) collective-permute-start(f32[4,56,512]{2,1,0:T(8,128)S(1)} %pad_maximum_fusion.refs_0_), channel_id=1, source_target_pairs={{0,224},{32,0},{64,32},{96,64},{128,96},{160,128},{192,160},{224,1... | collective-permute-start | bytes 1376264 | tf_op jit(solution)/shard_map/ppermute | solution.py:271
  15.2 14.1 %collective-permute-start.3 = (f32[4,56,512]{2,1,0:T(8,128)S(1)}, f32[4,56,512]{2,1,0:T(8,128)S(1)}, u32[]{:S(2)}, u32[]{:S(2)}) collective-permute-start(f32[4,56,512]{2,1,0:T(8,128)S(1)} %pad_maximum_fusion.refs_0_), channel_id=1, source_target_pairs={{0,32},{32,64},{64,96},{96,128},{128,160},{160,192},{192,224},{224... | collective-permute-start | bytes 1376264 | tf_op jit(solution)/shard_map/ppermute | solution.py:271
  24.2 13.6 %collective-permute-start.6 = (f32[4,56,512]{2,1,0:T(8,128)S(1)}, f32[4,56,512]{2,1,0:T(8,128)S(1)}, u32[]{:S(2)}, u32[]{:S(2)}) collective-permute-start(f32[4,56,512]{2,1,0:T(8,128)S(1)} %collective-permute-done.4.refs_2_), channel_id=1, source_target_pairs={{0,224},{32,0},{64,32},{96,64},{128,96},{160,128},{192,160},{224,1... | collective-permute-start | bytes 1376264 | tf_op jit(solution)/shard_map/ppermute | solution.py:271
  29.3 12.2 %collective-permute-start.5 = (f32[4,56,512]{2,1,0:T(8,128)S(1)}, f32[4,56,512]{2,1,0:T(8,128)S(1)}, u32[]{:S(2)}, u32[]{:S(2)}) collective-permute-start(f32[4,56,512]{2,1,0:T(8,128)S(1)} %collective-permute-done.3.refs_1_), channel_id=1, source_target_pairs={{0,32},{32,64},{64,96},{96,128},{128,160},{160,192},{192,224},{224... | collective-permute-start | bytes 1376264 | tf_op jit(solution)/shard_map/ppermute | solution.py:271
  37.8 11.7 %collective-permute-start.8 = (f32[4,56,512]{2,1,0:T(8,128)S(1)}, f32[4,56,512]{2,1,0:T(8,128)S(1)}, u32[]{:S(2)}, u32[]{:S(2)}) collective-permute-start(f32[4,56,512]{2,1,0:T(8,128)S(1)} %collective-permute-done.6.refs_4_), channel_id=1, source_target_pairs={{0,224},{32,0},{64,32},{96,64},{128,96},{160,128},{192,160},{224,1... | collective-permute-start | bytes 1376264 | tf_op jit(solution)/shard_map/ppermute | solution.py:271
  41.5 11.4 %collective-permute-start.7 = (f32[4,56,512]{2,1,0:T(8,128)S(1)}, f32[4,56,512]{2,1,0:T(8,128)S(1)}, u32[]{:S(2)}, u32[]{:S(2)}) collective-permute-start(f32[4,56,512]{2,1,0:T(8,128)S(1)} %collective-permute-done.5.refs_3_), channel_id=1, source_target_pairs={{0,32},{32,64},{64,96},{96,128},{128,160},{160,192},{192,224},{224... | collective-permute-start | bytes 1376264 | tf_op jit(solution)/shard_map/ppermute | solution.py:271
  49.6 11.6 %collective-permute-start.10 = (f32[2,56,512]{2,1,0:T(8,128)S(1)}, f32[2,56,512]{2,1,0:T(8,128)S(1)}, u32[]{:S(2)}, u32[]{:S(2)}) collective-permute-start(f32[2,56,512]{2,1,0:T(8,128)S(1)} %slice.61), channel_id=1, source_target_pairs={{0,224},{32,0},{64,32},{96,64},{128,96},{160,128},{192,160},{224,1... | collective-permute-start | bytes 688136 | tf_op jit(solution)/shard_map/ppermute | solution.py:271
  52.9 8.2 %collective-permute-start.9 = (f32[2,56,512]{2,1,0:T(8,128)S(1)}, f32[2,56,512]{2,1,0:T(8,128)S(1)}, u32[]{:S(2)}, u32[]{:S(2)}) collective-permute-start(f32[2,56,512]{2,1,0:T(8,128)S(1)} %slice.60), channel_id=1, source_target_pairs={{0,32},{32,64},{64,96},{96,128},{128,160},{160,192},{192,224},{224... | collective-permute-start | bytes 688136 | tf_op jit(solution)/shard_map/ppermute | solution.py:271
  75.5 21.9 %all-to-all-start = ((f32[32,8,512]{2,1,0:T(8,128)}), f32[32,8,512]{2,1,0:T(8,128)S(1)}, u32[]{:S(2)}, u32[]{:S(2)}) async-start(f32[32,8,512]{2,1,0:T(8,128)} %get-tuple-element.48), calls=%async_computation | async-start | bytes 1048576 | tf_op jit(solution)/shard_map/all_to_all | solution.py:370
  86.1 1.3 collective-permute-start.11
  87.4 10.1 %collective-permute-start.12 = (f32[8,512]{1,0:T(8,128)S(1)}, f32[8,512]{1,0:T(8,128)S(1)}, u32[]{:S(2)}, u32[]{:S(2)}) collective-permute-start(f32[8,512]{1,0:T(8,128)S(1)} %get-tuple-element.54), channel_id=1, source_target_pairs={{0,6},{2,0},{4,2},{6,4},{1,7},{3,1},{5,3},{7,5},{8,14},{10,8},{12,... | collective-permute-start | bytes 49160 | tf_op jit(solution)/shard_map/ppermute | solution.py:271
  90.3 7.2 %collective-permute-start.14 = (f32[8,512]{1,0:T(8,128)S(1)}, f32[8,512]{1,0:T(8,128)S(1)}, u32[]{:S(2)}, u32[]{:S(2)}) collective-permute-start(f32[8,512]{1,0:T(8,128)S(1)} %get-tuple-element.55), channel_id=1, source_target_pairs={{0,2},{2,4},{4,6},{6,0},{1,3},{3,5},{5,7},{7,1},{8,10},{10,12},{12... | collective-permute-start | bytes 49160 | tf_op jit(solution)/shard_map/ppermute | solution.py:271
  90.3 7.2 %collective-permute-start.13 = (f32[8,512]{1,0:T(8,128)S(1)}, f32[8,512]{1,0:T(8,128)S(1)}, u32[]{:S(2)}, u32[]{:S(2)}) collective-permute-start(f32[8,512]{1,0:T(8,128)S(1)} %get-tuple-element.56), channel_id=1, source_target_pairs={{0,4},{2,6},{4,0},{6,2},{1,5},{3,7},{5,1},{7,3},{8,12},{10,14},{12... | collective-permute-start | bytes 49160 | tf_op jit(solution)/shard_map/ppermute | solution.py:271
  98.4 25.7 %all-to-all-start.1 = ((f32[32,8,512]{2,1,0:T(8,128)}), f32[32,8,512]{2,1,0:T(8,128)S(1)}, u32[]{:S(2)}, u32[]{:S(2)}) async-start(f32[32,8,512]{2,1,0:T(8,128)} %broadcast_in_dim.13), calls=%async_computation.1 | async-start | bytes 1048576 | tf_op jit(solution)/shard_map/all_to_all | solution.py:276
  108.6 6.6 %collective-permute-start.21 = (f32[2,8,512]{2,1,0:T(8,128)S(1)}, f32[2,8,512]{2,1,0:T(8,128)S(1)}, u32[]{:S(2)}, u32[]{:S(2)}) collective-permute-start(f32[2,8,512]{2,1,0:T(8,128)S(1)} %get-tuple-element.58), channel_id=1, source_target_pairs={{0,4},{2,6},{4,0},{6,2},{1,5},{3,7},{5,1},{7,3},{8,12},{10,14},{12... | collective-permute-start | bytes 98312 | tf_op jit(solution)/shard_map/ppermute | solution.py:271
  111.9 5.1 %collective-permute-start.20 = (f32[2,8,512]{2,1,0:T(8,128)S(1)}, f32[2,8,512]{2,1,0:T(8,128)S(1)}, u32[]{:S(2)}, u32[]{:S(2)}) collective-permute-start(f32[2,8,512]{2,1,0:T(8,128)S(1)} %get-tuple-element.58), channel_id=1, source_target_pairs={{0,2},{2,4},{4,6},{6,0},{1,3},{3,5},{5,7},{7,1},{8,10},{10,12},{12... | collective-permute-start | bytes 98312 | tf_op jit(solution)/shard_map/ppermute | solution.py:271
  111.9 5.1 %collective-permute-start.22 = (f32[2,8,512]{2,1,0:T(8,128)S(1)}, f32[2,8,512]{2,1,0:T(8,128)S(1)}, u32[]{:S(2)}, u32[]{:S(2)}) collective-permute-start(f32[2,8,512]{2,1,0:T(8,128)S(1)} %get-tuple-element.58), channel_id=1, source_target_pairs={{0,6},{2,0},{4,2},{6,4},{1,7},{3,1},{5,3},{7,5},{8,14},{10,8},{12,... | collective-permute-start | bytes 98312 | tf_op jit(solution)/shard_map/ppermute | solution.py:271
  124.0 25.8 %all-to-all-start.2 = ((f32[32,8,512]{2,1,0:T(8,128)}), f32[32,8,512]{2,1,0:T(8,128)S(1)}, u32[]{:S(2)}, u32[]{:S(2)}) async-start(f32[32,8,512]{2,1,0:T(8,128)} %apply_cols.1), calls=%async_computation.2 | async-start | bytes 1048576 | tf_op jit(solution)/shard_map/all_to_all | solution.py:370
  140.0 9.8 %collective-permute-start.16 = (f32[8,512]{1,0:T(8,128)S(1)}, f32[8,512]{1,0:T(8,128)S(1)}, u32[]{:S(2)}, u32[]{:S(2)}) collective-permute-start(f32[8,512]{1,0:T(8,128)S(1)} %get-tuple-element.51), channel_id=1, source_target_pairs={{0,6},{2,0},{4,2},{6,4},{1,7},{3,1},{5,3},{7,5},{8,14},{10,8},{12,... | collective-permute-start | bytes 49160 | tf_op jit(solution)/shard_map/ppermute | solution.py:271
  143.0 6.8 %collective-permute-start.18 = (f32[8,512]{1,0:T(8,128)S(1)}, f32[8,512]{1,0:T(8,128)S(1)}, u32[]{:S(2)}, u32[]{:S(2)}) collective-permute-start(f32[8,512]{1,0:T(8,128)S(1)} %get-tuple-element.52), channel_id=1, source_target_pairs={{0,2},{2,4},{4,6},{6,0},{1,3},{3,5},{5,7},{7,1},{8,10},{10,12},{12... | collective-permute-start | bytes 49160 | tf_op jit(solution)/shard_map/ppermute | solution.py:271
  143.0 6.8 %collective-permute-start.17 = (f32[8,512]{1,0:T(8,128)S(1)}, f32[8,512]{1,0:T(8,128)S(1)}, u32[]{:S(2)}, u32[]{:S(2)}) collective-permute-start(f32[8,512]{1,0:T(8,128)S(1)} %get-tuple-element.53), channel_id=1, source_target_pairs={{0,4},{2,6},{4,0},{6,2},{1,5},{3,7},{5,1},{7,3},{8,12},{10,14},{12... | collective-permute-start | bytes 49160 | tf_op jit(solution)/shard_map/ppermute | solution.py:271
  (5 other events, 26.2 us)

commit v9 on v8

--- a/solution.py
+++ b/solution.py
@@ -14,7 +14,7 @@
 COL = ("x", "core")
 ROW_AT, ROW_NEAR, COL_AT, SOURCE, PLACE, STAGE, LIVE, CROSSING, LATE = range(9)
 LAST_STAGE = 4
-PER_STAGE = 2
+LAST_TURN = 6
 BY_ROWS = (((1,), (0,)), ((), ()))
 BY_COLS = (((1,), (1,)), ((), ()))
 LOG2E = math.log2(math.e)
@@ -38,7 +38,7 @@
     width = ref.shape[-1]
     place = lax.broadcasted_iota(jnp.int32, (8, width), 0)
     parts = [
-        jnp.broadcast_to(ref[16 * q + snapshot : 16 * q + snapshot + 1, :], (8, width))
+        jnp.broadcast_to(ref[pl.ds(16 * q + snapshot, 1), :], (8, width))
         for q in range(3)
     ]
     norm = (-0.5 * LOG2E) * (parts[0] * parts[0] + parts[1] * parts[1] + parts[2] * parts[2])
@@ -110,10 +110,14 @@
             def _():
                 tile[...] = places[source][table[PLACE, slot]]
 
-        for snapshot in range(16):
-            high, mid, low = split3(rows_of(tile, snapshot, 1.0, 3, 4))
-            stacked = jnp.concatenate([high, mid, high, mid, low, high], axis=0)
-            cols[snapshot] = stacked.astype(jnp.bfloat16)
+        def stack(at, carry):
+            for snapshot in (at * 4, at * 4 + 1, at * 4 + 2, at * 4 + 3):
+                high, mid, low = split3(rows_of(tile, snapshot, 1.0, 3, 4))
+                stacked = jnp.concatenate([high, mid, high, mid, low, high], axis=0)
+                cols[snapshot] = stacked.astype(jnp.bfloat16)
+            return carry
+
+        lax.fori_loop(0, 4, stack, 0)
         row_at = table[ROW_AT, slot]
 
         @pl.when(formed >= 2)
@@ -292,18 +296,20 @@
 
 
 def gather_y(piece):
-    return jnp.stack([piece] + [shift(piece, "y", d) for d in range(1, lax.axis_size("y"))])
+    size = lax.axis_size("y")
+    near = [piece] + [shift(piece, "y", d) for d in range(1, size)]
+    return [jnp.stack(near[: size // 2]), jnp.stack(near[size // 2 :])]
 
 
 def gather_z(near):
-    size, half = lax.axis_size("z"), near.shape[0] // 2
-    arrived = [[near]]
-    behind = ahead = near
-    for distance in range(1, size // 2 + 1):
-        if distance == size // 2:
-            behind, ahead = behind[:half], ahead[half:]
-        behind, ahead = shift(behind, "z", 1), shift(ahead, "z", size - 1)
-        arrived.append([behind, ahead])
+    size = lax.axis_size("z")
+    arrived = [near]
+    behind, ahead = near, near
+    for distance in range(1, size // 2):
+        behind = [shift(half, "z", 1) for half in behind]
+        ahead = [shift(half, "z", size - 1) for half in ahead]
+        arrived.append(behind + ahead)
+    arrived.append([shift(behind[0], "z", 1), shift(ahead[1], "z", size - 1)])
     return arrived
 
 
@@ -317,12 +323,11 @@
         row, col, live = pairs[0, slot], pairs[1, slot], valid[0, slot] != 0
         behind = lax.rem(z - col // size_y + size_z, size_z)
         place = lax.rem(y - lax.rem(col, size_y) + size_y, size_y)
-        upper = place >= size_y // 2
-        far = jnp.where(upper, size_z, size_z - 1)
-        source = jnp.where(behind < size_z // 2, 2 * behind - 1, 2 * (size_z - behind))
-        source = jnp.where(behind == size_z // 2, far, source)
-        source = jnp.where(behind == 0, 0, source)
-        place = jnp.where((behind == size_z // 2) & upper, place - size_y // 2, place)
+        half = place // (size_y // 2)
+        place = place - half * (size_y // 2)
+        distance = jnp.minimum(behind, size_z - behind)
+        source = 4 * distance - 2 + half + jnp.where(behind > size_z // 2, 2, 0)
+        source = jnp.where(distance == 0, half, source)
         crossing = ((z * size_y + y) * tiles + row) != (col * tiles + 2 * x + core)
         near = jnp.where(lax.rem(row, 2) == core, 0, size_x)
         near = near + lax.rem(x - row // 2 + size_x, size_x)
@@ -333,8 +338,8 @@
         out[PLACE, slot] = place
         out[LIVE, slot] = jnp.where(live, 1, 0)
         out[CROSSING, slot] = jnp.where(live & crossing, 1, 0)
-        stage = jnp.where(live, (source + 1) // 2, LAST_STAGE)
-        arrival.append(jnp.maximum(PER_STAGE * stage - 1, 0))
+        stage = jnp.where(live, distance, LAST_STAGE)
+        arrival.append(jnp.where(stage == LAST_STAGE, LAST_TURN, stage))
         keys.append(stage * slots + slot)
     ranks = [
         sum(jnp.where(other <= key, 1, 0) for other in keys) for key in keys
@@ -345,7 +350,7 @@
             if other != slot:
                 wait = arrival[other] + ranks[slot] - ranks[other]
                 turn = jnp.maximum(turn, jnp.where(keys[other] <= keys[slot], wait, 0))
-        stage = jnp.minimum((turn + 1) // PER_STAGE, LAST_STAGE)
+        stage = jnp.where(turn < LAST_TURN, jnp.minimum(turn, LAST_STAGE - 1), LAST_STAGE)
         live = valid[0, slot] != 0
         out[STAGE, slot] = jnp.where(live, stage, -1)
         out[LATE, slot] = jnp.where(live & (stage == LAST_STAGE), 1, 0)

time: 181 us -> 186 us (1.028)
  waiting for transfers between devices: 18.2 us -> 25.1 us
  starting transfers between devices: 65.1 us -> 63.2 us
    all_to_all x2, waiting for transfers between devices: 7.57 us -> 13 us  [combine(): by_col = lax.all_to_all(col_acc, ROW, 0, 0, tiled=True)]
    all_to_all x2, starting transfers between devices: 15.3 us -> 11.8 us  [combine(): by_col = lax.all_to_all(col_acc, ROW, 0, 0, tiled=True)]
    ppermute x23 -> x29, starting transfers between devices: 41 us -> 43 us  [shift(): lax.ppermute(value, axis, [(i, (i + distance) % size) for i in range(size)])]
    ppermute x23 -> x29, waiting for transfers between devices: 9.57 us -> 10.5 us  [shift(): lax.ppermute(value, axis, [(i, (i + distance) % size) for i in range(size)])]
  transfers between devices with their start and end apart: 26 -> 32, of which waited for: 10 -> 11; matrix products, arithmetic and copies ran while one was open for 0% -> 0% of each run, Pallas kernels for 27% -> 25%
where the time goes in v9:
time: 186 us; the launch traced here: 184 us
  Pallas kernels  63.3 us (34%)
  starting transfers between devices  63.2 us (34%)
  blocking collectives  27.7 us (15%)
  waiting for transfers between devices  25.1 us (13%)
  local copies, waits for them, and re-layouts  3.68 us (2%)
    ppermute x29, starting transfers between devices, shift(): lax.ppermute(value, axis, [(i, (i + distance) % size) for i in range(size)])  43 us
    pallas_call x5, Pallas kernels, form_stage(): pl.pallas_call(functools.partial(stage_kernel, stage, len(places)), in_sp...  40.1 us
    all_to_all x2, blocking collectives, spread(): return lax.all_to_all(copies, axes, 0, 0, tiled=True)  27.7 us
    pallas_call x3, Pallas kernels, apply_tiles(): pl.pallas_call(functools.partial(apply_kernel, wanted, col_at), in_specs=...  16.1 us
    all_to_all x2, waiting for transfers between devices, combine(): by_col = lax.all_to_all(col_acc, ROW, 0, 0, tiled=True)  13 us
    all_to_all x2, starting transfers between devices, combine(): by_col = lax.all_to_all(col_acc, ROW, 0, 0, tiled=True)  11.8 us
    ppermute x29, waiting for transfers between devices, shift(): lax.ppermute(value, axis, [(i, (i + distance) % size) for i in range(size)])  10.5 us
    all_to_all x1, starting transfers between devices, spread(): return lax.all_to_all(copies, axes, 0, 0, tiled=True)  8.34 us
  transfers between devices with their start and end apart: 32, of which 11 were waited for; matrix products, arithmetic and copies ran while one was open for 0% of the time, Pallas kernels for 25%

profile of v9, /device:TPU:0, one launch (start us, length us, event | category | flops | bytes accessed | tf_op | source)
XLA Modules:
  0.0 184.5 jit_solution(15832582498474736699)
XLA Ops:
  1.7 2.7 %collective-permute-start.1 = (f32[56,512]{1,0:T(8,128)S(1)}, f32[56,512]{1,0:T(8,128)S(1)}, u32[]{:S(2)}, u32[]{:S(2)}) collective-permute-start(f32[56,512]{1,0:T(8,128)S(1)} %get-tuple-element.52), channel_id=1, source_target_pairs={{0,16},{8,24},{16,0},{24,8},{1,17},{9,25},{17,1},{25,9},{2,18},{10... | collective-permute-start | bytes 344072 | tf_op jit(solution)/shard_map/ppermute | solution.py:275
  10.1 5.6 %collective-permute-start.5 = (f32[2,56,512]{2,1,0:T(8,128)S(1)}, f32[2,56,512]{2,1,0:T(8,128)S(1)}, u32[]{:S(2)}, u32[]{:S(2)}) collective-permute-start(f32[2,56,512]{2,1,0:T(8,128)S(1)} %pad_maximum_fusion.refs_0_), channel_id=1, source_target_pairs={{0,224},{32,0},{64,32},{96,64},{128,96},{160,128},{192,160},{224,1... | collective-permute-start | bytes 688136 | tf_op jit(solution)/shard_map/ppermute | solution.py:275
  15.8 3.2 %collective-permute-start.6 = (f32[2,56,512]{2,1,0:T(8,128)S(1)}, f32[2,56,512]{2,1,0:T(8,128)S(1)}, u32[]{:S(2)}, u32[]{:S(2)}) collective-permute-start(f32[2,56,512]{2,1,0:T(8,128)S(1)} %pad_maximum_fusion.1.refs_1_), channel_id=1, source_target_pairs={{0,224},{32,0},{64,32},{96,64},{128,96},{160,128},{192,160},{224,1... | collective-permute-start | bytes 688136 | tf_op jit(solution)/shard_map/ppermute | solution.py:275
  20.1 5.1 %prepare_rows.1.prepared_ref = bf16[8,16,512,48]{3,2,1,0:T(8,128)(2,1)S(1)} custom-call(f32[48,4096]{1,0:T(8,128)S(1)} %bitcast.67), custom_call_target="tpu_custom_call" | custom-call | flops 100000000 | bytes 8388608 | tf_op jit(solution)/shard_map/prepare_rows/pallas_call | solution.py:66
  26.2 6.9 %collective-permute-start.9 = (f32[2,56,512]{2,1,0:T(8,128)S(1)}, f32[2,56,512]{2,1,0:T(8,128)S(1)}, u32[]{:S(2)}, u32[]{:S(2)}) collective-permute-start(f32[2,56,512]{2,1,0:T(8,128)S(1)} %collective-permute-done.5.refs_4_), channel_id=1, source_target_pairs={{0,224},{32,0},{64,32},{96,64},{128,96},{160,128},{192,160},{224,1... | collective-permute-start | bytes 688136 | tf_op jit(solution)/shard_map/ppermute | solution.py:275
  33.2 3.2 %collective-permute-start.10 = (f32[2,56,512]{2,1,0:T(8,128)S(1)}, f32[2,56,512]{2,1,0:T(8,128)S(1)}, u32[]{:S(2)}, u32[]{:S(2)}) collective-permute-start(f32[2,56,512]{2,1,0:T(8,128)S(1)} %collective-permute-done.6.refs_5_), channel_id=1, source_target_pairs={{0,224},{32,0},{64,32},{96,64},{128,96},{160,128},{192,160},{224,1... | collective-permute-start | bytes 688136 | tf_op jit(solution)/shard_map/ppermute | solution.py:275
  36.4 4.7 %form_1.1 = (bf16[10,512,512]{2,1,0:T(8,128)(2,1)}, bf16[10,512,512]{2,1,0:T(8,128)(2,1)}, f32[8,8,512]{2,1,0:T(8,128)S(1)}, f32[32,8,512]{2,1,0:T(8,128)S(1)}) custom-call(s32[9,10]{1,0:T(8,128)S(1)} %copy-done.2, bf16[8,16,512,48]{3,2,1,0:T(8,128)(2,1)S(1)} %prepare_rows.1.prepared_ref, ...), custom_call_target="tpu_custom_call", output_to_operand_aliasing={{0}: (9, {}), {1}: (10, {}), {2}: (11, {}), {3}: (12, {})} | custom-call | flops 8000000000 | bytes 8388608 | tf_op jit(solution)/shard_map/form_1/pallas_call | solution.py:191
  41.1 3.2 %collective-permute-start.13 = (f32[2,56,512]{2,1,0:T(8,128)S(1)}, f32[2,56,512]{2,1,0:T(8,128)S(1)}, u32[]{:S(2)}, u32[]{:S(2)}) collective-permute-start(f32[2,56,512]{2,1,0:T(8,128)S(1)} %collective-permute-done.9.refs_8_), channel_id=1, source_target_pairs={{0,224},{32,0},{64,32},{96,64},{128,96},{160,128},{192,160},{224,1... | collective-permute-start | bytes 688136 | tf_op jit(solution)/shard_map/ppermute | solution.py:275
  44.3 3.2 %collective-permute-start.14 = (f32[2,56,512]{2,1,0:T(8,128)S(1)}, f32[2,56,512]{2,1,0:T(8,128)S(1)}, u32[]{:S(2)}, u32[]{:S(2)}) collective-permute-start(f32[2,56,512]{2,1,0:T(8,128)S(1)} %collective-permute-done.10.refs_9_), channel_id=1, source_target_pairs={{0,224},{32,0},{64,32},{96,64},{128,96},{160,128},{192,160},{224,1... | collective-permute-start | bytes 688136 | tf_op jit(solution)/shard_map/ppermute | solution.py:275
  47.6 4.8 %form_2.1 = (bf16[10,512,512]{2,1,0:T(8,128)(2,1)}, bf16[10,512,512]{2,1,0:T(8,128)(2,1)}, f32[8,8,512]{2,1,0:T(8,128)S(1)}, f32[32,8,512]{2,1,0:T(8,128)S(1)}) custom-call(s32[9,10]{1,0:T(8,128)S(1)} %copy-done.2, ...), custom_call_target="tpu_custom_call", output_to_operand_aliasing={{0}: (13, {}), {1}: (14, {}), {2}: (15, {}), {3}: (16, {})} | custom-call | flops 8000000000 | bytes 8388608 | tf_op jit(solution)/shard_map/form_2/pallas_call | solution.py:191
  52.5 3.2 %collective-permute-start.16 = (f32[2,56,512]{2,1,0:T(8,128)S(1)}, f32[2,56,512]{2,1,0:T(8,128)S(1)}, u32[]{:S(2)}, u32[]{:S(2)}) collective-permute-start(f32[2,56,512]{2,1,0:T(8,128)S(1)} %collective-permute-done.14.refs_13_), channel_id=1, source_target_pairs={{0,224},{32,0},{64,32},{96,64},{128,96},{160,128},{192,160},{224,1... | collective-permute-start | bytes 688136 | tf_op jit(solution)/shard_map/ppermute | solution.py:275
  57.1 11.7 %form_3.1 = (bf16[10,512,512]{2,1,0:T(8,128)(2,1)}, bf16[10,512,512]{2,1,0:T(8,128)(2,1)}, f32[8,8,512]{2,1,0:T(8,128)S(1)}, f32[32,8,512]{2,1,0:T(8,128)S(1)}) custom-call(s32[9,10]{1,0:T(8,128)S(1)} %copy-done.2, ...), custom_call_target="tpu_custom_call", output_to_operand_aliasing={{0}: (17, {}), {1}: (18, {}), {2}: (19, {}), {3}: (20, {})} | custom-call | flops 8000000000 | bytes 8388608 | tf_op jit(solution)/shard_map/form_3/pallas_call | solution.py:191
  68.8 17.9 %form_4.1 = (bf16[10,512,512]{2,1,0:T(8,128)(2,1)}, bf16[10,512,512]{2,1,0:T(8,128)(2,1)}, f32[10,8,512]{2,1,0:T(8,128)S(1)}, f32[32,8,512]{2,1,0:T(8,128)}) custom-call(s32[9,10]{1,0:T(8,128)S(1)} %copy-done.2, bf16[8,16,512,48]{3,2,1,0:T(8,128)(2,1)S(1)} %prepare_rows.1.prepared_ref, ...), custom_call_target="tpu_custom_call", output_to_operand_aliasing={{0}: (19, {}), {1}: (20, {})} | custom-call | flops 8000000000 | bytes 8388608 | tf_op jit(solution)/shard_map/form_4/pallas_call | solution.py:191
  86.7 4.1 %all-to-all-start = ((f32[32,8,512]{2,1,0:T(8,128)}), f32[32,8,512]{2,1,0:T(8,128)S(1)}, u32[]{:S(2)}, u32[]{:S(2)}) async-start(f32[32,8,512]{2,1,0:T(8,128)} %get-tuple-element.50), calls=%async_computation | async-start | bytes 1048576 | tf_op jit(solution)/shard_map/all_to_all | solution.py:375
  90.9 4.1 %apply_late.1 = f32[8,8,512]{2,1,0:T(8,128)S(1)} custom-call(s32[9,10]{1,0:T(8,128)S(1)} %copy-done.2, bf16[10,512,512]{2,1,0:T(8,128)(2,1)} %get-tuple-element.47.high_ref, bf16[10,512,512]{2,1,0:T(8,128)(2,1)} %get-tuple-element.48.low_ref, f32[10,8,512]{2,1,0:T(8,128)S(1)} %get-tuple-element.49.field, f32[8,8,512]{2,1,0:T(8,128)S(1)} %get-tuple-element.45.refs_18_.refs_0_), custom_call_target="tpu_custom_call" | custom-call | flops 3000000000 | bytes 12582912 | tf_op jit(solution)/shard_map/apply_late/pallas_call | solution.py:255
  98.5 6.1 %all-to-all-done = f32[32,8,512]{2,1,0:T(8,128)S(1)} async-done(((f32[32,8,512]{2,1,0:T(8,128)}), f32[32,8,512]{2,1,0:T(8,128)S(1)}, u32[]{:S(2)}, u32[]{:S(2)}) %all-to-all-start) | async-done | bytes 524320 | tf_op jit(solution)/shard_map/all_to_all | solution.py:375
  105.6 8.3 %all-to-all-start.1 = ((f32[32,8,512]{2,1,0:T(8,128)}), f32[32,8,512]{2,1,0:T(8,128)S(1)}, u32[]{:S(2)}, u32[]{:S(2)}) async-start(f32[32,8,512]{2,1,0:T(8,128)} %broadcast_in_dim.13), calls=%async_computation.1 | async-start | bytes 1048576 | tf_op jit(solution)/shard_map/all_to_all | solution.py:280
  116.7 2.5 %collective-permute-start.26 = (f32[2,8,512]{2,1,0:T(8,128)S(1)}, f32[2,8,512]{2,1,0:T(8,128)S(1)}, u32[]{:S(2)}, u32[]{:S(2)}) collective-permute-start(f32[2,8,512]{2,1,0:T(8,128)S(1)} %get-tuple-element.60), channel_id=1, source_target_pairs={{0,2},{2,4},{4,6},{6,0},{1,3},{3,5},{5,7},{7,1},{8,10},{10,12},{12... | collective-permute-start | bytes 98312 | tf_op jit(solution)/shard_map/ppermute | solution.py:275
  123.2 5.9 %apply_cols.1 = f32[32,8,512]{2,1,0:T(8,128)} custom-call(s32[9,10]{1,0:T(8,128)S(1)} %copy-done.2, bf16[10,512,512]{2,1,0:T(8,128)(2,1)} %get-tuple-element.47.high_ref, bf16[10,512,512]{2,1,0:T(8,128)(2,1)} %get-tuple-element.48.low_ref, f32[8,8,512]{2,1,0:T(8,128)S(1)} %bitcast.68), custom_call_target="tpu_custom_call" | custom-call | flops 3000000000 | bytes 12582912 | tf_op jit(solution)/shard_map/apply_cols/pallas_call | solution.py:255
  130.7 7.7 %all-to-all-start.2 = ((f32[32,8,512]{2,1,0:T(8,128)}), f32[32,8,512]{2,1,0:T(8,128)S(1)}, u32[]{:S(2)}, u32[]{:S(2)}) async-start(f32[32,8,512]{2,1,0:T(8,128)} %apply_cols.1), calls=%async_computation.2 | async-start | bytes 1048576 | tf_op jit(solution)/shard_map/all_to_all | solution.py:375
  138.3 6.1 %apply_rows.1 = f32[8,8,512]{2,1,0:T(8,128)S(1)} custom-call(s32[9,10]{1,0:T(8,128)S(1)} %copy-done.2, bf16[10,512,512]{2,1,0:T(8,128)(2,1)} %get-tuple-element.47.high_ref, bf16[10,512,512]{2,1,0:T(8,128)(2,1)} %get-tuple-element.48.low_ref, f32[32,8,512]{2,1,0:T(8,128)S(1)} %all-to-all-done.1.field), custom_call_target="tpu_custom_call" | custom-call | flops 3000000000 | bytes 12582912 | tf_op jit(solution)/shard_map/apply_rows/pallas_call | solution.py:255
  148.8 6.9 %all-to-all-done.2 = f32[32,8,512]{2,1,0:T(8,128)S(1)} async-done(((f32[32,8,512]{2,1,0:T(8,128)}), f32[32,8,512]{2,1,0:T(8,128)S(1)}, u32[]{:S(2)}, u32[]{:S(2)}) %all-to-all-start.2) | async-done | bytes 524320 | tf_op jit(solution)/shard_map/all_to_all | solution.py:375
  155.8 9.2 %all_to_all.25 = f32[8,8,512]{2,1,0:T(8,128)S(1)} all-to-all(f32[8,8,512]{2,1,0:T(8,128)S(1)} %broadcast_in_dim.14), channel_id=1, replica_groups=mesh['z'=8,'y'=4,'x'=4,'core'=2] {'x','core'}, dimensions={0} | all-to-all | bytes 262144 | tf_op jit(solution)/shard_map/all_to_all | solution.py:280
  165.2 18.5 %all_to_all.26 = f32[32,1,128]{2,1,0:T(1,128)S(1)} all-to-all(f32[32,1,128]{2,1,0:T(1,128)S(1)} %broadcast_in_dim.16), channel_id=1, replica_groups=mesh['z'=8,'y'=4,'x'=4,'core'=2] {'z','y'}, dimensions={0} | all-to-all | bytes 32768 | tf_op jit(solution)/shard_map/all_to_all | solution.py:280
  (84 shorter events, 28.9 us)
Async XLA Ops:
  1.6 8.4 %collective-permute-start = (f32[56,512]{1,0:T(8,128)S(1)}, f32[56,512]{1,0:T(8,128)S(1)}, u32[]{:S(2)}, u32[]{:S(2)}) collective-permute-start(f32[56,512]{1,0:T(8,128)S(1)} %get-tuple-element.52), channel_id=1, source_target_pairs={{0,8},{8,16},{16,24},{24,0},{1,9},{9,17},{17,25},{25,1},{2,10},{10... | collective-permute-start | bytes 344072 | tf_op jit(solution)/shard_map/ppermute | solution.py:275
  1.7 8.3 %collective-permute-start.1 = (f32[56,512]{1,0:T(8,128)S(1)}, f32[56,512]{1,0:T(8,128)S(1)}, u32[]{:S(2)}, u32[]{:S(2)}) collective-permute-start(f32[56,512]{1,0:T(8,128)S(1)} %get-tuple-element.52), channel_id=1, source_target_pairs={{0,16},{8,24},{16,0},{24,8},{1,17},{9,25},{17,1},{25,9},{2,18},{10... | collective-permute-start | bytes 344072 | tf_op jit(solution)/shard_map/ppermute | solution.py:275
  10.1 16.1 %collective-permute-start.5 = (f32[2,56,512]{2,1,0:T(8,128)S(1)}, f32[2,56,512]{2,1,0:T(8,128)S(1)}, u32[]{:S(2)}, u32[]{:S(2)}) collective-permute-start(f32[2,56,512]{2,1,0:T(8,128)S(1)} %pad_maximum_fusion.refs_0_), channel_id=1, source_target_pairs={{0,224},{32,0},{64,32},{96,64},{128,96},{160,128},{192,160},{224,1... | collective-permute-start | bytes 688136 | tf_op jit(solution)/shard_map/ppermute | solution.py:275
  15.7 17.4 %collective-permute-start.3 = (f32[2,56,512]{2,1,0:T(8,128)S(1)}, f32[2,56,512]{2,1,0:T(8,128)S(1)}, u32[]{:S(2)}, u32[]{:S(2)}) collective-permute-start(f32[2,56,512]{2,1,0:T(8,128)S(1)} %pad_maximum_fusion.refs_0_), channel_id=1, source_target_pairs={{0,32},{32,64},{64,96},{96,128},{128,160},{160,192},{192,224},{224... | collective-permute-start | bytes 688136 | tf_op jit(solution)/shard_map/ppermute | solution.py:275
  15.8 17.4 %collective-permute-start.6 = (f32[2,56,512]{2,1,0:T(8,128)S(1)}, f32[2,56,512]{2,1,0:T(8,128)S(1)}, u32[]{:S(2)}, u32[]{:S(2)}) collective-permute-start(f32[2,56,512]{2,1,0:T(8,128)S(1)} %pad_maximum_fusion.1.refs_1_), channel_id=1, source_target_pairs={{0,224},{32,0},{64,32},{96,64},{128,96},{160,128},{192,160},{224,1... | collective-permute-start | bytes 688136 | tf_op jit(solution)/shard_map/ppermute | solution.py:275
  19.0 17.4 %collective-permute-start.4 = (f32[2,56,512]{2,1,0:T(8,128)S(1)}, f32[2,56,512]{2,1,0:T(8,128)S(1)}, u32[]{:S(2)}, u32[]{:S(2)}) collective-permute-start(f32[2,56,512]{2,1,0:T(8,128)S(1)} %pad_maximum_fusion.1.refs_1_), channel_id=1, source_target_pairs={{0,32},{32,64},{64,96},{96,128},{128,160},{160,192},{192,224},{224... | collective-permute-start | bytes 688136 | tf_op jit(solution)/shard_map/ppermute | solution.py:275
  26.2 14.9 %collective-permute-start.9 = (f32[2,56,512]{2,1,0:T(8,128)S(1)}, f32[2,56,512]{2,1,0:T(8,128)S(1)}, u32[]{:S(2)}, u32[]{:S(2)}) collective-permute-start(f32[2,56,512]{2,1,0:T(8,128)S(1)} %collective-permute-done.5.refs_4_), channel_id=1, source_target_pairs={{0,224},{32,0},{64,32},{96,64},{128,96},{160,128},{192,160},{224,1... | collective-permute-start | bytes 688136 | tf_op jit(solution)/shard_map/ppermute | solution.py:275
  33.2 11.2 %collective-permute-start.7 = (f32[2,56,512]{2,1,0:T(8,128)S(1)}, f32[2,56,512]{2,1,0:T(8,128)S(1)}, u32[]{:S(2)}, u32[]{:S(2)}) collective-permute-start(f32[2,56,512]{2,1,0:T(8,128)S(1)} %collective-permute-done.3.refs_2_), channel_id=1, source_target_pairs={{0,32},{32,64},{64,96},{96,128},{128,160},{160,192},{192,224},{224... | collective-permute-start | bytes 688136 | tf_op jit(solution)/shard_map/ppermute | solution.py:275
  33.2 11.2 %collective-permute-start.10 = (f32[2,56,512]{2,1,0:T(8,128)S(1)}, f32[2,56,512]{2,1,0:T(8,128)S(1)}, u32[]{:S(2)}, u32[]{:S(2)}) collective-permute-start(f32[2,56,512]{2,1,0:T(8,128)S(1)} %collective-permute-done.6.refs_5_), channel_id=1, source_target_pairs={{0,224},{32,0},{64,32},{96,64},{128,96},{160,128},{192,160},{224,1... | collective-permute-start | bytes 688136 | tf_op jit(solution)/shard_map/ppermute | solution.py:275
  36.4 11.2 %collective-permute-start.8 = (f32[2,56,512]{2,1,0:T(8,128)S(1)}, f32[2,56,512]{2,1,0:T(8,128)S(1)}, u32[]{:S(2)}, u32[]{:S(2)}) collective-permute-start(f32[2,56,512]{2,1,0:T(8,128)S(1)} %collective-permute-done.4.refs_3_), channel_id=1, source_target_pairs={{0,32},{32,64},{64,96},{96,128},{128,160},{160,192},{192,224},{224... | collective-permute-start | bytes 688136 | tf_op jit(solution)/shard_map/ppermute | solution.py:275
  41.1 14.6 %collective-permute-start.13 = (f32[2,56,512]{2,1,0:T(8,128)S(1)}, f32[2,56,512]{2,1,0:T(8,128)S(1)}, u32[]{:S(2)}, u32[]{:S(2)}) collective-permute-start(f32[2,56,512]{2,1,0:T(8,128)S(1)} %collective-permute-done.9.refs_8_), channel_id=1, source_target_pairs={{0,224},{32,0},{64,32},{96,64},{128,96},{160,128},{192,160},{224,1... | collective-permute-start | bytes 688136 | tf_op jit(solution)/shard_map/ppermute | solution.py:275
  44.3 8.1 %collective-permute-start.11 = (f32[2,56,512]{2,1,0:T(8,128)S(1)}, f32[2,56,512]{2,1,0:T(8,128)S(1)}, u32[]{:S(2)}, u32[]{:S(2)}) collective-permute-start(f32[2,56,512]{2,1,0:T(8,128)S(1)} %collective-permute-done.7.refs_6_), channel_id=1, source_target_pairs={{0,32},{32,64},{64,96},{96,128},{128,160},{160,192},{192,224},{224... | collective-permute-start | bytes 688136 | tf_op jit(solution)/shard_map/ppermute | solution.py:275
  44.3 8.2 %collective-permute-start.14 = (f32[2,56,512]{2,1,0:T(8,128)S(1)}, f32[2,56,512]{2,1,0:T(8,128)S(1)}, u32[]{:S(2)}, u32[]{:S(2)}) collective-permute-start(f32[2,56,512]{2,1,0:T(8,128)S(1)} %collective-permute-done.10.refs_9_), channel_id=1, source_target_pairs={{0,224},{32,0},{64,32},{96,64},{128,96},{160,128},{192,160},{224,1... | collective-permute-start | bytes 688136 | tf_op jit(solution)/shard_map/ppermute | solution.py:275
  47.6 9.5 %collective-permute-start.12 = (f32[2,56,512]{2,1,0:T(8,128)S(1)}, f32[2,56,512]{2,1,0:T(8,128)S(1)}, u32[]{:S(2)}, u32[]{:S(2)}) collective-permute-start(f32[2,56,512]{2,1,0:T(8,128)S(1)} %collective-permute-done.8.refs_7_), channel_id=1, source_target_pairs={{0,32},{32,64},{64,96},{96,128},{128,160},{160,192},{192,224},{224... | collective-permute-start | bytes 688136 | tf_op jit(solution)/shard_map/ppermute | solution.py:275
  52.4 16.4 %collective-permute-start.15 = (f32[2,56,512]{2,1,0:T(8,128)S(1)}, f32[2,56,512]{2,1,0:T(8,128)S(1)}, u32[]{:S(2)}, u32[]{:S(2)}) collective-permute-start(f32[2,56,512]{2,1,0:T(8,128)S(1)} %collective-permute-done.11.refs_10_), channel_id=1, source_target_pairs={{0,32},{32,64},{64,96},{96,128},{128,160},{160,192},{192,224},{224... | collective-permute-start | bytes 688136 | tf_op jit(solution)/shard_map/ppermute | solution.py:275
  52.5 16.3 %collective-permute-start.16 = (f32[2,56,512]{2,1,0:T(8,128)S(1)}, f32[2,56,512]{2,1,0:T(8,128)S(1)}, u32[]{:S(2)}, u32[]{:S(2)}) collective-permute-start(f32[2,56,512]{2,1,0:T(8,128)S(1)} %collective-permute-done.14.refs_13_), channel_id=1, source_target_pairs={{0,224},{32,0},{64,32},{96,64},{128,96},{160,128},{192,160},{224,1... | collective-permute-start | bytes 688136 | tf_op jit(solution)/shard_map/ppermute | solution.py:275
  86.7 17.9 %all-to-all-start = ((f32[32,8,512]{2,1,0:T(8,128)}), f32[32,8,512]{2,1,0:T(8,128)S(1)}, u32[]{:S(2)}, u32[]{:S(2)}) async-start(f32[32,8,512]{2,1,0:T(8,128)} %get-tuple-element.50), calls=%async_computation | async-start | bytes 1048576 | tf_op jit(solution)/shard_map/all_to_all | solution.py:375
  96.4 8.3 %collective-permute-start.18 = (f32[8,512]{1,0:T(8,128)S(1)}, f32[8,512]{1,0:T(8,128)S(1)}, u32[]{:S(2)}, u32[]{:S(2)}) collective-permute-start(f32[8,512]{1,0:T(8,128)S(1)} %get-tuple-element.56), channel_id=1, source_target_pairs={{0,6},{2,0},{4,2},{6,4},{1,7},{3,1},{5,3},{7,5},{8,14},{10,8},{12,... | collective-permute-start | bytes 49160 | tf_op jit(solution)/shard_map/ppermute | solution.py:275
  96.4 8.2 %collective-permute-start.20 = (f32[8,512]{1,0:T(8,128)S(1)}, f32[8,512]{1,0:T(8,128)S(1)}, u32[]{:S(2)}, u32[]{:S(2)}) collective-permute-start(f32[8,512]{1,0:T(8,128)S(1)} %get-tuple-element.57), channel_id=1, source_target_pairs={{0,2},{2,4},{4,6},{6,0},{1,3},{3,5},{5,7},{7,1},{8,10},{10,12},{12... | collective-permute-start | bytes 49160 | tf_op jit(solution)/shard_map/ppermute | solution.py:275
  105.6 25.1 %all-to-all-start.1 = ((f32[32,8,512]{2,1,0:T(8,128)}), f32[32,8,512]{2,1,0:T(8,128)S(1)}, u32[]{:S(2)}, u32[]{:S(2)}) async-start(f32[32,8,512]{2,1,0:T(8,128)} %broadcast_in_dim.13), calls=%async_computation.1 | async-start | bytes 1048576 | tf_op jit(solution)/shard_map/all_to_all | solution.py:280
  130.7 25.0 %all-to-all-start.2 = ((f32[32,8,512]{2,1,0:T(8,128)}), f32[32,8,512]{2,1,0:T(8,128)S(1)}, u32[]{:S(2)}, u32[]{:S(2)}) async-start(f32[32,8,512]{2,1,0:T(8,128)} %apply_cols.1), calls=%async_computation.2 | async-start | bytes 1048576 | tf_op jit(solution)/shard_map/all_to_all | solution.py:375
  145.9 9.8 %collective-permute-start.22 = (f32[8,512]{1,0:T(8,128)S(1)}, f32[8,512]{1,0:T(8,128)S(1)}, u32[]{:S(2)}, u32[]{:S(2)}) collective-permute-start(f32[8,512]{1,0:T(8,128)S(1)} %get-tuple-element.53), channel_id=1, source_target_pairs={{0,6},{2,0},{4,2},{6,4},{1,7},{3,1},{5,3},{7,5},{8,14},{10,8},{12,... | collective-permute-start | bytes 49160 | tf_op jit(solution)/shard_map/ppermute | solution.py:275
  147.2 8.5 %collective-permute-start.24 = (f32[8,512]{1,0:T(8,128)S(1)}, f32[8,512]{1,0:T(8,128)S(1)}, u32[]{:S(2)}, u32[]{:S(2)}) collective-permute-start(f32[8,512]{1,0:T(8,128)S(1)} %get-tuple-element.54), channel_id=1, source_target_pairs={{0,2},{2,4},{4,6},{6,0},{1,3},{3,5},{5,7},{7,1},{8,10},{10,12},{12... | collective-permute-start | bytes 49160 | tf_op jit(solution)/shard_map/ppermute | solution.py:275
  148.0 7.8 %collective-permute-start.23 = (f32[8,512]{1,0:T(8,128)S(1)}, f32[8,512]{1,0:T(8,128)S(1)}, u32[]{:S(2)}, u32[]{:S(2)}) collective-permute-start(f32[8,512]{1,0:T(8,128)S(1)} %get-tuple-element.55), channel_id=1, source_target_pairs={{0,4},{2,6},{4,0},{6,2},{1,5},{3,7},{5,1},{7,3},{8,12},{10,14},{12... | collective-permute-start | bytes 49160 | tf_op jit(solution)/shard_map/ppermute | solution.py:275
  (11 other events, 61.8 us)

commit v10 on v8

--- a/solution.py
+++ b/solution.py
@@ -87,20 +87,17 @@
 def stage_kernel(stage, sources, table, prepared_ref, row_vec, *refs):
     places = refs[:sources]
     last = stage == LAST_STAGE
-    high_ref, low_ref, rows_out, col_acc, tile, cols, high_tile, low_tile, sems = refs[-9:]
+    pair_ref, rows_out, col_acc, tile, cols, pair, sems = refs[-7:]
     if stage == 0:
         rows_out[...] = jnp.zeros_like(rows_out)
         col_acc[...] = jnp.zeros_like(col_acc)
     else:
         if not last:
-            rows_out[...] = refs[sources + 2][...]
-        col_acc[...] = refs[sources + 3][...]
-
-    def copies(slot, buffer):
-        return [
-            pltpu.make_async_copy(high_tile.at[buffer], high_ref.at[slot], sems.at[0, buffer]),
-            pltpu.make_async_copy(low_tile.at[buffer], low_ref.at[slot], sems.at[1, buffer]),
-        ]
+            rows_out[...] = refs[sources + 1][...]
+        col_acc[...] = refs[sources + 2][...]
+
+    def copy(slot, buffer):
+        return pltpu.make_async_copy(pair.at[buffer], pair_ref.at[slot], sems.at[buffer])
 
     def form(slot, formed):
         buffer = lax.rem(formed, 2)
@@ -118,8 +115,7 @@
 
         @pl.when(formed >= 2)
         def _():
-            for copy in copies(slot, buffer):
-                copy.wait()
+            copy(slot, buffer).wait()
 
         def step(at, carry):
             part = pl.ds(pl.multiple_of(at * HALF, HALF), HALF)
@@ -133,24 +129,23 @@
                 term = jnp.exp2(exponent)
                 total = term if total is None else total + term
             high = total.astype(jnp.bfloat16)
-            high_tile[buffer, :, part] = high
-            low_tile[buffer, :, part] = (total - high.astype(jnp.float32)).astype(jnp.bfloat16)
+            pair[buffer, 0, :, part] = high
+            pair[buffer, 1, :, part] = (total - high.astype(jnp.float32)).astype(jnp.bfloat16)
             return carry
 
         lax.fori_loop(0, TILE // HALF, step, 0)
-        for copy in copies(slot, buffer):
-            copy.start()
+        copy(slot, buffer).start()
         if last:
             rows_out[slot] = tile[48:56, :]
         else:
             rows_out[table[ROW_NEAR, slot]] += multiply(
-                tile[48:56, :], high_tile[buffer], low_tile[buffer], BY_COLS
+                tile[48:56, :], pair[buffer, 0], pair[buffer, 1], BY_COLS
             )
 
         @pl.when(table[CROSSING, slot] != 0)
         def _():
             col_acc[table[COL_AT, slot]] += multiply(
-                row_vec[row_at], high_tile[buffer], low_tile[buffer], BY_ROWS
+                row_vec[row_at], pair[buffer, 0], pair[buffer, 1], BY_ROWS
             )
 
     def visit(slot, formed):
@@ -162,13 +157,12 @@
 
         return formed + jnp.where(mine, 1, 0)
 
-    formed = lax.fori_loop(0, high_ref.shape[0], visit, 0)
+    formed = lax.fori_loop(0, pair_ref.shape[0], visit, 0)
     for back in (1, 2):
 
         @pl.when(formed >= back)
         def _():
-            for copy in copies(0, lax.rem(formed + back, 2)):
-                copy.wait()
+            copy(0, lax.rem(formed + back, 2)).wait()
 
 
 def form_stage(stage, table, prepared, row_vec, places, state, blocks):
@@ -176,8 +170,7 @@
     vmem = pl.BlockSpec(memory_space=pltpu.VMEM)
     hbm = pl.BlockSpec(memory_space=pltpu.HBM)
     shapes = [
-        pltpu.HBM((slots, TILE, TILE), jnp.bfloat16),
-        pltpu.HBM((slots, TILE, TILE), jnp.bfloat16),
+        pltpu.HBM((slots, 2, TILE, TILE), jnp.bfloat16),
         jax.ShapeDtypeStruct(
             (slots if stage == LAST_STAGE else row_vec.shape[0], 8, TILE), jnp.float32
         ),
@@ -188,18 +181,17 @@
         functools.partial(stage_kernel, stage, len(places)),
         in_specs=[pl.BlockSpec(memory_space=pltpu.SMEM)]
         + [vmem] * (2 + len(places))
-        + ([hbm, hbm, vmem, vmem] if state else []),
-        out_specs=[hbm, hbm, vmem, vmem],
+        + ([hbm, vmem, vmem] if state else []),
+        out_specs=[hbm, vmem, vmem],
         out_shape=shapes,
         input_output_aliases={
-            first + i: i for i in range(2 if stage == LAST_STAGE else len(state))
+            first + i: i for i in range(1 if stage == LAST_STAGE else len(state))
         },
         scratch_shapes=[
             pltpu.VMEM((56, TILE), jnp.float32),
             pltpu.VMEM((16, DEPTH, TILE), jnp.bfloat16),
-            pltpu.VMEM((2, TILE, TILE), jnp.bfloat16),
-            pltpu.VMEM((2, TILE, TILE), jnp.bfloat16),
-            pltpu.SemaphoreType.DMA((2, 2)),
+            pltpu.VMEM((2, 2, TILE, TILE), jnp.bfloat16),
+            pltpu.SemaphoreType.DMA((2,)),
         ],
         compiler_params=pltpu.CompilerParams(vmem_limit_bytes=8 << 20),
         cost_estimate=pl.CostEstimate(
@@ -209,61 +201,55 @@
     )(table, prepared, row_vec, *places, *state)
 
 
-def apply_kernel(wanted, col_at, table, high_ref, low_ref, field, *refs):
-    acc, high, low, sems = refs[-4:]
-    slots = high_ref.shape[0]
-
-    def copies(slot):
-        return [
-            pltpu.make_async_copy(high_ref.at[slot], high.at[slot], sems.at[0, slot]),
-            pltpu.make_async_copy(low_ref.at[slot], low.at[slot], sems.at[1, slot]),
-        ]
+def apply_kernel(wanted, col_at, table, pair_ref, field, *refs):
+    acc, pair, sems = refs[-3:]
+    slots = pair_ref.shape[0]
+
+    def copy(slot):
+        return pltpu.make_async_copy(pair_ref.at[slot], pair.at[slot], sems.at[slot])
 
     for slot in range(slots):
 
         @pl.when(table[wanted, slot] != 0)
         def _():
-            for copy in copies(slot):
-                copy.start()
-
-    acc[...] = jnp.zeros_like(acc) if len(refs) == 4 else refs[0][...]
+            copy(slot).start()
+
+    acc[...] = jnp.zeros_like(acc) if len(refs) == 3 else refs[0][...]
 
     def visit(slot, carry):
         @pl.when(table[wanted, slot] != 0)
         def _():
-            for copy in copies(slot):
-                copy.wait()
+            copy(slot).wait()
             row = table[ROW_NEAR, slot]
             col = slot if col_at is None else table[col_at, slot]
             if wanted != CROSSING:
-                acc[row] += multiply(field[col], high[slot], low[slot], BY_COLS)
+                acc[row] += multiply(field[col], pair[slot, 0], pair[slot, 1], BY_COLS)
             else:
-                acc[col] += multiply(field[row], high[slot], low[slot], BY_ROWS)
+                acc[col] += multiply(field[row], pair[slot, 0], pair[slot, 1], BY_ROWS)
 
         return carry
 
     lax.fori_loop(0, slots, visit, 0)
 
 
-def apply_tiles(wanted, col_at, name, table, high, low, field, count, start=()):
+def apply_tiles(wanted, col_at, name, table, pair, field, count, start=()):
     vmem = pl.BlockSpec(memory_space=pltpu.VMEM)
     hbm = pl.BlockSpec(memory_space=pltpu.HBM)
     return pl.pallas_call(
         functools.partial(apply_kernel, wanted, col_at),
-        in_specs=[pl.BlockSpec(memory_space=pltpu.SMEM), hbm, hbm, vmem] + [vmem] * len(start),
+        in_specs=[pl.BlockSpec(memory_space=pltpu.SMEM), hbm, vmem] + [vmem] * len(start),
         out_specs=vmem,
         out_shape=jax.ShapeDtypeStruct((count, 8, TILE), jnp.float32),
         scratch_shapes=[
-            pltpu.VMEM(high.shape, high.dtype),
-            pltpu.VMEM(low.shape, low.dtype),
-            pltpu.SemaphoreType.DMA((2, high.shape[0])),
+            pltpu.VMEM(pair.shape, pair.dtype),
+            pltpu.SemaphoreType.DMA((pair.shape[0],)),
         ],
         compiler_params=pltpu.CompilerParams(vmem_limit_bytes=16 << 20),
         cost_estimate=pl.CostEstimate(
             flops=3 * 10**9, bytes_accessed=12 << 20, transcendentals=0
         ),
         name=name,
-    )(table, in_hbm(high), in_hbm(low), field, *start)
+    )(table, in_hbm(pair), field, *start)
 
 
 def shift(value, axis, distance):
@@ -396,15 +382,15 @@
         places = places + arrived
         early = state
         state = form_stage(stage, table, prepared, row_vec, places, state, blocks)
-    high, low, slot_vec, col_acc = state
+    pair, slot_vec, col_acc = state
     row_acc = apply_tiles(
-        LATE, None, "apply_late", table, high, low, slot_vec, tiles, (early[2],)
+        LATE, None, "apply_late", table, pair, slot_vec, tiles, (early[1],)
     )
     first = combine(row_acc, col_acc)
 
     col_vec = spread(first, ROW)
-    col_acc = apply_tiles(CROSSING, COL_AT, "apply_cols", table, high, low, spread_near(first), blocks)
-    row_acc = apply_tiles(LIVE, COL_AT, "apply_rows", table, high, low, col_vec, tiles)
+    col_acc = apply_tiles(CROSSING, COL_AT, "apply_cols", table, pair, spread_near(first), blocks)
+    row_acc = apply_tiles(LIVE, COL_AT, "apply_rows", table, pair, col_vec, tiles)
     second = combine(row_acc, col_acc)
 
     rows = spread(second, COL)

time: 181 us -> 178 us (0.983)
  starting transfers between devices: 65.1 us -> 59.4 us
  waiting for transfers between devices: 18.2 us -> 21.9 us
    ppermute x23, starting transfers between devices: 41 us -> 34.6 us  [shift(): lax.ppermute(value, axis, [(i, (i + distance) % size) for i in range(size)])]
    all_to_all x2, waiting for transfers between devices: 7.57 us -> 11.1 us  [combine(): by_col = lax.all_to_all(col_acc, ROW, 0, 0, tiled=True)]
    all_to_all x2, starting transfers between devices: 15.3 us -> 17.2 us  [combine(): by_col = lax.all_to_all(col_acc, ROW, 0, 0, tiled=True)]
  transfers between devices with their start and end apart: 26 -> 26, of which waited for: 10 -> 11; matrix products, arithmetic and copies ran while one was open for 0% -> 0% of each run, Pallas kernels for 27% -> 29%
where the time goes in v10:
time: 178 us; the launch traced here: 176 us
  Pallas kernels  62.4 us (35%)
  starting transfers between devices  59.4 us (33%)
  blocking collectives  26.6 us (15%)
  waiting for transfers between devices  21.9 us (12%)
  local copies, waits for them, and re-layouts  3.78 us (2%)
    pallas_call x5, Pallas kernels, form_stage(): pl.pallas_call(functools.partial(stage_kernel, stage, len(places)), in_sp...  40.1 us
    ppermute x23, starting transfers between devices, shift(): lax.ppermute(value, axis, [(i, (i + distance) % size) for i in range(size)])  34.6 us
    all_to_all x2, blocking collectives, spread(): return lax.all_to_all(copies, axes, 0, 0, tiled=True)  26.6 us
    all_to_all x2, starting transfers between devices, combine(): by_col = lax.all_to_all(col_acc, ROW, 0, 0, tiled=True)  17.2 us
    pallas_call x3, Pallas kernels, apply_tiles(): pl.pallas_call(functools.partial(apply_kernel, wanted, col_at), in_specs=...  15.1 us
    all_to_all x2, waiting for transfers between devices, combine(): by_col = lax.all_to_all(col_acc, ROW, 0, 0, tiled=True)  11.1 us
    ppermute x23, waiting for transfers between devices, shift(): lax.ppermute(value, axis, [(i, (i + distance) % size) for i in range(size)])  9.16 us
    all_to_all x1, starting transfers between devices, spread(): return lax.all_to_all(copies, axes, 0, 0, tiled=True)  7.63 us
  transfers between devices with their start and end apart: 26, of which 11 were waited for; matrix products, arithmetic and copies ran while one was open for 0% of the time, Pallas kernels for 29%

profile of v10, /device:TPU:0, one launch (start us, length us, event | category | flops | bytes accessed | tf_op | source)
XLA Modules:
  0.0 175.6 jit_solution(8498545293763858086)
XLA Ops:
  3.9 2.6 %collective-permute-start.2 = (f32[56,512]{1,0:T(8,128)S(1)}, f32[56,512]{1,0:T(8,128)S(1)}, u32[]{:S(2)}, u32[]{:S(2)}) collective-permute-start(f32[56,512]{1,0:T(8,128)S(1)} %get-tuple-element.40), channel_id=1, source_target_pairs={{0,24},{8,0},{16,8},{24,16},{1,25},{9,1},{17,9},{25,17},{2,26},{10... | collective-permute-start | bytes 344072 | tf_op jit(solution)/shard_map/ppermute | solution.py:257
  6.5 2.0 %slot_table.1.table = s32[9,10]{1,0:T(8,128)} custom-call(s32[2,10]{1,0:T(2,128)} %bitcast.77, s32[1,10]{1,0:T(1,128)} %bitcast.79), custom_call_target="tpu_custom_call" | custom-call | tf_op jit(solution)/shard_map/slot_table/pallas_call | solution.py:346
  10.3 4.9 %collective-permute-start.4 = (f32[4,56,512]{2,1,0:T(8,128)S(1)}, f32[4,56,512]{2,1,0:T(8,128)S(1)}, u32[]{:S(2)}, u32[]{:S(2)}) collective-permute-start(f32[4,56,512]{2,1,0:T(8,128)S(1)} %pad_maximum_fusion.refs_0_), channel_id=1, source_target_pairs={{0,224},{32,0},{64,32},{96,64},{128,96},{160,128},{192,160},{224,1... | collective-permute-start | bytes 1376264 | tf_op jit(solution)/shard_map/ppermute | solution.py:257
  16.4 5.1 %prepare_rows.1.prepared_ref = bf16[8,16,512,48]{3,2,1,0:T(8,128)(2,1)S(1)} custom-call(f32[48,4096]{1,0:T(8,128)S(1)} %bitcast.67), custom_call_target="tpu_custom_call" | custom-call | flops 100000000 | bytes 8388608 | tf_op jit(solution)/shard_map/prepare_rows/pallas_call | solution.py:66
  21.6 4.5 %form_0.1 = (bf16[10,2,512,512]{3,2,1,0:T(8,128)(2,1)}, f32[8,8,512]{2,1,0:T(8,128)S(1)}, f32[32,8,512]{2,1,0:T(8,128)S(1)}) custom-call(s32[9,10]{1,0:T(8,128)S(1)} %copy-done.2, bf16[8,16,512,48]{3,2,1,0:T(8,128)(2,1)S(1)} %prepare_rows.1.prepared_ref, f32[8,8,512]{2,1,0:T(8,128)S(1)} %bitcast.61, f32[4,56,512]{2,1,0:T(8,128)S(1)} %pad_maximum_fusion.refs_0_), custom_call_target="tpu_custom_call" | custom-call | flops 8000000000 | bytes 8388608 | tf_op jit(solution)/shard_map/form_0/pallas_call | solution.py:180
  26.1 3.2 %collective-permute-start.6 = (f32[4,56,512]{2,1,0:T(8,128)S(1)}, f32[4,56,512]{2,1,0:T(8,128)S(1)}, u32[]{:S(2)}, u32[]{:S(2)}) collective-permute-start(f32[4,56,512]{2,1,0:T(8,128)S(1)} %collective-permute-done.4.refs_2_), channel_id=1, source_target_pairs={{0,224},{32,0},{64,32},{96,64},{128,96},{160,128},{192,160},{224,1... | collective-permute-start | bytes 1376264 | tf_op jit(solution)/shard_map/ppermute | solution.py:257
  29.4 7.9 %form_1.1 = (bf16[10,2,512,512]{3,2,1,0:T(8,128)(2,1)}, f32[8,8,512]{2,1,0:T(8,128)S(1)}, f32[32,8,512]{2,1,0:T(8,128)S(1)}) custom-call(s32[9,10]{1,0:T(8,128)S(1)} %copy-done.2, bf16[8,16,512,48]{3,2,1,0:T(8,128)(2,1)S(1)} %prepare_rows.1.prepared_ref, f32[8,8,512]{2,1,0:T(8,128)S(1)} %bitcast.62, ...), custom_call_target="tpu_custom_call", output_to_operand_aliasing={{0}: (6, {}), {1}: (7, {}), {2}: (8, {})} | custom-call | flops 8000000000 | bytes 8388608 | tf_op jit(solution)/shard_map/form_1/pallas_call | solution.py:180
  37.8 3.7 %collective-permute-start.8 = (f32[4,56,512]{2,1,0:T(8,128)S(1)}, f32[4,56,512]{2,1,0:T(8,128)S(1)}, u32[]{:S(2)}, u32[]{:S(2)}) collective-permute-start(f32[4,56,512]{2,1,0:T(8,128)S(1)} %collective-permute-done.6.refs_4_), channel_id=1, source_target_pairs={{0,224},{32,0},{64,32},{96,64},{128,96},{160,128},{192,160},{224,1... | collective-permute-start | bytes 1376264 | tf_op jit(solution)/shard_map/ppermute | solution.py:257
  41.5 8.0 %form_2.1 = (bf16[10,2,512,512]{3,2,1,0:T(8,128)(2,1)}, f32[8,8,512]{2,1,0:T(8,128)S(1)}, f32[32,8,512]{2,1,0:T(8,128)S(1)}) custom-call(s32[9,10]{1,0:T(8,128)S(1)} %copy-done.2, bf16[8,16,512,48]{3,2,1,0:T(8,128)(2,1)S(1)} %prepare_rows.1.prepared_ref, f32[8,8,512]{2,1,0:T(8,128)S(1)} %bitcast.63, ...), custom_call_target="tpu_custom_call", output_to_operand_aliasing={{0}: (8, {}), {1}: (9, {}), {2}: (10, {})} | custom-call | flops 8000000000 | bytes 8388608 | tf_op jit(solution)/shard_map/form_2/pallas_call | solution.py:180
  49.6 3.3 %collective-permute-start.10 = (f32[2,56,512]{2,1,0:T(8,128)S(1)}, f32[2,56,512]{2,1,0:T(8,128)S(1)}, u32[]{:S(2)}, u32[]{:S(2)}) collective-permute-start(f32[2,56,512]{2,1,0:T(8,128)S(1)} %slice.61), channel_id=1, source_target_pairs={{0,224},{32,0},{64,32},{96,64},{128,96},{160,128},{192,160},{224,1... | collective-permute-start | bytes 688136 | tf_op jit(solution)/shard_map/ppermute | solution.py:257
  53.0 8.1 %form_3.1 = (bf16[10,2,512,512]{3,2,1,0:T(8,128)(2,1)}, f32[8,8,512]{2,1,0:T(8,128)S(1)}, f32[32,8,512]{2,1,0:T(8,128)S(1)}) custom-call(s32[9,10]{1,0:T(8,128)S(1)} %copy-done.2, bf16[8,16,512,48]{3,2,1,0:T(8,128)(2,1)S(1)} %prepare_rows.1.prepared_ref, f32[8,8,512]{2,1,0:T(8,128)S(1)} %bitcast.64, ...), custom_call_target="tpu_custom_call", output_to_operand_aliasing={{0}: (10, {}), {1}: (11, {}), {2}: (12, {})} | custom-call | flops 8000000000 | bytes 8388608 | tf_op jit(solution)/shard_map/form_3/pallas_call | solution.py:180
  61.2 11.5 %form_4.1 = (bf16[10,2,512,512]{3,2,1,0:T(8,128)(2,1)}, f32[10,8,512]{2,1,0:T(8,128)S(1)}, f32[32,8,512]{2,1,0:T(8,128)}) custom-call(s32[9,10]{1,0:T(8,128)S(1)} %copy-done.2, bf16[8,16,512,48]{3,2,1,0:T(8,128)(2,1)S(1)} %prepare_rows.1.prepared_ref, f32[8,8,512]{2,1,0:T(8,128)S(1)} %bitcast.65, ...), custom_call_target="tpu_custom_call", output_to_operand_aliasing={{0}: (12, {})} | custom-call | flops 8000000000 | bytes 8388608 | tf_op jit(solution)/shard_map/form_4/pallas_call | solution.py:180
  72.6 9.6 %all-to-all-start = ((f32[32,8,512]{2,1,0:T(8,128)}), f32[32,8,512]{2,1,0:T(8,128)S(1)}, u32[]{:S(2)}, u32[]{:S(2)}) async-start(f32[32,8,512]{2,1,0:T(8,128)} %get-tuple-element.38), calls=%async_computation | async-start | bytes 1048576 | tf_op jit(solution)/shard_map/all_to_all | solution.py:356
  82.3 3.2 %apply_late.1 = f32[8,8,512]{2,1,0:T(8,128)S(1)} custom-call(s32[9,10]{1,0:T(8,128)S(1)} %copy-done.2, bf16[10,2,512,512]{3,2,1,0:T(8,128)(2,1)} %get-tuple-element.36.pair_ref, f32[10,8,512]{2,1,0:T(8,128)S(1)} %get-tuple-element.37.field, f32[8,8,512]{2,1,0:T(8,128)S(1)} %get-tuple-element.34.refs_10_.refs_0_), custom_call_target="tpu_custom_call" | custom-call | flops 3000000000 | bytes 12582912 | tf_op jit(solution)/shard_map/apply_late/pallas_call | solution.py:238
  86.9 4.6 %collective-permute-start.12 = (f32[8,512]{1,0:T(8,128)S(1)}, f32[8,512]{1,0:T(8,128)S(1)}, u32[]{:S(2)}, u32[]{:S(2)}) collective-permute-start(f32[8,512]{1,0:T(8,128)S(1)} %get-tuple-element.44), channel_id=1, source_target_pairs={{0,6},{2,0},{4,2},{6,4},{1,7},{3,1},{5,3},{7,5},{8,14},{10,8},{12,... | collective-permute-start | bytes 49160 | tf_op jit(solution)/shard_map/ppermute | solution.py:257
  93.0 5.4 %all-to-all-done = f32[32,8,512]{2,1,0:T(8,128)S(1)} async-done(((f32[32,8,512]{2,1,0:T(8,128)}), f32[32,8,512]{2,1,0:T(8,128)S(1)}, u32[]{:S(2)}, u32[]{:S(2)}) %all-to-all-start) | async-done | bytes 524320 | tf_op jit(solution)/shard_map/all_to_all | solution.py:356
  99.3 7.6 %all-to-all-start.1 = ((f32[32,8,512]{2,1,0:T(8,128)}), f32[32,8,512]{2,1,0:T(8,128)S(1)}, u32[]{:S(2)}, u32[]{:S(2)}) async-start(f32[32,8,512]{2,1,0:T(8,128)} %broadcast_in_dim.13), calls=%async_computation.1 | async-start | bytes 1048576 | tf_op jit(solution)/shard_map/all_to_all | solution.py:262
  109.7 2.5 %collective-permute-start.20 = (f32[2,8,512]{2,1,0:T(8,128)S(1)}, f32[2,8,512]{2,1,0:T(8,128)S(1)}, u32[]{:S(2)}, u32[]{:S(2)}) collective-permute-start(f32[2,8,512]{2,1,0:T(8,128)S(1)} %get-tuple-element.48), channel_id=1, source_target_pairs={{0,2},{2,4},{4,6},{6,0},{1,3},{3,5},{5,7},{7,1},{8,10},{10,12},{12... | collective-permute-start | bytes 98312 | tf_op jit(solution)/shard_map/ppermute | solution.py:257
  116.2 5.8 %apply_cols.1 = f32[32,8,512]{2,1,0:T(8,128)} custom-call(s32[9,10]{1,0:T(8,128)S(1)} %copy-done.2, bf16[10,2,512,512]{3,2,1,0:T(8,128)(2,1)} %get-tuple-element.36.pair_ref, f32[8,8,512]{2,1,0:T(8,128)S(1)} %bitcast.68), custom_call_target="tpu_custom_call" | custom-call | flops 3000000000 | bytes 12582912 | tf_op jit(solution)/shard_map/apply_cols/pallas_call | solution.py:238
  123.7 7.6 %all-to-all-start.2 = ((f32[32,8,512]{2,1,0:T(8,128)}), f32[32,8,512]{2,1,0:T(8,128)S(1)}, u32[]{:S(2)}, u32[]{:S(2)}) async-start(f32[32,8,512]{2,1,0:T(8,128)} %apply_cols.1), calls=%async_computation.2 | async-start | bytes 1048576 | tf_op jit(solution)/shard_map/all_to_all | solution.py:356
  131.3 6.1 %apply_rows.1 = f32[8,8,512]{2,1,0:T(8,128)S(1)} custom-call(s32[9,10]{1,0:T(8,128)S(1)} %copy-done.2, bf16[10,2,512,512]{3,2,1,0:T(8,128)(2,1)} %get-tuple-element.36.pair_ref, f32[32,8,512]{2,1,0:T(8,128)S(1)} %all-to-all-done.1.field), custom_call_target="tpu_custom_call" | custom-call | flops 3000000000 | bytes 12582912 | tf_op jit(solution)/shard_map/apply_rows/pallas_call | solution.py:238
  142.1 5.8 %all-to-all-done.2 = f32[32,8,512]{2,1,0:T(8,128)S(1)} async-done(((f32[32,8,512]{2,1,0:T(8,128)}), f32[32,8,512]{2,1,0:T(8,128)S(1)}, u32[]{:S(2)}, u32[]{:S(2)}) %all-to-all-start.2) | async-done | bytes 524320 | tf_op jit(solution)/shard_map/all_to_all | solution.py:356
  148.0 9.6 %all_to_all.25 = f32[8,8,512]{2,1,0:T(8,128)S(1)} all-to-all(f32[8,8,512]{2,1,0:T(8,128)S(1)} %broadcast_in_dim.14), channel_id=1, replica_groups=mesh['z'=8,'y'=4,'x'=4,'core'=2] {'x','core'}, dimensions={0} | all-to-all | bytes 262144 | tf_op jit(solution)/shard_map/all_to_all | solution.py:262
  157.8 17.0 %all_to_all.26 = f32[32,1,128]{2,1,0:T(1,128)S(1)} all-to-all(f32[32,1,128]{2,1,0:T(1,128)S(1)} %broadcast_in_dim.16), channel_id=1, replica_groups=mesh['z'=8,'y'=4,'x'=4,'core'=2] {'z','y'}, dimensions={0} | all-to-all | bytes 32768 | tf_op jit(solution)/shard_map/all_to_all | solution.py:262
  (73 shorter events, 25.4 us)
Async XLA Ops:
  1.7 6.8 %collective-permute-start.1 = (f32[56,512]{1,0:T(8,128)S(1)}, f32[56,512]{1,0:T(8,128)S(1)}, u32[]{:S(2)}, u32[]{:S(2)}) collective-permute-start(f32[56,512]{1,0:T(8,128)S(1)} %get-tuple-element.40), channel_id=1, source_target_pairs={{0,16},{8,24},{16,0},{24,8},{1,17},{9,25},{17,1},{25,9},{2,18},{10... | collective-permute-start | bytes 344072 | tf_op jit(solution)/shard_map/ppermute | solution.py:257
  3.3 7.0 %collective-permute-start = (f32[56,512]{1,0:T(8,128)S(1)}, f32[56,512]{1,0:T(8,128)S(1)}, u32[]{:S(2)}, u32[]{:S(2)}) collective-permute-start(f32[56,512]{1,0:T(8,128)S(1)} %get-tuple-element.40), channel_id=1, source_target_pairs={{0,8},{8,16},{16,24},{24,0},{1,9},{9,17},{17,25},{25,1},{2,10},{10... | collective-permute-start | bytes 344072 | tf_op jit(solution)/shard_map/ppermute | solution.py:257
  3.9 6.4 %collective-permute-start.2 = (f32[56,512]{1,0:T(8,128)S(1)}, f32[56,512]{1,0:T(8,128)S(1)}, u32[]{:S(2)}, u32[]{:S(2)}) collective-permute-start(f32[56,512]{1,0:T(8,128)S(1)} %get-tuple-element.40), channel_id=1, source_target_pairs={{0,24},{8,0},{16,8},{24,16},{1,25},{9,1},{17,9},{25,17},{2,26},{10... | collective-permute-start | bytes 344072 | tf_op jit(solution)/shard_map/ppermute | solution.py:257
  10.3 15.8 %collective-permute-start.4 = (f32[4,56,512]{2,1,0:T(8,128)S(1)}, f32[4,56,512]{2,1,0:T(8,128)S(1)}, u32[]{:S(2)}, u32[]{:S(2)}) collective-permute-start(f32[4,56,512]{2,1,0:T(8,128)S(1)} %pad_maximum_fusion.refs_0_), channel_id=1, source_target_pairs={{0,224},{32,0},{64,32},{96,64},{128,96},{160,128},{192,160},{224,1... | collective-permute-start | bytes 1376264 | tf_op jit(solution)/shard_map/ppermute | solution.py:257
  15.3 14.1 %collective-permute-start.3 = (f32[4,56,512]{2,1,0:T(8,128)S(1)}, f32[4,56,512]{2,1,0:T(8,128)S(1)}, u32[]{:S(2)}, u32[]{:S(2)}) collective-permute-start(f32[4,56,512]{2,1,0:T(8,128)S(1)} %pad_maximum_fusion.refs_0_), channel_id=1, source_target_pairs={{0,32},{32,64},{64,96},{96,128},{128,160},{160,192},{192,224},{224... | collective-permute-start | bytes 1376264 | tf_op jit(solution)/shard_map/ppermute | solution.py:257
  26.1 11.7 %collective-permute-start.6 = (f32[4,56,512]{2,1,0:T(8,128)S(1)}, f32[4,56,512]{2,1,0:T(8,128)S(1)}, u32[]{:S(2)}, u32[]{:S(2)}) collective-permute-start(f32[4,56,512]{2,1,0:T(8,128)S(1)} %collective-permute-done.4.refs_2_), channel_id=1, source_target_pairs={{0,224},{32,0},{64,32},{96,64},{128,96},{160,128},{192,160},{224,1... | collective-permute-start | bytes 1376264 | tf_op jit(solution)/shard_map/ppermute | solution.py:257
  29.4 12.2 %collective-permute-start.5 = (f32[4,56,512]{2,1,0:T(8,128)S(1)}, f32[4,56,512]{2,1,0:T(8,128)S(1)}, u32[]{:S(2)}, u32[]{:S(2)}) collective-permute-start(f32[4,56,512]{2,1,0:T(8,128)S(1)} %collective-permute-done.3.refs_1_), channel_id=1, source_target_pairs={{0,32},{32,64},{64,96},{96,128},{128,160},{160,192},{192,224},{224... | collective-permute-start | bytes 1376264 | tf_op jit(solution)/shard_map/ppermute | solution.py:257
  37.8 11.7 %collective-permute-start.8 = (f32[4,56,512]{2,1,0:T(8,128)S(1)}, f32[4,56,512]{2,1,0:T(8,128)S(1)}, u32[]{:S(2)}, u32[]{:S(2)}) collective-permute-start(f32[4,56,512]{2,1,0:T(8,128)S(1)} %collective-permute-done.6.refs_4_), channel_id=1, source_target_pairs={{0,224},{32,0},{64,32},{96,64},{128,96},{160,128},{192,160},{224,1... | collective-permute-start | bytes 1376264 | tf_op jit(solution)/shard_map/ppermute | solution.py:257
  41.5 11.4 %collective-permute-start.7 = (f32[4,56,512]{2,1,0:T(8,128)S(1)}, f32[4,56,512]{2,1,0:T(8,128)S(1)}, u32[]{:S(2)}, u32[]{:S(2)}) collective-permute-start(f32[4,56,512]{2,1,0:T(8,128)S(1)} %collective-permute-done.5.refs_3_), channel_id=1, source_target_pairs={{0,32},{32,64},{64,96},{96,128},{128,160},{160,192},{192,224},{224... | collective-permute-start | bytes 1376264 | tf_op jit(solution)/shard_map/ppermute | solution.py:257
  49.6 11.6 %collective-permute-start.10 = (f32[2,56,512]{2,1,0:T(8,128)S(1)}, f32[2,56,512]{2,1,0:T(8,128)S(1)}, u32[]{:S(2)}, u32[]{:S(2)}) collective-permute-start(f32[2,56,512]{2,1,0:T(8,128)S(1)} %slice.61), channel_id=1, source_target_pairs={{0,224},{32,0},{64,32},{96,64},{128,96},{160,128},{192,160},{224,1... | collective-permute-start | bytes 688136 | tf_op jit(solution)/shard_map/ppermute | solution.py:257
  52.9 8.3 %collective-permute-start.9 = (f32[2,56,512]{2,1,0:T(8,128)S(1)}, f32[2,56,512]{2,1,0:T(8,128)S(1)}, u32[]{:S(2)}, u32[]{:S(2)}) collective-permute-start(f32[2,56,512]{2,1,0:T(8,128)S(1)} %slice.60), channel_id=1, source_target_pairs={{0,32},{32,64},{64,96},{96,128},{128,160},{160,192},{192,224},{224... | collective-permute-start | bytes 688136 | tf_op jit(solution)/shard_map/ppermute | solution.py:257
  72.6 25.7 %all-to-all-start = ((f32[32,8,512]{2,1,0:T(8,128)}), f32[32,8,512]{2,1,0:T(8,128)S(1)}, u32[]{:S(2)}, u32[]{:S(2)}) async-start(f32[32,8,512]{2,1,0:T(8,128)} %get-tuple-element.38), calls=%async_computation | async-start | bytes 1048576 | tf_op jit(solution)/shard_map/all_to_all | solution.py:356
  85.5 1.3 collective-permute-start.11
  86.9 11.5 %collective-permute-start.12 = (f32[8,512]{1,0:T(8,128)S(1)}, f32[8,512]{1,0:T(8,128)S(1)}, u32[]{:S(2)}, u32[]{:S(2)}) collective-permute-start(f32[8,512]{1,0:T(8,128)S(1)} %get-tuple-element.44), channel_id=1, source_target_pairs={{0,6},{2,0},{4,2},{6,4},{1,7},{3,1},{5,3},{7,5},{8,14},{10,8},{12,... | collective-permute-start | bytes 49160 | tf_op jit(solution)/shard_map/ppermute | solution.py:257
  91.4 7.0 %collective-permute-start.14 = (f32[8,512]{1,0:T(8,128)S(1)}, f32[8,512]{1,0:T(8,128)S(1)}, u32[]{:S(2)}, u32[]{:S(2)}) collective-permute-start(f32[8,512]{1,0:T(8,128)S(1)} %get-tuple-element.45), channel_id=1, source_target_pairs={{0,2},{2,4},{4,6},{6,0},{1,3},{3,5},{5,7},{7,1},{8,10},{10,12},{12... | collective-permute-start | bytes 49160 | tf_op jit(solution)/shard_map/ppermute | solution.py:257
  91.4 7.0 %collective-permute-start.13 = (f32[8,512]{1,0:T(8,128)S(1)}, f32[8,512]{1,0:T(8,128)S(1)}, u32[]{:S(2)}, u32[]{:S(2)}) collective-permute-start(f32[8,512]{1,0:T(8,128)S(1)} %get-tuple-element.46), channel_id=1, source_target_pairs={{0,4},{2,6},{4,0},{6,2},{1,5},{3,7},{5,1},{7,3},{8,12},{10,14},{12... | collective-permute-start | bytes 49160 | tf_op jit(solution)/shard_map/ppermute | solution.py:257
  99.3 24.4 %all-to-all-start.1 = ((f32[32,8,512]{2,1,0:T(8,128)}), f32[32,8,512]{2,1,0:T(8,128)S(1)}, u32[]{:S(2)}, u32[]{:S(2)}) async-start(f32[32,8,512]{2,1,0:T(8,128)} %broadcast_in_dim.13), calls=%async_computation.1 | async-start | bytes 1048576 | tf_op jit(solution)/shard_map/all_to_all | solution.py:262
  108.2 5.4 %collective-permute-start.21 = (f32[2,8,512]{2,1,0:T(8,128)S(1)}, f32[2,8,512]{2,1,0:T(8,128)S(1)}, u32[]{:S(2)}, u32[]{:S(2)}) collective-permute-start(f32[2,8,512]{2,1,0:T(8,128)S(1)} %get-tuple-element.48), channel_id=1, source_target_pairs={{0,4},{2,6},{4,0},{6,2},{1,5},{3,7},{5,1},{7,3},{8,12},{10,14},{12... | collective-permute-start | bytes 98312 | tf_op jit(solution)/shard_map/ppermute | solution.py:257
  109.7 5.1 %collective-permute-start.20 = (f32[2,8,512]{2,1,0:T(8,128)S(1)}, f32[2,8,512]{2,1,0:T(8,128)S(1)}, u32[]{:S(2)}, u32[]{:S(2)}) collective-permute-start(f32[2,8,512]{2,1,0:T(8,128)S(1)} %get-tuple-element.48), channel_id=1, source_target_pairs={{0,2},{2,4},{4,6},{6,0},{1,3},{3,5},{5,7},{7,1},{8,10},{10,12},{12... | collective-permute-start | bytes 98312 | tf_op jit(solution)/shard_map/ppermute | solution.py:257
  112.3 3.9 %collective-permute-start.22 = (f32[2,8,512]{2,1,0:T(8,128)S(1)}, f32[2,8,512]{2,1,0:T(8,128)S(1)}, u32[]{:S(2)}, u32[]{:S(2)}) collective-permute-start(f32[2,8,512]{2,1,0:T(8,128)S(1)} %get-tuple-element.48), channel_id=1, source_target_pairs={{0,6},{2,0},{4,2},{6,4},{1,7},{3,1},{5,3},{7,5},{8,14},{10,8},{12,... | collective-permute-start | bytes 98312 | tf_op jit(solution)/shard_map/ppermute | solution.py:257
  123.7 24.2 %all-to-all-start.2 = ((f32[32,8,512]{2,1,0:T(8,128)}), f32[32,8,512]{2,1,0:T(8,128)S(1)}, u32[]{:S(2)}, u32[]{:S(2)}) async-start(f32[32,8,512]{2,1,0:T(8,128)} %apply_cols.1), calls=%async_computation.2 | async-start | bytes 1048576 | tf_op jit(solution)/shard_map/all_to_all | solution.py:356
  138.8 9.2 %collective-permute-start.16 = (f32[8,512]{1,0:T(8,128)S(1)}, f32[8,512]{1,0:T(8,128)S(1)}, u32[]{:S(2)}, u32[]{:S(2)}) collective-permute-start(f32[8,512]{1,0:T(8,128)S(1)} %get-tuple-element.41), channel_id=1, source_target_pairs={{0,6},{2,0},{4,2},{6,4},{1,7},{3,1},{5,3},{7,5},{8,14},{10,8},{12,... | collective-permute-start | bytes 49160 | tf_op jit(solution)/shard_map/ppermute | solution.py:257
  139.6 8.3 %collective-permute-start.18 = (f32[8,512]{1,0:T(8,128)S(1)}, f32[8,512]{1,0:T(8,128)S(1)}, u32[]{:S(2)}, u32[]{:S(2)}) collective-permute-start(f32[8,512]{1,0:T(8,128)S(1)} %get-tuple-element.42), channel_id=1, source_target_pairs={{0,2},{2,4},{4,6},{6,0},{1,3},{3,5},{5,7},{7,1},{8,10},{10,12},{12... | collective-permute-start | bytes 49160 | tf_op jit(solution)/shard_map/ppermute | solution.py:257
  140.9 7.1 %collective-permute-start.17 = (f32[8,512]{1,0:T(8,128)S(1)}, f32[8,512]{1,0:T(8,128)S(1)}, u32[]{:S(2)}, u32[]{:S(2)}) collective-permute-start(f32[8,512]{1,0:T(8,128)S(1)} %get-tuple-element.43), channel_id=1, source_target_pairs={{0,4},{2,6},{4,0},{6,2},{1,5},{3,7},{5,1},{7,3},{8,12},{10,14},{12... | collective-permute-start | bytes 49160 | tf_op jit(solution)/shard_map/ppermute | solution.py:257
  (5 other events, 38.3 us)

commit v11 on v10

--- a/solution.py
+++ b/solution.py
@@ -12,7 +12,7 @@
 TILE = 512
 ROW = ("z", "y")
 COL = ("x", "core")
-ROW_AT, ROW_NEAR, COL_AT, SOURCE, PLACE, STAGE, LIVE, CROSSING, LATE = range(9)
+ROW_AT, ROW_NEAR, COL_AT, SOURCE, PLACE, STAGE, LIVE, CROSSING, LATE, ROW_SEEN = range(10)
 LAST_STAGE = 4
 PER_STAGE = 2
 BY_ROWS = (((1,), (0,)), ((), ()))
@@ -252,6 +252,73 @@
     )(table, in_hbm(pair), field, *start)
 
 
+def fetch_kernel(table, pair_ref, after, out, sems):
+    slots = pair_ref.shape[0]
+
+    def copy(slot):
+        return pltpu.make_async_copy(pair_ref.at[slot], out.at[slot], sems.at[slot])
+
+    for slot in range(slots):
+
+        @pl.when(table[CROSSING, slot] != 0)
+        def _():
+            copy(slot).start()
+
+    for slot in range(slots):
+
+        @pl.when(table[CROSSING, slot] != 0)
+        def _():
+            copy(slot).wait()
+
+
+def fetch(table, pair, after):
+    vmem = pl.BlockSpec(memory_space=pltpu.VMEM)
+    return pl.pallas_call(
+        fetch_kernel,
+        in_specs=[
+            pl.BlockSpec(memory_space=pltpu.SMEM),
+            pl.BlockSpec(memory_space=pltpu.HBM),
+            vmem,
+        ],
+        out_specs=vmem,
+        out_shape=jax.ShapeDtypeStruct(pair.shape, pair.dtype),
+        scratch_shapes=[pltpu.SemaphoreType.DMA((pair.shape[0],))],
+        compiler_params=pltpu.CompilerParams(vmem_limit_bytes=2 << 20),
+        cost_estimate=pl.CostEstimate(flops=0, bytes_accessed=12 << 20, transcendentals=0),
+        name="fetch",
+    )(table, in_hbm(pair), after)
+
+
+def cols_kernel(table, pair, field, acc):
+    acc[...] = jnp.zeros_like(acc)
+
+    def visit(slot, carry):
+        @pl.when(table[CROSSING, slot] != 0)
+        def _():
+            acc[table[COL_AT, slot]] += multiply(
+                field[table[ROW_SEEN, slot]], pair[slot, 0], pair[slot, 1], BY_ROWS
+            )
+
+        return carry
+
+    lax.fori_loop(0, pair.shape[0], visit, 0)
+
+
+def apply_cols(table, pair, field, count):
+    vmem = pl.BlockSpec(memory_space=pltpu.VMEM)
+    return pl.pallas_call(
+        cols_kernel,
+        in_specs=[pl.BlockSpec(memory_space=pltpu.SMEM), vmem, vmem],
+        out_specs=vmem,
+        out_shape=jax.ShapeDtypeStruct((count, 8, TILE), jnp.float32),
+        compiler_params=pltpu.CompilerParams(vmem_limit_bytes=4 << 20),
+        cost_estimate=pl.CostEstimate(
+            flops=3 * 10**9, bytes_accessed=1 << 20, transcendentals=0
+        ),
+        name="apply_cols",
+    )(table, pair, field)
+
+
 def shift(value, axis, distance):
     size = lax.axis_size(axis)
     return lax.ppermute(value, axis, [(i, (i + distance) % size) for i in range(size)])
@@ -262,10 +329,9 @@
     return lax.all_to_all(copies, axes, 0, 0, tiled=True)
 
 
-def spread_near(piece):
-    both = jnp.stack([piece, shift(piece, "core", 1)])
+def spread_near(both):
     near = [both] + [shift(both, "x", d) for d in range(1, lax.axis_size("x"))]
-    return jnp.stack(near, axis=1).reshape(2 * len(near), *piece.shape)
+    return jnp.concatenate(near, axis=0)
 
 
 def reduce_near(row_acc):
@@ -310,10 +376,11 @@
         source = jnp.where(behind == 0, 0, source)
         place = jnp.where((behind == size_z // 2) & upper, place - size_y // 2, place)
         crossing = ((z * size_y + y) * tiles + row) != (col * tiles + 2 * x + core)
-        near = jnp.where(lax.rem(row, 2) == core, 0, size_x)
-        near = near + lax.rem(x - row // 2 + size_x, size_x)
+        other = jnp.where(lax.rem(row, 2) == core, 0, 1)
+        along = lax.rem(x - row // 2 + size_x, size_x)
         out[ROW_AT, slot] = row
-        out[ROW_NEAR, slot] = near
+        out[ROW_NEAR, slot] = other * size_x + along
+        out[ROW_SEEN, slot] = 2 * along + other
         out[COL_AT, slot] = col
         out[SOURCE, slot] = source
         out[PLACE, slot] = place
@@ -347,7 +414,7 @@
         kernel,
         in_specs=[smem, smem],
         out_specs=smem,
-        out_shape=jax.ShapeDtypeStruct((9, pairs.shape[1]), jnp.int32),
+        out_shape=jax.ShapeDtypeStruct((10, pairs.shape[1]), jnp.int32),
         name="slot_table",
     )(pairs, valid)
 
@@ -366,12 +433,8 @@
     table = slot_table(pairs[0, 0].transpose(1, 0), valid[0], sizes)
 
     flat = positions.transpose(1, 0, 2).reshape(48, block)
-    own = jnp.concatenate(
-        [
-            lax.dynamic_slice_in_dim(flat, grid_col * TILE, TILE, 1),
-            lax.dynamic_slice_in_dim(vectors, grid_col * TILE, TILE, 1),
-        ],
-        axis=0,
+    own = lax.dynamic_slice_in_dim(
+        jnp.concatenate([flat, vectors], axis=0), grid_col * TILE, TILE, 1
     )
     row_vec = vectors.reshape(8, tiles, TILE).transpose(1, 0, 2)
     near = gather_y(own)
@@ -389,7 +452,9 @@
     first = combine(row_acc, col_acc)
 
     col_vec = spread(first, ROW)
-    col_acc = apply_tiles(CROSSING, COL_AT, "apply_cols", table, pair, spread_near(first), blocks)
+    both = jnp.stack([first, shift(first, "core", 1)])
+    tiles_here = fetch(table, pair, both)
+    col_acc = apply_cols(table, tiles_here, spread_near(both), blocks)
     row_acc = apply_tiles(LIVE, COL_AT, "apply_rows", table, pair, col_vec, tiles)
     second = combine(row_acc, col_acc)
 

time: 178 us -> 179 us (level)
  Pallas kernels: 62.4 us -> 65.3 us
  starting transfers between devices: 59.4 us -> 57.4 us
    pallas_call x0 -> x2, Pallas kernels: none -> 9.03 us  [the longest x1 4.76 us: fetch(): pl.pallas_call(fetch_kernel, in_specs=[pl.BlockSpec(memory_space=pltpu.SM...]
    pallas_call x3 -> x2, Pallas kernels: 15.1 us -> 10.1 us  [apply_tiles(): pl.pallas_call(functools.partial(apply_kernel, wanted, col_at), in_specs=...]
    all_to_all x2, starting transfers between devices: 17.2 us -> 13 us  [combine(): by_col = lax.all_to_all(col_acc, ROW, 0, 0, tiled=True)]
    ppermute x23, waiting for transfers between devices: 9.16 us -> 11.4 us  [shift(): lax.ppermute(value, axis, [(i, (i + distance) % size) for i in range(size)])]
    all_to_all x2, waiting for transfers between devices: 11.1 us -> 9.14 us  [combine(): by_col = lax.all_to_all(col_acc, ROW, 0, 0, tiled=True)]
  transfers between devices with their start and end apart: 26 -> 26, of which waited for: 11 -> 10; matrix products, arithmetic and copies ran while one was open for 0% -> 0% of each run, Pallas kernels for 29% -> 27%
where the time goes in v11:
time: 179 us; the launch traced here: 178 us
  Pallas kernels  65.3 us (36%)
  starting transfers between devices  57.4 us (32%)
  blocking collectives  28.3 us (16%)
  waiting for transfers between devices  22.7 us (13%)
  local copies, waits for them, and re-layouts  2.1 us (1%)
  other arithmetic  2.06 us (1%)
    pallas_call x5, Pallas kernels, form_stage(): pl.pallas_call(functools.partial(stage_kernel, stage, len(places)), in_sp...  39 us
    ppermute x23, starting transfers between devices, shift(): lax.ppermute(value, axis, [(i, (i + distance) % size) for i in range(size)])  35 us
    all_to_all x2, blocking collectives, spread(): return lax.all_to_all(copies, axes, 0, 0, tiled=True)  28.3 us
    all_to_all x2, starting transfers between devices, combine(): by_col = lax.all_to_all(col_acc, ROW, 0, 0, tiled=True)  13 us
    ppermute x23, waiting for transfers between devices, shift(): lax.ppermute(value, axis, [(i, (i + distance) % size) for i in range(size)])  11.4 us
    pallas_call x2, Pallas kernels, apply_tiles(): pl.pallas_call(functools.partial(apply_kernel, wanted, col_at), in_specs=...  10.1 us
    all_to_all x1, starting transfers between devices, spread(): return lax.all_to_all(copies, axes, 0, 0, tiled=True)  9.35 us
    all_to_all x2, waiting for transfers between devices, combine(): by_col = lax.all_to_all(col_acc, ROW, 0, 0, tiled=True)  9.14 us
  transfers between devices with their start and end apart: 26, of which 10 were waited for; matrix products, arithmetic and copies ran while one was open for 0% of the time, Pallas kernels for 27%

profile of v11, /device:TPU:0, one launch (start us, length us, event | category | flops | bytes accessed | tf_op | source)
XLA Modules:
  0.0 178.2 jit_solution(6770198266662820271)
XLA Ops:
  3.2 2.6 %collective-permute-start.2 = (f32[56,512]{1,0:T(8,128)S(1)}, f32[56,512]{1,0:T(8,128)S(1)}, u32[]{:S(2)}, u32[]{:S(2)}) collective-permute-start(f32[56,512]{1,0:T(8,128)S(1)} %fusion), channel_id=1, source_target_pairs={{0,24},{8,0},{16,8},{24,16},{1,25},{9,1},{17,9},{25,17},{2,26},{10... | collective-permute-start | bytes 344072 | tf_op jit(solution)/shard_map/ppermute | solution.py:324
  9.6 4.9 %collective-permute-start.4 = (f32[4,56,512]{2,1,0:T(8,128)S(1)}, f32[4,56,512]{2,1,0:T(8,128)S(1)}, u32[]{:S(2)}, u32[]{:S(2)}) collective-permute-start(f32[4,56,512]{2,1,0:T(8,128)S(1)} %pad_maximum_fusion.refs_0_), channel_id=1, source_target_pairs={{0,224},{32,0},{64,32},{96,64},{128,96},{160,128},{192,160},{224,1... | collective-permute-start | bytes 1376264 | tf_op jit(solution)/shard_map/ppermute | solution.py:324
  15.6 5.1 %prepare_rows.1.prepared_ref = bf16[8,16,512,48]{3,2,1,0:T(8,128)(2,1)S(1)} custom-call(f32[48,4096]{1,0:T(8,128)S(1)} %bitcast.58), custom_call_target="tpu_custom_call" | custom-call | flops 100000000 | bytes 8388608 | tf_op jit(solution)/shard_map/prepare_rows/pallas_call | solution.py:66
  23.5 5.1 %collective-permute-start.6 = (f32[4,56,512]{2,1,0:T(8,128)S(1)}, f32[4,56,512]{2,1,0:T(8,128)S(1)}, u32[]{:S(2)}, u32[]{:S(2)}) collective-permute-start(f32[4,56,512]{2,1,0:T(8,128)S(1)} %collective-permute-done.4.refs_2_), channel_id=1, source_target_pairs={{0,224},{32,0},{64,32},{96,64},{128,96},{160,128},{192,160},{224,1... | collective-permute-start | bytes 1376264 | tf_op jit(solution)/shard_map/ppermute | solution.py:324
  28.6 4.5 %form_1.1 = (bf16[10,2,512,512]{3,2,1,0:T(8,128)(2,1)}, f32[8,8,512]{2,1,0:T(8,128)S(1)}, f32[32,8,512]{2,1,0:T(8,128)S(1)}) custom-call(s32[10,10]{1,0:T(8,128)S(1)} %copy-done.2, bf16[8,16,512,48]{3,2,1,0:T(8,128)(2,1)S(1)} %prepare_rows.1.prepared_ref, f32[8,8,512]{2,1,0:T(8,128)S(1)} %bitcast.60, ...), custom_call_target="tpu_custom_call", output_to_operand_aliasing={{0}: (6, {}), {1}: (7, {}), {2}: (8, {})} | custom-call | flops 8000000000 | bytes 8388608 | tf_op jit(solution)/shard_map/form_1/pallas_call | solution.py:180
  33.1 3.9 %collective-permute-done.6.refs_4_ = f32[4,56,512]{2,1,0:T(8,128)S(1)} collective-permute-done((f32[4,56,512]{2,1,0:T(8,128)S(1)}, f32[4,56,512]{2,1,0:T(8,128)S(1)}, u32[]{:S(2)}, u32[]{:S(2)}) %collective-permute-start.6) | collective-permute-done | bytes 458784 | tf_op jit(solution)/shard_map/ppermute | solution.py:324
  37.1 3.7 %collective-permute-start.8 = (f32[4,56,512]{2,1,0:T(8,128)S(1)}, f32[4,56,512]{2,1,0:T(8,128)S(1)}, u32[]{:S(2)}, u32[]{:S(2)}) collective-permute-start(f32[4,56,512]{2,1,0:T(8,128)S(1)} %collective-permute-done.6.refs_4_), channel_id=1, source_target_pairs={{0,224},{32,0},{64,32},{96,64},{128,96},{160,128},{192,160},{224,1... | collective-permute-start | bytes 1376264 | tf_op jit(solution)/shard_map/ppermute | solution.py:324
  40.8 7.9 %form_2.1 = (bf16[10,2,512,512]{3,2,1,0:T(8,128)(2,1)}, f32[8,8,512]{2,1,0:T(8,128)S(1)}, f32[32,8,512]{2,1,0:T(8,128)S(1)}) custom-call(s32[10,10]{1,0:T(8,128)S(1)} %copy-done.2, bf16[8,16,512,48]{3,2,1,0:T(8,128)(2,1)S(1)} %prepare_rows.1.prepared_ref, f32[8,8,512]{2,1,0:T(8,128)S(1)} %bitcast.61, ...), custom_call_target="tpu_custom_call", output_to_operand_aliasing={{0}: (8, {}), {1}: (9, {}), {2}: (10, {})} | custom-call | flops 8000000000 | bytes 8388608 | tf_op jit(solution)/shard_map/form_2/pallas_call | solution.py:180
  48.9 3.2 %collective-permute-start.10 = (f32[2,56,512]{2,1,0:T(8,128)S(1)}, f32[2,56,512]{2,1,0:T(8,128)S(1)}, u32[]{:S(2)}, u32[]{:S(2)}) collective-permute-start(f32[2,56,512]{2,1,0:T(8,128)S(1)} %slice.61), channel_id=1, source_target_pairs={{0,224},{32,0},{64,32},{96,64},{128,96},{160,128},{192,160},{224,1... | collective-permute-start | bytes 688136 | tf_op jit(solution)/shard_map/ppermute | solution.py:324
  52.3 8.1 %form_3.1 = (bf16[10,2,512,512]{3,2,1,0:T(8,128)(2,1)}, f32[8,8,512]{2,1,0:T(8,128)S(1)}, f32[32,8,512]{2,1,0:T(8,128)S(1)}) custom-call(s32[10,10]{1,0:T(8,128)S(1)} %copy-done.2, bf16[8,16,512,48]{3,2,1,0:T(8,128)(2,1)S(1)} %prepare_rows.1.prepared_ref, f32[8,8,512]{2,1,0:T(8,128)S(1)} %bitcast.62, ...), custom_call_target="tpu_custom_call", output_to_operand_aliasing={{0}: (10, {}), {1}: (11, {}), {2}: (12, {})} | custom-call | flops 8000000000 | bytes 8388608 | tf_op jit(solution)/shard_map/form_3/pallas_call | solution.py:180
  60.4 17.5 %form_4.1 = (bf16[10,2,512,512]{3,2,1,0:T(8,128)(2,1)}, f32[10,8,512]{2,1,0:T(8,128)S(1)}, f32[32,8,512]{2,1,0:T(8,128)}) custom-call(s32[10,10]{1,0:T(8,128)S(1)} %copy-done.2, bf16[8,16,512,48]{3,2,1,0:T(8,128)(2,1)S(1)} %prepare_rows.1.prepared_ref, f32[8,8,512]{2,1,0:T(8,128)S(1)} %bitcast.63, ...), custom_call_target="tpu_custom_call", output_to_operand_aliasing={{0}: (12, {})} | custom-call | flops 8000000000 | bytes 8388608 | tf_op jit(solution)/shard_map/form_4/pallas_call | solution.py:180
  77.9 6.5 %all-to-all-start = ((f32[32,8,512]{2,1,0:T(8,128)}), f32[32,8,512]{2,1,0:T(8,128)S(1)}, u32[]{:S(2)}, u32[]{:S(2)}) async-start(f32[32,8,512]{2,1,0:T(8,128)} %get-tuple-element.38), calls=%async_computation | async-start | bytes 1048576 | tf_op jit(solution)/shard_map/all_to_all | solution.py:423
  84.4 4.0 %apply_late.1 = f32[8,8,512]{2,1,0:T(8,128)S(1)} custom-call(s32[10,10]{1,0:T(8,128)S(1)} %copy-done.2, bf16[10,2,512,512]{3,2,1,0:T(8,128)(2,1)} %get-tuple-element.36.pair_ref, f32[10,8,512]{2,1,0:T(8,128)S(1)} %get-tuple-element.37.field, f32[8,8,512]{2,1,0:T(8,128)S(1)} %get-tuple-element.34.refs_10_.refs_0_), custom_call_target="tpu_custom_call" | custom-call | flops 3000000000 | bytes 12582912 | tf_op jit(solution)/shard_map/apply_late/pallas_call | solution.py:238
  93.4 4.8 %all-to-all-done = f32[32,8,512]{2,1,0:T(8,128)S(1)} async-done(((f32[32,8,512]{2,1,0:T(8,128)}), f32[32,8,512]{2,1,0:T(8,128)S(1)}, u32[]{:S(2)}, u32[]{:S(2)}) %all-to-all-start) | async-done | bytes 524320 | tf_op jit(solution)/shard_map/all_to_all | solution.py:423
  99.2 9.4 %all-to-all-start.1 = ((f32[32,8,512]{2,1,0:T(8,128)}), f32[32,8,512]{2,1,0:T(8,128)S(1)}, u32[]{:S(2)}, u32[]{:S(2)}) async-start(f32[32,8,512]{2,1,0:T(8,128)} %broadcast_in_dim.13), calls=%async_computation.1 | async-start | bytes 1048576 | tf_op jit(solution)/shard_map/all_to_all | solution.py:329
  109.9 3.2 %collective-permute-start.22 = (f32[2,8,512]{2,1,0:T(8,128)S(1)}, f32[2,8,512]{2,1,0:T(8,128)S(1)}, u32[]{:S(2)}, u32[]{:S(2)}) collective-permute-start(f32[2,8,512]{2,1,0:T(8,128)S(1)} %pad_maximum_fusion.1.after), channel_id=1, source_target_pairs={{0,6},{2,0},{4,2},{6,4},{1,7},{3,1},{5,3},{7,5},{8,14},{10,8},{12,... | collective-permute-start | bytes 98312 | tf_op jit(solution)/shard_map/ppermute | solution.py:324
  114.0 4.8 %fetch.1.pair = bf16[10,2,512,512]{3,2,1,0:T(8,128)(2,1)S(1)} custom-call(s32[10,10]{1,0:T(8,128)S(1)} %copy-done.2, bf16[10,2,512,512]{3,2,1,0:T(8,128)(2,1)} %get-tuple-element.36.pair_ref, f32[2,8,512]{2,1,0:T(8,128)S(1)} %pad_maximum_fusion.1.after), custom_call_target="tpu_custom_call" | custom-call | bytes 12582912 | tf_op jit(solution)/shard_map/fetch/pallas_call | solution.py:276
  118.9 4.3 %apply_cols.1 = f32[32,8,512]{2,1,0:T(8,128)} custom-call(s32[10,10]{1,0:T(8,128)S(1)} %copy-done.2, bf16[10,2,512,512]{3,2,1,0:T(8,128)(2,1)S(1)} %fetch.1.pair, f32[8,8,512]{2,1,0:T(8,128)S(1)} %constant_dynamic-update-slice_fusion.field), custom_call_target="tpu_custom_call" | custom-call | flops 3000000000 | bytes 1048576 | tf_op jit(solution)/shard_map/apply_cols/pallas_call | solution.py:309
  125.3 6.5 %all-to-all-start.2 = ((f32[32,8,512]{2,1,0:T(8,128)}), f32[32,8,512]{2,1,0:T(8,128)S(1)}, u32[]{:S(2)}, u32[]{:S(2)}) async-start(f32[32,8,512]{2,1,0:T(8,128)} %apply_cols.1), calls=%async_computation.2 | async-start | bytes 1048576 | tf_op jit(solution)/shard_map/all_to_all | solution.py:423
  131.9 6.1 %apply_rows.1 = f32[8,8,512]{2,1,0:T(8,128)S(1)} custom-call(s32[10,10]{1,0:T(8,128)S(1)} %copy-done.2, bf16[10,2,512,512]{3,2,1,0:T(8,128)(2,1)} %get-tuple-element.36.pair_ref, f32[32,8,512]{2,1,0:T(8,128)S(1)} %all-to-all-done.1.field), custom_call_target="tpu_custom_call" | custom-call | flops 3000000000 | bytes 12582912 | tf_op jit(solution)/shard_map/apply_rows/pallas_call | solution.py:238
  139.3 2.4 %collective-permute-start.16 = (f32[8,512]{1,0:T(8,128)S(1)}, f32[8,512]{1,0:T(8,128)S(1)}, u32[]{:S(2)}, u32[]{:S(2)}) collective-permute-start(f32[8,512]{1,0:T(8,128)S(1)} %get-tuple-element.41), channel_id=1, source_target_pairs={{0,6},{2,0},{4,2},{6,4},{1,7},{3,1},{5,3},{7,5},{8,14},{10,8},{12,... | collective-permute-start | bytes 49160 | tf_op jit(solution)/shard_map/ppermute | solution.py:324
  144.5 4.3 %all-to-all-done.2 = f32[32,8,512]{2,1,0:T(8,128)S(1)} async-done(((f32[32,8,512]{2,1,0:T(8,128)}), f32[32,8,512]{2,1,0:T(8,128)S(1)}, u32[]{:S(2)}, u32[]{:S(2)}) %all-to-all-start.2) | async-done | bytes 524320 | tf_op jit(solution)/shard_map/all_to_all | solution.py:423
  148.9 11.1 %all_to_all.25 = f32[8,8,512]{2,1,0:T(8,128)S(1)} all-to-all(f32[8,8,512]{2,1,0:T(8,128)S(1)} %broadcast_in_dim.14), channel_id=1, replica_groups=mesh['z'=8,'y'=4,'x'=4,'core'=2] {'x','core'}, dimensions={0} | all-to-all | bytes 262144 | tf_op jit(solution)/shard_map/all_to_all | solution.py:329
  160.2 17.1 %all_to_all.26 = f32[32,1,128]{2,1,0:T(1,128)S(1)} all-to-all(f32[32,1,128]{2,1,0:T(1,128)S(1)} %broadcast_in_dim.16), channel_id=1, replica_groups=mesh['z'=8,'y'=4,'x'=4,'core'=2] {'z','y'}, dimensions={0} | all-to-all | bytes 32768 | tf_op jit(solution)/shard_map/all_to_all | solution.py:329
  (74 shorter events, 26.7 us)
Async XLA Ops:
  0.9 6.9 %collective-permute-start.1 = (f32[56,512]{1,0:T(8,128)S(1)}, f32[56,512]{1,0:T(8,128)S(1)}, u32[]{:S(2)}, u32[]{:S(2)}) collective-permute-start(f32[56,512]{1,0:T(8,128)S(1)} %fusion), channel_id=1, source_target_pairs={{0,16},{8,24},{16,0},{24,8},{1,17},{9,25},{17,1},{25,9},{2,18},{10... | collective-permute-start | bytes 344072 | tf_op jit(solution)/shard_map/ppermute | solution.py:324
  2.5 7.0 %collective-permute-start = (f32[56,512]{1,0:T(8,128)S(1)}, f32[56,512]{1,0:T(8,128)S(1)}, u32[]{:S(2)}, u32[]{:S(2)}) collective-permute-start(f32[56,512]{1,0:T(8,128)S(1)} %fusion), channel_id=1, source_target_pairs={{0,8},{8,16},{16,24},{24,0},{1,9},{9,17},{17,25},{25,1},{2,10},{10... | collective-permute-start | bytes 344072 | tf_op jit(solution)/shard_map/ppermute | solution.py:324
  3.2 6.4 %collective-permute-start.2 = (f32[56,512]{1,0:T(8,128)S(1)}, f32[56,512]{1,0:T(8,128)S(1)}, u32[]{:S(2)}, u32[]{:S(2)}) collective-permute-start(f32[56,512]{1,0:T(8,128)S(1)} %fusion), channel_id=1, source_target_pairs={{0,24},{8,0},{16,8},{24,16},{1,25},{9,1},{17,9},{25,17},{2,26},{10... | collective-permute-start | bytes 344072 | tf_op jit(solution)/shard_map/ppermute | solution.py:324
  9.6 13.9 %collective-permute-start.4 = (f32[4,56,512]{2,1,0:T(8,128)S(1)}, f32[4,56,512]{2,1,0:T(8,128)S(1)}, u32[]{:S(2)}, u32[]{:S(2)}) collective-permute-start(f32[4,56,512]{2,1,0:T(8,128)S(1)} %pad_maximum_fusion.refs_0_), channel_id=1, source_target_pairs={{0,224},{32,0},{64,32},{96,64},{128,96},{160,128},{192,160},{224,1... | collective-permute-start | bytes 1376264 | tf_op jit(solution)/shard_map/ppermute | solution.py:324
  14.5 14.1 %collective-permute-start.3 = (f32[4,56,512]{2,1,0:T(8,128)S(1)}, f32[4,56,512]{2,1,0:T(8,128)S(1)}, u32[]{:S(2)}, u32[]{:S(2)}) collective-permute-start(f32[4,56,512]{2,1,0:T(8,128)S(1)} %pad_maximum_fusion.refs_0_), channel_id=1, source_target_pairs={{0,32},{32,64},{64,96},{96,128},{128,160},{160,192},{192,224},{224... | collective-permute-start | bytes 1376264 | tf_op jit(solution)/shard_map/ppermute | solution.py:324
  23.5 13.6 %collective-permute-start.6 = (f32[4,56,512]{2,1,0:T(8,128)S(1)}, f32[4,56,512]{2,1,0:T(8,128)S(1)}, u32[]{:S(2)}, u32[]{:S(2)}) collective-permute-start(f32[4,56,512]{2,1,0:T(8,128)S(1)} %collective-permute-done.4.refs_2_), channel_id=1, source_target_pairs={{0,224},{32,0},{64,32},{96,64},{128,96},{160,128},{192,160},{224,1... | collective-permute-start | bytes 1376264 | tf_op jit(solution)/shard_map/ppermute | solution.py:324
  28.6 12.2 %collective-permute-start.5 = (f32[4,56,512]{2,1,0:T(8,128)S(1)}, f32[4,56,512]{2,1,0:T(8,128)S(1)}, u32[]{:S(2)}, u32[]{:S(2)}) collective-permute-start(f32[4,56,512]{2,1,0:T(8,128)S(1)} %collective-permute-done.3.refs_1_), channel_id=1, source_target_pairs={{0,32},{32,64},{64,96},{96,128},{128,160},{160,192},{192,224},{224... | collective-permute-start | bytes 1376264 | tf_op jit(solution)/shard_map/ppermute | solution.py:324
  37.1 11.8 %collective-permute-start.8 = (f32[4,56,512]{2,1,0:T(8,128)S(1)}, f32[4,56,512]{2,1,0:T(8,128)S(1)}, u32[]{:S(2)}, u32[]{:S(2)}) collective-permute-start(f32[4,56,512]{2,1,0:T(8,128)S(1)} %collective-permute-done.6.refs_4_), channel_id=1, source_target_pairs={{0,224},{32,0},{64,32},{96,64},{128,96},{160,128},{192,160},{224,1... | collective-permute-start | bytes 1376264 | tf_op jit(solution)/shard_map/ppermute | solution.py:324
  40.8 11.4 %collective-permute-start.7 = (f32[4,56,512]{2,1,0:T(8,128)S(1)}, f32[4,56,512]{2,1,0:T(8,128)S(1)}, u32[]{:S(2)}, u32[]{:S(2)}) collective-permute-start(f32[4,56,512]{2,1,0:T(8,128)S(1)} %collective-permute-done.5.refs_3_), channel_id=1, source_target_pairs={{0,32},{32,64},{64,96},{96,128},{128,160},{160,192},{192,224},{224... | collective-permute-start | bytes 1376264 | tf_op jit(solution)/shard_map/ppermute | solution.py:324
  48.9 11.5 %collective-permute-start.10 = (f32[2,56,512]{2,1,0:T(8,128)S(1)}, f32[2,56,512]{2,1,0:T(8,128)S(1)}, u32[]{:S(2)}, u32[]{:S(2)}) collective-permute-start(f32[2,56,512]{2,1,0:T(8,128)S(1)} %slice.61), channel_id=1, source_target_pairs={{0,224},{32,0},{64,32},{96,64},{128,96},{160,128},{192,160},{224,1... | collective-permute-start | bytes 688136 | tf_op jit(solution)/shard_map/ppermute | solution.py:324
  52.2 8.2 %collective-permute-start.9 = (f32[2,56,512]{2,1,0:T(8,128)S(1)}, f32[2,56,512]{2,1,0:T(8,128)S(1)}, u32[]{:S(2)}, u32[]{:S(2)}) collective-permute-start(f32[2,56,512]{2,1,0:T(8,128)S(1)} %slice.60), channel_id=1, source_target_pairs={{0,32},{32,64},{64,96},{96,128},{128,160},{160,192},{192,224},{224... | collective-permute-start | bytes 688136 | tf_op jit(solution)/shard_map/ppermute | solution.py:324
  77.9 20.3 %all-to-all-start = ((f32[32,8,512]{2,1,0:T(8,128)}), f32[32,8,512]{2,1,0:T(8,128)S(1)}, u32[]{:S(2)}, u32[]{:S(2)}) async-start(f32[32,8,512]{2,1,0:T(8,128)} %get-tuple-element.38), calls=%async_computation | async-start | bytes 1048576 | tf_op jit(solution)/shard_map/all_to_all | solution.py:423
  88.5 1.3 collective-permute-start.11
  89.9 8.5 %collective-permute-start.12 = (f32[8,512]{1,0:T(8,128)S(1)}, f32[8,512]{1,0:T(8,128)S(1)}, u32[]{:S(2)}, u32[]{:S(2)}) collective-permute-start(f32[8,512]{1,0:T(8,128)S(1)} %get-tuple-element.44), channel_id=1, source_target_pairs={{0,6},{2,0},{4,2},{6,4},{1,7},{3,1},{5,3},{7,5},{8,14},{10,8},{12,... | collective-permute-start | bytes 49160 | tf_op jit(solution)/shard_map/ppermute | solution.py:324
  91.9 6.5 %collective-permute-start.14 = (f32[8,512]{1,0:T(8,128)S(1)}, f32[8,512]{1,0:T(8,128)S(1)}, u32[]{:S(2)}, u32[]{:S(2)}) collective-permute-start(f32[8,512]{1,0:T(8,128)S(1)} %get-tuple-element.45), channel_id=1, source_target_pairs={{0,2},{2,4},{4,6},{6,0},{1,3},{3,5},{5,7},{7,1},{8,10},{10,12},{12... | collective-permute-start | bytes 49160 | tf_op jit(solution)/shard_map/ppermute | solution.py:324
  92.0 6.4 %collective-permute-start.13 = (f32[8,512]{1,0:T(8,128)S(1)}, f32[8,512]{1,0:T(8,128)S(1)}, u32[]{:S(2)}, u32[]{:S(2)}) collective-permute-start(f32[8,512]{1,0:T(8,128)S(1)} %get-tuple-element.46), channel_id=1, source_target_pairs={{0,4},{2,6},{4,0},{6,2},{1,5},{3,7},{5,1},{7,3},{8,12},{10,14},{12... | collective-permute-start | bytes 49160 | tf_op jit(solution)/shard_map/ppermute | solution.py:324
  99.2 26.1 %all-to-all-start.1 = ((f32[32,8,512]{2,1,0:T(8,128)}), f32[32,8,512]{2,1,0:T(8,128)S(1)}, u32[]{:S(2)}, u32[]{:S(2)}) async-start(f32[32,8,512]{2,1,0:T(8,128)} %broadcast_in_dim.13), calls=%async_computation.1 | async-start | bytes 1048576 | tf_op jit(solution)/shard_map/all_to_all | solution.py:329
  109.9 9.0 %collective-permute-start.22 = (f32[2,8,512]{2,1,0:T(8,128)S(1)}, f32[2,8,512]{2,1,0:T(8,128)S(1)}, u32[]{:S(2)}, u32[]{:S(2)}) collective-permute-start(f32[2,8,512]{2,1,0:T(8,128)S(1)} %pad_maximum_fusion.1.after), channel_id=1, source_target_pairs={{0,6},{2,0},{4,2},{6,4},{1,7},{3,1},{5,3},{7,5},{8,14},{10,8},{12,... | collective-permute-start | bytes 98312 | tf_op jit(solution)/shard_map/ppermute | solution.py:324
  113.1 5.7 %collective-permute-start.21 = (f32[2,8,512]{2,1,0:T(8,128)S(1)}, f32[2,8,512]{2,1,0:T(8,128)S(1)}, u32[]{:S(2)}, u32[]{:S(2)}) collective-permute-start(f32[2,8,512]{2,1,0:T(8,128)S(1)} %pad_maximum_fusion.1.after), channel_id=1, source_target_pairs={{0,4},{2,6},{4,0},{6,2},{1,5},{3,7},{5,1},{7,3},{8,12},{10,14},{12... | collective-permute-start | bytes 98312 | tf_op jit(solution)/shard_map/ppermute | solution.py:324
  113.1 5.7 %collective-permute-start.20 = (f32[2,8,512]{2,1,0:T(8,128)S(1)}, f32[2,8,512]{2,1,0:T(8,128)S(1)}, u32[]{:S(2)}, u32[]{:S(2)}) collective-permute-start(f32[2,8,512]{2,1,0:T(8,128)S(1)} %pad_maximum_fusion.1.after), channel_id=1, source_target_pairs={{0,2},{2,4},{4,6},{6,0},{1,3},{3,5},{5,7},{7,1},{8,10},{10,12},{12... | collective-permute-start | bytes 98312 | tf_op jit(solution)/shard_map/ppermute | solution.py:324
  125.3 23.5 %all-to-all-start.2 = ((f32[32,8,512]{2,1,0:T(8,128)}), f32[32,8,512]{2,1,0:T(8,128)S(1)}, u32[]{:S(2)}, u32[]{:S(2)}) async-start(f32[32,8,512]{2,1,0:T(8,128)} %apply_cols.1), calls=%async_computation.2 | async-start | bytes 1048576 | tf_op jit(solution)/shard_map/all_to_all | solution.py:423
  139.3 9.6 %collective-permute-start.16 = (f32[8,512]{1,0:T(8,128)S(1)}, f32[8,512]{1,0:T(8,128)S(1)}, u32[]{:S(2)}, u32[]{:S(2)}) collective-permute-start(f32[8,512]{1,0:T(8,128)S(1)} %get-tuple-element.41), channel_id=1, source_target_pairs={{0,6},{2,0},{4,2},{6,4},{1,7},{3,1},{5,3},{7,5},{8,14},{10,8},{12,... | collective-permute-start | bytes 49160 | tf_op jit(solution)/shard_map/ppermute | solution.py:324
  141.7 7.2 %collective-permute-start.18 = (f32[8,512]{1,0:T(8,128)S(1)}, f32[8,512]{1,0:T(8,128)S(1)}, u32[]{:S(2)}, u32[]{:S(2)}) collective-permute-start(f32[8,512]{1,0:T(8,128)S(1)} %get-tuple-element.42), channel_id=1, source_target_pairs={{0,2},{2,4},{4,6},{6,0},{1,3},{3,5},{5,7},{7,1},{8,10},{10,12},{12... | collective-permute-start | bytes 49160 | tf_op jit(solution)/shard_map/ppermute | solution.py:324
  142.3 6.6 %collective-permute-start.17 = (f32[8,512]{1,0:T(8,128)S(1)}, f32[8,512]{1,0:T(8,128)S(1)}, u32[]{:S(2)}, u32[]{:S(2)}) collective-permute-start(f32[8,512]{1,0:T(8,128)S(1)} %get-tuple-element.43), channel_id=1, source_target_pairs={{0,4},{2,6},{4,0},{6,2},{1,5},{3,7},{5,1},{7,3},{8,12},{10,14},{12... | collective-permute-start | bytes 49160 | tf_op jit(solution)/shard_map/ppermute | solution.py:324
  (5 other events, 37.5 us)

commit v12 on v11

--- a/solution.py
+++ b/solution.py
@@ -75,13 +75,13 @@
 
 
 def multiply(field, high, low, dims):
-    terms = jnp.concatenate(split3(field), axis=0).astype(jnp.bfloat16)
+    upper = field.astype(jnp.bfloat16).astype(jnp.float32)
+    terms = jnp.concatenate([upper, field - upper], axis=0).astype(jnp.bfloat16)
     dot = functools.partial(
         lax.dot_general, dimension_numbers=dims, preferred_element_type=jnp.float32
     )
-    by_high = dot(terms, high)
-    by_low = dot(terms[:16], low)
-    return (by_high[0:8] + by_low[0:8]) + (by_high[8:16] + by_low[8:16]) + by_high[16:24]
+    product = dot(terms, high) + dot(terms, low)
+    return product[0:8] + product[8:16]
 
 
 def stage_kernel(stage, sources, table, prepared_ref, row_vec, *refs):

time: 179 us -> 180 us (level)
  starting transfers between devices: 57.4 us -> 70.3 us
  Pallas kernels: 65.3 us -> 56.1 us
  waiting for transfers between devices: 22.7 us -> 20.1 us
    all_to_all x2, starting transfers between devices: 13 us -> 24.5 us  [combine(): by_col = lax.all_to_all(col_acc, ROW, 0, 0, tiled=True)]
    pallas_call x5, Pallas kernels: 39 us -> 33.3 us  [form_stage(): pl.pallas_call(functools.partial(stage_kernel, stage, len(places)), in_sp...]
    pallas_call x2, Pallas kernels: 10.1 us -> 7.86 us  [apply_tiles(): pl.pallas_call(functools.partial(apply_kernel, wanted, col_at), in_specs=...]
    ppermute x23, waiting for transfers between devices: 11.4 us -> 9.57 us  [shift(): lax.ppermute(value, axis, [(i, (i + distance) % size) for i in range(size)])]
  transfers between devices with their start and end apart: 26 -> 26, of which waited for: 10 -> 10; matrix products, arithmetic and copies ran while one was open for 0% -> 0% of each run, Pallas kernels for 27% -> 26%
where the time goes in v12:
time: 180 us
  starting transfers between devices  70.3 us (39%)
  Pallas kernels  56.1 us (31%)
  blocking collectives  29 us (16%)
  waiting for transfers between devices  20.1 us (11%)
  local copies, waits for them, and re-layouts  2.1 us (1%)
  other arithmetic  2.06 us (1%)
    ppermute x23, starting transfers between devices, shift(): lax.ppermute(value, axis, [(i, (i + distance) % size) for i in range(size)])  36.1 us
    pallas_call x5, Pallas kernels, form_stage(): pl.pallas_call(functools.partial(stage_kernel, stage, len(places)), in_sp...  33.3 us
    all_to_all x2, blocking collectives, spread(): return lax.all_to_all(copies, axes, 0, 0, tiled=True)  29 us
    all_to_all x2, starting transfers between devices, combine(): by_col = lax.all_to_all(col_acc, ROW, 0, 0, tiled=True)  24.5 us
    all_to_all x1, starting transfers between devices, spread(): return lax.all_to_all(copies, axes, 0, 0, tiled=True)  9.69 us
    ppermute x23, waiting for transfers between devices, shift(): lax.ppermute(value, axis, [(i, (i + distance) % size) for i in range(size)])  9.57 us
    pallas_call x2, Pallas kernels, apply_tiles(): pl.pallas_call(functools.partial(apply_kernel, wanted, col_at), in_specs=...  7.86 us
    all_to_all x2, waiting for transfers between devices, combine(): by_col = lax.all_to_all(col_acc, ROW, 0, 0, tiled=True)  7.74 us
  transfers between devices with their start and end apart: 26, of which 10 were waited for; matrix products, arithmetic and copies ran while one was open for 0% of the time, Pallas kernels for 26%

profile of v12, /device:TPU:0, one launch (start us, length us, event | category | flops | bytes accessed | tf_op | source)
XLA Modules:
  0.0 180.0 jit_solution(6894257230017691372)
XLA Ops:
  9.6 4.9 %collective-permute-start.4 = (f32[4,56,512]{2,1,0:T(8,128)S(1)}, f32[4,56,512]{2,1,0:T(8,128)S(1)}, u32[]{:S(2)}, u32[]{:S(2)}) collective-permute-start(f32[4,56,512]{2,1,0:T(8,128)S(1)} %pad_maximum_fusion.refs_0_), channel_id=1, source_target_pairs={{0,224},{32,0},{64,32},{96,64},{128,96},{160,128},{192,160},{224,1... | collective-permute-start | bytes 1376264 | tf_op jit(solution)/shard_map/ppermute | solution.py:324
  15.6 5.1 %prepare_rows.1.prepared_ref = bf16[8,16,512,48]{3,2,1,0:T(8,128)(2,1)S(1)} custom-call(f32[48,4096]{1,0:T(8,128)S(1)} %bitcast.58), custom_call_target="tpu_custom_call" | custom-call | flops 100000000 | bytes 8388608 | tf_op jit(solution)/shard_map/prepare_rows/pallas_call | solution.py:66
  20.8 4.5 %form_0.1 = (bf16[10,2,512,512]{3,2,1,0:T(8,128)(2,1)}, f32[8,8,512]{2,1,0:T(8,128)S(1)}, f32[32,8,512]{2,1,0:T(8,128)S(1)}) custom-call(s32[10,10]{1,0:T(8,128)S(1)} %copy-done.2, bf16[8,16,512,48]{3,2,1,0:T(8,128)(2,1)S(1)} %prepare_rows.1.prepared_ref, f32[8,8,512]{2,1,0:T(8,128)S(1)} %bitcast.59, f32[4,56,512]{2,1,0:T(8,128)S(1)} %pad_maximum_fusion.refs_0_), custom_call_target="tpu_custom_call" | custom-call | flops 8000000000 | bytes 8388608 | tf_op jit(solution)/shard_map/form_0/pallas_call | solution.py:180
  25.3 3.3 %collective-permute-start.6 = (f32[4,56,512]{2,1,0:T(8,128)S(1)}, f32[4,56,512]{2,1,0:T(8,128)S(1)}, u32[]{:S(2)}, u32[]{:S(2)}) collective-permute-start(f32[4,56,512]{2,1,0:T(8,128)S(1)} %collective-permute-done.4.refs_2_), channel_id=1, source_target_pairs={{0,224},{32,0},{64,32},{96,64},{128,96},{160,128},{192,160},{224,1... | collective-permute-start | bytes 1376264 | tf_op jit(solution)/shard_map/ppermute | solution.py:324
  28.6 7.8 %form_1.1 = (bf16[10,2,512,512]{3,2,1,0:T(8,128)(2,1)}, f32[8,8,512]{2,1,0:T(8,128)S(1)}, f32[32,8,512]{2,1,0:T(8,128)S(1)}) custom-call(s32[10,10]{1,0:T(8,128)S(1)} %copy-done.2, bf16[8,16,512,48]{3,2,1,0:T(8,128)(2,1)S(1)} %prepare_rows.1.prepared_ref, f32[8,8,512]{2,1,0:T(8,128)S(1)} %bitcast.60, ...), custom_call_target="tpu_custom_call", output_to_operand_aliasing={{0}: (6, {}), {1}: (7, {}), {2}: (8, {})} | custom-call | flops 8000000000 | bytes 8388608 | tf_op jit(solution)/shard_map/form_1/pallas_call | solution.py:180
  37.1 3.7 %collective-permute-start.8 = (f32[4,56,512]{2,1,0:T(8,128)S(1)}, f32[4,56,512]{2,1,0:T(8,128)S(1)}, u32[]{:S(2)}, u32[]{:S(2)}) collective-permute-start(f32[4,56,512]{2,1,0:T(8,128)S(1)} %collective-permute-done.6.refs_4_), channel_id=1, source_target_pairs={{0,224},{32,0},{64,32},{96,64},{128,96},{160,128},{192,160},{224,1... | collective-permute-start | bytes 1376264 | tf_op jit(solution)/shard_map/ppermute | solution.py:324
  40.8 7.9 %form_2.1 = (bf16[10,2,512,512]{3,2,1,0:T(8,128)(2,1)}, f32[8,8,512]{2,1,0:T(8,128)S(1)}, f32[32,8,512]{2,1,0:T(8,128)S(1)}) custom-call(s32[10,10]{1,0:T(8,128)S(1)} %copy-done.2, bf16[8,16,512,48]{3,2,1,0:T(8,128)(2,1)S(1)} %prepare_rows.1.prepared_ref, f32[8,8,512]{2,1,0:T(8,128)S(1)} %bitcast.61, ...), custom_call_target="tpu_custom_call", output_to_operand_aliasing={{0}: (8, {}), {1}: (9, {}), {2}: (10, {})} | custom-call | flops 8000000000 | bytes 8388608 | tf_op jit(solution)/shard_map/form_2/pallas_call | solution.py:180
  48.7 3.4 %collective-permute-start.10 = (f32[2,56,512]{2,1,0:T(8,128)S(1)}, f32[2,56,512]{2,1,0:T(8,128)S(1)}, u32[]{:S(2)}, u32[]{:S(2)}) collective-permute-start(f32[2,56,512]{2,1,0:T(8,128)S(1)} %slice.61), channel_id=1, source_target_pairs={{0,224},{32,0},{64,32},{96,64},{128,96},{160,128},{192,160},{224,1... | collective-permute-start | bytes 688136 | tf_op jit(solution)/shard_map/ppermute | solution.py:324
  52.2 4.6 %form_3.1 = (bf16[10,2,512,512]{3,2,1,0:T(8,128)(2,1)}, f32[8,8,512]{2,1,0:T(8,128)S(1)}, f32[32,8,512]{2,1,0:T(8,128)S(1)}) custom-call(s32[10,10]{1,0:T(8,128)S(1)} %copy-done.2, bf16[8,16,512,48]{3,2,1,0:T(8,128)(2,1)S(1)} %prepare_rows.1.prepared_ref, f32[8,8,512]{2,1,0:T(8,128)S(1)} %bitcast.62, ...), custom_call_target="tpu_custom_call", output_to_operand_aliasing={{0}: (10, {}), {1}: (11, {}), {2}: (12, {})} | custom-call | flops 8000000000 | bytes 8388608 | tf_op jit(solution)/shard_map/form_3/pallas_call | solution.py:180
  59.4 8.5 %form_4.1 = (bf16[10,2,512,512]{3,2,1,0:T(8,128)(2,1)}, f32[10,8,512]{2,1,0:T(8,128)S(1)}, f32[32,8,512]{2,1,0:T(8,128)}) custom-call(s32[10,10]{1,0:T(8,128)S(1)} %copy-done.2, bf16[8,16,512,48]{3,2,1,0:T(8,128)(2,1)S(1)} %prepare_rows.1.prepared_ref, f32[8,8,512]{2,1,0:T(8,128)S(1)} %bitcast.63, ...), custom_call_target="tpu_custom_call", output_to_operand_aliasing={{0}: (12, {})} | custom-call | flops 8000000000 | bytes 8388608 | tf_op jit(solution)/shard_map/form_4/pallas_call | solution.py:180
  67.9 17.0 %all-to-all-start = ((f32[32,8,512]{2,1,0:T(8,128)}), f32[32,8,512]{2,1,0:T(8,128)S(1)}, u32[]{:S(2)}, u32[]{:S(2)}) async-start(f32[32,8,512]{2,1,0:T(8,128)} %get-tuple-element.38), calls=%async_computation | async-start | bytes 1048576 | tf_op jit(solution)/shard_map/all_to_all | solution.py:423
  89.3 4.2 %collective-permute-start.14 = (f32[8,512]{1,0:T(8,128)S(1)}, f32[8,512]{1,0:T(8,128)S(1)}, u32[]{:S(2)}, u32[]{:S(2)}) collective-permute-start(f32[8,512]{1,0:T(8,128)S(1)} %get-tuple-element.45), channel_id=1, source_target_pairs={{0,2},{2,4},{4,6},{6,0},{1,3},{3,5},{5,7},{7,1},{8,10},{10,12},{12... | collective-permute-start | bytes 49160 | tf_op jit(solution)/shard_map/ppermute | solution.py:324
  95.4 3.4 %all-to-all-done = f32[32,8,512]{2,1,0:T(8,128)S(1)} async-done(((f32[32,8,512]{2,1,0:T(8,128)}), f32[32,8,512]{2,1,0:T(8,128)S(1)}, u32[]{:S(2)}, u32[]{:S(2)}) %all-to-all-start) | async-done | bytes 524320 | tf_op jit(solution)/shard_map/all_to_all | solution.py:423
  99.7 9.7 %all-to-all-start.1 = ((f32[32,8,512]{2,1,0:T(8,128)}), f32[32,8,512]{2,1,0:T(8,128)S(1)}, u32[]{:S(2)}, u32[]{:S(2)}) async-start(f32[32,8,512]{2,1,0:T(8,128)} %broadcast_in_dim.13), calls=%async_computation.1 | async-start | bytes 1048576 | tf_op jit(solution)/shard_map/all_to_all | solution.py:329
  111.8 2.9 %collective-permute-start.21 = (f32[2,8,512]{2,1,0:T(8,128)S(1)}, f32[2,8,512]{2,1,0:T(8,128)S(1)}, u32[]{:S(2)}, u32[]{:S(2)}) collective-permute-start(f32[2,8,512]{2,1,0:T(8,128)S(1)} %pad_maximum_fusion.1.after), channel_id=1, source_target_pairs={{0,4},{2,6},{4,0},{6,2},{1,5},{3,7},{5,1},{7,3},{8,12},{10,14},{12... | collective-permute-start | bytes 98312 | tf_op jit(solution)/shard_map/ppermute | solution.py:324
  114.7 4.2 %fetch.1.pair = bf16[10,2,512,512]{3,2,1,0:T(8,128)(2,1)S(1)} custom-call(s32[10,10]{1,0:T(8,128)S(1)} %copy-done.2, bf16[10,2,512,512]{3,2,1,0:T(8,128)(2,1)} %get-tuple-element.36.pair_ref, f32[2,8,512]{2,1,0:T(8,128)S(1)} %pad_maximum_fusion.1.after), custom_call_target="tpu_custom_call" | custom-call | bytes 12582912 | tf_op jit(solution)/shard_map/fetch/pallas_call | solution.py:276
  119.9 3.5 %apply_cols.1 = f32[32,8,512]{2,1,0:T(8,128)} custom-call(s32[10,10]{1,0:T(8,128)S(1)} %copy-done.2, bf16[10,2,512,512]{3,2,1,0:T(8,128)(2,1)S(1)} %fetch.1.pair, f32[8,8,512]{2,1,0:T(8,128)S(1)} %constant_dynamic-update-slice_fusion.field), custom_call_target="tpu_custom_call" | custom-call | flops 3000000000 | bytes 1048576 | tf_op jit(solution)/shard_map/apply_cols/pallas_call | solution.py:309
  123.4 2.8 %all-to-all-done.1.field = f32[32,8,512]{2,1,0:T(8,128)S(1)} async-done(((f32[32,8,512]{2,1,0:T(8,128)}), f32[32,8,512]{2,1,0:T(8,128)S(1)}, u32[]{:S(2)}, u32[]{:S(2)}) %all-to-all-start.1) | async-done | bytes 524320 | tf_op jit(solution)/shard_map/all_to_all | solution.py:329
  126.2 7.5 %all-to-all-start.2 = ((f32[32,8,512]{2,1,0:T(8,128)}), f32[32,8,512]{2,1,0:T(8,128)S(1)}, u32[]{:S(2)}, u32[]{:S(2)}) async-start(f32[32,8,512]{2,1,0:T(8,128)} %apply_cols.1), calls=%async_computation.2 | async-start | bytes 1048576 | tf_op jit(solution)/shard_map/all_to_all | solution.py:423
  133.7 5.1 %apply_rows.1 = f32[8,8,512]{2,1,0:T(8,128)S(1)} custom-call(s32[10,10]{1,0:T(8,128)S(1)} %copy-done.2, bf16[10,2,512,512]{3,2,1,0:T(8,128)(2,1)} %get-tuple-element.36.pair_ref, f32[32,8,512]{2,1,0:T(8,128)S(1)} %all-to-all-done.1.field), custom_call_target="tpu_custom_call" | custom-call | flops 3000000000 | bytes 12582912 | tf_op jit(solution)/shard_map/apply_rows/pallas_call | solution.py:238
  140.2 3.8 %collective-permute-start.16 = (f32[8,512]{1,0:T(8,128)S(1)}, f32[8,512]{1,0:T(8,128)S(1)}, u32[]{:S(2)}, u32[]{:S(2)}) collective-permute-start(f32[8,512]{1,0:T(8,128)S(1)} %get-tuple-element.41), channel_id=1, source_target_pairs={{0,6},{2,0},{4,2},{6,4},{1,7},{3,1},{5,3},{7,5},{8,14},{10,8},{12,... | collective-permute-start | bytes 49160 | tf_op jit(solution)/shard_map/ppermute | solution.py:324
  145.5 4.4 %all-to-all-done.2 = f32[32,8,512]{2,1,0:T(8,128)S(1)} async-done(((f32[32,8,512]{2,1,0:T(8,128)}), f32[32,8,512]{2,1,0:T(8,128)S(1)}, u32[]{:S(2)}, u32[]{:S(2)}) %all-to-all-start.2) | async-done | bytes 524320 | tf_op jit(solution)/shard_map/all_to_all | solution.py:423
  150.0 11.2 %all_to_all.25 = f32[8,8,512]{2,1,0:T(8,128)S(1)} all-to-all(f32[8,8,512]{2,1,0:T(8,128)S(1)} %broadcast_in_dim.14), channel_id=1, replica_groups=mesh['z'=8,'y'=4,'x'=4,'core'=2] {'x','core'}, dimensions={0} | all-to-all | bytes 262144 | tf_op jit(solution)/shard_map/all_to_all | solution.py:329
  161.4 17.8 %all_to_all.26 = f32[32,1,128]{2,1,0:T(1,128)S(1)} all-to-all(f32[32,1,128]{2,1,0:T(1,128)S(1)} %broadcast_in_dim.16), channel_id=1, replica_groups=mesh['z'=8,'y'=4,'x'=4,'core'=2] {'z','y'}, dimensions={0} | all-to-all | bytes 32768 | tf_op jit(solution)/shard_map/all_to_all | solution.py:329
  (74 shorter events, 28.5 us)
Async XLA Ops:
  0.9 6.9 %collective-permute-start.1 = (f32[56,512]{1,0:T(8,128)S(1)}, f32[56,512]{1,0:T(8,128)S(1)}, u32[]{:S(2)}, u32[]{:S(2)}) collective-permute-start(f32[56,512]{1,0:T(8,128)S(1)} %fusion), channel_id=1, source_target_pairs={{0,16},{8,24},{16,0},{24,8},{1,17},{9,25},{17,1},{25,9},{2,18},{10... | collective-permute-start | bytes 344072 | tf_op jit(solution)/shard_map/ppermute | solution.py:324
  2.5 7.0 %collective-permute-start = (f32[56,512]{1,0:T(8,128)S(1)}, f32[56,512]{1,0:T(8,128)S(1)}, u32[]{:S(2)}, u32[]{:S(2)}) collective-permute-start(f32[56,512]{1,0:T(8,128)S(1)} %fusion), channel_id=1, source_target_pairs={{0,8},{8,16},{16,24},{24,0},{1,9},{9,17},{17,25},{25,1},{2,10},{10... | collective-permute-start | bytes 344072 | tf_op jit(solution)/shard_map/ppermute | solution.py:324
  3.2 6.4 %collective-permute-start.2 = (f32[56,512]{1,0:T(8,128)S(1)}, f32[56,512]{1,0:T(8,128)S(1)}, u32[]{:S(2)}, u32[]{:S(2)}) collective-permute-start(f32[56,512]{1,0:T(8,128)S(1)} %fusion), channel_id=1, source_target_pairs={{0,24},{8,0},{16,8},{24,16},{1,25},{9,1},{17,9},{25,17},{2,26},{10... | collective-permute-start | bytes 344072 | tf_op jit(solution)/shard_map/ppermute | solution.py:324
  9.6 15.7 %collective-permute-start.4 = (f32[4,56,512]{2,1,0:T(8,128)S(1)}, f32[4,56,512]{2,1,0:T(8,128)S(1)}, u32[]{:S(2)}, u32[]{:S(2)}) collective-permute-start(f32[4,56,512]{2,1,0:T(8,128)S(1)} %pad_maximum_fusion.refs_0_), channel_id=1, source_target_pairs={{0,224},{32,0},{64,32},{96,64},{128,96},{160,128},{192,160},{224,1... | collective-permute-start | bytes 1376264 | tf_op jit(solution)/shard_map/ppermute | solution.py:324
  14.5 14.1 %collective-permute-start.3 = (f32[4,56,512]{2,1,0:T(8,128)S(1)}, f32[4,56,512]{2,1,0:T(8,128)S(1)}, u32[]{:S(2)}, u32[]{:S(2)}) collective-permute-start(f32[4,56,512]{2,1,0:T(8,128)S(1)} %pad_maximum_fusion.refs_0_), channel_id=1, source_target_pairs={{0,32},{32,64},{64,96},{96,128},{128,160},{160,192},{192,224},{224... | collective-permute-start | bytes 1376264 | tf_op jit(solution)/shard_map/ppermute | solution.py:324
  25.3 11.8 %collective-permute-start.6 = (f32[4,56,512]{2,1,0:T(8,128)S(1)}, f32[4,56,512]{2,1,0:T(8,128)S(1)}, u32[]{:S(2)}, u32[]{:S(2)}) collective-permute-start(f32[4,56,512]{2,1,0:T(8,128)S(1)} %collective-permute-done.4.refs_2_), channel_id=1, source_target_pairs={{0,224},{32,0},{64,32},{96,64},{128,96},{160,128},{192,160},{224,1... | collective-permute-start | bytes 1376264 | tf_op jit(solution)/shard_map/ppermute | solution.py:324
  28.6 12.2 %collective-permute-start.5 = (f32[4,56,512]{2,1,0:T(8,128)S(1)}, f32[4,56,512]{2,1,0:T(8,128)S(1)}, u32[]{:S(2)}, u32[]{:S(2)}) collective-permute-start(f32[4,56,512]{2,1,0:T(8,128)S(1)} %collective-permute-done.3.refs_1_), channel_id=1, source_target_pairs={{0,32},{32,64},{64,96},{96,128},{128,160},{160,192},{192,224},{224... | collective-permute-start | bytes 1376264 | tf_op jit(solution)/shard_map/ppermute | solution.py:324
  37.1 11.6 %collective-permute-start.8 = (f32[4,56,512]{2,1,0:T(8,128)S(1)}, f32[4,56,512]{2,1,0:T(8,128)S(1)}, u32[]{:S(2)}, u32[]{:S(2)}) collective-permute-start(f32[4,56,512]{2,1,0:T(8,128)S(1)} %collective-permute-done.6.refs_4_), channel_id=1, source_target_pairs={{0,224},{32,0},{64,32},{96,64},{128,96},{160,128},{192,160},{224,1... | collective-permute-start | bytes 1376264 | tf_op jit(solution)/shard_map/ppermute | solution.py:324
  40.8 11.3 %collective-permute-start.7 = (f32[4,56,512]{2,1,0:T(8,128)S(1)}, f32[4,56,512]{2,1,0:T(8,128)S(1)}, u32[]{:S(2)}, u32[]{:S(2)}) collective-permute-start(f32[4,56,512]{2,1,0:T(8,128)S(1)} %collective-permute-done.5.refs_3_), channel_id=1, source_target_pairs={{0,32},{32,64},{64,96},{96,128},{128,160},{160,192},{192,224},{224... | collective-permute-start | bytes 1376264 | tf_op jit(solution)/shard_map/ppermute | solution.py:324
  48.7 8.1 %collective-permute-start.10 = (f32[2,56,512]{2,1,0:T(8,128)S(1)}, f32[2,56,512]{2,1,0:T(8,128)S(1)}, u32[]{:S(2)}, u32[]{:S(2)}) collective-permute-start(f32[2,56,512]{2,1,0:T(8,128)S(1)} %slice.61), channel_id=1, source_target_pairs={{0,224},{32,0},{64,32},{96,64},{128,96},{160,128},{192,160},{224,1... | collective-permute-start | bytes 688136 | tf_op jit(solution)/shard_map/ppermute | solution.py:324
  52.1 7.3 %collective-permute-start.9 = (f32[2,56,512]{2,1,0:T(8,128)S(1)}, f32[2,56,512]{2,1,0:T(8,128)S(1)}, u32[]{:S(2)}, u32[]{:S(2)}) collective-permute-start(f32[2,56,512]{2,1,0:T(8,128)S(1)} %slice.60), channel_id=1, source_target_pairs={{0,32},{32,64},{64,96},{96,128},{128,160},{160,192},{192,224},{224... | collective-permute-start | bytes 688136 | tf_op jit(solution)/shard_map/ppermute | solution.py:324
  67.9 30.9 %all-to-all-start = ((f32[32,8,512]{2,1,0:T(8,128)}), f32[32,8,512]{2,1,0:T(8,128)S(1)}, u32[]{:S(2)}, u32[]{:S(2)}) async-start(f32[32,8,512]{2,1,0:T(8,128)} %get-tuple-element.38), calls=%async_computation | async-start | bytes 1048576 | tf_op jit(solution)/shard_map/all_to_all | solution.py:423
  87.7 1.3 collective-permute-start.11
  89.1 9.7 %collective-permute-start.12 = (f32[8,512]{1,0:T(8,128)S(1)}, f32[8,512]{1,0:T(8,128)S(1)}, u32[]{:S(2)}, u32[]{:S(2)}) collective-permute-start(f32[8,512]{1,0:T(8,128)S(1)} %get-tuple-element.44), channel_id=1, source_target_pairs={{0,6},{2,0},{4,2},{6,4},{1,7},{3,1},{5,3},{7,5},{8,14},{10,8},{12,... | collective-permute-start | bytes 49160 | tf_op jit(solution)/shard_map/ppermute | solution.py:324
  89.3 9.6 %collective-permute-start.14 = (f32[8,512]{1,0:T(8,128)S(1)}, f32[8,512]{1,0:T(8,128)S(1)}, u32[]{:S(2)}, u32[]{:S(2)}) collective-permute-start(f32[8,512]{1,0:T(8,128)S(1)} %get-tuple-element.45), channel_id=1, source_target_pairs={{0,2},{2,4},{4,6},{6,0},{1,3},{3,5},{5,7},{7,1},{8,10},{10,12},{12... | collective-permute-start | bytes 49160 | tf_op jit(solution)/shard_map/ppermute | solution.py:324
  93.4 5.4 %collective-permute-start.13 = (f32[8,512]{1,0:T(8,128)S(1)}, f32[8,512]{1,0:T(8,128)S(1)}, u32[]{:S(2)}, u32[]{:S(2)}) collective-permute-start(f32[8,512]{1,0:T(8,128)S(1)} %get-tuple-element.46), channel_id=1, source_target_pairs={{0,4},{2,6},{4,0},{6,2},{1,5},{3,7},{5,1},{7,3},{8,12},{10,14},{12... | collective-permute-start | bytes 49160 | tf_op jit(solution)/shard_map/ppermute | solution.py:324
  99.7 26.5 %all-to-all-start.1 = ((f32[32,8,512]{2,1,0:T(8,128)}), f32[32,8,512]{2,1,0:T(8,128)S(1)}, u32[]{:S(2)}, u32[]{:S(2)}) async-start(f32[32,8,512]{2,1,0:T(8,128)} %broadcast_in_dim.13), calls=%async_computation.1 | async-start | bytes 1048576 | tf_op jit(solution)/shard_map/all_to_all | solution.py:329
  110.7 9.1 %collective-permute-start.22 = (f32[2,8,512]{2,1,0:T(8,128)S(1)}, f32[2,8,512]{2,1,0:T(8,128)S(1)}, u32[]{:S(2)}, u32[]{:S(2)}) collective-permute-start(f32[2,8,512]{2,1,0:T(8,128)S(1)} %pad_maximum_fusion.1.after), channel_id=1, source_target_pairs={{0,6},{2,0},{4,2},{6,4},{1,7},{3,1},{5,3},{7,5},{8,14},{10,8},{12,... | collective-permute-start | bytes 98312 | tf_op jit(solution)/shard_map/ppermute | solution.py:324
  111.8 8.1 %collective-permute-start.21 = (f32[2,8,512]{2,1,0:T(8,128)S(1)}, f32[2,8,512]{2,1,0:T(8,128)S(1)}, u32[]{:S(2)}, u32[]{:S(2)}) collective-permute-start(f32[2,8,512]{2,1,0:T(8,128)S(1)} %pad_maximum_fusion.1.after), channel_id=1, source_target_pairs={{0,4},{2,6},{4,0},{6,2},{1,5},{3,7},{5,1},{7,3},{8,12},{10,14},{12... | collective-permute-start | bytes 98312 | tf_op jit(solution)/shard_map/ppermute | solution.py:324
  114.7 5.1 %collective-permute-start.20 = (f32[2,8,512]{2,1,0:T(8,128)S(1)}, f32[2,8,512]{2,1,0:T(8,128)S(1)}, u32[]{:S(2)}, u32[]{:S(2)}) collective-permute-start(f32[2,8,512]{2,1,0:T(8,128)S(1)} %pad_maximum_fusion.1.after), channel_id=1, source_target_pairs={{0,2},{2,4},{4,6},{6,0},{1,3},{3,5},{5,7},{7,1},{8,10},{10,12},{12... | collective-permute-start | bytes 98312 | tf_op jit(solution)/shard_map/ppermute | solution.py:324
  126.2 23.7 %all-to-all-start.2 = ((f32[32,8,512]{2,1,0:T(8,128)}), f32[32,8,512]{2,1,0:T(8,128)S(1)}, u32[]{:S(2)}, u32[]{:S(2)}) async-start(f32[32,8,512]{2,1,0:T(8,128)} %apply_cols.1), calls=%async_computation.2 | async-start | bytes 1048576 | tf_op jit(solution)/shard_map/all_to_all | solution.py:423
  140.2 9.8 %collective-permute-start.16 = (f32[8,512]{1,0:T(8,128)S(1)}, f32[8,512]{1,0:T(8,128)S(1)}, u32[]{:S(2)}, u32[]{:S(2)}) collective-permute-start(f32[8,512]{1,0:T(8,128)S(1)} %get-tuple-element.41), channel_id=1, source_target_pairs={{0,6},{2,0},{4,2},{6,4},{1,7},{3,1},{5,3},{7,5},{8,14},{10,8},{12,... | collective-permute-start | bytes 49160 | tf_op jit(solution)/shard_map/ppermute | solution.py:324
  144.0 6.0 %collective-permute-start.18 = (f32[8,512]{1,0:T(8,128)S(1)}, f32[8,512]{1,0:T(8,128)S(1)}, u32[]{:S(2)}, u32[]{:S(2)}) collective-permute-start(f32[8,512]{1,0:T(8,128)S(1)} %get-tuple-element.42), channel_id=1, source_target_pairs={{0,2},{2,4},{4,6},{6,0},{1,3},{3,5},{5,7},{7,1},{8,10},{10,12},{12... | collective-permute-start | bytes 49160 | tf_op jit(solution)/shard_map/ppermute | solution.py:324
  144.0 6.0 %collective-permute-start.17 = (f32[8,512]{1,0:T(8,128)S(1)}, f32[8,512]{1,0:T(8,128)S(1)}, u32[]{:S(2)}, u32[]{:S(2)}) collective-permute-start(f32[8,512]{1,0:T(8,128)S(1)} %get-tuple-element.43), channel_id=1, source_target_pairs={{0,4},{2,6},{4,0},{6,2},{1,5},{3,7},{5,1},{7,3},{8,12},{10,14},{12... | collective-permute-start | bytes 49160 | tf_op jit(solution)/shard_map/ppermute | solution.py:324
  (5 other events, 37.5 us)

commit v13 on v10

--- a/solution.py
+++ b/solution.py
@@ -366,12 +366,8 @@
     table = slot_table(pairs[0, 0].transpose(1, 0), valid[0], sizes)
 
     flat = positions.transpose(1, 0, 2).reshape(48, block)
-    own = jnp.concatenate(
-        [
-            lax.dynamic_slice_in_dim(flat, grid_col * TILE, TILE, 1),
-            lax.dynamic_slice_in_dim(vectors, grid_col * TILE, TILE, 1),
-        ],
-        axis=0,
+    own = lax.dynamic_slice_in_dim(
+        jnp.concatenate([flat, vectors], axis=0), grid_col * TILE, TILE, 1
     )
     row_vec = vectors.reshape(8, tiles, TILE).transpose(1, 0, 2)
     near = gather_y(own)

time: 178 us -> 180 us (1.011)
  starting transfers between devices: 59.4 us -> 65.3 us
  Pallas kernels: 62.4 us -> 58 us
  blocking collectives: 26.6 us -> 28.5 us
    ppermute x23, starting transfers between devices: 34.6 us -> 39.8 us  [shift(): lax.ppermute(value, axis, [(i, (i + distance) % size) for i in range(size)])]
    pallas_call x5, Pallas kernels: 40.1 us -> 36 us  [form_stage(): pl.pallas_call(functools.partial(stage_kernel, stage, len(places)), in_sp...]
    ppermute x23, waiting for transfers between devices: 9.16 us -> 13.1 us  [shift(): lax.ppermute(value, axis, [(i, (i + distance) % size) for i in range(size)])]
    all_to_all x2, waiting for transfers between devices: 11.1 us -> 7.5 us  [combine(): by_col = lax.all_to_all(col_acc, ROW, 0, 0, tiled=True)]
    all_to_all x2, blocking collectives: 26.6 us -> 28.5 us  [spread(): return lax.all_to_all(copies, axes, 0, 0, tiled=True)]
  transfers between devices with their start and end apart: 26 -> 26, of which waited for: 11 -> 11; matrix products, arithmetic and copies ran while one was open for 0% -> 0% of each run, Pallas kernels for 29% -> 24%
where the time goes in v13:
time: 180 us; the launch traced here: 179 us
  starting transfers between devices  65.3 us (36%)
  Pallas kernels  58 us (32%)
  blocking collectives  28.5 us (16%)
  waiting for transfers between devices  22.2 us (12%)
  local copies, waits for them, and re-layouts  2.09 us (1%)
  other arithmetic  2.07 us (1%)
    ppermute x23, starting transfers between devices, shift(): lax.ppermute(value, axis, [(i, (i + distance) % size) for i in range(size)])  39.8 us
    pallas_call x5, Pallas kernels, form_stage(): pl.pallas_call(functools.partial(stage_kernel, stage, len(places)), in_sp...  36 us
    all_to_all x2, blocking collectives, spread(): return lax.all_to_all(copies, axes, 0, 0, tiled=True)  28.5 us
    all_to_all x2, starting transfers between devices, combine(): by_col = lax.all_to_all(col_acc, ROW, 0, 0, tiled=True)  17.6 us
    pallas_call x3, Pallas kernels, apply_tiles(): pl.pallas_call(functools.partial(apply_kernel, wanted, col_at), in_specs=...  14.8 us
    ppermute x23, waiting for transfers between devices, shift(): lax.ppermute(value, axis, [(i, (i + distance) % size) for i in range(size)])  13.1 us
    all_to_all x1, starting transfers between devices, spread(): return lax.all_to_all(copies, axes, 0, 0, tiled=True)  7.94 us
    all_to_all x2, waiting for transfers between devices, combine(): by_col = lax.all_to_all(col_acc, ROW, 0, 0, tiled=True)  7.5 us
  transfers between devices with their start and end apart: 26, of which 11 were waited for; matrix products, arithmetic and copies ran while one was open for 0% of the time, Pallas kernels for 24%

profile of v13, /device:TPU:0, one launch (start us, length us, event | category | flops | bytes accessed | tf_op | source)
XLA Modules:
  0.0 178.6 jit_solution(14581462948805667379)
XLA Ops:
  9.6 4.9 %collective-permute-start.4 = (f32[4,56,512]{2,1,0:T(8,128)S(1)}, f32[4,56,512]{2,1,0:T(8,128)S(1)}, u32[]{:S(2)}, u32[]{:S(2)}) collective-permute-start(f32[4,56,512]{2,1,0:T(8,128)S(1)} %pad_maximum_fusion.refs_0_), channel_id=1, source_target_pairs={{0,224},{32,0},{64,32},{96,64},{128,96},{160,128},{192,160},{224,1... | collective-permute-start | bytes 1376264 | tf_op jit(solution)/shard_map/ppermute | solution.py:257
  15.6 5.1 %prepare_rows.1.prepared_ref = bf16[8,16,512,48]{3,2,1,0:T(8,128)(2,1)S(1)} custom-call(f32[48,4096]{1,0:T(8,128)S(1)} %bitcast.61), custom_call_target="tpu_custom_call" | custom-call | flops 100000000 | bytes 8388608 | tf_op jit(solution)/shard_map/prepare_rows/pallas_call | solution.py:66
  23.5 5.1 %collective-permute-start.6 = (f32[4,56,512]{2,1,0:T(8,128)S(1)}, f32[4,56,512]{2,1,0:T(8,128)S(1)}, u32[]{:S(2)}, u32[]{:S(2)}) collective-permute-start(f32[4,56,512]{2,1,0:T(8,128)S(1)} %collective-permute-done.4.refs_2_), channel_id=1, source_target_pairs={{0,224},{32,0},{64,32},{96,64},{128,96},{160,128},{192,160},{224,1... | collective-permute-start | bytes 1376264 | tf_op jit(solution)/shard_map/ppermute | solution.py:257
  28.6 4.6 %form_1.1 = (bf16[10,2,512,512]{3,2,1,0:T(8,128)(2,1)}, f32[8,8,512]{2,1,0:T(8,128)S(1)}, f32[32,8,512]{2,1,0:T(8,128)S(1)}) custom-call(s32[9,10]{1,0:T(8,128)S(1)} %copy-done.2, bf16[8,16,512,48]{3,2,1,0:T(8,128)(2,1)S(1)} %prepare_rows.1.prepared_ref, f32[8,8,512]{2,1,0:T(8,128)S(1)} %bitcast.63, ...), custom_call_target="tpu_custom_call", output_to_operand_aliasing={{0}: (6, {}), {1}: (7, {}), {2}: (8, {})} | custom-call | flops 8000000000 | bytes 8388608 | tf_op jit(solution)/shard_map/form_1/pallas_call | solution.py:180
  33.2 3.9 %collective-permute-done.6.refs_4_ = f32[4,56,512]{2,1,0:T(8,128)S(1)} collective-permute-done((f32[4,56,512]{2,1,0:T(8,128)S(1)}, f32[4,56,512]{2,1,0:T(8,128)S(1)}, u32[]{:S(2)}, u32[]{:S(2)}) %collective-permute-start.6) | collective-permute-done | bytes 458784 | tf_op jit(solution)/shard_map/ppermute | solution.py:257
  37.1 3.7 %collective-permute-start.8 = (f32[4,56,512]{2,1,0:T(8,128)S(1)}, f32[4,56,512]{2,1,0:T(8,128)S(1)}, u32[]{:S(2)}, u32[]{:S(2)}) collective-permute-start(f32[4,56,512]{2,1,0:T(8,128)S(1)} %collective-permute-done.6.refs_4_), channel_id=1, source_target_pairs={{0,224},{32,0},{64,32},{96,64},{128,96},{160,128},{192,160},{224,1... | collective-permute-start | bytes 1376264 | tf_op jit(solution)/shard_map/ppermute | solution.py:257
  40.8 8.0 %form_2.1 = (bf16[10,2,512,512]{3,2,1,0:T(8,128)(2,1)}, f32[8,8,512]{2,1,0:T(8,128)S(1)}, f32[32,8,512]{2,1,0:T(8,128)S(1)}) custom-call(s32[9,10]{1,0:T(8,128)S(1)} %copy-done.2, bf16[8,16,512,48]{3,2,1,0:T(8,128)(2,1)S(1)} %prepare_rows.1.prepared_ref, f32[8,8,512]{2,1,0:T(8,128)S(1)} %bitcast.64, ...), custom_call_target="tpu_custom_call", output_to_operand_aliasing={{0}: (8, {}), {1}: (9, {}), {2}: (10, {})} | custom-call | flops 8000000000 | bytes 8388608 | tf_op jit(solution)/shard_map/form_2/pallas_call | solution.py:180
  48.8 3.3 %collective-permute-start.10 = (f32[2,56,512]{2,1,0:T(8,128)S(1)}, f32[2,56,512]{2,1,0:T(8,128)S(1)}, u32[]{:S(2)}, u32[]{:S(2)}) collective-permute-start(f32[2,56,512]{2,1,0:T(8,128)S(1)} %slice.61), channel_id=1, source_target_pairs={{0,224},{32,0},{64,32},{96,64},{128,96},{160,128},{192,160},{224,1... | collective-permute-start | bytes 688136 | tf_op jit(solution)/shard_map/ppermute | solution.py:257
  52.3 8.2 %form_3.1 = (bf16[10,2,512,512]{3,2,1,0:T(8,128)(2,1)}, f32[8,8,512]{2,1,0:T(8,128)S(1)}, f32[32,8,512]{2,1,0:T(8,128)S(1)}) custom-call(s32[9,10]{1,0:T(8,128)S(1)} %copy-done.2, bf16[8,16,512,48]{3,2,1,0:T(8,128)(2,1)S(1)} %prepare_rows.1.prepared_ref, f32[8,8,512]{2,1,0:T(8,128)S(1)} %bitcast.65, ...), custom_call_target="tpu_custom_call", output_to_operand_aliasing={{0}: (10, {}), {1}: (11, {}), {2}: (12, {})} | custom-call | flops 8000000000 | bytes 8388608 | tf_op jit(solution)/shard_map/form_3/pallas_call | solution.py:180
  60.5 14.4 %form_4.1 = (bf16[10,2,512,512]{3,2,1,0:T(8,128)(2,1)}, f32[10,8,512]{2,1,0:T(8,128)S(1)}, f32[32,8,512]{2,1,0:T(8,128)}) custom-call(s32[9,10]{1,0:T(8,128)S(1)} %copy-done.2, bf16[8,16,512,48]{3,2,1,0:T(8,128)(2,1)S(1)} %prepare_rows.1.prepared_ref, f32[8,8,512]{2,1,0:T(8,128)S(1)} %bitcast.66, ...), custom_call_target="tpu_custom_call", output_to_operand_aliasing={{0}: (12, {})} | custom-call | flops 8000000000 | bytes 8388608 | tf_op jit(solution)/shard_map/form_4/pallas_call | solution.py:180
  74.9 9.5 %all-to-all-start = ((f32[32,8,512]{2,1,0:T(8,128)}), f32[32,8,512]{2,1,0:T(8,128)S(1)}, u32[]{:S(2)}, u32[]{:S(2)}) async-start(f32[32,8,512]{2,1,0:T(8,128)} %get-tuple-element.38), calls=%async_computation | async-start | bytes 1048576 | tf_op jit(solution)/shard_map/all_to_all | solution.py:356
  84.3 3.6 %apply_late.1 = f32[8,8,512]{2,1,0:T(8,128)S(1)} custom-call(s32[9,10]{1,0:T(8,128)S(1)} %copy-done.2, bf16[10,2,512,512]{3,2,1,0:T(8,128)(2,1)} %get-tuple-element.36.pair_ref, f32[10,8,512]{2,1,0:T(8,128)S(1)} %get-tuple-element.37.field, f32[8,8,512]{2,1,0:T(8,128)S(1)} %get-tuple-element.34.refs_10_.refs_0_), custom_call_target="tpu_custom_call" | custom-call | flops 3000000000 | bytes 12582912 | tf_op jit(solution)/shard_map/apply_late/pallas_call | solution.py:238
  91.4 3.6 %collective-permute-start.13 = (f32[8,512]{1,0:T(8,128)S(1)}, f32[8,512]{1,0:T(8,128)S(1)}, u32[]{:S(2)}, u32[]{:S(2)}) collective-permute-start(f32[8,512]{1,0:T(8,128)S(1)} %get-tuple-element.44), channel_id=1, source_target_pairs={{0,4},{2,6},{4,0},{6,2},{1,5},{3,7},{5,1},{7,3},{8,12},{10,14},{12... | collective-permute-start | bytes 49160 | tf_op jit(solution)/shard_map/ppermute | solution.py:257
  95.1 3.1 %all-to-all-done = f32[32,8,512]{2,1,0:T(8,128)S(1)} async-done(((f32[32,8,512]{2,1,0:T(8,128)}), f32[32,8,512]{2,1,0:T(8,128)S(1)}, u32[]{:S(2)}, u32[]{:S(2)}) %all-to-all-start) | async-done | bytes 524320 | tf_op jit(solution)/shard_map/all_to_all | solution.py:356
  99.1 7.9 %all-to-all-start.1 = ((f32[32,8,512]{2,1,0:T(8,128)}), f32[32,8,512]{2,1,0:T(8,128)S(1)}, u32[]{:S(2)}, u32[]{:S(2)}) async-start(f32[32,8,512]{2,1,0:T(8,128)} %broadcast_in_dim.13), calls=%async_computation.1 | async-start | bytes 1048576 | tf_op jit(solution)/shard_map/all_to_all | solution.py:262
  108.3 3.4 %collective-permute-start.21 = (f32[2,8,512]{2,1,0:T(8,128)S(1)}, f32[2,8,512]{2,1,0:T(8,128)S(1)}, u32[]{:S(2)}, u32[]{:S(2)}) collective-permute-start(f32[2,8,512]{2,1,0:T(8,128)S(1)} %get-tuple-element.46), channel_id=1, source_target_pairs={{0,4},{2,6},{4,0},{6,2},{1,5},{3,7},{5,1},{7,3},{8,12},{10,14},{12... | collective-permute-start | bytes 98312 | tf_op jit(solution)/shard_map/ppermute | solution.py:257
  111.7 3.2 %collective-permute-start.22 = (f32[2,8,512]{2,1,0:T(8,128)S(1)}, f32[2,8,512]{2,1,0:T(8,128)S(1)}, u32[]{:S(2)}, u32[]{:S(2)}) collective-permute-start(f32[2,8,512]{2,1,0:T(8,128)S(1)} %get-tuple-element.46), channel_id=1, source_target_pairs={{0,6},{2,0},{4,2},{6,4},{1,7},{3,1},{5,3},{7,5},{8,14},{10,8},{12,... | collective-permute-start | bytes 98312 | tf_op jit(solution)/shard_map/ppermute | solution.py:257
  116.8 5.5 %apply_cols.1 = f32[32,8,512]{2,1,0:T(8,128)} custom-call(s32[9,10]{1,0:T(8,128)S(1)} %copy-done.2, bf16[10,2,512,512]{3,2,1,0:T(8,128)(2,1)} %get-tuple-element.36.pair_ref, f32[8,8,512]{2,1,0:T(8,128)S(1)} %bitcast.67), custom_call_target="tpu_custom_call" | custom-call | flops 3000000000 | bytes 12582912 | tf_op jit(solution)/shard_map/apply_cols/pallas_call | solution.py:238
  124.0 8.2 %all-to-all-start.2 = ((f32[32,8,512]{2,1,0:T(8,128)}), f32[32,8,512]{2,1,0:T(8,128)S(1)}, u32[]{:S(2)}, u32[]{:S(2)}) async-start(f32[32,8,512]{2,1,0:T(8,128)} %apply_cols.1), calls=%async_computation.2 | async-start | bytes 1048576 | tf_op jit(solution)/shard_map/all_to_all | solution.py:356
  132.2 5.7 %apply_rows.1 = f32[8,8,512]{2,1,0:T(8,128)S(1)} custom-call(s32[9,10]{1,0:T(8,128)S(1)} %copy-done.2, bf16[10,2,512,512]{3,2,1,0:T(8,128)(2,1)} %get-tuple-element.36.pair_ref, f32[32,8,512]{2,1,0:T(8,128)S(1)} %all-to-all-done.1.field), custom_call_target="tpu_custom_call" | custom-call | flops 3000000000 | bytes 12582912 | tf_op jit(solution)/shard_map/apply_rows/pallas_call | solution.py:238
  139.2 3.7 %collective-permute-start.16 = (f32[8,512]{1,0:T(8,128)S(1)}, f32[8,512]{1,0:T(8,128)S(1)}, u32[]{:S(2)}, u32[]{:S(2)}) collective-permute-start(f32[8,512]{1,0:T(8,128)S(1)} %get-tuple-element.39), channel_id=1, source_target_pairs={{0,6},{2,0},{4,2},{6,4},{1,7},{3,1},{5,3},{7,5},{8,14},{10,8},{12,... | collective-permute-start | bytes 49160 | tf_op jit(solution)/shard_map/ppermute | solution.py:257
  144.5 4.4 %all-to-all-done.2 = f32[32,8,512]{2,1,0:T(8,128)S(1)} async-done(((f32[32,8,512]{2,1,0:T(8,128)}), f32[32,8,512]{2,1,0:T(8,128)S(1)}, u32[]{:S(2)}, u32[]{:S(2)}) %all-to-all-start.2) | async-done | bytes 524320 | tf_op jit(solution)/shard_map/all_to_all | solution.py:356
  149.1 10.3 %all_to_all.25 = f32[8,8,512]{2,1,0:T(8,128)S(1)} all-to-all(f32[8,8,512]{2,1,0:T(8,128)S(1)} %broadcast_in_dim.14), channel_id=1, replica_groups=mesh['z'=8,'y'=4,'x'=4,'core'=2] {'x','core'}, dimensions={0} | all-to-all | bytes 262144 | tf_op jit(solution)/shard_map/all_to_all | solution.py:262
  159.5 18.3 %all_to_all.26 = f32[32,1,128]{2,1,0:T(1,128)S(1)} all-to-all(f32[32,1,128]{2,1,0:T(1,128)S(1)} %broadcast_in_dim.16), channel_id=1, replica_groups=mesh['z'=8,'y'=4,'x'=4,'core'=2] {'z','y'}, dimensions={0} | all-to-all | bytes 32768 | tf_op jit(solution)/shard_map/all_to_all | solution.py:262
  (71 shorter events, 26.7 us)
Async XLA Ops:
  0.9 6.8 %collective-permute-start.1 = (f32[56,512]{1,0:T(8,128)S(1)}, f32[56,512]{1,0:T(8,128)S(1)}, u32[]{:S(2)}, u32[]{:S(2)}) collective-permute-start(f32[56,512]{1,0:T(8,128)S(1)} %fusion), channel_id=1, source_target_pairs={{0,16},{8,24},{16,0},{24,8},{1,17},{9,25},{17,1},{25,9},{2,18},{10... | collective-permute-start | bytes 344072 | tf_op jit(solution)/shard_map/ppermute | solution.py:257
  2.5 7.0 %collective-permute-start = (f32[56,512]{1,0:T(8,128)S(1)}, f32[56,512]{1,0:T(8,128)S(1)}, u32[]{:S(2)}, u32[]{:S(2)}) collective-permute-start(f32[56,512]{1,0:T(8,128)S(1)} %fusion), channel_id=1, source_target_pairs={{0,8},{8,16},{16,24},{24,0},{1,9},{9,17},{17,25},{25,1},{2,10},{10... | collective-permute-start | bytes 344072 | tf_op jit(solution)/shard_map/ppermute | solution.py:257
  3.2 6.4 %collective-permute-start.2 = (f32[56,512]{1,0:T(8,128)S(1)}, f32[56,512]{1,0:T(8,128)S(1)}, u32[]{:S(2)}, u32[]{:S(2)}) collective-permute-start(f32[56,512]{1,0:T(8,128)S(1)} %fusion), channel_id=1, source_target_pairs={{0,24},{8,0},{16,8},{24,16},{1,25},{9,1},{17,9},{25,17},{2,26},{10... | collective-permute-start | bytes 344072 | tf_op jit(solution)/shard_map/ppermute | solution.py:257
  9.6 13.9 %collective-permute-start.4 = (f32[4,56,512]{2,1,0:T(8,128)S(1)}, f32[4,56,512]{2,1,0:T(8,128)S(1)}, u32[]{:S(2)}, u32[]{:S(2)}) collective-permute-start(f32[4,56,512]{2,1,0:T(8,128)S(1)} %pad_maximum_fusion.refs_0_), channel_id=1, source_target_pairs={{0,224},{32,0},{64,32},{96,64},{128,96},{160,128},{192,160},{224,1... | collective-permute-start | bytes 1376264 | tf_op jit(solution)/shard_map/ppermute | solution.py:257
  14.5 14.1 %collective-permute-start.3 = (f32[4,56,512]{2,1,0:T(8,128)S(1)}, f32[4,56,512]{2,1,0:T(8,128)S(1)}, u32[]{:S(2)}, u32[]{:S(2)}) collective-permute-start(f32[4,56,512]{2,1,0:T(8,128)S(1)} %pad_maximum_fusion.refs_0_), channel_id=1, source_target_pairs={{0,32},{32,64},{64,96},{96,128},{128,160},{160,192},{192,224},{224... | collective-permute-start | bytes 1376264 | tf_op jit(solution)/shard_map/ppermute | solution.py:257
  23.5 13.6 %collective-permute-start.6 = (f32[4,56,512]{2,1,0:T(8,128)S(1)}, f32[4,56,512]{2,1,0:T(8,128)S(1)}, u32[]{:S(2)}, u32[]{:S(2)}) collective-permute-start(f32[4,56,512]{2,1,0:T(8,128)S(1)} %collective-permute-done.4.refs_2_), channel_id=1, source_target_pairs={{0,224},{32,0},{64,32},{96,64},{128,96},{160,128},{192,160},{224,1... | collective-permute-start | bytes 1376264 | tf_op jit(solution)/shard_map/ppermute | solution.py:257
  28.6 12.2 %collective-permute-start.5 = (f32[4,56,512]{2,1,0:T(8,128)S(1)}, f32[4,56,512]{2,1,0:T(8,128)S(1)}, u32[]{:S(2)}, u32[]{:S(2)}) collective-permute-start(f32[4,56,512]{2,1,0:T(8,128)S(1)} %collective-permute-done.3.refs_1_), channel_id=1, source_target_pairs={{0,32},{32,64},{64,96},{96,128},{128,160},{160,192},{192,224},{224... | collective-permute-start | bytes 1376264 | tf_op jit(solution)/shard_map/ppermute | solution.py:257
  37.1 11.8 %collective-permute-start.8 = (f32[4,56,512]{2,1,0:T(8,128)S(1)}, f32[4,56,512]{2,1,0:T(8,128)S(1)}, u32[]{:S(2)}, u32[]{:S(2)}) collective-permute-start(f32[4,56,512]{2,1,0:T(8,128)S(1)} %collective-permute-done.6.refs_4_), channel_id=1, source_target_pairs={{0,224},{32,0},{64,32},{96,64},{128,96},{160,128},{192,160},{224,1... | collective-permute-start | bytes 1376264 | tf_op jit(solution)/shard_map/ppermute | solution.py:257
  40.8 11.4 %collective-permute-start.7 = (f32[4,56,512]{2,1,0:T(8,128)S(1)}, f32[4,56,512]{2,1,0:T(8,128)S(1)}, u32[]{:S(2)}, u32[]{:S(2)}) collective-permute-start(f32[4,56,512]{2,1,0:T(8,128)S(1)} %collective-permute-done.5.refs_3_), channel_id=1, source_target_pairs={{0,32},{32,64},{64,96},{96,128},{128,160},{160,192},{192,224},{224... | collective-permute-start | bytes 1376264 | tf_op jit(solution)/shard_map/ppermute | solution.py:257
  48.8 11.6 %collective-permute-start.10 = (f32[2,56,512]{2,1,0:T(8,128)S(1)}, f32[2,56,512]{2,1,0:T(8,128)S(1)}, u32[]{:S(2)}, u32[]{:S(2)}) collective-permute-start(f32[2,56,512]{2,1,0:T(8,128)S(1)} %slice.61), channel_id=1, source_target_pairs={{0,224},{32,0},{64,32},{96,64},{128,96},{160,128},{192,160},{224,1... | collective-permute-start | bytes 688136 | tf_op jit(solution)/shard_map/ppermute | solution.py:257
  52.2 8.3 %collective-permute-start.9 = (f32[2,56,512]{2,1,0:T(8,128)S(1)}, f32[2,56,512]{2,1,0:T(8,128)S(1)}, u32[]{:S(2)}, u32[]{:S(2)}) collective-permute-start(f32[2,56,512]{2,1,0:T(8,128)S(1)} %slice.60), channel_id=1, source_target_pairs={{0,32},{32,64},{64,96},{96,128},{128,160},{160,192},{192,224},{224... | collective-permute-start | bytes 688136 | tf_op jit(solution)/shard_map/ppermute | solution.py:257
  74.9 23.3 %all-to-all-start = ((f32[32,8,512]{2,1,0:T(8,128)}), f32[32,8,512]{2,1,0:T(8,128)S(1)}, u32[]{:S(2)}, u32[]{:S(2)}) async-start(f32[32,8,512]{2,1,0:T(8,128)} %get-tuple-element.38), calls=%async_computation | async-start | bytes 1048576 | tf_op jit(solution)/shard_map/all_to_all | solution.py:356
  88.0 1.3 collective-permute-start.11
  89.3 8.9 %collective-permute-start.12 = (f32[8,512]{1,0:T(8,128)S(1)}, f32[8,512]{1,0:T(8,128)S(1)}, u32[]{:S(2)}, u32[]{:S(2)}) collective-permute-start(f32[8,512]{1,0:T(8,128)S(1)} %get-tuple-element.42), channel_id=1, source_target_pairs={{0,6},{2,0},{4,2},{6,4},{1,7},{3,1},{5,3},{7,5},{8,14},{10,8},{12,... | collective-permute-start | bytes 49160 | tf_op jit(solution)/shard_map/ppermute | solution.py:257
  89.4 8.8 %collective-permute-start.14 = (f32[8,512]{1,0:T(8,128)S(1)}, f32[8,512]{1,0:T(8,128)S(1)}, u32[]{:S(2)}, u32[]{:S(2)}) collective-permute-start(f32[8,512]{1,0:T(8,128)S(1)} %get-tuple-element.43), channel_id=1, source_target_pairs={{0,2},{2,4},{4,6},{6,0},{1,3},{3,5},{5,7},{7,1},{8,10},{10,12},{12... | collective-permute-start | bytes 49160 | tf_op jit(solution)/shard_map/ppermute | solution.py:257
  91.4 6.8 %collective-permute-start.13 = (f32[8,512]{1,0:T(8,128)S(1)}, f32[8,512]{1,0:T(8,128)S(1)}, u32[]{:S(2)}, u32[]{:S(2)}) collective-permute-start(f32[8,512]{1,0:T(8,128)S(1)} %get-tuple-element.44), channel_id=1, source_target_pairs={{0,4},{2,6},{4,0},{6,2},{1,5},{3,7},{5,1},{7,3},{8,12},{10,14},{12... | collective-permute-start | bytes 49160 | tf_op jit(solution)/shard_map/ppermute | solution.py:257
  99.1 24.9 %all-to-all-start.1 = ((f32[32,8,512]{2,1,0:T(8,128)}), f32[32,8,512]{2,1,0:T(8,128)S(1)}, u32[]{:S(2)}, u32[]{:S(2)}) async-start(f32[32,8,512]{2,1,0:T(8,128)} %broadcast_in_dim.13), calls=%async_computation.1 | async-start | bytes 1048576 | tf_op jit(solution)/shard_map/all_to_all | solution.py:262
  108.3 6.6 %collective-permute-start.21 = (f32[2,8,512]{2,1,0:T(8,128)S(1)}, f32[2,8,512]{2,1,0:T(8,128)S(1)}, u32[]{:S(2)}, u32[]{:S(2)}) collective-permute-start(f32[2,8,512]{2,1,0:T(8,128)S(1)} %get-tuple-element.46), channel_id=1, source_target_pairs={{0,4},{2,6},{4,0},{6,2},{1,5},{3,7},{5,1},{7,3},{8,12},{10,14},{12... | collective-permute-start | bytes 98312 | tf_op jit(solution)/shard_map/ppermute | solution.py:257
  111.7 5.1 %collective-permute-start.20 = (f32[2,8,512]{2,1,0:T(8,128)S(1)}, f32[2,8,512]{2,1,0:T(8,128)S(1)}, u32[]{:S(2)}, u32[]{:S(2)}) collective-permute-start(f32[2,8,512]{2,1,0:T(8,128)S(1)} %get-tuple-element.46), channel_id=1, source_target_pairs={{0,2},{2,4},{4,6},{6,0},{1,3},{3,5},{5,7},{7,1},{8,10},{10,12},{12... | collective-permute-start | bytes 98312 | tf_op jit(solution)/shard_map/ppermute | solution.py:257
  111.7 5.1 %collective-permute-start.22 = (f32[2,8,512]{2,1,0:T(8,128)S(1)}, f32[2,8,512]{2,1,0:T(8,128)S(1)}, u32[]{:S(2)}, u32[]{:S(2)}) collective-permute-start(f32[2,8,512]{2,1,0:T(8,128)S(1)} %get-tuple-element.46), channel_id=1, source_target_pairs={{0,6},{2,0},{4,2},{6,4},{1,7},{3,1},{5,3},{7,5},{8,14},{10,8},{12,... | collective-permute-start | bytes 98312 | tf_op jit(solution)/shard_map/ppermute | solution.py:257
  124.0 25.0 %all-to-all-start.2 = ((f32[32,8,512]{2,1,0:T(8,128)}), f32[32,8,512]{2,1,0:T(8,128)S(1)}, u32[]{:S(2)}, u32[]{:S(2)}) async-start(f32[32,8,512]{2,1,0:T(8,128)} %apply_cols.1), calls=%async_computation.2 | async-start | bytes 1048576 | tf_op jit(solution)/shard_map/all_to_all | solution.py:356
  139.2 9.8 %collective-permute-start.16 = (f32[8,512]{1,0:T(8,128)S(1)}, f32[8,512]{1,0:T(8,128)S(1)}, u32[]{:S(2)}, u32[]{:S(2)}) collective-permute-start(f32[8,512]{1,0:T(8,128)S(1)} %get-tuple-element.39), channel_id=1, source_target_pairs={{0,6},{2,0},{4,2},{6,4},{1,7},{3,1},{5,3},{7,5},{8,14},{10,8},{12,... | collective-permute-start | bytes 49160 | tf_op jit(solution)/shard_map/ppermute | solution.py:257
  143.0 6.0 %collective-permute-start.18 = (f32[8,512]{1,0:T(8,128)S(1)}, f32[8,512]{1,0:T(8,128)S(1)}, u32[]{:S(2)}, u32[]{:S(2)}) collective-permute-start(f32[8,512]{1,0:T(8,128)S(1)} %get-tuple-element.40), channel_id=1, source_target_pairs={{0,2},{2,4},{4,6},{6,0},{1,3},{3,5},{5,7},{7,1},{8,10},{10,12},{12... | collective-permute-start | bytes 49160 | tf_op jit(solution)/shard_map/ppermute | solution.py:257
  143.0 6.1 %collective-permute-start.17 = (f32[8,512]{1,0:T(8,128)S(1)}, f32[8,512]{1,0:T(8,128)S(1)}, u32[]{:S(2)}, u32[]{:S(2)}) collective-permute-start(f32[8,512]{1,0:T(8,128)S(1)} %get-tuple-element.41), channel_id=1, source_target_pairs={{0,4},{2,6},{4,0},{6,2},{1,5},{3,7},{5,1},{7,3},{8,12},{10,14},{12... | collective-permute-start | bytes 49160 | tf_op jit(solution)/shard_map/ppermute | solution.py:257
  (5 other events, 37.5 us)

commit v14 on v13

--- a/solution.py
+++ b/solution.py
@@ -12,7 +12,7 @@
 TILE = 512
 ROW = ("z", "y")
 COL = ("x", "core")
-ROW_AT, ROW_NEAR, COL_AT, SOURCE, PLACE, STAGE, LIVE, CROSSING, LATE = range(9)
+ROW_AT, ROW_NEAR, COL_AT, SOURCE, PLACE, STAGE, LIVE, CROSSING, LATE, ROW_SEEN = range(10)
 LAST_STAGE = 4
 PER_STAGE = 2
 BY_ROWS = (((1,), (0,)), ((), ()))
@@ -220,7 +220,7 @@
         @pl.when(table[wanted, slot] != 0)
         def _():
             copy(slot).wait()
-            row = table[ROW_NEAR, slot]
+            row = table[ROW_SEEN if wanted == CROSSING else ROW_NEAR, slot]
             col = slot if col_at is None else table[col_at, slot]
             if wanted != CROSSING:
                 acc[row] += multiply(field[col], pair[slot, 0], pair[slot, 1], BY_COLS)
@@ -265,7 +265,7 @@
 def spread_near(piece):
     both = jnp.stack([piece, shift(piece, "core", 1)])
     near = [both] + [shift(both, "x", d) for d in range(1, lax.axis_size("x"))]
-    return jnp.stack(near, axis=1).reshape(2 * len(near), *piece.shape)
+    return jnp.concatenate(near, axis=0)
 
 
 def reduce_near(row_acc):
@@ -310,10 +310,11 @@
         source = jnp.where(behind == 0, 0, source)
         place = jnp.where((behind == size_z // 2) & upper, place - size_y // 2, place)
         crossing = ((z * size_y + y) * tiles + row) != (col * tiles + 2 * x + core)
-        near = jnp.where(lax.rem(row, 2) == core, 0, size_x)
-        near = near + lax.rem(x - row // 2 + size_x, size_x)
+        other = jnp.where(lax.rem(row, 2) == core, 0, 1)
+        along = lax.rem(x - row // 2 + size_x, size_x)
         out[ROW_AT, slot] = row
-        out[ROW_NEAR, slot] = near
+        out[ROW_NEAR, slot] = other * size_x + along
+        out[ROW_SEEN, slot] = 2 * along + other
         out[COL_AT, slot] = col
         out[SOURCE, slot] = source
         out[PLACE, slot] = place
@@ -347,7 +348,7 @@
         kernel,
         in_specs=[smem, smem],
         out_specs=smem,
-        out_shape=jax.ShapeDtypeStruct((9, pairs.shape[1]), jnp.int32),
+        out_shape=jax.ShapeDtypeStruct((10, pairs.shape[1]), jnp.int32),
         name="slot_table",
     )(pairs, valid)
 

time: 180 us -> 178 us (0.989)
  blocking collectives: 28.5 us -> 25.9 us
    ppermute x23, starting transfers between devices: 39.8 us -> 31.8 us  [shift(): lax.ppermute(value, axis, [(i, (i + distance) % size) for i in range(size)])]
    all_to_all x2, starting transfers between devices: 17.6 us -> 24.4 us  [combine(): by_col = lax.all_to_all(col_acc, ROW, 0, 0, tiled=True)]
    all_to_all x2, waiting for transfers between devices: 7.5 us -> 12.3 us  [combine(): by_col = lax.all_to_all(col_acc, ROW, 0, 0, tiled=True)]
    ppermute x23, waiting for transfers between devices: 13.1 us -> 10.5 us  [shift(): lax.ppermute(value, axis, [(i, (i + distance) % size) for i in range(size)])]
    all_to_all x2, blocking collectives: 28.5 us -> 25.9 us  [spread(): return lax.all_to_all(copies, axes, 0, 0, tiled=True)]
  transfers between devices with their start and end apart: 26 -> 26, of which waited for: 11 -> 9; matrix products, arithmetic and copies ran while one was open for 0% -> 0% of each run, Pallas kernels for 24% -> 28%
where the time goes in v14:
time: 178 us; the launch traced here: 177 us
  starting transfers between devices  64.3 us (36%)
  Pallas kernels  58.3 us (33%)
  blocking collectives  25.9 us (15%)
  waiting for transfers between devices  23.9 us (13%)
  local copies, waits for them, and re-layouts  2.1 us (1%)
  other arithmetic  2.06 us (1%)
    pallas_call x5, Pallas kernels, form_stage(): pl.pallas_call(functools.partial(stage_kernel, stage, len(places)), in_sp...  37.1 us
    ppermute x23, starting transfers between devices, shift(): lax.ppermute(value, axis, [(i, (i + distance) % size) for i in range(size)])  31.8 us
    all_to_all x2, blocking collectives, spread(): return lax.all_to_all(copies, axes, 0, 0, tiled=True)  25.9 us
    all_to_all x2, starting transfers between devices, combine(): by_col = lax.all_to_all(col_acc, ROW, 0, 0, tiled=True)  24.4 us
    pallas_call x3, Pallas kernels, apply_tiles(): pl.pallas_call(functools.partial(apply_kernel, wanted, col_at), in_specs=...  14 us
    all_to_all x2, waiting for transfers between devices, combine(): by_col = lax.all_to_all(col_acc, ROW, 0, 0, tiled=True)  12.3 us
    ppermute x23, waiting for transfers between devices, shift(): lax.ppermute(value, axis, [(i, (i + distance) % size) for i in range(size)])  10.5 us
    all_to_all x1, starting transfers between devices, spread(): return lax.all_to_all(copies, axes, 0, 0, tiled=True)  8.17 us
  transfers between devices with their start and end apart: 26, of which 9 were waited for; matrix products, arithmetic and copies ran while one was open for 0% of the time, Pallas kernels for 28%

profile of v14, /device:TPU:0, one launch (start us, length us, event | category | flops | bytes accessed | tf_op | source)
XLA Modules:
  0.0 177.0 jit_solution(3867963694503712234)
XLA Ops:
  3.2 2.6 %collective-permute-start.2 = (f32[56,512]{1,0:T(8,128)S(1)}, f32[56,512]{1,0:T(8,128)S(1)}, u32[]{:S(2)}, u32[]{:S(2)}) collective-permute-start(f32[56,512]{1,0:T(8,128)S(1)} %fusion), channel_id=1, source_target_pairs={{0,24},{8,0},{16,8},{24,16},{1,25},{9,1},{17,9},{25,17},{2,26},{10... | collective-permute-start | bytes 344072 | tf_op jit(solution)/shard_map/ppermute | solution.py:257
  9.6 4.9 %collective-permute-start.4 = (f32[4,56,512]{2,1,0:T(8,128)S(1)}, f32[4,56,512]{2,1,0:T(8,128)S(1)}, u32[]{:S(2)}, u32[]{:S(2)}) collective-permute-start(f32[4,56,512]{2,1,0:T(8,128)S(1)} %pad_maximum_fusion.refs_0_), channel_id=1, source_target_pairs={{0,224},{32,0},{64,32},{96,64},{128,96},{160,128},{192,160},{224,1... | collective-permute-start | bytes 1376264 | tf_op jit(solution)/shard_map/ppermute | solution.py:257
  15.6 5.1 %prepare_rows.1.prepared_ref = bf16[8,16,512,48]{3,2,1,0:T(8,128)(2,1)S(1)} custom-call(f32[48,4096]{1,0:T(8,128)S(1)} %bitcast.58), custom_call_target="tpu_custom_call" | custom-call | flops 100000000 | bytes 8388608 | tf_op jit(solution)/shard_map/prepare_rows/pallas_call | solution.py:66
  20.8 4.7 %form_0.1 = (bf16[10,2,512,512]{3,2,1,0:T(8,128)(2,1)}, f32[8,8,512]{2,1,0:T(8,128)S(1)}, f32[32,8,512]{2,1,0:T(8,128)S(1)}) custom-call(s32[10,10]{1,0:T(8,128)S(1)} %copy-done.2, bf16[8,16,512,48]{3,2,1,0:T(8,128)(2,1)S(1)} %prepare_rows.1.prepared_ref, f32[8,8,512]{2,1,0:T(8,128)S(1)} %bitcast.59, f32[4,56,512]{2,1,0:T(8,128)S(1)} %pad_maximum_fusion.refs_0_), custom_call_target="tpu_custom_call" | custom-call | flops 8000000000 | bytes 8388608 | tf_op jit(solution)/shard_map/form_0/pallas_call | solution.py:180
  25.5 3.1 %collective-permute-start.6 = (f32[4,56,512]{2,1,0:T(8,128)S(1)}, f32[4,56,512]{2,1,0:T(8,128)S(1)}, u32[]{:S(2)}, u32[]{:S(2)}) collective-permute-start(f32[4,56,512]{2,1,0:T(8,128)S(1)} %collective-permute-done.4.refs_2_), channel_id=1, source_target_pairs={{0,224},{32,0},{64,32},{96,64},{128,96},{160,128},{192,160},{224,1... | collective-permute-start | bytes 1376264 | tf_op jit(solution)/shard_map/ppermute | solution.py:257
  28.6 7.9 %form_1.1 = (bf16[10,2,512,512]{3,2,1,0:T(8,128)(2,1)}, f32[8,8,512]{2,1,0:T(8,128)S(1)}, f32[32,8,512]{2,1,0:T(8,128)S(1)}) custom-call(s32[10,10]{1,0:T(8,128)S(1)} %copy-done.2, bf16[8,16,512,48]{3,2,1,0:T(8,128)(2,1)S(1)} %prepare_rows.1.prepared_ref, f32[8,8,512]{2,1,0:T(8,128)S(1)} %bitcast.60, ...), custom_call_target="tpu_custom_call", output_to_operand_aliasing={{0}: (6, {}), {1}: (7, {}), {2}: (8, {})} | custom-call | flops 8000000000 | bytes 8388608 | tf_op jit(solution)/shard_map/form_1/pallas_call | solution.py:180
  37.1 3.7 %collective-permute-start.8 = (f32[4,56,512]{2,1,0:T(8,128)S(1)}, f32[4,56,512]{2,1,0:T(8,128)S(1)}, u32[]{:S(2)}, u32[]{:S(2)}) collective-permute-start(f32[4,56,512]{2,1,0:T(8,128)S(1)} %collective-permute-done.6.refs_4_), channel_id=1, source_target_pairs={{0,224},{32,0},{64,32},{96,64},{128,96},{160,128},{192,160},{224,1... | collective-permute-start | bytes 1376264 | tf_op jit(solution)/shard_map/ppermute | solution.py:257
  40.8 7.9 %form_2.1 = (bf16[10,2,512,512]{3,2,1,0:T(8,128)(2,1)}, f32[8,8,512]{2,1,0:T(8,128)S(1)}, f32[32,8,512]{2,1,0:T(8,128)S(1)}) custom-call(s32[10,10]{1,0:T(8,128)S(1)} %copy-done.2, bf16[8,16,512,48]{3,2,1,0:T(8,128)(2,1)S(1)} %prepare_rows.1.prepared_ref, f32[8,8,512]{2,1,0:T(8,128)S(1)} %bitcast.61, ...), custom_call_target="tpu_custom_call", output_to_operand_aliasing={{0}: (8, {}), {1}: (9, {}), {2}: (10, {})} | custom-call | flops 8000000000 | bytes 8388608 | tf_op jit(solution)/shard_map/form_2/pallas_call | solution.py:180
  48.7 3.4 %collective-permute-start.10 = (f32[2,56,512]{2,1,0:T(8,128)S(1)}, f32[2,56,512]{2,1,0:T(8,128)S(1)}, u32[]{:S(2)}, u32[]{:S(2)}) collective-permute-start(f32[2,56,512]{2,1,0:T(8,128)S(1)} %slice.61), channel_id=1, source_target_pairs={{0,224},{32,0},{64,32},{96,64},{128,96},{160,128},{192,160},{224,1... | collective-permute-start | bytes 688136 | tf_op jit(solution)/shard_map/ppermute | solution.py:257
  52.3 8.0 %form_3.1 = (bf16[10,2,512,512]{3,2,1,0:T(8,128)(2,1)}, f32[8,8,512]{2,1,0:T(8,128)S(1)}, f32[32,8,512]{2,1,0:T(8,128)S(1)}) custom-call(s32[10,10]{1,0:T(8,128)S(1)} %copy-done.2, bf16[8,16,512,48]{3,2,1,0:T(8,128)(2,1)S(1)} %prepare_rows.1.prepared_ref, f32[8,8,512]{2,1,0:T(8,128)S(1)} %bitcast.62, ...), custom_call_target="tpu_custom_call", output_to_operand_aliasing={{0}: (10, {}), {1}: (11, {}), {2}: (12, {})} | custom-call | flops 8000000000 | bytes 8388608 | tf_op jit(solution)/shard_map/form_3/pallas_call | solution.py:180
  60.3 8.5 %form_4.1 = (bf16[10,2,512,512]{3,2,1,0:T(8,128)(2,1)}, f32[10,8,512]{2,1,0:T(8,128)S(1)}, f32[32,8,512]{2,1,0:T(8,128)}) custom-call(s32[10,10]{1,0:T(8,128)S(1)} %copy-done.2, bf16[8,16,512,48]{3,2,1,0:T(8,128)(2,1)S(1)} %prepare_rows.1.prepared_ref, f32[8,8,512]{2,1,0:T(8,128)S(1)} %bitcast.63, ...), custom_call_target="tpu_custom_call", output_to_operand_aliasing={{0}: (12, {})} | custom-call | flops 8000000000 | bytes 8388608 | tf_op jit(solution)/shard_map/form_4/pallas_call | solution.py:180
  68.9 15.8 %all-to-all-start = ((f32[32,8,512]{2,1,0:T(8,128)}), f32[32,8,512]{2,1,0:T(8,128)S(1)}, u32[]{:S(2)}, u32[]{:S(2)}) async-start(f32[32,8,512]{2,1,0:T(8,128)} %get-tuple-element.38), calls=%async_computation | async-start | bytes 1048576 | tf_op jit(solution)/shard_map/all_to_all | solution.py:357
  84.6 2.8 %apply_late.1 = f32[8,8,512]{2,1,0:T(8,128)S(1)} custom-call(s32[10,10]{1,0:T(8,128)S(1)} %copy-done.2, bf16[10,2,512,512]{3,2,1,0:T(8,128)(2,1)} %get-tuple-element.36.pair_ref, f32[10,8,512]{2,1,0:T(8,128)S(1)} %get-tuple-element.37.field, f32[8,8,512]{2,1,0:T(8,128)S(1)} %get-tuple-element.34.refs_10_.refs_0_), custom_call_target="tpu_custom_call" | custom-call | flops 3000000000 | bytes 12582912 | tf_op jit(solution)/shard_map/apply_late/pallas_call | solution.py:238
  88.8 2.0 %collective-permute-start.12 = (f32[8,512]{1,0:T(8,128)S(1)}, f32[8,512]{1,0:T(8,128)S(1)}, u32[]{:S(2)}, u32[]{:S(2)}) collective-permute-start(f32[8,512]{1,0:T(8,128)S(1)} %get-tuple-element.44), channel_id=1, source_target_pairs={{0,6},{2,0},{4,2},{6,4},{1,7},{3,1},{5,3},{7,5},{8,14},{10,8},{12,... | collective-permute-start | bytes 49160 | tf_op jit(solution)/shard_map/ppermute | solution.py:257
  92.4 6.0 %all-to-all-done = f32[32,8,512]{2,1,0:T(8,128)S(1)} async-done(((f32[32,8,512]{2,1,0:T(8,128)}), f32[32,8,512]{2,1,0:T(8,128)S(1)}, u32[]{:S(2)}, u32[]{:S(2)}) %all-to-all-start) | async-done | bytes 524320 | tf_op jit(solution)/shard_map/all_to_all | solution.py:357
  99.4 8.2 %all-to-all-start.1 = ((f32[32,8,512]{2,1,0:T(8,128)}), f32[32,8,512]{2,1,0:T(8,128)S(1)}, u32[]{:S(2)}, u32[]{:S(2)}) async-start(f32[32,8,512]{2,1,0:T(8,128)} %broadcast_in_dim.13), calls=%async_computation.1 | async-start | bytes 1048576 | tf_op jit(solution)/shard_map/all_to_all | solution.py:262
  108.9 3.2 %collective-permute-start.22 = (f32[2,8,512]{2,1,0:T(8,128)S(1)}, f32[2,8,512]{2,1,0:T(8,128)S(1)}, u32[]{:S(2)}, u32[]{:S(2)}) collective-permute-start(f32[2,8,512]{2,1,0:T(8,128)S(1)} %pad_maximum_fusion.1), channel_id=1, source_target_pairs={{0,6},{2,0},{4,2},{6,4},{1,7},{3,1},{5,3},{7,5},{8,14},{10,8},{12,... | collective-permute-start | bytes 98312 | tf_op jit(solution)/shard_map/ppermute | solution.py:257
  113.0 4.5 %collective-permute-done.20 = f32[2,8,512]{2,1,0:T(8,128)S(1)} collective-permute-done((f32[2,8,512]{2,1,0:T(8,128)S(1)}, f32[2,8,512]{2,1,0:T(8,128)S(1)}, u32[]{:S(2)}, u32[]{:S(2)}) %collective-permute-start.20) | collective-permute-done | bytes 32800 | tf_op jit(solution)/shard_map/ppermute | solution.py:257
  117.6 5.5 %apply_cols.1 = f32[32,8,512]{2,1,0:T(8,128)} custom-call(s32[10,10]{1,0:T(8,128)S(1)} %copy-done.2, bf16[10,2,512,512]{3,2,1,0:T(8,128)(2,1)} %get-tuple-element.36.pair_ref, f32[8,8,512]{2,1,0:T(8,128)S(1)} %constant_dynamic-update-slice_fusion.field), custom_call_target="tpu_custom_call" | custom-call | flops 3000000000 | bytes 12582912 | tf_op jit(solution)/shard_map/apply_cols/pallas_call | solution.py:238
  124.3 8.6 %all-to-all-start.2 = ((f32[32,8,512]{2,1,0:T(8,128)}), f32[32,8,512]{2,1,0:T(8,128)S(1)}, u32[]{:S(2)}, u32[]{:S(2)}) async-start(f32[32,8,512]{2,1,0:T(8,128)} %apply_cols.1), calls=%async_computation.2 | async-start | bytes 1048576 | tf_op jit(solution)/shard_map/all_to_all | solution.py:357
  133.0 5.7 %apply_rows.1 = f32[8,8,512]{2,1,0:T(8,128)S(1)} custom-call(s32[10,10]{1,0:T(8,128)S(1)} %copy-done.2, bf16[10,2,512,512]{3,2,1,0:T(8,128)(2,1)} %get-tuple-element.36.pair_ref, f32[32,8,512]{2,1,0:T(8,128)S(1)} %all-to-all-done.1.field), custom_call_target="tpu_custom_call" | custom-call | flops 3000000000 | bytes 12582912 | tf_op jit(solution)/shard_map/apply_rows/pallas_call | solution.py:238
  143.7 6.2 %all-to-all-done.2 = f32[32,8,512]{2,1,0:T(8,128)S(1)} async-done(((f32[32,8,512]{2,1,0:T(8,128)}), f32[32,8,512]{2,1,0:T(8,128)S(1)}, u32[]{:S(2)}, u32[]{:S(2)}) %all-to-all-start.2) | async-done | bytes 524320 | tf_op jit(solution)/shard_map/all_to_all | solution.py:357
  150.1 8.8 %all_to_all.25 = f32[8,8,512]{2,1,0:T(8,128)S(1)} all-to-all(f32[8,8,512]{2,1,0:T(8,128)S(1)} %broadcast_in_dim.14), channel_id=1, replica_groups=mesh['z'=8,'y'=4,'x'=4,'core'=2] {'x','core'}, dimensions={0} | all-to-all | bytes 262144 | tf_op jit(solution)/shard_map/all_to_all | solution.py:262
  159.0 17.2 %all_to_all.26 = f32[32,1,128]{2,1,0:T(1,128)S(1)} all-to-all(f32[32,1,128]{2,1,0:T(1,128)S(1)} %broadcast_in_dim.16), channel_id=1, replica_groups=mesh['z'=8,'y'=4,'x'=4,'core'=2] {'z','y'}, dimensions={0} | all-to-all | bytes 32768 | tf_op jit(solution)/shard_map/all_to_all | solution.py:262
  (73 shorter events, 22.1 us)
Async XLA Ops:
  0.9 6.9 %collective-permute-start.1 = (f32[56,512]{1,0:T(8,128)S(1)}, f32[56,512]{1,0:T(8,128)S(1)}, u32[]{:S(2)}, u32[]{:S(2)}) collective-permute-start(f32[56,512]{1,0:T(8,128)S(1)} %fusion), channel_id=1, source_target_pairs={{0,16},{8,24},{16,0},{24,8},{1,17},{9,25},{17,1},{25,9},{2,18},{10... | collective-permute-start | bytes 344072 | tf_op jit(solution)/shard_map/ppermute | solution.py:257
  2.5 7.0 %collective-permute-start = (f32[56,512]{1,0:T(8,128)S(1)}, f32[56,512]{1,0:T(8,128)S(1)}, u32[]{:S(2)}, u32[]{:S(2)}) collective-permute-start(f32[56,512]{1,0:T(8,128)S(1)} %fusion), channel_id=1, source_target_pairs={{0,8},{8,16},{16,24},{24,0},{1,9},{9,17},{17,25},{25,1},{2,10},{10... | collective-permute-start | bytes 344072 | tf_op jit(solution)/shard_map/ppermute | solution.py:257
  3.2 6.4 %collective-permute-start.2 = (f32[56,512]{1,0:T(8,128)S(1)}, f32[56,512]{1,0:T(8,128)S(1)}, u32[]{:S(2)}, u32[]{:S(2)}) collective-permute-start(f32[56,512]{1,0:T(8,128)S(1)} %fusion), channel_id=1, source_target_pairs={{0,24},{8,0},{16,8},{24,16},{1,25},{9,1},{17,9},{25,17},{2,26},{10... | collective-permute-start | bytes 344072 | tf_op jit(solution)/shard_map/ppermute | solution.py:257
  9.6 15.9 %collective-permute-start.4 = (f32[4,56,512]{2,1,0:T(8,128)S(1)}, f32[4,56,512]{2,1,0:T(8,128)S(1)}, u32[]{:S(2)}, u32[]{:S(2)}) collective-permute-start(f32[4,56,512]{2,1,0:T(8,128)S(1)} %pad_maximum_fusion.refs_0_), channel_id=1, source_target_pairs={{0,224},{32,0},{64,32},{96,64},{128,96},{160,128},{192,160},{224,1... | collective-permute-start | bytes 1376264 | tf_op jit(solution)/shard_map/ppermute | solution.py:257
  14.5 14.1 %collective-permute-start.3 = (f32[4,56,512]{2,1,0:T(8,128)S(1)}, f32[4,56,512]{2,1,0:T(8,128)S(1)}, u32[]{:S(2)}, u32[]{:S(2)}) collective-permute-start(f32[4,56,512]{2,1,0:T(8,128)S(1)} %pad_maximum_fusion.refs_0_), channel_id=1, source_target_pairs={{0,32},{32,64},{64,96},{96,128},{128,160},{160,192},{192,224},{224... | collective-permute-start | bytes 1376264 | tf_op jit(solution)/shard_map/ppermute | solution.py:257
  25.5 11.6 %collective-permute-start.6 = (f32[4,56,512]{2,1,0:T(8,128)S(1)}, f32[4,56,512]{2,1,0:T(8,128)S(1)}, u32[]{:S(2)}, u32[]{:S(2)}) collective-permute-start(f32[4,56,512]{2,1,0:T(8,128)S(1)} %collective-permute-done.4.refs_2_), channel_id=1, source_target_pairs={{0,224},{32,0},{64,32},{96,64},{128,96},{160,128},{192,160},{224,1... | collective-permute-start | bytes 1376264 | tf_op jit(solution)/shard_map/ppermute | solution.py:257
  28.6 12.2 %collective-permute-start.5 = (f32[4,56,512]{2,1,0:T(8,128)S(1)}, f32[4,56,512]{2,1,0:T(8,128)S(1)}, u32[]{:S(2)}, u32[]{:S(2)}) collective-permute-start(f32[4,56,512]{2,1,0:T(8,128)S(1)} %collective-permute-done.3.refs_1_), channel_id=1, source_target_pairs={{0,32},{32,64},{64,96},{96,128},{128,160},{160,192},{192,224},{224... | collective-permute-start | bytes 1376264 | tf_op jit(solution)/shard_map/ppermute | solution.py:257
  37.1 11.6 %collective-permute-start.8 = (f32[4,56,512]{2,1,0:T(8,128)S(1)}, f32[4,56,512]{2,1,0:T(8,128)S(1)}, u32[]{:S(2)}, u32[]{:S(2)}) collective-permute-start(f32[4,56,512]{2,1,0:T(8,128)S(1)} %collective-permute-done.6.refs_4_), channel_id=1, source_target_pairs={{0,224},{32,0},{64,32},{96,64},{128,96},{160,128},{192,160},{224,1... | collective-permute-start | bytes 1376264 | tf_op jit(solution)/shard_map/ppermute | solution.py:257
  40.8 11.4 %collective-permute-start.7 = (f32[4,56,512]{2,1,0:T(8,128)S(1)}, f32[4,56,512]{2,1,0:T(8,128)S(1)}, u32[]{:S(2)}, u32[]{:S(2)}) collective-permute-start(f32[4,56,512]{2,1,0:T(8,128)S(1)} %collective-permute-done.5.refs_3_), channel_id=1, source_target_pairs={{0,32},{32,64},{64,96},{96,128},{128,160},{160,192},{192,224},{224... | collective-permute-start | bytes 1376264 | tf_op jit(solution)/shard_map/ppermute | solution.py:257
  48.7 11.6 %collective-permute-start.10 = (f32[2,56,512]{2,1,0:T(8,128)S(1)}, f32[2,56,512]{2,1,0:T(8,128)S(1)}, u32[]{:S(2)}, u32[]{:S(2)}) collective-permute-start(f32[2,56,512]{2,1,0:T(8,128)S(1)} %slice.61), channel_id=1, source_target_pairs={{0,224},{32,0},{64,32},{96,64},{128,96},{160,128},{192,160},{224,1... | collective-permute-start | bytes 688136 | tf_op jit(solution)/shard_map/ppermute | solution.py:257
  52.2 8.1 %collective-permute-start.9 = (f32[2,56,512]{2,1,0:T(8,128)S(1)}, f32[2,56,512]{2,1,0:T(8,128)S(1)}, u32[]{:S(2)}, u32[]{:S(2)}) collective-permute-start(f32[2,56,512]{2,1,0:T(8,128)S(1)} %slice.60), channel_id=1, source_target_pairs={{0,32},{32,64},{64,96},{96,128},{128,160},{160,192},{192,224},{224... | collective-permute-start | bytes 688136 | tf_op jit(solution)/shard_map/ppermute | solution.py:257
  68.9 29.6 %all-to-all-start = ((f32[32,8,512]{2,1,0:T(8,128)}), f32[32,8,512]{2,1,0:T(8,128)S(1)}, u32[]{:S(2)}, u32[]{:S(2)}) async-start(f32[32,8,512]{2,1,0:T(8,128)} %get-tuple-element.38), calls=%async_computation | async-start | bytes 1048576 | tf_op jit(solution)/shard_map/all_to_all | solution.py:357
  87.5 1.3 collective-permute-start.11
  88.8 9.7 %collective-permute-start.12 = (f32[8,512]{1,0:T(8,128)S(1)}, f32[8,512]{1,0:T(8,128)S(1)}, u32[]{:S(2)}, u32[]{:S(2)}) collective-permute-start(f32[8,512]{1,0:T(8,128)S(1)} %get-tuple-element.44), channel_id=1, source_target_pairs={{0,6},{2,0},{4,2},{6,4},{1,7},{3,1},{5,3},{7,5},{8,14},{10,8},{12,... | collective-permute-start | bytes 49160 | tf_op jit(solution)/shard_map/ppermute | solution.py:257
  90.9 7.6 %collective-permute-start.14 = (f32[8,512]{1,0:T(8,128)S(1)}, f32[8,512]{1,0:T(8,128)S(1)}, u32[]{:S(2)}, u32[]{:S(2)}) collective-permute-start(f32[8,512]{1,0:T(8,128)S(1)} %get-tuple-element.45), channel_id=1, source_target_pairs={{0,2},{2,4},{4,6},{6,0},{1,3},{3,5},{5,7},{7,1},{8,10},{10,12},{12... | collective-permute-start | bytes 49160 | tf_op jit(solution)/shard_map/ppermute | solution.py:257
  90.9 7.6 %collective-permute-start.13 = (f32[8,512]{1,0:T(8,128)S(1)}, f32[8,512]{1,0:T(8,128)S(1)}, u32[]{:S(2)}, u32[]{:S(2)}) collective-permute-start(f32[8,512]{1,0:T(8,128)S(1)} %get-tuple-element.46), channel_id=1, source_target_pairs={{0,4},{2,6},{4,0},{6,2},{1,5},{3,7},{5,1},{7,3},{8,12},{10,14},{12... | collective-permute-start | bytes 49160 | tf_op jit(solution)/shard_map/ppermute | solution.py:257
  99.4 24.9 %all-to-all-start.1 = ((f32[32,8,512]{2,1,0:T(8,128)}), f32[32,8,512]{2,1,0:T(8,128)S(1)}, u32[]{:S(2)}, u32[]{:S(2)}) async-start(f32[32,8,512]{2,1,0:T(8,128)} %broadcast_in_dim.13), calls=%async_computation.1 | async-start | bytes 1048576 | tf_op jit(solution)/shard_map/all_to_all | solution.py:262
  108.9 8.7 %collective-permute-start.22 = (f32[2,8,512]{2,1,0:T(8,128)S(1)}, f32[2,8,512]{2,1,0:T(8,128)S(1)}, u32[]{:S(2)}, u32[]{:S(2)}) collective-permute-start(f32[2,8,512]{2,1,0:T(8,128)S(1)} %pad_maximum_fusion.1), channel_id=1, source_target_pairs={{0,6},{2,0},{4,2},{6,4},{1,7},{3,1},{5,3},{7,5},{8,14},{10,8},{12,... | collective-permute-start | bytes 98312 | tf_op jit(solution)/shard_map/ppermute | solution.py:257
  112.1 5.5 %collective-permute-start.21 = (f32[2,8,512]{2,1,0:T(8,128)S(1)}, f32[2,8,512]{2,1,0:T(8,128)S(1)}, u32[]{:S(2)}, u32[]{:S(2)}) collective-permute-start(f32[2,8,512]{2,1,0:T(8,128)S(1)} %pad_maximum_fusion.1), channel_id=1, source_target_pairs={{0,4},{2,6},{4,0},{6,2},{1,5},{3,7},{5,1},{7,3},{8,12},{10,14},{12... | collective-permute-start | bytes 98312 | tf_op jit(solution)/shard_map/ppermute | solution.py:257
  112.1 5.5 %collective-permute-start.20 = (f32[2,8,512]{2,1,0:T(8,128)S(1)}, f32[2,8,512]{2,1,0:T(8,128)S(1)}, u32[]{:S(2)}, u32[]{:S(2)}) collective-permute-start(f32[2,8,512]{2,1,0:T(8,128)S(1)} %pad_maximum_fusion.1), channel_id=1, source_target_pairs={{0,2},{2,4},{4,6},{6,0},{1,3},{3,5},{5,7},{7,1},{8,10},{10,12},{12... | collective-permute-start | bytes 98312 | tf_op jit(solution)/shard_map/ppermute | solution.py:257
  124.3 25.6 %all-to-all-start.2 = ((f32[32,8,512]{2,1,0:T(8,128)}), f32[32,8,512]{2,1,0:T(8,128)S(1)}, u32[]{:S(2)}, u32[]{:S(2)}) async-start(f32[32,8,512]{2,1,0:T(8,128)} %apply_cols.1), calls=%async_computation.2 | async-start | bytes 1048576 | tf_op jit(solution)/shard_map/all_to_all | solution.py:357
  140.0 10.0 %collective-permute-start.16 = (f32[8,512]{1,0:T(8,128)S(1)}, f32[8,512]{1,0:T(8,128)S(1)}, u32[]{:S(2)}, u32[]{:S(2)}) collective-permute-start(f32[8,512]{1,0:T(8,128)S(1)} %get-tuple-element.41), channel_id=1, source_target_pairs={{0,6},{2,0},{4,2},{6,4},{1,7},{3,1},{5,3},{7,5},{8,14},{10,8},{12,... | collective-permute-start | bytes 49160 | tf_op jit(solution)/shard_map/ppermute | solution.py:257
  140.5 9.5 %collective-permute-start.18 = (f32[8,512]{1,0:T(8,128)S(1)}, f32[8,512]{1,0:T(8,128)S(1)}, u32[]{:S(2)}, u32[]{:S(2)}) collective-permute-start(f32[8,512]{1,0:T(8,128)S(1)} %get-tuple-element.42), channel_id=1, source_target_pairs={{0,2},{2,4},{4,6},{6,0},{1,3},{3,5},{5,7},{7,1},{8,10},{10,12},{12... | collective-permute-start | bytes 49160 | tf_op jit(solution)/shard_map/ppermute | solution.py:257
  142.1 7.9 %collective-permute-start.17 = (f32[8,512]{1,0:T(8,128)S(1)}, f32[8,512]{1,0:T(8,128)S(1)}, u32[]{:S(2)}, u32[]{:S(2)}) collective-permute-start(f32[8,512]{1,0:T(8,128)S(1)} %get-tuple-element.43), channel_id=1, source_target_pairs={{0,4},{2,6},{4,0},{6,2},{1,5},{3,7},{5,1},{7,3},{8,12},{10,14},{12... | collective-permute-start | bytes 49160 | tf_op jit(solution)/shard_map/ppermute | solution.py:257
  (5 other events, 37.5 us)
